TPU v7x, 32 devices: a whole 2x2x4 slice. The times are simulated.
32 devices in a mesh: wide: 16 (over z, x, core), narrow: 2 (over y).
Axes of the slice: x: 2, y: 2, z: 4, core: 2. Of those that a mesh axis runs over, the one named last changes fastest.
Arguments:
- object_field: float32 [2, 4096, 1024], P(None, 'wide', 'narrow'), may hold values from -1 to 1
- probe: float32 [2, 256, 256], replicated, may hold values from -6 to 6
- intensity: float32 [16, 2, 8, 256, 256], P('wide', 'narrow'), may hold values from 0.05 to 4
- row_offsets: int32 [16, 2, 8], P('wide', 'narrow'), may hold values from 0 to 255
- col_offsets: int32 [16, 2, 8], P('wide', 'narrow'), may hold values from 0 to 511
- counts: int32 [16, 2], P('wide', 'narrow'), may hold values from 2 to 8, as said below
Outputs:
- new_object: float32 [2, 4096, 1024], P(None, 'wide', 'narrow')
- new_probe: float32 [2, 256, 256], replicated
Inputs may be any that keep to these rules, and one draw needn't show every extreme that they name: `counts`: the number of live slots of each tile; slots at or beyond it hold offsets and intensities that are not used; some tile has exactly 8, some exactly 2.
All inputs are finite; a program needn't handle non-finite values.
Results may differ from a plain program's by a relative error of at most 0.0003.
Values sent between devices are 32-bit elements; how exact they have to be, the bound alone decides.
No kernel may reach another device: no remote copies, remote signals or barrier semaphores. Data moves between devices by JAX's collectives and lax.ppermute only.
A program may use at most 64 MiB of HBM per device.

v0:
```python
import math

import jax
import jax.numpy as jnp
from jax import lax
from jax.sharding import PartitionSpec as P

PR = 256
H = 128
TR = 256
TC = 512


mix_object = 0.5
mix_probe = 0.5


def from_behind(x, axis, by):
    peers = lax.axis_size(axis)
    pairs = [(i, i + by) for i in range(peers) if 0 <= i + by < peers]
    return lax.ppermute(x, axis, pairs)


def extended_2(x, sides, width):
    for axis, dim in sides:
        peers, length = (lax.axis_size(axis), x.shape[dim])
        up = [(i, (i + 1) % peers) for i in range(peers - 1)]
        down = [(j, i) for i, j in up]
        last = lax.slice_in_dim(x, length - width, length, axis=dim)
        initial = lax.slice_in_dim(x, 0, width, axis=dim)
        before = lax.ppermute(last, axis, up)
        after = lax.ppermute(initial, axis, down)
        x = jnp.concatenate([before, x, after], axis=dim)
    return x


def dft_tables(length):
    indices = lax.iota(jnp.int32, length)
    product = indices[:, None] * indices[None, :] % length
    angles = product.astype(jnp.float32) * (2.0 * math.pi / length)
    norm_scale = 1.0 / math.sqrt(length)
    return (jnp.cos(angles) * norm_scale, -jnp.sin(angles) * norm_scale)


def dot_high(left_matrix, right_matrix):
    return jnp.dot(
        left_matrix,
        right_matrix,
        preferred_element_type=jnp.float32,
        precision=lax.Precision.HIGHEST,
    )


def complex_product(left_real, left_imag, right_real, right_imag):
    out_real = dot_high(left_real, right_real) - dot_high(left_imag, right_imag)
    out_imag = dot_high(left_real, right_imag) + dot_high(left_imag, right_real)
    return (out_real, out_imag)


def exit_difference(probe, patch, measured, cos_table, sin_table):
    exit_real = probe[0] * patch[0] - probe[1] * patch[1]
    exit_imag = probe[0] * patch[1] + probe[1] * patch[0]
    half_real, half_imag = complex_product(cos_table, sin_table, exit_real, exit_imag)
    far_real, far_imag = complex_product(half_real, half_imag, cos_table, sin_table)
    factor = jnp.sqrt(measured) / jnp.sqrt(far_real * far_real + far_imag * far_imag + 1.0)
    proj_real = far_real * factor
    proj_imag = far_imag * factor
    back_half_real, back_half_imag = complex_product(cos_table, -sin_table, proj_real, proj_imag)
    back_real, back_imag = complex_product(back_half_real, back_half_imag, cos_table, -sin_table)
    return (back_real - exit_real, back_imag - exit_imag)


def fold_rims(stacked):
    from_right = from_behind(stacked[:, :, :H], "narrow", -1)
    from_left = from_behind(stacked[:, :, TC + H :], "narrow", 1)
    middle = stacked[:, :, H : TC + H]
    middle = middle.at[:, :, TC - H :].add(from_right)
    middle = middle.at[:, :, :H].add(from_left)
    from_below = from_behind(middle[:, :H, :], "wide", -1)
    from_above = from_behind(middle[:, TR + H :, :], "wide", 1)
    centre = middle[:, H : TR + H, :]
    centre = centre.at[:, TR - H :, :].add(from_below)
    centre = centre.at[:, :H, :].add(from_above)
    return centre


def body(object_field, probe, intensity, row_offsets, col_offsets, counts):
    extended = extended_2(object_field, (("wide", 1), ("narrow", 2)), H)
    cos_table, sin_table = dft_tables(PR)
    power = probe[0] * probe[0] + probe[1] * probe[1]
    channels = 3

    def visit(slot_index, totals):
        grad_ext, probe_grad, probe_weight = totals
        row_start = row_offsets[0, 0, slot_index]
        col_start = col_offsets[0, 0, slot_index]
        zero_index = row_start * 0
        patch = lax.dynamic_slice(extended, (zero_index, row_start, col_start), (2, PR, PR))
        diff_real, diff_imag = exit_difference(
            probe, patch, intensity[0, 0, slot_index], cos_table, sin_table
        )
        object_real = probe[0] * diff_real + probe[1] * diff_imag
        object_imag = probe[0] * diff_imag - probe[1] * diff_real
        pieces = [object_real, object_imag, power]
        old_grad = lax.dynamic_slice(
            grad_ext, (zero_index, row_start, col_start), (channels, PR, PR)
        )
        grad_ext = lax.dynamic_update_slice(
            grad_ext, old_grad + jnp.stack(pieces), (zero_index, row_start, col_start)
        )
        grad_real = patch[0] * diff_real + patch[1] * diff_imag
        grad_imag = patch[0] * diff_imag - patch[1] * diff_real
        probe_grad = probe_grad + jnp.stack([grad_real, grad_imag])
        probe_weight = probe_weight + patch[0] * patch[0] + patch[1] * patch[1]
        return (grad_ext, probe_grad, probe_weight)

    initial = (
        jnp.zeros((channels, TR + 2 * H, TC + 2 * H), jnp.float32),
        jnp.zeros((2, PR, PR), jnp.float32),
        jnp.zeros((PR, PR), jnp.float32),
    )
    grad_ext, probe_grad, probe_weight = lax.fori_loop(0, counts[0, 0], visit, initial)
    folded = fold_rims(grad_ext)
    coverage = folded[2]
    cover_peak = lax.pmax(jnp.max(coverage), ("wide", "narrow"))
    object_denom = (1.0 - mix_object) * coverage + mix_object * cover_peak
    new_object = object_field + folded[:2] / object_denom[None]
    terms = jnp.concatenate([probe_grad, probe_weight[None]], axis=0)
    summed = lax.psum(terms, ("wide", "narrow"))
    probe_denom = (1.0 - mix_probe) * summed[2] + mix_probe * jnp.max(summed[2])
    new_probe = probe + summed[:2] / probe_denom[None]
    return (new_object, new_probe)


def solution(mesh):
    placed = (
        P(None, "wide", "narrow"),
        P(),
        P("wide", "narrow", None, None, None),
        P("wide", "narrow", None),
        P("wide", "narrow", None),
        P("wide", "narrow"),
    )
    return jax.shard_map(
        body,
        mesh=mesh,
        in_specs=placed,
        out_specs=(P(None, "wide", "narrow"), P()),
        check_vma=False,
    )
```

profile of v0, /device:TPU:0, one launch (start us, length us, event | category | flops | bytes accessed | tf_op | source)
XLA Modules:
  0.0 618.5 jit_solution(11390885341970221944)
XLA Ops:
  8.6 2.4 collective-permute-start
  12.6 4.4 collective-permute-done.1
  18.4 3.5 collective-permute-start.2
  23.3 5.3 collective-permute-done.2
  28.6 4.4 collective-permute-done.3
  33.0 3.4 pad_maximum_fusion
  36.5 2.5 broadcast_in_dim.16
  39.0 172.8 %while.21 = (s32[]{:T(128)}, f32[3,512,768]{2,1,0:T(8,128)}, f32[2,256,256]{2,1,0:T(8,128)S(1)}, f32[256,256]{1,0:T(8,128)S(1)}, s32[]{:T(128)}, /*index=5*/s32[...) while((s32[]{:T(128)}, f32[3,512,768]{2,1,0:T(8,128)}, ...), condition=%wide.region_1.2_spmd.clone.clone, body=%wide.region_0.1_spmd.clone.clone.sunk | while | flops 3241148416 | bytes 21496148 | solution.py:122
  54.1 1.5 convolution_subtract_fusion.8
  55.6 2.5 fusion.197
  59.6 1.5 convolution_subtract_fusion.9
  62.5 1.5 convolution_add_fusion.7
  68.5 2.8 add_bitcast_fusion.5
  71.2 1.6 maximum_add_fusion.4
  72.9 9.2 %dynamic_update_slice.7 = f32[3,512,768]{2,1,0:T(8,128)} dynamic-update-slice(f32[3,512,768]{2,1,0:T(8,128)} %get-tuple-element.447, f32[3,256,256]{2,1,0:T(8,128)S(1)} %maximum_add_fusion.4, s32[]{:T(128)} %constant.146.clone.1..sunk, s32[]{:T(128)S(6)} %select_n.147, s32[]{:T(128)S(6)} %select_n.148) | dynamic-update-slice | bytes 1572868 | tf_op jit(solution)/shard_map/while/body/dynamic_update_slice | solution.py:108
  97.3 1.5 convolution_subtract_fusion.8
  98.7 2.5 fusion.197
  102.7 1.5 convolution_subtract_fusion.9
  105.7 1.5 convolution_add_fusion.7
  111.6 2.8 add_bitcast_fusion.5
  114.4 1.6 maximum_add_fusion.4
  116.1 9.1 %dynamic_update_slice.7 = f32[3,512,768]{2,1,0:T(8,128)} dynamic-update-slice(f32[3,512,768]{2,1,0:T(8,128)} %get-tuple-element.447, f32[3,256,256]{2,1,0:T(8,128)S(1)} %maximum_add_fusion.4, s32[]{:T(128)} %constant.146.clone.1..sunk, s32[]{:T(128)S(6)} %select_n.147, s32[]{:T(128)S(6)} %select_n.148) | dynamic-update-slice | bytes 1572868 | tf_op jit(solution)/shard_map/while/body/dynamic_update_slice | solution.py:108
  140.3 1.5 convolution_subtract_fusion.8
  141.7 2.5 fusion.197
  145.7 1.5 convolution_subtract_fusion.9
  148.7 1.5 convolution_add_fusion.7
  154.6 2.8 add_bitcast_fusion.5
  157.4 1.6 maximum_add_fusion.4
  159.1 8.8 %dynamic_update_slice.7 = f32[3,512,768]{2,1,0:T(8,128)} dynamic-update-slice(f32[3,512,768]{2,1,0:T(8,128)} %get-tuple-element.447, f32[3,256,256]{2,1,0:T(8,128)S(1)} %maximum_add_fusion.4, s32[]{:T(128)} %constant.146.clone.1..sunk, s32[]{:T(128)S(6)} %select_n.147, s32[]{:T(128)S(6)} %select_n.148) | dynamic-update-slice | bytes 1572868 | tf_op jit(solution)/shard_map/while/body/dynamic_update_slice | solution.py:108
  183.0 1.5 convolution_subtract_fusion.8
  184.5 2.5 fusion.197
  188.4 1.5 convolution_subtract_fusion.9
  191.4 1.5 convolution_add_fusion.7
  197.3 2.8 add_bitcast_fusion.5
  200.1 1.6 maximum_add_fusion.4
  201.8 9.2 %dynamic_update_slice.7 = f32[3,512,768]{2,1,0:T(8,128)} dynamic-update-slice(f32[3,512,768]{2,1,0:T(8,128)} %get-tuple-element.447, f32[3,256,256]{2,1,0:T(8,128)S(1)} %maximum_add_fusion.4, s32[]{:T(128)} %constant.146.clone.1..sunk, s32[]{:T(128)S(6)} %select_n.147, s32[]{:T(128)S(6)} %select_n.148) | dynamic-update-slice | bytes 1572868 | tf_op jit(solution)/shard_map/while/body/dynamic_update_slice | solution.py:108
  214.3 2.2 slice.187
  216.5 51.4 %collective-permute-done.4 = f32[3,512,128]{2,1,0:T(8,128)S(1)} collective-permute-done((f32[3,512,128]{2,1,0:T(8,128)S(1)}, f32[3,512,128]{2,1,0:T(8,128)S(1)}, u32[]{:S(2)}, u32[]{:S(2)}) %collective-permute-start.4) | collective-permute-done | bytes 786464 | tf_op jit(solution)/shard_map/ppermute | solution.py:21
  267.9 1.6 fusion.119
  269.5 1.5 collective-permute-start.5
  271.0 9.4 %collective-permute-done.5 = f32[3,512,128]{2,1,0:T(8,128)S(1)} collective-permute-done((f32[3,512,128]{2,1,0:T(8,128)S(1)}, f32[3,512,128]{2,1,0:T(8,128)S(1)}, u32[]{:S(2)}, u32[]{:S(2)}) %collective-permute-start.5) | collective-permute-done | bytes 786464 | tf_op jit(solution)/shard_map/ppermute | solution.py:21
  280.6 1.6 copy-done.1
  285.8 3.9 collective-permute-start.7
  289.8 271.0 %all-reduce.2.cloned.1.call-done = f32[3,256,256]{2,1,0:T(8,128)} async-done(((f32[3,256,256]{2,1,0:T(8,128)}), f32[3,256,256]{2,1,0:T(8,128)}) %all-reduce.2.cloned.1.call-update) | async-done | bytes 786448 | tf_op jit(solution)/shard_map/psum | solution.py:129
  560.8 1.6 slice_reduce_fusion.1
  564.0 1.5 slice.212
  565.6 1.6 fusion.116
  570.2 39.4 %pmax.7 = f32[]{:T(128)} all-reduce(f32[]{:T(128)} %slice_reduce_fusion), channel_id=1, replica_groups=mesh['wide'=16,'narrow'=2] {'wide','narrow'}, use_global_device_ids=true, to_apply=%region_3.4 | all-reduce | flops 1 | bytes 8 | tf_op jit(solution)/shard_map/pmax | solution.py:125
  (98 shorter events, 90.3 us)
Async XLA Ops:
  7.2 5.3 copy-start.2
  7.2 553.6 %all-reduce.2.cloned.1.call-start = ((), (), s32[]{:S(2)}) async-start(), calls=%async_computation | async-start | bytes 1572864 | tf_op jit(solution)/shard_map/psum | solution.py:129
  8.6 3.9 collective-permute-start
  11.0 12.2 %copy-start = (f32[2,256,256]{2,1,0:T(8,128)S(1)}, f32[2,256,256]{2,1,0:T(8,128)}, u32[]{:S(2)}) copy-start(f32[2,256,256]{2,1,0:T(8,128)} %param.17) | copy-start | bytes 1572868
  11.0 6.0 collective-permute-start.1
  17.0 1.3 copy-start.4
  18.4 10.1 %collective-permute-start.2 = (f32[2,512,128]{2,1,0:T(8,128)S(1)}, f32[2,512,128]{2,1,0:T(8,128)S(1)}, u32[]{:S(2)}, u32[]{:S(2)}) collective-permute-start(f32[2,512,128]{2,1,0:T(8,128)S(1)} %get-tuple-element.335), channel_id=1, source_target_pairs={{0,1},{2,3},{4,5},{6,7},{8,9},{10,11},{12,13},{14,15},{16,17},{18,... | collective-permute-start | bytes 1572872 | tf_op jit(solution)/shard_map/ppermute | solution.py:31
  21.9 11.1 %collective-permute-start.3 = (f32[2,512,128]{2,1,0:T(8,128)S(1)}, f32[2,512,128]{2,1,0:T(8,128)S(1)}, u32[]{:S(2)}, u32[]{:S(2)}) collective-permute-start(f32[2,512,128]{2,1,0:T(8,128)S(1)} %get-tuple-element.336), channel_id=1, source_target_pairs={{1,0},{3,2},{5,4},{7,6},{9,8},{11,10},{13,12},{15,14},{17,16},{19,... | collective-permute-start | bytes 1572872 | tf_op jit(solution)/shard_map/ppermute | solution.py:32
  36.4 2.6 copy-start.6
  36.4 2.6 copy-start.7
  213.0 54.9 %collective-permute-start.4 = (f32[3,512,128]{2,1,0:T(8,128)S(1)}, f32[3,512,128]{2,1,0:T(8,128)S(1)}, u32[]{:S(2)}, u32[]{:S(2)}) collective-permute-start(f32[3,512,128]{2,1,0:T(8,128)S(1)} %slice.189), channel_id=1, source_target_pairs={{1,0},{3,2},{5,4},{7,6},{9,8},{11,10},{13,12},{15,14},{17,16},{19,... | collective-permute-start | bytes 2359304 | tf_op jit(solution)/shard_map/ppermute | solution.py:21
  269.5 10.9 %collective-permute-start.5 = (f32[3,512,128]{2,1,0:T(8,128)S(1)}, f32[3,512,128]{2,1,0:T(8,128)S(1)}, u32[]{:S(2)}, u32[]{:S(2)}) collective-permute-start(f32[3,512,128]{2,1,0:T(8,128)S(1)} %get-tuple-element.331), channel_id=1, source_target_pairs={{0,1},{2,3},{4,5},{6,7},{8,9},{10,11},{12,13},{14,15},{16,17},{18,... | collective-permute-start | bytes 2359304 | tf_op jit(solution)/shard_map/ppermute | solution.py:21
  280.6 1.7 copy-start.1
  283.6 282.0 %collective-permute-start.6 = (f32[3,128,512]{2,1,0:T(8,128)}, f32[3,128,512]{2,1,0:T(8,128)}, u32[]{:S(2)}, u32[]{:S(2)}) collective-permute-start(f32[3,128,512]{2,1,0:T(8,128)} %get-tuple-element.334), channel_id=1, source_target_pairs={{2,0},{4,2},{6,4},{8,6},{10,8},{12,10},{14,12},{16,14},{18,16},{20... | collective-permute-start | bytes 2359304 | tf_op jit(solution)/shard_map/ppermute | solution.py:21
  285.8 281.4 %collective-permute-start.7 = (f32[3,128,512]{2,1,0:T(8,128)}, f32[3,128,512]{2,1,0:T(8,128)}, u32[]{:S(2)}, u32[]{:S(2)}) collective-permute-start(f32[3,128,512]{2,1,0:T(8,128)} %get-tuple-element.333), channel_id=1, source_target_pairs={{0,2},{2,4},{4,6},{6,8},{8,10},{10,12},{12,14},{14,16},{16,18},{18... | collective-permute-start | bytes 2359304 | tf_op jit(solution)/shard_map/ppermute | solution.py:21
  565.6 3.8 copy-start.5
  567.2 43.2 %copy-start.3 = (f32[2,256,512]{2,1,0:T(8,128)S(1)}, f32[2,256,512]{2,1,0:T(8,128)}, u32[]{:S(2)}) copy-start(f32[2,256,512]{2,1,0:T(8,128)} %param.16) | copy-start | bytes 3145732
Sparse Core Ops, SparseCore 0:
  285.9 274.8 all-reduce.1
where the time goes:
time: 629 us; the launch traced here: 618 us
  waiting for transfers between devices  346 us (55%)
  matrix products  103 us (16%)
  local copies, waits for them, and re-layouts  51.9 us (8%)
  blocking collectives  39.4 us (6%)
  other arithmetic  26.9 us (4%)
  loops' own time  18.6 us (3%)
  starting transfers between devices  16.6 us (3%)
  between operations  15.6 us (2%)
    psum x1, waiting for transfers between devices, body(): summed = lax.psum(terms, ('wide', 'narrow'))  271 us
    dot_general x64, matrix products, dot_high(): jnp.dot(left_matrix, right_matrix, preferred_element_type=jnp.float32, pr...  103 us
    ppermute x4, waiting for transfers between devices, from_behind(): return lax.ppermute(x, axis, pairs)  60.8 us
    pmax x1, blocking collectives, body(): cover_peak = lax.pmax(jnp.max(coverage), ('wide', 'narrow'))  39.4 us
    dynamic_update_slice x4, local copies, waits for them, and re-layouts, visit(): lax.dynamic_update_slice(grad_ext, old_grad + jnp.stack(pieces), (zero_in...  36.2 us
    another operation x1, loops' own time, body(): lax.fori_loop(0, counts[0, 0], visit, initial)  18.6 us
  transfers between devices with their start and end apart: 9, of which 6 were waited for; matrix products, arithmetic and copies ran while one was open for 1% of the time, Pallas kernels for 0%

commit v1 on v0

v1 whole, which is shorter than its diff:
```python
import functools
import math

import jax
import jax.numpy as jnp
import ml_dtypes
import numpy as np
from jax import lax
from jax.experimental import pallas as pl
from jax.experimental.pallas import tpu as pltpu
from jax.sharding import PartitionSpec as P

H = 128
LANES = 128
CHUNK = 32
INFO = 8
BF = jnp.bfloat16
F32 = jnp.float32
MIX_OBJECT = 0.5
MIX_PROBE = 0.5
VMEM = pl.BlockSpec(memory_space=pltpu.VMEM)
SMEM = pl.BlockSpec(memory_space=pltpu.SMEM)


def rounded_pair(table):
    table = table.astype(np.float32)
    high = table.astype(ml_dtypes.bfloat16)
    low = (table - high.astype(np.float32)).astype(ml_dtypes.bfloat16)
    return high, low


def dft_tables(length):
    index = np.arange(length)
    angle = 2.0 * np.pi * ((index[:, None] * index[None, :]) % length) / length
    cos_high, cos_low = rounded_pair(np.cos(angle) / math.sqrt(length))
    sin_high, sin_low = rounded_pair(-np.sin(angle) / math.sqrt(length))
    left_high = np.block([[cos_high, -sin_high], [sin_high, cos_high]])
    left_low = np.block([[cos_low, -sin_low], [sin_low, cos_low]])
    right_high = np.block([[cos_high, sin_high], [-sin_high, cos_high]])
    right_low = np.block([[cos_low, sin_low], [-sin_low, cos_low]])
    left = np.concatenate([left_high, left_high, left_low], axis=1)
    right = np.concatenate([right_high, right_high, right_low], axis=0)
    return left, right


def split(x):
    high = x.astype(BF)
    return high, (x - high.astype(F32)).astype(BF)


def side_block(place, side, sides, blocks):
    if sides == 1:
        return jnp.where(place[1] == 0, blocks - 1, 0)
    return 0 if side == 0 else blocks - 1


def side_step(place, side, sides):
    if sides == 1:
        return jnp.where(place[1] == 0, 1, -1)
    return -1 if side == 0 else 1


def cover_kernel(tile_rows, tile_cols, sides, place, info, probe, cover, peak, total, power):
    pr = probe.shape[1]
    pieces = pr // LANES
    for j in range(pieces):
        cut = slice(j * LANES, (j + 1) * LANES)
        power[j] = probe[0, :, cut] * probe[0, :, cut] + probe[1, :, cut] * probe[1, :, cut]
    total[...] = jnp.zeros_like(total)
    lanes = lax.broadcasted_iota(jnp.int32, (CHUNK, LANES), 1)
    even = place[0] % 2 == 0
    steps_down = (0, jnp.where(even, 1, -1), jnp.where(even, -1, 1))
    steps_right = (0,) + tuple(side_step(place, s, sides) for s in range(sides))
    for v in range(3):
        for h in range(1 + sides):
            source = v * (1 + sides) + h
            down, right = steps_down[v], steps_right[h]

            def visit(k, carry):
                row = info[source, k] + pr - H + down * tile_rows
                col = info[source, 8 + k] + pr - H + right * tile_cols
                inside = (row > 0) & (row < pr + tile_rows) & (col > 0) & (col < pr + tile_cols)

                @pl.when(inside)
                def _():
                    shift = col & (LANES - 1)
                    block = col >> 7
                    low = lanes < shift
                    for q in range(pr // CHUNK):
                        turned = [
                            pltpu.roll(power[j, q * CHUNK : (q + 1) * CHUNK, :], shift, 1)
                            for j in range(pieces)
                        ]
                        here = pl.ds(row + q * CHUNK, CHUNK)
                        zero = jnp.zeros((CHUNK, LANES), F32)
                        total[block, here, :] += jnp.where(low, zero, turned[0])
                        for j in range(1, pieces):
                            total[block + j, here, :] += jnp.where(low, turned[j - 1], turned[j])
                        total[block + pieces, here, :] += jnp.where(low, turned[-1], zero)

                return carry

            lax.fori_loop(0, info[source, 16], visit, 0)
    first = pr // LANES
    best = jnp.zeros((8, LANES), F32)
    for b in range(tile_cols // LANES):
        own = total[first + b, pr : pr + tile_rows, :]
        cover[:, b * LANES : (b + 1) * LANES] = own
        best = jnp.maximum(best, jnp.max(own.reshape(tile_rows // 8, 8, LANES), axis=0))
    peak[...] = jnp.full((8, LANES), jnp.max(best), F32)


def cover_call(place, info, probe, tile_rows, tile_cols, sides):
    pr = probe.shape[1]
    blocks = (tile_cols + 2 * pr) // LANES + 1
    return pl.pallas_call(
        functools.partial(cover_kernel, tile_rows, tile_cols, sides),
        out_shape=(
            jax.ShapeDtypeStruct((tile_rows, tile_cols), F32),
            jax.ShapeDtypeStruct((8, LANES), F32),
        ),
        in_specs=[SMEM, SMEM, VMEM],
        out_specs=(VMEM, VMEM),
        scratch_shapes=[
            pltpu.VMEM((blocks, tile_rows + 2 * pr, LANES), F32),
            pltpu.VMEM((pr // LANES, pr, LANES), F32),
        ],
        compiler_params=pltpu.CompilerParams(vmem_limit_bytes=24 << 20),
        cost_estimate=pl.CostEstimate(flops=4_000_000, bytes_accessed=8_000_000, transcendentals=0),
        name="cover",
    )(place, info, probe)


def positions_kernel(sides, *refs):
    place, rows, cols, count = refs[:4]
    tile, near, far_side = refs[4:7]
    side_in = refs[7 : 7 + sides]
    probe, measured, left, right = refs[7 + sides : 11 + sides]
    outs = refs[11 + sides :]
    middle, near_rim, far_rim = outs[:3]
    side_out = outs[3 : 3 + sides]
    probe_sums = outs[3 + sides]
    ext, grad, patch, exits, data, wide_data, half = outs[4 + sides :]

    pr = probe.shape[1]
    pieces = pr // LANES
    tile_rows, tile_cols = tile.shape[1:]
    ext_rows = tile_rows + 2 * H
    blocks = (tile_cols + 2 * H) // LANES
    own_blocks = tile_cols // LANES
    even = place[0] % 2 == 0
    near_row = pl.multiple_of(jnp.where(even, tile_rows + H, 0), 8)
    far_row = pl.multiple_of(jnp.where(even, 0, tile_rows + H), 8)
    side_blocks = [side_block(place, s, sides, blocks) for s in range(sides)]
    own = pl.ds(H, tile_rows)
    for ch in range(2):
        if sides == 1:
            ext[ch * blocks + blocks - 1 - side_blocks[0]] = jnp.zeros((ext_rows, LANES), F32)
        for b in range(own_blocks):
            at, cut = ch * blocks + 1 + b, slice(b * LANES, (b + 1) * LANES)
            ext[at, own, :] = tile[ch, :, cut]
            ext[at, pl.ds(near_row, H), :] = near[ch, 0:H, cut]
            ext[at, pl.ds(far_row, H), :] = far_side[ch, 0:H, cut]
        for s in range(sides):
            at = ch * blocks + side_blocks[s]
            cut = slice(tile_cols + s * LANES, tile_cols + (s + 1) * LANES)
            ext[at, own, :] = side_in[s][ch, 0:tile_rows, :]
            ext[at, pl.ds(near_row, H), :] = near[ch, 0:H, cut]
            ext[at, pl.ds(far_row, H), :] = far_side[ch, 0:H, cut]
    grad[...] = jnp.zeros_like(grad)
    probe_sums[...] = jnp.zeros_like(probe_sums)
    lanes = lax.broadcasted_iota(jnp.int32, (CHUNK, LANES), 1)

    def times_left():
        stack = jnp.concatenate([data[...], data[0 : 2 * pr]], axis=0)
        return jnp.dot(left[...], stack, preferred_element_type=F32)

    def times_right():
        for q in range(pr // CHUNK):
            cut = slice(q * CHUNK, (q + 1) * CHUNK)
            high, low = split(half[cut, :])
            wide_data[cut, 0:pr] = high
            wide_data[cut, 2 * pr : 3 * pr] = low
            high, low = split(half[pr + q * CHUNK : pr + (q + 1) * CHUNK, :])
            wide_data[cut, pr : 2 * pr] = high
            wide_data[cut, 3 * pr : 4 * pr] = low
        stack = jnp.concatenate([wide_data[...], wide_data[:, 0 : 2 * pr]], axis=1)
        return jnp.dot(stack, right[...], preferred_element_type=F32)

    def put(value, part, q, cut):
        high, low = split(value)
        data[part * pr + q * CHUNK : part * pr + (q + 1) * CHUNK, cut] = high
        data[(2 + part) * pr + q * CHUNK : (2 + part) * pr + (q + 1) * CHUNK, cut] = low

    def visit(k, carry):
        row, col = rows[0, 0, k], cols[0, 0, k]
        shift, block = col & (LANES - 1), col >> 7
        back = (LANES - shift) & (LANES - 1)
        keep = lanes < LANES - shift
        for q in range(pr // CHUNK):
            cut = slice(q * CHUNK, (q + 1) * CHUNK)
            here = pl.ds(row + q * CHUNK, CHUNK)
            seen = []
            for ch in range(2):
                turned = [
                    pltpu.roll(ext[ch * blocks + block + j, here, :], back, 1)
                    for j in range(pieces + 1)
                ]
                seen.append([jnp.where(keep, turned[j], turned[j + 1]) for j in range(pieces)])
            for j in range(pieces):
                part = slice(j * LANES, (j + 1) * LANES)
                probe_real, probe_imag = probe[0, cut, part], probe[1, cut, part]
                real, imag = seen[0][j], seen[1][j]
                patch[0, cut, part], patch[1, cut, part] = real, imag
                exit_real = probe_real * real - probe_imag * imag
                exit_imag = probe_real * imag + probe_imag * real
                exits[0, cut, part], exits[1, cut, part] = exit_real, exit_imag
                put(exit_real, 0, q, part)
                put(exit_imag, 1, q, part)
        half[...] = times_left()
        far = times_right()
        for q in range(pr // CHUNK):
            cut = slice(q * CHUNK, (q + 1) * CHUNK)
            real, imag = far[cut, 0:pr], far[cut, pr : 2 * pr]
            factor = jnp.sqrt(measured[0, 0, k, cut, :]) * lax.rsqrt(real * real + imag * imag + 1.0)
            put(real * factor, 0, q, slice(0, pr))
            put(-(imag * factor), 1, q, slice(0, pr))
        half[...] = times_left()
        conj_back = times_right()
        low = lanes < shift
        zero = jnp.zeros((CHUNK, LANES), F32)
        for q in range(pr // CHUNK):
            cut = slice(q * CHUNK, (q + 1) * CHUNK)
            here = pl.ds(row + q * CHUNK, CHUNK)
            turned = [[], []]
            for j in range(pieces):
                part = slice(j * LANES, (j + 1) * LANES)
                other = slice(pr + j * LANES, pr + (j + 1) * LANES)
                diff_real = conj_back[cut, part] - exits[0, cut, part]
                diff_imag = -conj_back[cut, other] - exits[1, cut, part]
                probe_real, probe_imag = probe[0, cut, part], probe[1, cut, part]
                turned[0].append(pltpu.roll(probe_real * diff_real + probe_imag * diff_imag, shift, 1))
                turned[1].append(pltpu.roll(probe_real * diff_imag - probe_imag * diff_real, shift, 1))
                real, imag = patch[0, cut, part], patch[1, cut, part]
                probe_sums[0, j, cut, :] += real * diff_real + imag * diff_imag
                probe_sums[1, j, cut, :] += real * diff_imag - imag * diff_real
                probe_sums[2, j, cut, :] += real * real + imag * imag
            for ch in range(2):
                at = ch * blocks + block
                grad[at, here, :] += jnp.where(low, zero, turned[ch][0])
                for j in range(1, pieces):
                    grad[at + j, here, :] += jnp.where(low, turned[ch][j - 1], turned[ch][j])
                grad[at + pieces, here, :] += jnp.where(low, turned[ch][-1], zero)
        return carry

    lax.fori_loop(0, count[0, 0], visit, 0)
    for ch in range(2):
        for b in range(own_blocks):
            at, cut = ch * blocks + 1 + b, slice(b * LANES, (b + 1) * LANES)
            middle[ch, :, cut] = grad[at, own, :]
            near_rim[ch, :, cut] = grad[at, pl.ds(near_row, H), :]
            far_rim[ch, :, cut] = grad[at, pl.ds(far_row, H), :]
        for s in range(sides):
            at = ch * blocks + side_blocks[s]
            side_out[s][ch, 0:H, :] = grad[at, pl.ds(near_row, H), :]
            side_out[s][ch, H : H + tile_rows, :] = grad[at, own, :]
            side_out[s][ch, H + tile_rows :, :] = grad[at, pl.ds(far_row, H), :]


def positions_call(place, rows, cols, count, tile, near, far_side, side_in, probe, measured):
    pr = probe.shape[1]
    sides = len(side_in)
    tile_rows, tile_cols = tile.shape[1:]
    ext_rows = tile_rows + 2 * H
    blocks = (tile_cols + 2 * H) // LANES
    left, right = dft_tables(pr)
    shape = lambda *dims: jax.ShapeDtypeStruct(dims, F32)
    slots = measured.shape[2]
    return pl.pallas_call(
        functools.partial(positions_kernel, sides),
        out_shape=(
            shape(2, tile_rows, tile_cols),
            shape(2, H, tile_cols),
            shape(2, H, tile_cols),
            *[shape(2, ext_rows, LANES)] * sides,
            shape(3, pr // LANES, pr, LANES),
        ),
        in_specs=[SMEM] * 4 + [VMEM] * (7 + sides),
        out_specs=(VMEM,) * (4 + sides),
        scratch_shapes=[
            pltpu.VMEM((2 * blocks, ext_rows, LANES), F32),
            pltpu.VMEM((2 * blocks, ext_rows, LANES), F32),
            pltpu.VMEM((2, pr, pr), F32),
            pltpu.VMEM((2, pr, pr), F32),
            pltpu.VMEM((4 * pr, pr), BF),
            pltpu.VMEM((pr, 4 * pr), BF),
            pltpu.VMEM((2 * pr, pr), F32),
        ],
        compiler_params=pltpu.CompilerParams(vmem_limit_bytes=52 << 20),
        cost_estimate=pl.CostEstimate(
            flops=slots * 96 * pr * pr * pr, bytes_accessed=16_000_000, transcendentals=slots * 2 * pr * pr
        ),
        name="positions",
    )(place, rows, cols, count, tile, near, far_side, *side_in, probe, measured, jnp.asarray(left), jnp.asarray(right))


def object_kernel(sides, *refs):
    place, tile, middle, cover, peak, near, far_side = refs[:7]
    side_in = refs[7 : 7 + sides]
    out = refs[7 + sides]
    tile_rows, tile_cols = tile.shape[1:]
    own_blocks = tile_cols // LANES
    even = place[0] % 2 == 0
    sums = refs[8 + sides]
    sums[...] = middle[...]
    near_row = pl.multiple_of(jnp.where(even, tile_rows - H, 0), 8)
    far_row = pl.multiple_of(jnp.where(even, 0, tile_rows - H), 8)
    sums[:, pl.ds(near_row, H), :] += near[...]
    sums[:, pl.ds(far_row, H), :] += far_side[...]
    for s in range(sides):
        received = side_in[s][:, H : H + tile_rows, :]
        if sides == 1:
            for edge, where in ((0, own_blocks - 1), (1, 0)):

                @pl.when((place[1] == 0) == (edge == 0))
                def _():
                    sums[:, :, where * LANES : (where + 1) * LANES] += received
        else:
            where = 0 if s == 0 else own_blocks - 1
            sums[:, :, where * LANES : (where + 1) * LANES] += received
    top = MIX_OBJECT * peak[0:1, 0:1]
    inverse = 1.0 / ((1.0 - MIX_OBJECT) * cover[...] + top)
    for ch in range(2):
        out[ch] = tile[ch] + sums[ch] * inverse


def object_call(place, tile, middle, cover, peak, near, far_side, side_in):
    sides = len(side_in)
    return pl.pallas_call(
        functools.partial(object_kernel, sides),
        out_shape=jax.ShapeDtypeStruct(tile.shape, F32),
        in_specs=[SMEM] + [VMEM] * (6 + sides),
        out_specs=VMEM,
        scratch_shapes=[pltpu.VMEM(tile.shape, F32)],
        compiler_params=pltpu.CompilerParams(vmem_limit_bytes=24 << 20),
        name="object_update",
    )(place, tile, middle, cover, peak, near, far_side, *side_in)


def probe_kernel(sums, probe, out):
    pr = probe.shape[1]
    pieces = pr // LANES
    weights = sums[2 * pieces * pr : 3 * pieces * pr, :]
    best = jnp.max(jnp.max(weights.reshape(-1, 8, LANES), axis=0), keepdims=True)
    for j in range(pieces):
        cut = slice(j * LANES, (j + 1) * LANES)
        weight = sums[(2 * pieces + j) * pr : (2 * pieces + j + 1) * pr, :]
        inverse = 1.0 / ((1.0 - MIX_PROBE) * weight + MIX_PROBE * best)
        for ch in range(2):
            at = (ch * pieces + j) * pr
            out[ch, :, cut] = probe[ch, :, cut] + sums[at : at + pr, :] * inverse


def probe_call(sums, probe):
    return pl.pallas_call(
        probe_kernel,
        out_shape=jax.ShapeDtypeStruct(probe.shape, F32),
        in_specs=[VMEM, VMEM],
        out_specs=VMEM,
        name="probe_update",
    )(sums, probe)


def swap(x, axis, first):
    size = lax.axis_size(axis)
    pairs = []
    for i in range(first, size - 1, 2):
        pairs += [(i, i + 1), (i + 1, i)]
    return lax.ppermute(x, axis, pairs)


def shifted(x, axis, by):
    size = lax.axis_size(axis)
    return lax.ppermute(x, axis, [(i, i + by) for i in range(size) if 0 <= i + by < size])


def to_sides(pieces):
    if len(pieces) == 1:
        return [swap(pieces[0], "narrow", 0)]
    return [shifted(pieces[1], "narrow", 1), shifted(pieces[0], "narrow", -1)]


def bits_of(axis):
    size = lax.axis_size(axis)
    return [1 << b for b in range(size.bit_length() - 1)]


def partner(x, axis, bit):
    size = lax.axis_size(axis)
    return lax.ppermute(x, axis, [(i, i ^ bit) for i in range(size)])


def half_of(x, which):
    rows = x.shape[0] // 2
    return lax.dynamic_slice_in_dim(x, which * rows, rows, axis=0)


def sum_everywhere(terms, peak):
    wide, narrow = bits_of("wide"), bits_of("narrow")
    halving = [("wide", b) for b in wide[:2]] + [("narrow", b) for b in narrow]
    doubling = [("wide", b) for b in wide[2:]]
    state = lambda axis, bit: (lax.axis_index(axis) // bit) % 2
    for axis, bit in halving:
        mine = state(axis, bit)
        got = partner(jnp.concatenate([half_of(terms, 1 - mine), peak], axis=0), axis, bit)
        rows = terms.shape[0] // 2
        terms = half_of(terms, mine) + got[:rows]
        peak = jnp.maximum(peak, got[rows:])
    for axis, bit in doubling:
        got = partner(jnp.concatenate([terms, peak], axis=0), axis, bit)
        rows = terms.shape[0]
        terms = terms + got[:rows]
        peak = jnp.maximum(peak, got[rows:])
    for axis, bit in halving[::-1]:
        first = state(axis, bit) == 0
        got = partner(terms, axis, bit)
        terms = jnp.concatenate([jnp.where(first, terms, got), jnp.where(first, got, terms)], axis=0)
    return terms, peak


def body(tile, probe, measured, rows, cols, counts):
    wide, narrow = lax.axis_index("wide"), lax.axis_index("narrow")
    sides = 1 if lax.axis_size("narrow") == 2 else 2
    tile_rows, tile_cols = tile.shape[1:]
    even = wide % 2 == 0
    place = jnp.stack([wide, narrow]).astype(jnp.int32)

    own_info = jnp.concatenate(
        [rows.reshape(-1), cols.reshape(-1), counts.reshape(-1), jnp.zeros((LANES - 17,), jnp.int32)]
    ).astype(F32)
    info_rows = jnp.broadcast_to(own_info, (2, INFO, LANES))

    def with_info(x):
        return jnp.concatenate([x, info_rows], axis=1)

    if sides == 1:
        edge = jnp.where(narrow == 0, tile_cols - H, 0)
        edges = [with_info(lax.dynamic_slice_in_dim(tile, edge, H, axis=2))]
    else:
        edges = [with_info(tile[:, :, :H]), with_info(tile[:, :, tile_cols - H :])]
    side_in = to_sides(edges)

    def band(at_end):
        start = jnp.where(at_end, tile_rows - H, 0)
        mine = lax.dynamic_slice_in_dim(tile, start, H, axis=1)
        mine = jnp.concatenate([mine, jnp.pad(info_rows, ((0, 0), (0, 0), (0, tile_cols - LANES)))], axis=1)
        others = [
            jnp.concatenate([lax.dynamic_slice_in_dim(s, start, H, axis=1), s[:, tile_rows:]], axis=1)
            for s in side_in
        ]
        return jnp.concatenate([mine] + others, axis=2)

    near = swap(band(even), "wide", 0)
    far_side = swap(band(~even), "wide", 1)

    def infos(x, row):
        return [x[0, row, 0:32]] + [
            x[0, row, tile_cols + s * LANES : tile_cols + s * LANES + 32] for s in range(sides)
        ]

    info = jnp.stack(
        [own_info[:32]] + [s[0, tile_rows, :32] for s in side_in] + infos(near, H) + infos(far_side, H)
    ).astype(jnp.int32)
    cover, peak = cover_call(place, info, probe, tile_rows, tile_cols, sides)

    out = positions_call(place, rows, cols, counts, tile, near, far_side, side_in, probe, measured)
    middle, near_rim, far_rim = out[:3]
    side_rims, probe_sums = list(out[3 : 3 + sides]), out[3 + sides]

    summed, peak = sum_everywhere(probe_sums.reshape(-1, LANES), peak)
    new_probe = probe_call(summed, probe)

    side_got = to_sides(side_rims)

    def with_sides(rim, part):
        for s, got in enumerate(side_got):
            if sides == 1:
                start = jnp.where(narrow == 0, tile_cols - H, 0)
            else:
                start = 0 if s == 0 else tile_cols - H
            old = lax.dynamic_slice_in_dim(rim, start, H, axis=2)
            rim = lax.dynamic_update_slice_in_dim(rim, old + got[:, part], start, axis=2)
        return rim

    near_got = swap(with_sides(near_rim, slice(0, H)), "wide", 0)
    far_got = swap(with_sides(far_rim, slice(H + tile_rows, None)), "wide", 1)
    new_object = object_call(place, tile, middle, cover, peak, near_got, far_got, side_got)
    return new_object, new_probe


def solution(mesh):
    placed = (
        P(None, "wide", "narrow"),
        P(),
        P("wide", "narrow", None, None, None),
        P("wide", "narrow", None),
        P("wide", "narrow", None),
        P("wide", "narrow"),
    )
    return jax.shard_map(
        body,
        mesh=mesh,
        in_specs=placed,
        out_specs=(P(None, "wide", "narrow"), P()),
        check_vma=False,
    )
```

time: 629 us -> 136 us (0.22)
  the two profiles are of different devices: /device:TPU:0 before, /device:TPU:9 now
where the time goes in v1:
time: 136 us
  waiting for transfers between devices  55.8 us (41%)
  starting transfers between devices  37.9 us (28%)
  Pallas kernels  33.1 us (24%)
  other arithmetic  4.79 us (4%)
  local copies, waits for them, and re-layouts  2.97 us (2%)
  between operations  1.66 us (1%)
    ppermute x6, waiting for transfers between devices, swap(): return lax.ppermute(x, axis, pairs)  34.3 us
    pallas_call x1, Pallas kernels, positions_call(): pl.pallas_call(functools.partial(positions_kernel, sides), out_shape=(sha...  25.5 us
    ppermute x8, starting transfers between devices, partner(): return lax.ppermute(x, axis, [(i, i ^ bit) for i in range(size)])  24 us
    ppermute x8, waiting for transfers between devices, partner(): return lax.ppermute(x, axis, [(i, i ^ bit) for i in range(size)])  21.6 us
    ppermute x6, starting transfers between devices, swap(): return lax.ppermute(x, axis, pairs)  13.9 us
    pallas_call x1, Pallas kernels, cover_call(): pl.pallas_call(functools.partial(cover_kernel, tile_rows, tile_cols, side...  3.27 us
  transfers between devices with their start and end apart: 14, of which 9 were waited for; matrix products, arithmetic and copies ran while one was open for 0% of the time, Pallas kernels for 1%

profile of v1, /device:TPU:9, one launch (start us, length us, event | category | flops | bytes accessed | tf_op | source)
XLA Modules:
  0.0 136.2 jit_solution(6155920735380047638)
XLA Ops:
  0.6 0.0 copy-start
  1.4 1.0 constant_dynamic-slice_fusion.6
  2.4 0.8 add_convert_fusion
  3.2 1.3 collective-permute-start
  4.5 0.1 constant_dynamic-slice_fusion.4
  4.6 6.0 %collective-permute-done.refs_7_ = f32[2,264,128]{2,1,0:T(8,128)S(1)} collective-permute-done((f32[2,264,128]{2,1,0:T(8,128)S(1)}, f32[2,264,128]{2,1,0:T(8,128)S(1)}, u32[]{:S(2)}, u32[]{:S(2)}) %collective-permute-start) | collective-permute-done | bytes 270368 | tf_op jit(solution)/shard_map/ppermute | solution.py:379
  10.6 0.0 copy-start.4
  10.6 0.0 copy-start.5
  10.6 0.1 fusion.1
  10.7 1.6 %collective-permute-start.1 = (f32[2,136,640]{2,1,0:T(8,128)S(1)}, f32[2,136,640]{2,1,0:T(8,128)S(1)}, u32[]{:S(2)}, u32[]{:S(2)}) collective-permute-start(f32[2,136,640]{2,1,0:T(8,128)S(1)} %get-tuple-element.33), channel_id=1, source_target_pairs={{0,2},{2,0},{4,6},{6,4},{8,10},{10,8},{12,14},{14,12},{16,18},{18,... | collective-permute-start | bytes 2088968 | tf_op jit(solution)/shard_map/ppermute | solution.py:379
  12.3 3.0 %collective-permute-start.2 = (f32[2,136,640]{2,1,0:T(8,128)S(1)}, f32[2,136,640]{2,1,0:T(8,128)}, u32[]{:S(2)}, u32[]{:S(2)}) collective-permute-start(f32[2,136,640]{2,1,0:T(8,128)S(1)} %get-tuple-element.32), channel_id=1, source_target_pairs={{2,4},{4,2},{6,8},{8,6},{10,12},{12,10},{14,16},{16,14},{18,20},{2... | collective-permute-start | bytes 2088968 | tf_op jit(solution)/shard_map/ppermute | solution.py:379
  15.4 0.1 pad_add_fusion.refs_0_.place
  15.5 0.0 collective-permute-done.1.refs_5_
  15.5 16.8 %collective-permute-done.2.refs_6_ = f32[2,136,640]{2,1,0:T(8,128)} collective-permute-done((f32[2,136,640]{2,1,0:T(8,128)S(1)}, f32[2,136,640]{2,1,0:T(8,128)}, u32[]{:S(2)}, u32[]{:S(2)}) %collective-permute-start.2) | collective-permute-done | bytes 696352 | tf_op jit(solution)/shard_map/ppermute | solution.py:379
  32.2 0.7 slice_bitcast_fusion
  33.0 3.3 %cover.1 = (f32[256,512]{1,0:T(8,128)S(1)}, f32[8,128]{1,0:T(8,128)S(1)}) custom-call(s32[2]{0:T(128)S(1)} %pad_add_fusion.refs_0_.place, s32[6,32]{1,0:T(8,128)S(1)} %convert_element_type.10.info, f32[2,256,256]{2,1,0:T(8,128)S(1)} %copy-done.2), custom_call_target="tpu_custom_call" | custom-call | flops 4000000 | bytes 8000000 | tf_op jit(solution)/shard_map/cover/pallas_call | solution.py:116
  36.3 25.5 %positions.1 = (f32[2,256,512]{2,1,0:T(8,128)}, f32[2,128,512]{2,1,0:T(8,128)S(1)}, f32[2,128,512]{2,1,0:T(8,128)S(1)}, f32[2,512,128]{2,1,0:T(8,128)S(1)}, f32[3,2,256,128]{3,2,1,0:T(8,128)}) custom-call(s32[2]{0:T(128)S(1)} %pad_add_fusion.refs_0_.place, s32[1,1,8]{2,1,0:T(1,128)S(1)} %copy-done.4, s32[1,1,8]{2,1,0:T(1,128)S(1)} %copy-done.5, ...), custom_call_target="tpu_custom_call" | custom-call | flops 12884901888 | bytes 16000000 | tf_op jit(solution)/shard_map/positions/pallas_call | solution.py:279
  61.8 1.1 constant_dynamic-slice_fusion.2
  62.9 0.8 pad_maximum_fusion.3
  63.7 6.1 %collective-permute-start.3 = (f32[776,128]{1,0:T(8,128)}, f32[776,128]{1,0:T(8,128)}, u32[]{:S(2)}, u32[]{:S(2)}) collective-permute-start(f32[776,128]{1,0:T(8,128)} %pad_maximum_fusion.3), channel_id=1, source_target_pairs={{0,2},{2,0},{4,6},{6,4},{8,10},{10,8},{12,14},{14,12},{16,18},{18,... | collective-permute-start | bytes 1191944 | tf_op jit(solution)/shard_map/ppermute | solution.py:400
  69.7 1.7 %collective-permute-done.3 = f32[776,128]{1,0:T(8,128)} collective-permute-done((f32[776,128]{1,0:T(8,128)}, f32[776,128]{1,0:T(8,128)}, u32[]{:S(2)}, u32[]{:S(2)}) %collective-permute-start.3) | collective-permute-done | bytes 397344 | tf_op jit(solution)/shard_map/ppermute | solution.py:400
  71.4 1.0 slice_add_fusion
  72.5 0.7 slice_maximum_fusion.4
  73.2 0.1 collective-permute-start.4
  73.3 6.2 %collective-permute-done.4 = f32[392,128]{1,0:T(8,128)S(1)} collective-permute-done((f32[392,128]{1,0:T(8,128)S(1)}, f32[392,128]{1,0:T(8,128)S(1)}, u32[]{:S(2)}, u32[]{:S(2)}) %collective-permute-start.4) | collective-permute-done | bytes 200736 | tf_op jit(solution)/shard_map/ppermute | solution.py:400
  79.6 3.4 %collective-permute-start.5 = (f32[200,128]{1,0:T(8,128)S(1)}, f32[200,128]{1,0:T(8,128)S(1)}, u32[]{:S(2)}, u32[]{:S(2)}) collective-permute-start(f32[200,128]{1,0:T(8,128)S(1)} %pad_maximum_fusion.8), channel_id=1, source_target_pairs={{0,1},{1,0},{2,3},{3,2},{4,5},{5,4},{6,7},{7,6},{8,9},{9,8},{10,11... | collective-permute-start | bytes 307208 | tf_op jit(solution)/shard_map/ppermute | solution.py:400
  82.9 2.4 %collective-permute-done.5 = f32[200,128]{1,0:T(8,128)S(1)} collective-permute-done((f32[200,128]{1,0:T(8,128)S(1)}, f32[200,128]{1,0:T(8,128)S(1)}, u32[]{:S(2)}, u32[]{:S(2)}) %collective-permute-start.5) | collective-permute-done | bytes 102432 | tf_op jit(solution)/shard_map/ppermute | solution.py:400
  85.3 4.6 %collective-permute-start.6 = (f32[200,128]{1,0:T(8,128)S(1)}, f32[200,128]{1,0:T(8,128)S(1)}, u32[]{:S(2)}, u32[]{:S(2)}) collective-permute-start(f32[200,128]{1,0:T(8,128)S(1)} %pad_maximum_fusion.9), channel_id=1, source_target_pairs={{0,8},{2,10},{4,12},{6,14},{8,0},{10,2},{12,4},{14,6},{16,24},{18,... | collective-permute-start | bytes 307208 | tf_op jit(solution)/shard_map/ppermute | solution.py:400
  90.0 2.1 %collective-permute-done.6 = f32[200,128]{1,0:T(8,128)S(1)} collective-permute-done((f32[200,128]{1,0:T(8,128)S(1)}, f32[200,128]{1,0:T(8,128)S(1)}, u32[]{:S(2)}, u32[]{:S(2)}) %collective-permute-start.6) | collective-permute-done | bytes 102432 | tf_op jit(solution)/shard_map/ppermute | solution.py:400
  92.0 5.0 %collective-permute-start.7 = (f32[200,128]{1,0:T(8,128)S(1)}, f32[200,128]{1,0:T(8,128)S(1)}, u32[]{:S(2)}, u32[]{:S(2)}) collective-permute-start(f32[200,128]{1,0:T(8,128)S(1)} %pad_maximum_fusion.10), channel_id=1, source_target_pairs={{0,16},{2,18},{4,20},{6,22},{8,24},{10,26},{12,28},{14,30},{16,0},... | collective-permute-start | bytes 307208 | tf_op jit(solution)/shard_map/ppermute | solution.py:400
  97.0 1.5 %collective-permute-start.8 = (f32[2,512,128]{2,1,0:T(8,128)S(1)}, f32[2,512,128]{2,1,0:T(8,128)S(1)}, u32[]{:S(2)}, u32[]{:S(2)}) collective-permute-start(f32[2,512,128]{2,1,0:T(8,128)S(1)} %get-tuple-element.14), channel_id=1, source_target_pairs={{0,1},{1,0},{2,3},{3,2},{4,5},{5,4},{6,7},{7,6},{8,9},{9,8},{10,11... | collective-permute-start | bytes 1572872 | tf_op jit(solution)/shard_map/ppermute | solution.py:379
  98.5 1.0 collective-permute-done.7
  99.5 1.5 %collective-permute-start.11 = (f32[192,128]{1,0:T(8,128)S(1)}, f32[192,128]{1,0:T(8,128)S(1)}, u32[]{:S(2)}, u32[]{:S(2)}) collective-permute-start(f32[192,128]{1,0:T(8,128)S(1)} %slice_add_fusion.4), channel_id=1, source_target_pairs={{0,1},{1,0},{2,3},{3,2},{4,5},{5,4},{6,7},{7,6},{8,9},{9,8},{10,11... | collective-permute-start | bytes 294920 | tf_op jit(solution)/shard_map/ppermute | solution.py:400
  101.0 8.3 %collective-permute-done.11 = f32[192,128]{1,0:T(8,128)S(1)} collective-permute-done((f32[192,128]{1,0:T(8,128)S(1)}, f32[192,128]{1,0:T(8,128)S(1)}, u32[]{:S(2)}, u32[]{:S(2)}) %collective-permute-start.11) | collective-permute-done | bytes 98336 | tf_op jit(solution)/shard_map/ppermute | solution.py:400
  109.3 1.4 %collective-permute-start.12 = (f32[384,128]{1,0:T(8,128)S(1)}, f32[384,128]{1,0:T(8,128)S(1)}, u32[]{:S(2)}, u32[]{:S(2)}) collective-permute-start(f32[384,128]{1,0:T(8,128)S(1)} %pad_maximum_fusion.7), channel_id=1, source_target_pairs={{0,4},{2,6},{4,0},{6,2},{8,12},{10,14},{12,8},{14,10},{16,20},{18,... | collective-permute-start | bytes 589832 | tf_op jit(solution)/shard_map/ppermute | solution.py:400
  110.7 0.0 collective-permute-done.8.refs_7_
  110.7 0.1 fusion.5
  110.8 4.0 %collective-permute-start.9 = (f32[2,128,512]{2,1,0:T(8,128)S(1)}, f32[2,128,512]{2,1,0:T(8,128)S(1)}, u32[]{:S(2)}, u32[]{:S(2)}) collective-permute-start(f32[2,128,512]{2,1,0:T(8,128)S(1)} %get-tuple-element.25), channel_id=1, source_target_pairs={{0,2},{2,0},{4,6},{6,4},{8,10},{10,8},{12,14},{14,12},{16,18},{18,... | collective-permute-start | bytes 1572872 | tf_op jit(solution)/shard_map/ppermute | solution.py:379
  114.8 2.5 %collective-permute-start.10 = (f32[2,128,512]{2,1,0:T(8,128)S(1)}, f32[2,128,512]{2,1,0:T(8,128)S(1)}, u32[]{:S(2)}, u32[]{:S(2)}) collective-permute-start(f32[2,128,512]{2,1,0:T(8,128)S(1)} %get-tuple-element.24), channel_id=1, source_target_pairs={{2,4},{4,2},{6,8},{8,6},{10,12},{12,10},{14,16},{16,14},{18,20},{2... | collective-permute-start | bytes 1572872 | tf_op jit(solution)/shard_map/ppermute | solution.py:379
  117.3 0.0 collective-permute-done.12
  117.4 2.0 %collective-permute-start.13 = (f32[768,128]{1,0:T(8,128)S(1)}, f32[768,128]{1,0:T(8,128)S(1)}, u32[]{:S(2)}, u32[]{:S(2)}) collective-permute-start(f32[768,128]{1,0:T(8,128)S(1)} %pad_maximum_fusion.4), channel_id=1, source_target_pairs={{0,2},{2,0},{4,6},{6,4},{8,10},{10,8},{12,14},{14,12},{16,18},{18,... | collective-permute-start | bytes 1179656 | tf_op jit(solution)/shard_map/ppermute | solution.py:400
  119.4 0.0 collective-permute-done.9.refs_5_
  119.4 11.5 %collective-permute-done.10.refs_6_ = f32[2,128,512]{2,1,0:T(8,128)S(1)} collective-permute-done((f32[2,128,512]{2,1,0:T(8,128)S(1)}, f32[2,128,512]{2,1,0:T(8,128)S(1)}, u32[]{:S(2)}, u32[]{:S(2)}) %collective-permute-start.10) | collective-permute-done | bytes 524320 | tf_op jit(solution)/shard_map/ppermute | solution.py:379
  130.9 2.0 %object_update.1 = f32[2,256,512]{2,1,0:T(8,128)} custom-call(s32[2]{0:T(128)S(1)} %pad_add_fusion.refs_0_.place, f32[2,256,512]{2,1,0:T(8,128)S(1)} %copy-done.1, f32[2,256,512]{2,1,0:T(8,128)S(1)} %copy-done.3, f32[256,512]{1,0:T(8,128)S(1)} %get-tuple-element.10.refs_3_, f32[8,128]{1,0:T(8,128)S(1)} %slice_maximum_fusion.refs_4_, ...), custom_call_target="tpu_custom_call" | custom-call | tf_op jit(solution)/shard_map/object_update/pallas_call | solution.py:339
  132.9 0.0 collective-permute-done.13
  132.9 0.1 broadcast_select_fusion.1
  133.0 0.9 pad_maximum_fusion.2.sums
  133.9 2.3 %probe_update.1 = f32[2,256,256]{2,1,0:T(8,128)} custom-call(f32[1536,128]{1,0:T(8,128)} %pad_maximum_fusion.2.sums, f32[2,256,256]{2,1,0:T(8,128)} %probe.3), custom_call_target="tpu_custom_call" | custom-call | tf_op jit(solution)/shard_map/probe_update/pallas_call | solution.py:365
  (41 shorter events, 0.4 us)
Async XLA Ops:
  0.6 3.8 %copy-start = (f32[2,256,512]{2,1,0:T(8,128)S(1)}, f32[2,256,512]{2,1,0:T(8,128)}, u32[]{:S(2)}) copy-start(f32[2,256,512]{2,1,0:T(8,128)} %refs_1_.3) | copy-start | bytes 3145732
  3.2 7.4 %collective-permute-start = (f32[2,264,128]{2,1,0:T(8,128)S(1)}, f32[2,264,128]{2,1,0:T(8,128)S(1)}, u32[]{:S(2)}, u32[]{:S(2)}) collective-permute-start(f32[2,264,128]{2,1,0:T(8,128)S(1)} %pad_maximum_fusion.5), channel_id=1, source_target_pairs={{0,1},{1,0},{2,3},{3,2},{4,5},{5,4},{6,7},{7,6},{8,9},{9,8},{10,11... | collective-permute-start | bytes 811016 | tf_op jit(solution)/shard_map/ppermute | solution.py:379
  10.6 22.4 %copy-start.2 = (f32[2,256,256]{2,1,0:T(8,128)S(1)}, f32[2,256,256]{2,1,0:T(8,128)}, u32[]{:S(2)}) copy-start(f32[2,256,256]{2,1,0:T(8,128)} %probe.3) | copy-start | bytes 1572868
  10.6 25.7 %copy-start.4 = (s32[1,1,8]{2,1,0:T(1,128)S(1)}, s32[1,1,8]{2,1,0:T(1,128)}, u32[]{:S(2)}) copy-start(s32[1,1,8]{2,1,0:T(1,128)} %refs_1_.2) | copy-start | bytes 100
  10.6 25.7 %copy-start.5 = (s32[1,1,8]{2,1,0:T(1,128)S(1)}, s32[1,1,8]{2,1,0:T(1,128)}, u32[]{:S(2)}) copy-start(s32[1,1,8]{2,1,0:T(1,128)} %refs_2_.1) | copy-start | bytes 100
  10.7 4.7 %collective-permute-start.1 = (f32[2,136,640]{2,1,0:T(8,128)S(1)}, f32[2,136,640]{2,1,0:T(8,128)S(1)}, u32[]{:S(2)}, u32[]{:S(2)}) collective-permute-start(f32[2,136,640]{2,1,0:T(8,128)S(1)} %get-tuple-element.33), channel_id=1, source_target_pairs={{0,2},{2,0},{4,6},{6,4},{8,10},{10,8},{12,14},{14,12},{16,18},{18,... | collective-permute-start | bytes 2088968 | tf_op jit(solution)/shard_map/ppermute | solution.py:379
  12.3 19.9 %collective-permute-start.2 = (f32[2,136,640]{2,1,0:T(8,128)S(1)}, f32[2,136,640]{2,1,0:T(8,128)}, u32[]{:S(2)}, u32[]{:S(2)}) collective-permute-start(f32[2,136,640]{2,1,0:T(8,128)S(1)} %get-tuple-element.32), channel_id=1, source_target_pairs={{2,4},{4,2},{6,8},{8,6},{10,12},{12,10},{14,16},{16,14},{18,20},{2... | collective-permute-start | bytes 2088968 | tf_op jit(solution)/shard_map/ppermute | solution.py:379
  15.5 17.5 %copy-start.7 = (f32[2,136,640]{2,1,0:T(8,128)}, f32[2,136,640]{2,1,0:T(8,128)S(1)}, u32[]{:S(2)}) copy-start(f32[2,136,640]{2,1,0:T(8,128)S(1)} %collective-permute-done.1.refs_5_) | copy-start | bytes 2088964
  61.8 9.6 %copy-start.6 = (f32[3,2,256,128]{3,2,1,0:T(8,128)S(1)}, f32[3,2,256,128]{3,2,1,0:T(8,128)}, u32[]{:S(2)}) copy-start(f32[3,2,256,128]{3,2,1,0:T(8,128)} %get-tuple-element.12) | copy-start | bytes 2359300
  63.7 7.8 %collective-permute-start.3 = (f32[776,128]{1,0:T(8,128)}, f32[776,128]{1,0:T(8,128)}, u32[]{:S(2)}, u32[]{:S(2)}) collective-permute-start(f32[776,128]{1,0:T(8,128)} %pad_maximum_fusion.3), channel_id=1, source_target_pairs={{0,2},{2,0},{4,6},{6,4},{8,10},{10,8},{12,14},{14,12},{16,18},{18,... | collective-permute-start | bytes 1191944 | tf_op jit(solution)/shard_map/ppermute | solution.py:400
  73.2 6.3 %collective-permute-start.4 = (f32[392,128]{1,0:T(8,128)S(1)}, f32[392,128]{1,0:T(8,128)S(1)}, u32[]{:S(2)}, u32[]{:S(2)}) collective-permute-start(f32[392,128]{1,0:T(8,128)S(1)} %pad_maximum_fusion.6), channel_id=1, source_target_pairs={{0,4},{2,6},{4,0},{6,2},{8,12},{10,14},{12,8},{14,10},{16,20},{18,... | collective-permute-start | bytes 602120 | tf_op jit(solution)/shard_map/ppermute | solution.py:400
  79.6 5.7 %collective-permute-start.5 = (f32[200,128]{1,0:T(8,128)S(1)}, f32[200,128]{1,0:T(8,128)S(1)}, u32[]{:S(2)}, u32[]{:S(2)}) collective-permute-start(f32[200,128]{1,0:T(8,128)S(1)} %pad_maximum_fusion.8), channel_id=1, source_target_pairs={{0,1},{1,0},{2,3},{3,2},{4,5},{5,4},{6,7},{7,6},{8,9},{9,8},{10,11... | collective-permute-start | bytes 307208 | tf_op jit(solution)/shard_map/ppermute | solution.py:400
  85.3 6.7 %collective-permute-start.6 = (f32[200,128]{1,0:T(8,128)S(1)}, f32[200,128]{1,0:T(8,128)S(1)}, u32[]{:S(2)}, u32[]{:S(2)}) collective-permute-start(f32[200,128]{1,0:T(8,128)S(1)} %pad_maximum_fusion.9), channel_id=1, source_target_pairs={{0,8},{2,10},{4,12},{6,14},{8,0},{10,2},{12,4},{14,6},{16,24},{18,... | collective-permute-start | bytes 307208 | tf_op jit(solution)/shard_map/ppermute | solution.py:400
  92.0 7.4 %collective-permute-start.7 = (f32[200,128]{1,0:T(8,128)S(1)}, f32[200,128]{1,0:T(8,128)S(1)}, u32[]{:S(2)}, u32[]{:S(2)}) collective-permute-start(f32[200,128]{1,0:T(8,128)S(1)} %pad_maximum_fusion.10), channel_id=1, source_target_pairs={{0,16},{2,18},{4,20},{6,22},{8,24},{10,26},{12,28},{14,30},{16,0},... | collective-permute-start | bytes 307208 | tf_op jit(solution)/shard_map/ppermute | solution.py:400
  97.0 13.7 %collective-permute-start.8 = (f32[2,512,128]{2,1,0:T(8,128)S(1)}, f32[2,512,128]{2,1,0:T(8,128)S(1)}, u32[]{:S(2)}, u32[]{:S(2)}) collective-permute-start(f32[2,512,128]{2,1,0:T(8,128)S(1)} %get-tuple-element.14), channel_id=1, source_target_pairs={{0,1},{1,0},{2,3},{3,2},{4,5},{5,4},{6,7},{7,6},{8,9},{9,8},{10,11... | collective-permute-start | bytes 1572872 | tf_op jit(solution)/shard_map/ppermute | solution.py:379
  99.5 9.8 %collective-permute-start.11 = (f32[192,128]{1,0:T(8,128)S(1)}, f32[192,128]{1,0:T(8,128)S(1)}, u32[]{:S(2)}, u32[]{:S(2)}) collective-permute-start(f32[192,128]{1,0:T(8,128)S(1)} %slice_add_fusion.4), channel_id=1, source_target_pairs={{0,1},{1,0},{2,3},{3,2},{4,5},{5,4},{6,7},{7,6},{8,9},{9,8},{10,11... | collective-permute-start | bytes 294920 | tf_op jit(solution)/shard_map/ppermute | solution.py:400
  101.0 29.9 %copy-start.1 = (f32[2,256,512]{2,1,0:T(8,128)S(1)}, f32[2,256,512]{2,1,0:T(8,128)}, u32[]{:S(2)}) copy-start(f32[2,256,512]{2,1,0:T(8,128)} %refs_1_.3) | copy-start | bytes 3145732
  101.0 29.9 %copy-start.3 = (f32[2,256,512]{2,1,0:T(8,128)S(1)}, f32[2,256,512]{2,1,0:T(8,128)}, u32[]{:S(2)}) copy-start(f32[2,256,512]{2,1,0:T(8,128)} %get-tuple-element.9.refs_2_) | copy-start | bytes 3145732
  109.3 7.9 %collective-permute-start.12 = (f32[384,128]{1,0:T(8,128)S(1)}, f32[384,128]{1,0:T(8,128)S(1)}, u32[]{:S(2)}, u32[]{:S(2)}) collective-permute-start(f32[384,128]{1,0:T(8,128)S(1)} %pad_maximum_fusion.7), channel_id=1, source_target_pairs={{0,4},{2,6},{4,0},{6,2},{8,12},{10,14},{12,8},{14,10},{16,20},{18,... | collective-permute-start | bytes 589832 | tf_op jit(solution)/shard_map/ppermute | solution.py:400
  110.8 8.6 %collective-permute-start.9 = (f32[2,128,512]{2,1,0:T(8,128)S(1)}, f32[2,128,512]{2,1,0:T(8,128)S(1)}, u32[]{:S(2)}, u32[]{:S(2)}) collective-permute-start(f32[2,128,512]{2,1,0:T(8,128)S(1)} %get-tuple-element.25), channel_id=1, source_target_pairs={{0,2},{2,0},{4,6},{6,4},{8,10},{10,8},{12,14},{14,12},{16,18},{18,... | collective-permute-start | bytes 1572872 | tf_op jit(solution)/shard_map/ppermute | solution.py:379
  114.8 16.1 %collective-permute-start.10 = (f32[2,128,512]{2,1,0:T(8,128)S(1)}, f32[2,128,512]{2,1,0:T(8,128)S(1)}, u32[]{:S(2)}, u32[]{:S(2)}) collective-permute-start(f32[2,128,512]{2,1,0:T(8,128)S(1)} %get-tuple-element.24), channel_id=1, source_target_pairs={{2,4},{4,2},{6,8},{8,6},{10,12},{12,10},{14,16},{16,14},{18,20},{2... | collective-permute-start | bytes 1572872 | tf_op jit(solution)/shard_map/ppermute | solution.py:379
  117.4 15.5 %collective-permute-start.13 = (f32[768,128]{1,0:T(8,128)S(1)}, f32[768,128]{1,0:T(8,128)S(1)}, u32[]{:S(2)}, u32[]{:S(2)}) collective-permute-start(f32[768,128]{1,0:T(8,128)S(1)} %pad_maximum_fusion.4), channel_id=1, source_target_pairs={{0,2},{2,0},{4,6},{6,4},{8,10},{10,8},{12,14},{14,12},{16,18},{18,... | collective-permute-start | bytes 1179656 | tf_op jit(solution)/shard_map/ppermute | solution.py:400

commit v2 on v1

v2 whole, which is shorter than its diff:
```python
import functools
import math

import jax
import jax.numpy as jnp
import ml_dtypes
import numpy as np
from jax import lax
from jax.experimental import pallas as pl
from jax.experimental.pallas import tpu as pltpu
from jax.sharding import PartitionSpec as P

H = 128
LANES = 128
CHUNK = 32
WAYS = 2
INFO = 8
BF = jnp.bfloat16
F32 = jnp.float32
MIX_OBJECT = 0.5
MIX_PROBE = 0.5
VMEM = pl.BlockSpec(memory_space=pltpu.VMEM)
SMEM = pl.BlockSpec(memory_space=pltpu.SMEM)


def rounded_pair(table):
    table = table.astype(np.float32)
    high = table.astype(ml_dtypes.bfloat16)
    low = (table - high.astype(np.float32)).astype(ml_dtypes.bfloat16)
    return high, low


def dft_tables(length):
    index = np.arange(length)
    angle = 2.0 * np.pi * ((index[:, None] * index[None, :]) % length) / length
    cos_high, cos_low = rounded_pair(np.cos(angle) / math.sqrt(length))
    sin_high, sin_low = rounded_pair(-np.sin(angle) / math.sqrt(length))
    left = np.concatenate([cos_high, sin_high, cos_high, sin_high, cos_low, sin_low], axis=1)
    right_high = np.block([[cos_high, sin_high], [-sin_high, cos_high]])
    right_low = np.block([[cos_low, sin_low], [-sin_low, cos_low]])
    right = np.concatenate([right_high, right_high, right_low], axis=0)
    return left, right


def split(x):
    high = x.astype(BF)
    return high, (x - high.astype(F32)).astype(BF)


def side_block(place, side, sides, blocks):
    if sides == 1:
        return jnp.where(place[1] == 0, blocks - 1, 0)
    return 0 if side == 0 else blocks - 1


def side_step(place, side, sides):
    if sides == 1:
        return jnp.where(place[1] == 0, 1, -1)
    return -1 if side == 0 else 1


def cover_kernel(tile_rows, tile_cols, sides, place, info, probe, cover, peak, total, power):
    pr = probe.shape[1]
    pieces = pr // LANES
    for j in range(pieces):
        cut = slice(j * LANES, (j + 1) * LANES)
        power[j] = probe[0, :, cut] * probe[0, :, cut] + probe[1, :, cut] * probe[1, :, cut]
    total[...] = jnp.zeros_like(total)
    lanes = lax.broadcasted_iota(jnp.int32, (CHUNK, LANES), 1)
    even = place[0] % 2 == 0
    steps_down = (0, jnp.where(even, 1, -1), jnp.where(even, -1, 1))
    steps_right = (0,) + tuple(side_step(place, s, sides) for s in range(sides))
    for v in range(3):
        for h in range(1 + sides):
            source = v * (1 + sides) + h
            down, right = steps_down[v], steps_right[h]

            def visit(k, carry):
                row = info[source, k] + pr - H + down * tile_rows
                col = info[source, 8 + k] + pr - H + right * tile_cols
                inside = (row > 0) & (row < pr + tile_rows) & (col > 0) & (col < pr + tile_cols)

                @pl.when(inside)
                def _():
                    shift = col & (LANES - 1)
                    block = col >> 7
                    low = lanes < shift
                    for q in range(pr // CHUNK):
                        turned = [
                            pltpu.roll(power[j, q * CHUNK : (q + 1) * CHUNK, :], shift, 1)
                            for j in range(pieces)
                        ]
                        here = pl.ds(row + q * CHUNK, CHUNK)
                        zero = jnp.zeros((CHUNK, LANES), F32)
                        total[block, here, :] += jnp.where(low, zero, turned[0])
                        for j in range(1, pieces):
                            total[block + j, here, :] += jnp.where(low, turned[j - 1], turned[j])
                        total[block + pieces, here, :] += jnp.where(low, turned[-1], zero)

                return carry

            lax.fori_loop(0, info[source, 16], visit, 0)
    first = pr // LANES
    best = jnp.zeros((8, LANES), F32)
    for b in range(tile_cols // LANES):
        own = total[first + b, pr : pr + tile_rows, :]
        cover[:, b * LANES : (b + 1) * LANES] = own
        best = jnp.maximum(best, jnp.max(own.reshape(tile_rows // 8, 8, LANES), axis=0))
    peak[...] = jnp.full((8, LANES), jnp.max(best), F32)


def cover_call(place, info, probe, tile_rows, tile_cols, sides):
    pr = probe.shape[1]
    blocks = (tile_cols + 2 * pr) // LANES + 1
    return pl.pallas_call(
        functools.partial(cover_kernel, tile_rows, tile_cols, sides),
        out_shape=(
            jax.ShapeDtypeStruct((tile_rows, tile_cols), F32),
            jax.ShapeDtypeStruct((8, LANES), F32),
        ),
        in_specs=[SMEM, SMEM, VMEM],
        out_specs=(VMEM, VMEM),
        scratch_shapes=[
            pltpu.VMEM((blocks, tile_rows + 2 * pr, LANES), F32),
            pltpu.VMEM((pr // LANES, pr, LANES), F32),
        ],
        compiler_params=pltpu.CompilerParams(vmem_limit_bytes=24 << 20),
        cost_estimate=pl.CostEstimate(flops=4_000_000, bytes_accessed=8_000_000, transcendentals=0),
        name="cover",
    )(place, info, probe)


def positions_kernel(sides, *refs):
    place, rows, cols, count = refs[:4]
    tile, near, far_side = refs[4:7]
    side_in, corners = refs[7 : 7 + sides], refs[7 + sides : 7 + 2 * sides]
    probe, measured, left, right = refs[7 + 2 * sides : 11 + 2 * sides]
    outs = refs[11 + 2 * sides :]
    middle, near_rim, far_rim = outs[:3]
    side_out = outs[3 : 3 + sides]
    probe_sums = outs[3 + sides]
    ext, grad = outs[4 + sides : 6 + sides]
    scratch = outs[6 + sides :]
    patches, exits, stacks, wides, fields = [scratch[i * WAYS : (i + 1) * WAYS] for i in range(5)]

    pr = probe.shape[1]
    pieces = pr // LANES
    tile_rows, tile_cols = tile.shape[1:]
    ext_rows = tile_rows + 2 * H
    blocks = (tile_cols + 2 * H) // LANES
    own_blocks = tile_cols // LANES
    even = place[0] % 2 == 0
    near_row = pl.multiple_of(jnp.where(even, tile_rows + H, 0), 8)
    far_row = pl.multiple_of(jnp.where(even, 0, tile_rows + H), 8)
    side_blocks = [side_block(place, s, sides, blocks) for s in range(sides)]
    own, near_rows, far_rows = pl.ds(H, tile_rows), pl.ds(near_row, H), pl.ds(far_row, H)
    for ch in range(2):
        if sides == 1:
            ext[ch * blocks + blocks - 1 - side_blocks[0]] = jnp.zeros((ext_rows, LANES), F32)
        for b in range(own_blocks):
            at, cut = ch * blocks + 1 + b, slice(b * LANES, (b + 1) * LANES)
            ext[at, own, :] = tile[ch, :, cut]
            ext[at, near_rows, :] = near[ch, 0:H, cut]
            ext[at, far_rows, :] = far_side[ch, :, cut]
        for s in range(sides):
            at = ch * blocks + side_blocks[s]
            cut = slice(tile_cols + s * LANES, tile_cols + (s + 1) * LANES)
            ext[at, own, :] = side_in[s][ch, 0:tile_rows, :]
            ext[at, near_rows, :] = near[ch, 0:H, cut]
            ext[at, far_rows, :] = corners[s][ch]
    grad[...] = jnp.zeros_like(grad)
    probe_sums[...] = jnp.zeros_like(probe_sums)
    lanes = lax.broadcasted_iota(jnp.int32, (CHUNK, LANES), 1)

    def put(stack, value, part, q, first):
        width = value.shape[1]
        high, low = split(value)
        rows_at = lambda block: slice(block * pr + q * CHUNK, block * pr + (q + 1) * CHUNK)
        here, there = slice(first, first + width), slice(pr + first, pr + first + width)
        if part == 0:
            stack[rows_at(0), here], stack[rows_at(1), there] = high, high
            stack[rows_at(2), here], stack[rows_at(3), there] = low, low
        else:
            stack[rows_at(0), there], stack[rows_at(1), here] = high, -high
            stack[rows_at(2), there], stack[rows_at(3), here] = low, -low

    def times_left(w):
        stack = jnp.concatenate([stacks[w][...], stacks[w][0 : 2 * pr]], axis=0)
        fields[w][...] = jnp.dot(left[...], stack, preferred_element_type=F32)

    def times_right(w):
        for q in range(pr // CHUNK):
            cut = slice(q * CHUNK, (q + 1) * CHUNK)
            high, low = split(fields[w][cut, :])
            wides[w][cut, 0 : 2 * pr] = high
            wides[w][cut, 2 * pr : 4 * pr] = low
        stack = jnp.concatenate([wides[w][...], wides[w][:, 0 : 2 * pr]], axis=1)
        fields[w][...] = jnp.dot(stack, right[...], preferred_element_type=F32)

    def load(w, k):
        row, col = rows[0, 0, k], cols[0, 0, k]
        shift, block = col & (LANES - 1), col >> 7
        back = (LANES - shift) & (LANES - 1)
        keep = lanes < LANES - shift
        for q in range(pr // CHUNK):
            cut = slice(q * CHUNK, (q + 1) * CHUNK)
            here = pl.ds(row + q * CHUNK, CHUNK)
            seen = []
            for ch in range(2):
                turned = [
                    pltpu.roll(ext[ch * blocks + block + j, here, :], back, 1)
                    for j in range(pieces + 1)
                ]
                seen.append([jnp.where(keep, turned[j], turned[j + 1]) for j in range(pieces)])
            for j in range(pieces):
                part = slice(j * LANES, (j + 1) * LANES)
                probe_real, probe_imag = probe[0, cut, part], probe[1, cut, part]
                real, imag = seen[0][j], seen[1][j]
                patches[w][0, cut, part], patches[w][1, cut, part] = real, imag
                exit_real = probe_real * real - probe_imag * imag
                exit_imag = probe_real * imag + probe_imag * real
                exits[w][0, cut, part], exits[w][1, cut, part] = exit_real, exit_imag
                put(stacks[w], exit_real, 0, q, j * LANES)
                put(stacks[w], exit_imag, 1, q, j * LANES)

    def project(w, k):
        for q in range(pr // CHUNK):
            cut = slice(q * CHUNK, (q + 1) * CHUNK)
            real, imag = fields[w][cut, 0:pr], fields[w][cut, pr : 2 * pr]
            factor = jnp.sqrt(measured[0, 0, k, cut, :]) * lax.rsqrt(real * real + imag * imag + 1.0)
            put(stacks[w], real * factor, 0, q, 0)
            put(stacks[w], -(imag * factor), 1, q, 0)

    def finish(w, k, live):
        row, col = rows[0, 0, k], cols[0, 0, k]
        shift, block = col & (LANES - 1), col >> 7
        low = lanes < shift
        zero = jnp.zeros((CHUNK, LANES), F32)
        for q in range(pr // CHUNK):
            cut = slice(q * CHUNK, (q + 1) * CHUNK)
            here = pl.ds(row + q * CHUNK, CHUNK)
            turned = [[], []]
            for j in range(pieces):
                part = slice(j * LANES, (j + 1) * LANES)
                other = slice(pr + j * LANES, pr + (j + 1) * LANES)
                diff_real = fields[w][cut, part] - exits[w][0, cut, part]
                diff_imag = -fields[w][cut, other] - exits[w][1, cut, part]
                real, imag = patches[w][0, cut, part], patches[w][1, cut, part]
                weight = real * real + imag * imag
                if live is not None:
                    diff_real, diff_imag = diff_real * live, diff_imag * live
                    weight = weight * live
                probe_real, probe_imag = probe[0, cut, part], probe[1, cut, part]
                turned[0].append(pltpu.roll(probe_real * diff_real + probe_imag * diff_imag, shift, 1))
                turned[1].append(pltpu.roll(probe_real * diff_imag - probe_imag * diff_real, shift, 1))
                probe_sums[j, 0, cut, :] += real * diff_real + imag * diff_imag
                probe_sums[j, 1, cut, :] += real * diff_imag - imag * diff_real
                probe_sums[j, 2, cut, :] += weight
            for ch in range(2):
                at = ch * blocks + block
                grad[at, here, :] += jnp.where(low, zero, turned[ch][0])
                for j in range(1, pieces):
                    grad[at + j, here, :] += jnp.where(low, turned[ch][j - 1], turned[ch][j])
                grad[at + pieces, here, :] += jnp.where(low, turned[ch][-1], zero)

    live_slots = count[0, 0]

    def visit(i, carry):
        slots = [jnp.minimum(i * WAYS + w, live_slots - 1) for w in range(WAYS)]
        lives = [None] + [jnp.where(i * WAYS + w < live_slots, 1.0, 0.0) for w in range(1, WAYS)]
        for w in range(WAYS):
            load(w, slots[w])
            times_left(w)
        for w in range(WAYS):
            times_right(w)
        for w in range(WAYS):
            project(w, slots[w])
            times_left(w)
        for w in range(WAYS):
            times_right(w)
        for w in range(WAYS):
            finish(w, slots[w], lives[w])
        return carry

    lax.fori_loop(0, (live_slots + WAYS - 1) // WAYS, visit, 0)
    for ch in range(2):
        for b in range(own_blocks):
            at, cut = ch * blocks + 1 + b, slice(b * LANES, (b + 1) * LANES)
            middle[ch, :, cut] = grad[at, own, :]
            near_rim[ch, :, cut] = grad[at, near_rows, :]
            far_rim[ch, :, cut] = grad[at, far_rows, :]
        for s in range(sides):
            at = ch * blocks + side_blocks[s]
            cut = slice(tile_cols + s * LANES, tile_cols + (s + 1) * LANES)
            side_out[s][ch] = grad[at, own, :]
            near_rim[ch, :, cut] = grad[at, near_rows, :]
            far_rim[ch, :, cut] = grad[at, far_rows, :]


def positions_call(place, rows, cols, count, tile, near, far_side, side_in, corners, probe, measured):
    pr = probe.shape[1]
    sides = len(side_in)
    tile_rows, tile_cols = tile.shape[1:]
    ext_rows = tile_rows + 2 * H
    blocks = (tile_cols + 2 * H) // LANES
    left, right = dft_tables(pr)
    shape = lambda *dims: jax.ShapeDtypeStruct(dims, F32)
    slots = measured.shape[2]
    return pl.pallas_call(
        functools.partial(positions_kernel, sides),
        out_shape=(
            shape(2, tile_rows, tile_cols),
            shape(2, H, tile_cols + sides * LANES),
            shape(2, H, tile_cols + sides * LANES),
            *[shape(2, tile_rows, LANES)] * sides,
            shape(pr // LANES, 3, pr, LANES),
        ),
        in_specs=[SMEM] * 4 + [VMEM] * (7 + 2 * sides),
        out_specs=(VMEM,) * (4 + sides),
        scratch_shapes=[
            pltpu.VMEM((2 * blocks, ext_rows, LANES), F32),
            pltpu.VMEM((2 * blocks, ext_rows, LANES), F32),
            *[pltpu.VMEM((2, pr, pr), F32)] * (2 * WAYS),
            *[pltpu.VMEM((4 * pr, 2 * pr), BF)] * WAYS,
            *[pltpu.VMEM((pr, 4 * pr), BF)] * WAYS,
            *[pltpu.VMEM((pr, 2 * pr), F32)] * WAYS,
        ],
        compiler_params=pltpu.CompilerParams(vmem_limit_bytes=44 << 20),
        cost_estimate=pl.CostEstimate(
            flops=slots * 96 * pr * pr * pr, bytes_accessed=16_000_000, transcendentals=slots * 2 * pr * pr
        ),
        name="positions",
    )(place, rows, cols, count, tile, near, far_side, *side_in, *corners, probe, measured,
      jnp.asarray(left), jnp.asarray(right))


def update_kernel(sides, *refs):
    place, tile, middle, cover, peak, near, far_side = refs[:7]
    side_in = refs[7 : 7 + sides]
    own_terms, other_terms, probe, out, new_probe, sums = refs[7 + sides :]
    tile_rows, tile_cols = tile.shape[1:]
    own_blocks = tile_cols // LANES
    even = place[0] % 2 == 0
    sums[...] = middle[...]
    near_row = pl.multiple_of(jnp.where(even, tile_rows - H, 0), 8)
    far_row = pl.multiple_of(jnp.where(even, 0, tile_rows - H), 8)
    sums[:, pl.ds(near_row, H), :] += near[:, :, 0:tile_cols]
    sums[:, pl.ds(far_row, H), :] += far_side[:, :, 0:tile_cols]
    for s in range(sides):
        if sides == 1:
            for edge, where in ((0, own_blocks - 1), (1, 0)):

                @pl.when((place[1] == 0) == (edge == 0))
                def _():
                    sums[:, :, where * LANES : (where + 1) * LANES] += side_in[s][...]
        else:
            where = 0 if s == 0 else own_blocks - 1
            sums[:, :, where * LANES : (where + 1) * LANES] += side_in[s][...]
    top = MIX_OBJECT * peak[0:1, 0:1]
    inverse = 1.0 / ((1.0 - MIX_OBJECT) * cover[...] + top)
    for ch in range(2):
        out[ch] = tile[ch] + sums[ch] * inverse

    pr = probe.shape[1]
    pieces = pr // LANES
    both = (own_terms, other_terms)

    def update(parts):
        flat = [parts[j * len(parts) // pieces] for j in range(pieces)]
        span = flat[0].shape[0] // (pieces // len(parts))
        term = lambda j, ch: flat[j][(j % (pieces // len(parts))) * span + ch * pr :][:pr]
        weights = [term(j, 2) for j in range(pieces)]
        best = functools.reduce(jnp.maximum, weights)
        best = jnp.max(jnp.max(best.reshape(-1, 8, LANES), axis=0), keepdims=True)
        for j in range(pieces):
            cut = slice(j * LANES, (j + 1) * LANES)
            scale = 1.0 / ((1.0 - MIX_PROBE) * weights[j] + MIX_PROBE * best)
            for ch in range(2):
                new_probe[ch, :, cut] = probe[ch, :, cut] + term(j, ch) * scale

    for first in (0, 1):

        @pl.when(place[0] % 2 == first)
        def _():
            update([both[first][...], both[1 - first][...]])


def update_call(place, tile, middle, cover, peak, near, far_side, side_in, own_terms, other_terms, probe):
    sides = len(side_in)
    return pl.pallas_call(
        functools.partial(update_kernel, sides),
        out_shape=(jax.ShapeDtypeStruct(tile.shape, F32), jax.ShapeDtypeStruct(probe.shape, F32)),
        in_specs=[SMEM] + [VMEM] * (9 + sides),
        out_specs=(VMEM, VMEM),
        scratch_shapes=[pltpu.VMEM(tile.shape, F32)],
        compiler_params=pltpu.CompilerParams(vmem_limit_bytes=32 << 20),
        name="update",
    )(place, tile, middle, cover, peak, near, far_side, *side_in, own_terms, other_terms, probe)


def swap(x, axis, first):
    size = lax.axis_size(axis)
    pairs = []
    for i in range(first, size - 1, 2):
        pairs += [(i, i + 1), (i + 1, i)]
    return lax.ppermute(x, axis, pairs)


def shifted(x, axis, by):
    size = lax.axis_size(axis)
    return lax.ppermute(x, axis, [(i, i + by) for i in range(size) if 0 <= i + by < size])


def to_sides(pieces):
    if len(pieces) == 1:
        return [swap(pieces[0], "narrow", 0)]
    return [shifted(pieces[1], "narrow", 1), shifted(pieces[0], "narrow", -1)]


def bits_of(axis):
    size = lax.axis_size(axis)
    return [1 << b for b in range(size.bit_length() - 1)]


def partner(x, axis, bit):
    size = lax.axis_size(axis)
    return lax.ppermute(x, axis, [(i, i ^ bit) for i in range(size)])


def half_of(x, which):
    rows = x.shape[0] // 2
    return lax.dynamic_slice_in_dim(x, which * rows, rows, axis=0)


def bit_state(axis, bit):
    return (lax.axis_index(axis) // bit) % 2


def halve(terms, peak, axis, bit):
    mine = bit_state(axis, bit)
    got = partner(jnp.concatenate([half_of(terms, 1 - mine), peak], axis=0), axis, bit)
    rows = terms.shape[0] // 2
    return half_of(terms, mine) + got[:rows], jnp.maximum(peak, got[rows:])


def double(terms, peak, axis, bit):
    got = partner(jnp.concatenate([terms, peak], axis=0), axis, bit)
    rows = terms.shape[0]
    return terms + got[:rows], jnp.maximum(peak, got[rows:])


def gather(terms, axis, bit):
    first = bit_state(axis, bit) == 0
    got = partner(terms, axis, bit)
    return jnp.concatenate([jnp.where(first, terms, got), jnp.where(first, got, terms)], axis=0)


def to_corners(bands):
    wide, narrow = lax.axis_size("wide"), lax.axis_size("narrow")
    steps = [0] if len(bands) == 1 else [-1, 1]
    got = []
    for s, step in enumerate(steps):
        pairs = []
        for i in range(1, wide - 1, 2):
            for n in range(narrow):
                m = 1 - n if step == 0 else n - step
                if 0 <= m < narrow:
                    pairs += [(i * narrow + n, (i + 1) * narrow + m), ((i + 1) * narrow + n, i * narrow + m)]
        band = bands[0] if step == 0 else bands[1 - s]
        got.append(lax.ppermute(band, ("wide", "narrow"), pairs))
    return got


def after(x, *others):
    return lax.optimization_barrier((x, *others))[0]


def body(tile, probe, measured, rows, cols, counts):
    wide, narrow = lax.axis_index("wide"), lax.axis_index("narrow")
    sides = 1 if lax.axis_size("narrow") == 2 else 2
    tile_rows, tile_cols = tile.shape[1:]
    even = wide % 2 == 0
    place = jnp.stack([wide, narrow]).astype(jnp.int32)

    own_info = jnp.concatenate(
        [rows.reshape(-1), cols.reshape(-1), counts.reshape(-1), jnp.zeros((LANES - 17,), jnp.int32)]
    ).astype(F32)
    info_rows = jnp.broadcast_to(own_info, (2, INFO, LANES))

    near_start = jnp.where(even, tile_rows - H, 0)
    far_start = jnp.where(even, 0, tile_rows - H)
    side_start = jnp.where(narrow == 0, tile_cols - H, 0)
    side_starts = [side_start] if sides == 1 else [0, tile_cols - H]
    edges = [lax.dynamic_slice_in_dim(tile, start, H, axis=2) for start in side_starts]

    side_in = to_sides([jnp.concatenate([e, info_rows], axis=1) for e in edges])
    far_side = swap(lax.dynamic_slice_in_dim(tile, far_start, H, axis=1), "wide", 1)
    corners = to_corners([lax.dynamic_slice_in_dim(e, far_start, H, axis=1) for e in edges])

    mine = lax.dynamic_slice_in_dim(tile, near_start, H, axis=1)
    mine = jnp.concatenate([mine, jnp.pad(info_rows, ((0, 0), (0, 0), (0, tile_cols - LANES)))], axis=1)
    others = [
        jnp.concatenate([lax.dynamic_slice_in_dim(s, near_start, H, axis=1), s[:, tile_rows:]], axis=1)
        for s in side_in
    ]
    near = swap(jnp.concatenate([mine] + others, axis=2), "wide", 0)
    own_infos = jnp.concatenate([info_rows[:1]] + [s[:1, tile_rows:] for s in side_in], axis=0)
    far_infos = swap(own_infos, "wide", 1)
    near_infos = jnp.stack(
        [near[0, H:, :LANES]] + [near[0, H:, tile_cols + s * LANES : tile_cols + (s + 1) * LANES] for s in range(sides)]
    )
    info = jnp.concatenate([own_infos, near_infos, far_infos], axis=0)[:, 0, :32].astype(jnp.int32)
    cover, peak = cover_call(place, info, probe, tile_rows, tile_cols, sides)

    out = positions_call(place, rows, cols, counts, tile, near, far_side, side_in, corners, probe, measured)
    middle, near_rim, far_rim = out[:3]
    side_rims, probe_sums = list(out[3 : 3 + sides]), out[3 + sides]

    terms = probe_sums.reshape(-1, LANES)
    wide_bits, narrow_bits = bits_of("wide"), bits_of("narrow")
    terms, peak = halve(terms, peak, "wide", wide_bits[0])
    near_got = swap(after(near_rim, terms), "wide", 0)
    terms, peak = halve(terms, peak, "wide", wide_bits[1])
    far_got = swap(after(far_rim, terms), "wide", 1)
    for bit in narrow_bits:
        terms, peak = halve(terms, peak, "narrow", bit)
    for bit in wide_bits[2:]:
        terms, peak = double(terms, peak, "wide", bit)
    for bit in narrow_bits[::-1]:
        terms = gather(terms, "narrow", bit)

    def with_rims(piece, s):
        cut = slice(tile_cols + s * LANES, tile_cols + (s + 1) * LANES)
        below = jnp.where(even, near_got[:, :, cut], far_got[:, :, cut])
        above = jnp.where(even, far_got[:, :, cut], near_got[:, :, cut])
        return piece + jnp.concatenate([above, below], axis=1)

    side_got = to_sides([with_rims(piece, s) for s, piece in enumerate(side_rims)])
    terms = gather(terms, "wide", wide_bits[1])
    other_terms = partner(terms, "wide", wide_bits[0])
    return update_call(
        place, tile, middle, cover, peak, near_got, far_got, side_got, terms, other_terms, probe
    )


def solution(mesh):
    placed = (
        P(None, "wide", "narrow"),
        P(),
        P("wide", "narrow", None, None, None),
        P("wide", "narrow", None),
        P("wide", "narrow", None),
        P("wide", "narrow"),
    )
    return jax.shard_map(
        body,
        mesh=mesh,
        in_specs=placed,
        out_specs=(P(None, "wide", "narrow"), P()),
        check_vma=False,
    )
```

time: 136 us -> 136 us (level)
  the two profiles are of different devices: /device:TPU:9 before, /device:TPU:0 now
where the time goes in v2:
time: 136 us; the launch traced here: 135 us
  starting transfers between devices  48.3 us (36%)
  waiting for transfers between devices  37.8 us (28%)
  Pallas kernels  21.5 us (16%)
  local copies, waits for them, and re-layouts  14.6 us (11%)
  other arithmetic  10.7 us (8%)
  between operations  1.69 us (1%)
    ppermute x8, starting transfers between devices, partner(): return lax.ppermute(x, axis, [(i, i ^ bit) for i in range(size)])  39.7 us
    ppermute x8, waiting for transfers between devices, partner(): return lax.ppermute(x, axis, [(i, i ^ bit) for i in range(size)])  26.8 us
    pallas_call x1, Pallas kernels, positions_call(): pl.pallas_call(functools.partial(positions_kernel, sides), out_shape=(sha...  15.8 us
    ppermute x7, waiting for transfers between devices, swap(): return lax.ppermute(x, axis, pairs)  11 us
    unnamed x42, local copies, waits for them, and re-layouts  10.9 us
    ppermute x7, starting transfers between devices, swap(): return lax.ppermute(x, axis, pairs)  8.01 us
    pallas_call x1, Pallas kernels, update_call(): pl.pallas_call(functools.partial(update_kernel, sides), out_shape=(jax.Sh...  2.98 us
  transfers between devices with their start and end apart: 16, of which 9 were waited for; matrix products, arithmetic and copies ran while one was open for 6% of the time, Pallas kernels for 2%

profile of v2, /device:TPU:0, one launch (start us, length us, event | category | flops | bytes accessed | tf_op | source)
XLA Modules:
  0.0 134.6 jit_solution(6738088805069906651)
XLA Ops:
  1.4 1.0 constant_dynamic-slice_fusion.6
  2.6 0.8 add_convert_fusion
  3.5 3.0 %collective-permute-start = (f32[2,264,128]{2,0,1:T(2,128)S(1)}, f32[2,264,128]{2,0,1:T(2,128)S(1)}, u32[]{:S(2)}, u32[]{:S(2)}) collective-permute-start(f32[2,264,128]{2,0,1:T(2,128)S(1)} %pad_maximum_fusion.2), channel_id=1, source_target_pairs={{0,1},{1,0},{2,3},{3,2},{4,5},{5,4},{6,7},{7,6},{8,9},{9,8},{10,11... | collective-permute-start | bytes 811016 | tf_op jit(solution)/shard_map/ppermute | solution.py:406
  6.5 0.9 constant_dynamic-slice_fusion.4
  7.8 5.2 %collective-permute-done = f32[2,264,128]{2,0,1:T(2,128)S(1)} collective-permute-done((f32[2,264,128]{2,0,1:T(2,128)S(1)}, f32[2,264,128]{2,0,1:T(2,128)S(1)}, u32[]{:S(2)}, u32[]{:S(2)}) %collective-permute-start) | collective-permute-done | bytes 270368 | tf_op jit(solution)/shard_map/ppermute | solution.py:406
  13.0 1.2 fusion.1
  15.0 0.7 collective-permute-start.2
  16.4 0.7 copy.13.refs_7_
  17.2 0.9 copy.12.refs_5_
  18.2 2.7 %cover.1 = (f32[256,512]{1,0:T(8,128)S(1)}, f32[8,128]{1,0:T(8,128)S(1)}) custom-call(s32[2]{0:T(128)S(1)} %pad_add_fusion.refs_0_.place, s32[6,32]{1,0:T(8,128)S(1)} %fusion.2.info, f32[2,256,256]{2,1,0:T(8,128)S(1)} %copy-done.1), custom_call_target="tpu_custom_call" | custom-call | flops 4000000 | bytes 8000000 | tf_op jit(solution)/shard_map/cover/pallas_call | solution.py:115
  20.8 0.8 copy-done.3
  21.6 0.8 copy-done.12
  22.4 1.1 copy-done.2
  23.5 1.0 copy-done.5
  24.5 1.0 copy-done.13
  25.5 1.4 %copy-done.14 = bf16[1536,512]{1,0:T(8,128)(2,1)S(1)} copy-done((bf16[1536,512]{1,0:T(8,128)(2,1)S(1)}, bf16[1536,512]{1,0:T(8,128)(2,1)}, u32[]{:S(2)}) %copy-start.14) | copy-done | bytes 1572888
  26.9 1.1 copy-done.15
  28.1 15.8 %positions.1 = (f32[2,256,512]{2,1,0:T(8,128)S(1)}, f32[2,128,640]{2,1,0:T(8,128)S(1)}, f32[2,128,640]{2,1,0:T(8,128)S(1)}, f32[2,256,128]{2,1,0:T(8,128)S(1)}, f32[2,3,256,128]{3,2,1,0:T(8,128)S(1)}) custom-call(s32[2]{0:T(128)S(1)} %pad_add_fusion.refs_0_.place, s32[1,1,8]{2,1,0:T(1,128)S(1)} %copy-done.8, s32[1,1,8]{2,1,0:T(1,128)S(1)} %copy-done.9, ...), custom_call_target="tpu_custom_call" | custom-call | flops 12884901888 | bytes 16000000 | tf_op jit(solution)/shard_map/positions/pallas_call | solution.py:309
  43.9 0.7 copy-done.6
  44.6 0.8 copy-done.10
  45.4 0.8 copy-done.11
  46.3 0.8 pad_maximum_fusion
  47.1 16.4 %collective-permute-start.5 = (f32[776,128]{1,0:T(8,128)}, f32[776,128]{1,0:T(8,128)}, u32[]{:S(2)}, u32[]{:S(2)}) collective-permute-start(f32[776,128]{1,0:T(8,128)} %pad_maximum_fusion), channel_id=1, source_target_pairs={{0,2},{2,0},{4,6},{6,4},{8,10},{10,8},{12,14},{14,12},{16,18},{18,... | collective-permute-start | bytes 1191944 | tf_op jit(solution)/shard_map/ppermute | solution.py:427
  63.4 1.7 %collective-permute-done.5 = f32[776,128]{1,0:T(8,128)} collective-permute-done((f32[776,128]{1,0:T(8,128)}, f32[776,128]{1,0:T(8,128)}, u32[]{:S(2)}, u32[]{:S(2)}) %collective-permute-start.5) | collective-permute-done | bytes 397344 | tf_op jit(solution)/shard_map/ppermute | solution.py:427
  65.1 1.0 slice_add_fusion
  66.2 0.7 slice_maximum_fusion.4
  67.0 3.2 %collective-permute-start.6 = (f32[392,128]{1,0:T(8,128)S(1)}, f32[392,128]{1,0:T(8,128)S(1)}, u32[]{:S(2)}, u32[]{:S(2)}) collective-permute-start(f32[392,128]{1,0:T(8,128)S(1)} %pad_maximum_fusion.3), channel_id=1, source_target_pairs={{0,4},{2,6},{4,0},{6,2},{8,12},{10,14},{12,8},{14,10},{16,20},{18,... | collective-permute-start | bytes 602120 | tf_op jit(solution)/shard_map/ppermute | solution.py:427
  70.1 5.5 %collective-permute-done.6 = f32[392,128]{1,0:T(8,128)S(1)} collective-permute-done((f32[392,128]{1,0:T(8,128)S(1)}, f32[392,128]{1,0:T(8,128)S(1)}, u32[]{:S(2)}, u32[]{:S(2)}) %collective-permute-start.6) | collective-permute-done | bytes 200736 | tf_op jit(solution)/shard_map/ppermute | solution.py:427
  75.7 1.0 slice_add_fusion.1
  76.7 4.1 %collective-permute-start.7 = (f32[200,128]{1,0:T(8,128)S(1)}, f32[200,128]{1,0:T(8,128)S(1)}, u32[]{:S(2)}, u32[]{:S(2)}) collective-permute-start(f32[200,128]{1,0:T(8,128)S(1)} %pad_maximum_fusion.5), channel_id=1, source_target_pairs={{0,1},{1,0},{2,3},{3,2},{4,5},{5,4},{6,7},{7,6},{8,9},{9,8},{10,11... | collective-permute-start | bytes 307208 | tf_op jit(solution)/shard_map/ppermute | solution.py:427
  80.7 2.6 %collective-permute-done.7 = f32[200,128]{1,0:T(8,128)S(1)} collective-permute-done((f32[200,128]{1,0:T(8,128)S(1)}, f32[200,128]{1,0:T(8,128)S(1)}, u32[]{:S(2)}, u32[]{:S(2)}) %collective-permute-start.7) | collective-permute-done | bytes 102432 | tf_op jit(solution)/shard_map/ppermute | solution.py:427
  83.4 5.0 %collective-permute-start.8 = (f32[200,128]{1,0:T(8,128)S(1)}, f32[200,128]{1,0:T(8,128)S(1)}, u32[]{:S(2)}, u32[]{:S(2)}) collective-permute-start(f32[200,128]{1,0:T(8,128)S(1)} %pad_maximum_fusion.6), channel_id=1, source_target_pairs={{0,8},{2,10},{4,12},{6,14},{8,0},{10,2},{12,4},{14,6},{16,24},{18,... | collective-permute-start | bytes 307208 | tf_op jit(solution)/shard_map/ppermute | solution.py:427
  88.4 2.6 %collective-permute-done.8 = f32[200,128]{1,0:T(8,128)S(1)} collective-permute-done((f32[200,128]{1,0:T(8,128)S(1)}, f32[200,128]{1,0:T(8,128)S(1)}, u32[]{:S(2)}, u32[]{:S(2)}) %collective-permute-start.8) | collective-permute-done | bytes 102432 | tf_op jit(solution)/shard_map/ppermute | solution.py:427
  91.1 3.0 %collective-permute-start.9 = (f32[200,128]{1,0:T(8,128)S(1)}, f32[200,128]{1,0:T(8,128)S(1)}, u32[]{:S(2)}, u32[]{:S(2)}) collective-permute-start(f32[200,128]{1,0:T(8,128)S(1)} %pad_maximum_fusion.7), channel_id=1, source_target_pairs={{0,16},{2,18},{4,20},{6,22},{8,24},{10,26},{12,28},{14,30},{16,0},... | collective-permute-start | bytes 307208 | tf_op jit(solution)/shard_map/ppermute | solution.py:427
  94.2 2.6 %collective-permute-done.9 = f32[200,128]{1,0:T(8,128)S(1)} collective-permute-done((f32[200,128]{1,0:T(8,128)S(1)}, f32[200,128]{1,0:T(8,128)S(1)}, u32[]{:S(2)}, u32[]{:S(2)}) %collective-permute-start.9) | collective-permute-done | bytes 102432 | tf_op jit(solution)/shard_map/ppermute | solution.py:427
  97.7 1.5 %collective-permute-start.11 = (f32[2,128,640]{2,1,0:T(8,128)}, f32[2,128,640]{2,1,0:T(8,128)}, u32[]{:S(2)}, u32[]{:S(2)}) collective-permute-start(f32[2,128,640]{2,1,0:T(8,128)} %copy-done.10), channel_id=1, source_target_pairs={{2,4},{4,2},{6,8},{8,6},{10,12},{12,10},{14,16},{16,14},{18,20},{2... | collective-permute-start | bytes 1966088 | tf_op jit(solution)/shard_map/ppermute | solution.py:406
  99.2 3.2 %collective-permute-done.13 = f32[192,128]{1,0:T(8,128)} collective-permute-done((f32[192,128]{1,0:T(8,128)}, f32[192,128]{1,0:T(8,128)}, u32[]{:S(2)}, u32[]{:S(2)}) %collective-permute-start.13) | collective-permute-done | bytes 98336 | tf_op jit(solution)/shard_map/ppermute | solution.py:427
  102.4 1.0 broadcast_select_fusion.3
  104.0 0.7 pad_maximum_fusion.4
  104.7 2.3 %collective-permute-start.14 = (f32[384,128]{1,0:T(8,128)}, f32[384,128]{1,0:T(8,128)}, u32[]{:S(2)}, u32[]{:S(2)}) collective-permute-start(f32[384,128]{1,0:T(8,128)} %pad_maximum_fusion.4), channel_id=1, source_target_pairs={{0,4},{2,6},{4,0},{6,2},{8,12},{10,14},{12,8},{14,10},{16,20},{18,... | collective-permute-start | bytes 589832 | tf_op jit(solution)/shard_map/ppermute | solution.py:427
  107.0 8.5 %collective-permute-done.14 = f32[384,128]{1,0:T(8,128)} collective-permute-done((f32[384,128]{1,0:T(8,128)}, f32[384,128]{1,0:T(8,128)}, u32[]{:S(2)}, u32[]{:S(2)}) %collective-permute-start.14) | collective-permute-done | bytes 196640 | tf_op jit(solution)/shard_map/ppermute | solution.py:427
  115.5 1.1 broadcast_select_fusion.1
  116.6 5.5 %collective-permute-start.15 = (f32[768,128]{1,0:T(8,128)S(1)}, f32[768,128]{1,0:T(8,128)S(1)}, u32[]{:S(2)}, u32[]{:S(2)}) collective-permute-start(f32[768,128]{1,0:T(8,128)S(1)} %pad_maximum_fusion.1.refs_8_), channel_id=1, source_target_pairs={{0,2},{2,0},{4,6},{6,4},{8,10},{10,8},{12,14},{14,12},{16,18},{18,... | collective-permute-start | bytes 1179656 | tf_op jit(solution)/shard_map/ppermute | solution.py:427
  122.1 0.9 slice_select_fusion.1
  123.0 2.1 %collective-permute-start.12 = (f32[2,256,128]{2,1,0:T(8,128)S(1)}, f32[2,256,128]{2,1,0:T(8,128)S(1)}, u32[]{:S(2)}, u32[]{:S(2)}) collective-permute-start(f32[2,256,128]{2,1,0:T(8,128)S(1)} %maximum_add_fusion), channel_id=1, source_target_pairs={{0,1},{1,0},{2,3},{3,2},{4,5},{5,4},{6,7},{7,6},{8,9},{9,8},{10,11... | collective-permute-start | bytes 786440 | tf_op jit(solution)/shard_map/ppermute | solution.py:406
  125.1 0.7 slice_maximum_fusion.refs_4_
  125.8 5.8 %collective-permute-done.12.refs_7_ = f32[2,256,128]{2,1,0:T(8,128)S(1)} collective-permute-done((f32[2,256,128]{2,1,0:T(8,128)S(1)}, f32[2,256,128]{2,1,0:T(8,128)S(1)}, u32[]{:S(2)}, u32[]{:S(2)}) %collective-permute-start.12) | collective-permute-done | bytes 262176 | tf_op jit(solution)/shard_map/ppermute | solution.py:406
  131.6 3.0 %update.1 = (f32[2,256,512]{2,1,0:T(8,128)}, f32[2,256,256]{2,1,0:T(8,128)}) custom-call(s32[2]{0:T(128)S(1)} %pad_add_fusion.refs_0_.place, f32[2,256,512]{2,1,0:T(8,128)S(1)} %copy-done, f32[2,256,512]{2,1,0:T(8,128)S(1)} %get-tuple-element.11.refs_2_, f32[256,512]{1,0:T(8,128)S(1)} %copy-done.4, f32[8,128]{1,0:T(8,128)S(1)} %slice_maximum_fusion.refs_4_, ...), custom_call_target="tpu_custom_call" | custom-call | tf_op jit(solution)/shard_map/update/pallas_call | solution.py:390
  (72 shorter events, 4.2 us)
Async XLA Ops:
  0.6 5.9 %copy-start = (f32[2,256,512]{2,1,0:T(8,128)S(1)}, f32[2,256,512]{2,1,0:T(8,128)}, u32[]{:S(2)}) copy-start(f32[2,256,512]{2,1,0:T(8,128)} %refs_1_.3) | copy-start | bytes 3145732
  3.5 9.5 %collective-permute-start = (f32[2,264,128]{2,0,1:T(2,128)S(1)}, f32[2,264,128]{2,0,1:T(2,128)S(1)}, u32[]{:S(2)}, u32[]{:S(2)}) collective-permute-start(f32[2,264,128]{2,0,1:T(2,128)S(1)} %pad_maximum_fusion.2), channel_id=1, source_target_pairs={{0,1},{1,0},{2,3},{3,2},{4,5},{5,4},{6,7},{7,6},{8,9},{9,8},{10,11... | collective-permute-start | bytes 811016 | tf_op jit(solution)/shard_map/ppermute | solution.py:406
  7.8 10.4 %copy-start.1 = (f32[2,256,256]{2,1,0:T(8,128)S(1)}, f32[2,256,256]{2,1,0:T(8,128)}, u32[]{:S(2)}) copy-start(f32[2,256,256]{2,1,0:T(8,128)} %refs_10_.3) | copy-start | bytes 1572868
  13.0 9.4 %copy-start.8 = (s32[1,1,8]{2,1,0:T(1,128)S(1)}, s32[1,1,8]{2,1,0:T(1,128)}, u32[]{:S(2)}) copy-start(s32[1,1,8]{2,1,0:T(1,128)} %refs_1_.2) | copy-start | bytes 100
  13.0 9.4 %copy-start.9 = (s32[1,1,8]{2,1,0:T(1,128)S(1)}, s32[1,1,8]{2,1,0:T(1,128)}, u32[]{:S(2)}) copy-start(s32[1,1,8]{2,1,0:T(1,128)} %refs_2_.1) | copy-start | bytes 100
  14.2 3.0 %collective-permute-start.1 = (f32[2,136,640]{2,0,1:T(2,128)}, f32[2,136,640]{2,0,1:T(2,128)S(1)}, u32[]{:S(2)}, u32[]{:S(2)}) collective-permute-start(f32[2,136,640]{2,0,1:T(2,128)} %fusion.1), channel_id=1, source_target_pairs={{0,2},{2,0},{4,6},{6,4},{8,10},{10,8},{12,14},{14,12},{16,18},{18,... | collective-permute-start | bytes 2088968 | tf_op jit(solution)/shard_map/ppermute | solution.py:406
  14.3 7.3 %collective-permute-start.3 = (f32[2,128,128]{2,1,0:T(8,128)S(1)}, f32[2,128,128]{2,1,0:T(8,128)S(1)}, u32[]{:S(2)}, u32[]{:S(2)}) collective-permute-start(f32[2,128,128]{2,1,0:T(8,128)S(1)} %constant_dynamic-slice_fusion.3), channel_id=1, source_target_pairs={{2,5},{4,3},{3,4},{5,2},{6,9},{8,7},{7,8},{9,6},{10,13},{12,11},{1... | collective-permute-start | bytes 393224 | tf_op jit(solution)/shard_map/ppermute | solution.py:470
  15.0 6.7 %collective-permute-start.2 = (f32[2,128,512]{2,1,0:T(8,128)}, f32[2,128,512]{2,1,0:T(8,128)S(1)}, u32[]{:S(2)}, u32[]{:S(2)}) collective-permute-start(f32[2,128,512]{2,1,0:T(8,128)} %get-tuple-element.22), channel_id=1, source_target_pairs={{2,4},{4,2},{6,8},{8,6},{10,12},{12,10},{14,16},{16,14},{18,20},{2... | collective-permute-start | bytes 1572872 | tf_op jit(solution)/shard_map/ppermute | solution.py:406
  15.8 2.3 %collective-permute-start.4 = (f32[2,8,128]{2,0,1:T(2,128)S(1)}, f32[2,8,128]{2,0,1:T(2,128)S(1)}, u32[]{:S(2)}, u32[]{:S(2)}) collective-permute-start(f32[2,8,128]{2,0,1:T(2,128)S(1)} %pad_maximum_fusion.8), channel_id=1, source_target_pairs={{2,4},{4,2},{6,8},{8,6},{10,12},{12,10},{14,16},{16,14},{18,20},{2... | collective-permute-start | bytes 24584 | tf_op jit(solution)/shard_map/ppermute | solution.py:406
  20.8 0.8 copy-start.3
  21.6 0.8 copy-start.12
  22.4 1.1 copy-start.2
  23.5 1.0 copy-start.5
  24.5 1.0 copy-start.13
  25.5 1.4 %copy-start.14 = (bf16[1536,512]{1,0:T(8,128)(2,1)S(1)}, bf16[1536,512]{1,0:T(8,128)(2,1)}, u32[]{:S(2)}) copy-start(bf16[1536,512]{1,0:T(8,128)(2,1)} %constant.108.clone.refs_12_) | copy-start | bytes 4718596
  26.9 1.1 copy-start.15
  43.9 0.7 copy-start.6
  44.6 0.8 copy-start.10
  45.4 0.8 copy-start.11
  47.1 18.1 %collective-permute-start.5 = (f32[776,128]{1,0:T(8,128)}, f32[776,128]{1,0:T(8,128)}, u32[]{:S(2)}, u32[]{:S(2)}) collective-permute-start(f32[776,128]{1,0:T(8,128)} %pad_maximum_fusion), channel_id=1, source_target_pairs={{0,2},{2,0},{4,6},{6,4},{8,10},{10,8},{12,14},{14,12},{16,18},{18,... | collective-permute-start | bytes 1191944 | tf_op jit(solution)/shard_map/ppermute | solution.py:427
  66.2 0.7 copy-start.16
  67.0 8.7 %collective-permute-start.6 = (f32[392,128]{1,0:T(8,128)S(1)}, f32[392,128]{1,0:T(8,128)S(1)}, u32[]{:S(2)}, u32[]{:S(2)}) collective-permute-start(f32[392,128]{1,0:T(8,128)S(1)} %pad_maximum_fusion.3), channel_id=1, source_target_pairs={{0,4},{2,6},{4,0},{6,2},{8,12},{10,14},{12,8},{14,10},{16,20},{18,... | collective-permute-start | bytes 602120 | tf_op jit(solution)/shard_map/ppermute | solution.py:427
  76.7 6.7 %collective-permute-start.7 = (f32[200,128]{1,0:T(8,128)S(1)}, f32[200,128]{1,0:T(8,128)S(1)}, u32[]{:S(2)}, u32[]{:S(2)}) collective-permute-start(f32[200,128]{1,0:T(8,128)S(1)} %pad_maximum_fusion.5), channel_id=1, source_target_pairs={{0,1},{1,0},{2,3},{3,2},{4,5},{5,4},{6,7},{7,6},{8,9},{9,8},{10,11... | collective-permute-start | bytes 307208 | tf_op jit(solution)/shard_map/ppermute | solution.py:427
  83.4 39.6 %copy-start.7 = (f32[2,256,128]{2,1,0:T(8,128)S(1)}, f32[2,256,128]{2,1,0:T(8,128)}, u32[]{:S(2)}) copy-start(f32[2,256,128]{2,1,0:T(8,128)} %copy-done.6) | copy-start | bytes 786436
  83.4 7.7 %collective-permute-start.8 = (f32[200,128]{1,0:T(8,128)S(1)}, f32[200,128]{1,0:T(8,128)S(1)}, u32[]{:S(2)}, u32[]{:S(2)}) collective-permute-start(f32[200,128]{1,0:T(8,128)S(1)} %pad_maximum_fusion.6), channel_id=1, source_target_pairs={{0,8},{2,10},{4,12},{6,14},{8,0},{10,2},{12,4},{14,6},{16,24},{18,... | collective-permute-start | bytes 307208 | tf_op jit(solution)/shard_map/ppermute | solution.py:427
  91.1 5.7 %collective-permute-start.9 = (f32[200,128]{1,0:T(8,128)S(1)}, f32[200,128]{1,0:T(8,128)S(1)}, u32[]{:S(2)}, u32[]{:S(2)}) collective-permute-start(f32[200,128]{1,0:T(8,128)S(1)} %pad_maximum_fusion.7), channel_id=1, source_target_pairs={{0,16},{2,18},{4,20},{6,22},{8,24},{10,26},{12,28},{14,30},{16,0},... | collective-permute-start | bytes 307208 | tf_op jit(solution)/shard_map/ppermute | solution.py:427
  96.8 0.7 copy-start.19
  97.5 4.9 %collective-permute-start.13 = (f32[192,128]{1,0:T(8,128)}, f32[192,128]{1,0:T(8,128)}, u32[]{:S(2)}, u32[]{:S(2)}) collective-permute-start(f32[192,128]{1,0:T(8,128)} %slice_add_fusion.2), channel_id=1, source_target_pairs={{0,1},{1,0},{2,3},{3,2},{4,5},{5,4},{6,7},{7,6},{8,9},{9,8},{10,11... | collective-permute-start | bytes 294920 | tf_op jit(solution)/shard_map/ppermute | solution.py:427
  97.7 24.4 %collective-permute-start.10 = (f32[2,128,640]{2,1,0:T(8,128)}, f32[2,128,640]{2,1,0:T(8,128)S(1)}, u32[]{:S(2)}, u32[]{:S(2)}) collective-permute-start(f32[2,128,640]{2,1,0:T(8,128)} %copy-done.11), channel_id=1, source_target_pairs={{0,2},{2,0},{4,6},{6,4},{8,10},{10,8},{12,14},{14,12},{16,18},{18,... | collective-permute-start | bytes 1966088 | tf_op jit(solution)/shard_map/ppermute | solution.py:406
  97.7 24.4 %collective-permute-start.11 = (f32[2,128,640]{2,1,0:T(8,128)}, f32[2,128,640]{2,1,0:T(8,128)}, u32[]{:S(2)}, u32[]{:S(2)}) collective-permute-start(f32[2,128,640]{2,1,0:T(8,128)} %copy-done.10), channel_id=1, source_target_pairs={{2,4},{4,2},{6,8},{8,6},{10,12},{12,10},{14,16},{16,14},{18,20},{2... | collective-permute-start | bytes 1966088 | tf_op jit(solution)/shard_map/ppermute | solution.py:406
  103.4 0.6 copy-start.17
  103.4 1.3 copy-start.18
  104.7 10.8 %collective-permute-start.14 = (f32[384,128]{1,0:T(8,128)}, f32[384,128]{1,0:T(8,128)}, u32[]{:S(2)}, u32[]{:S(2)}) collective-permute-start(f32[384,128]{1,0:T(8,128)} %pad_maximum_fusion.4), channel_id=1, source_target_pairs={{0,4},{2,6},{4,0},{6,2},{8,12},{10,14},{12,8},{14,10},{16,20},{18,... | collective-permute-start | bytes 589832 | tf_op jit(solution)/shard_map/ppermute | solution.py:427
  107.0 24.6 %copy-start.4 = (f32[256,512]{1,0:T(8,128)S(1)}, f32[256,512]{1,0:T(8,128)}, u32[]{:S(2)}) copy-start(f32[256,512]{1,0:T(8,128)} %copy-done.3) | copy-start | bytes 1572868
  116.6 15.0 %collective-permute-start.15 = (f32[768,128]{1,0:T(8,128)S(1)}, f32[768,128]{1,0:T(8,128)S(1)}, u32[]{:S(2)}, u32[]{:S(2)}) collective-permute-start(f32[768,128]{1,0:T(8,128)S(1)} %pad_maximum_fusion.1.refs_8_), channel_id=1, source_target_pairs={{0,2},{2,0},{4,6},{6,4},{8,10},{10,8},{12,14},{14,12},{16,18},{18,... | collective-permute-start | bytes 1179656 | tf_op jit(solution)/shard_map/ppermute | solution.py:427
  123.0 8.6 %collective-permute-start.12 = (f32[2,256,128]{2,1,0:T(8,128)S(1)}, f32[2,256,128]{2,1,0:T(8,128)S(1)}, u32[]{:S(2)}, u32[]{:S(2)}) collective-permute-start(f32[2,256,128]{2,1,0:T(8,128)S(1)} %maximum_add_fusion), channel_id=1, source_target_pairs={{0,1},{1,0},{2,3},{3,2},{4,5},{5,4},{6,7},{7,6},{8,9},{9,8},{10,11... | collective-permute-start | bytes 786440 | tf_op jit(solution)/shard_map/ppermute | solution.py:406

commit v3 on v2

--- a/solution.py
+++ b/solution.py
@@ -133,9 +133,9 @@
 def positions_kernel(sides, *refs):
     place, rows, cols, count = refs[:4]
     tile, near, far_side = refs[4:7]
-    side_in, corners = refs[7 : 7 + sides], refs[7 + sides : 7 + 2 * sides]
-    probe, measured, left, right = refs[7 + 2 * sides : 11 + 2 * sides]
-    outs = refs[11 + 2 * sides :]
+    side_in, near_corners, far_corners = [refs[7 + i * sides : 7 + (i + 1) * sides] for i in range(3)]
+    probe, measured, left, right = refs[7 + 3 * sides : 11 + 3 * sides]
+    outs = refs[11 + 3 * sides :]
     middle, near_rim, far_rim = outs[:3]
     side_out = outs[3 : 3 + sides]
     probe_sums = outs[3 + sides]
@@ -161,13 +161,12 @@
             at, cut = ch * blocks + 1 + b, slice(b * LANES, (b + 1) * LANES)
             ext[at, own, :] = tile[ch, :, cut]
             ext[at, near_rows, :] = near[ch, 0:H, cut]
-            ext[at, far_rows, :] = far_side[ch, :, cut]
+            ext[at, far_rows, :] = far_side[ch, 0:H, cut]
         for s in range(sides):
             at = ch * blocks + side_blocks[s]
-            cut = slice(tile_cols + s * LANES, tile_cols + (s + 1) * LANES)
             ext[at, own, :] = side_in[s][ch, 0:tile_rows, :]
-            ext[at, near_rows, :] = near[ch, 0:H, cut]
-            ext[at, far_rows, :] = corners[s][ch]
+            ext[at, near_rows, :] = near_corners[s][ch, 0:H, :]
+            ext[at, far_rows, :] = far_corners[s][ch, 0:H, :]
     grad[...] = jnp.zeros_like(grad)
     probe_sums[...] = jnp.zeros_like(probe_sums)
     lanes = lax.broadcasted_iota(jnp.int32, (CHUNK, LANES), 1)
@@ -297,7 +296,9 @@
             far_rim[ch, :, cut] = grad[at, far_rows, :]
 
 
-def positions_call(place, rows, cols, count, tile, near, far_side, side_in, corners, probe, measured):
+def positions_call(
+    place, rows, cols, count, tile, near, far_side, side_in, near_corners, far_corners, probe, measured
+):
     pr = probe.shape[1]
     sides = len(side_in)
     tile_rows, tile_cols = tile.shape[1:]
@@ -315,7 +316,7 @@
             *[shape(2, tile_rows, LANES)] * sides,
             shape(pr // LANES, 3, pr, LANES),
         ),
-        in_specs=[SMEM] * 4 + [VMEM] * (7 + 2 * sides),
+        in_specs=[SMEM] * 4 + [VMEM] * (7 + 3 * sides),
         out_specs=(VMEM,) * (4 + sides),
         scratch_shapes=[
             pltpu.VMEM((2 * blocks, ext_rows, LANES), F32),
@@ -325,12 +326,12 @@
             *[pltpu.VMEM((pr, 4 * pr), BF)] * WAYS,
             *[pltpu.VMEM((pr, 2 * pr), F32)] * WAYS,
         ],
-        compiler_params=pltpu.CompilerParams(vmem_limit_bytes=44 << 20),
+        compiler_params=pltpu.CompilerParams(vmem_limit_bytes=28 << 20),
         cost_estimate=pl.CostEstimate(
             flops=slots * 96 * pr * pr * pr, bytes_accessed=16_000_000, transcendentals=slots * 2 * pr * pr
         ),
         name="positions",
-    )(place, rows, cols, count, tile, near, far_side, *side_in, *corners, probe, measured,
+    )(place, rows, cols, count, tile, near, far_side, *side_in, *near_corners, *far_corners, probe, measured,
       jnp.asarray(left), jnp.asarray(right))
 
 
@@ -356,7 +357,8 @@
         else:
             where = 0 if s == 0 else own_blocks - 1
             sums[:, :, where * LANES : (where + 1) * LANES] += side_in[s][...]
-    top = MIX_OBJECT * peak[0:1, 0:1]
+    rows = own_terms.shape[0]
+    top = MIX_OBJECT * jnp.maximum(peak[0:1, 0:1], other_terms[rows : rows + 1, 0:1])
     inverse = 1.0 / ((1.0 - MIX_OBJECT) * cover[...] + top)
     for ch in range(2):
         out[ch] = tile[ch] + sums[ch] * inverse
@@ -382,7 +384,7 @@
 
         @pl.when(place[0] % 2 == first)
         def _():
-            update([both[first][...], both[1 - first][...]])
+            update([both[first][0:rows, :], both[1 - first][0:rows, :]])
 
 
 def update_call(place, tile, middle, cover, peak, near, far_side, side_in, own_terms, other_terms, probe):
@@ -436,11 +438,9 @@
     return (lax.axis_index(axis) // bit) % 2
 
 
-def halve(terms, peak, axis, bit):
+def halve(terms, axis, bit):
     mine = bit_state(axis, bit)
-    got = partner(jnp.concatenate([half_of(terms, 1 - mine), peak], axis=0), axis, bit)
-    rows = terms.shape[0] // 2
-    return half_of(terms, mine) + got[:rows], jnp.maximum(peak, got[rows:])
+    return half_of(terms, mine) + partner(half_of(terms, 1 - mine), axis, bit)
 
 
 def double(terms, peak, axis, bit):
@@ -449,19 +449,21 @@
     return terms + got[:rows], jnp.maximum(peak, got[rows:])
 
 
-def gather(terms, axis, bit):
+def gather(terms, peak, axis, bit):
     first = bit_state(axis, bit) == 0
-    got = partner(terms, axis, bit)
-    return jnp.concatenate([jnp.where(first, terms, got), jnp.where(first, got, terms)], axis=0)
-
-
-def to_corners(bands):
+    got = partner(jnp.concatenate([terms, peak], axis=0), axis, bit)
+    rows = terms.shape[0]
+    other, peak = got[:rows], jnp.maximum(peak, got[rows:])
+    return jnp.concatenate([jnp.where(first, terms, other), jnp.where(first, other, terms)], axis=0), peak
+
+
+def to_corners(bands, first):
     wide, narrow = lax.axis_size("wide"), lax.axis_size("narrow")
     steps = [0] if len(bands) == 1 else [-1, 1]
     got = []
     for s, step in enumerate(steps):
         pairs = []
-        for i in range(1, wide - 1, 2):
+        for i in range(first, wide - 1, 2):
             for n in range(narrow):
                 m = 1 - n if step == 0 else n - step
                 if 0 <= m < narrow:
@@ -491,43 +493,47 @@
     far_start = jnp.where(even, 0, tile_rows - H)
     side_start = jnp.where(narrow == 0, tile_cols - H, 0)
     side_starts = [side_start] if sides == 1 else [0, tile_cols - H]
-    edges = [lax.dynamic_slice_in_dim(tile, start, H, axis=2) for start in side_starts]
-
-    side_in = to_sides([jnp.concatenate([e, info_rows], axis=1) for e in edges])
-    far_side = swap(lax.dynamic_slice_in_dim(tile, far_start, H, axis=1), "wide", 1)
-    corners = to_corners([lax.dynamic_slice_in_dim(e, far_start, H, axis=1) for e in edges])
-
-    mine = lax.dynamic_slice_in_dim(tile, near_start, H, axis=1)
-    mine = jnp.concatenate([mine, jnp.pad(info_rows, ((0, 0), (0, 0), (0, tile_cols - LANES)))], axis=1)
-    others = [
-        jnp.concatenate([lax.dynamic_slice_in_dim(s, near_start, H, axis=1), s[:, tile_rows:]], axis=1)
-        for s in side_in
-    ]
-    near = swap(jnp.concatenate([mine] + others, axis=2), "wide", 0)
-    own_infos = jnp.concatenate([info_rows[:1]] + [s[:1, tile_rows:] for s in side_in], axis=0)
-    far_infos = swap(own_infos, "wide", 1)
-    near_infos = jnp.stack(
-        [near[0, H:, :LANES]] + [near[0, H:, tile_cols + s * LANES : tile_cols + (s + 1) * LANES] for s in range(sides)]
+
+    def cut_out(row, height, col, width):
+        piece = lax.dynamic_slice(tile, (0, row, col), (2, height, width))
+        notes = jnp.pad(info_rows, ((0, 0), (0, 0), (0, width - LANES)))
+        return jnp.concatenate([piece, notes], axis=1)
+
+    far_band = cut_out(far_start, H, 0, tile_cols)
+    near_band = cut_out(near_start, H, 0, tile_cols)
+    edges = [cut_out(0, tile_rows, start, H) for start in side_starts]
+    far_ends = [cut_out(far_start, H, start, H) for start in side_starts]
+    near_ends = [cut_out(near_start, H, start, H) for start in side_starts]
+    far_band, near_band, edges, far_ends, near_ends = lax.optimization_barrier(
+        (far_band, near_band, edges, far_ends, near_ends)
     )
-    info = jnp.concatenate([own_infos, near_infos, far_infos], axis=0)[:, 0, :32].astype(jnp.int32)
-    cover, peak = cover_call(place, info, probe, tile_rows, tile_cols, sides)
-
-    out = positions_call(place, rows, cols, counts, tile, near, far_side, side_in, corners, probe, measured)
+    far_side = swap(far_band, "wide", 1)
+    far_corners = to_corners(far_ends, 1)
+    side_in = to_sides(edges)
+    near_corners = to_corners(near_ends, 0)
+    near = swap(near_band, "wide", 0)
+
+    out = positions_call(place, rows, cols, counts, tile, near, far_side, side_in, near_corners, far_corners, probe, measured)
     middle, near_rim, far_rim = out[:3]
     side_rims, probe_sums = list(out[3 : 3 + sides]), out[3 + sides]
 
     terms = probe_sums.reshape(-1, LANES)
     wide_bits, narrow_bits = bits_of("wide"), bits_of("narrow")
-    terms, peak = halve(terms, peak, "wide", wide_bits[0])
+    terms = halve(terms, "wide", wide_bits[0])
     near_got = swap(after(near_rim, terms), "wide", 0)
-    terms, peak = halve(terms, peak, "wide", wide_bits[1])
+    notes = [side_in[s][0, tile_rows:] for s in range(sides)]
+    notes += [near[0, H:, :LANES]] + [c[0, H:] for c in near_corners]
+    notes += [far_side[0, H:, :LANES]] + [c[0, H:] for c in far_corners]
+    info = jnp.stack([own_info[:32]] + [x[0, :32] for x in notes]).astype(jnp.int32)
+    cover, peak = cover_call(place, after(info, terms), probe, tile_rows, tile_cols, sides)
+    terms = halve(terms, "wide", wide_bits[1])
     far_got = swap(after(far_rim, terms), "wide", 1)
     for bit in narrow_bits:
-        terms, peak = halve(terms, peak, "narrow", bit)
+        terms = halve(terms, "narrow", bit)
     for bit in wide_bits[2:]:
         terms, peak = double(terms, peak, "wide", bit)
     for bit in narrow_bits[::-1]:
-        terms = gather(terms, "narrow", bit)
+        terms, peak = gather(terms, peak, "narrow", bit)
 
     def with_rims(piece, s):
         cut = slice(tile_cols + s * LANES, tile_cols + (s + 1) * LANES)
@@ -536,8 +542,8 @@
         return piece + jnp.concatenate([above, below], axis=1)
 
     side_got = to_sides([with_rims(piece, s) for s, piece in enumerate(side_rims)])
-    terms = gather(terms, "wide", wide_bits[1])
-    other_terms = partner(terms, "wide", wide_bits[0])
+    terms, peak = gather(terms, peak, "wide", wide_bits[1])
+    other_terms = partner(jnp.concatenate([terms, peak], axis=0), "wide", wide_bits[0])
     return update_call(
         place, tile, middle, cover, peak, near_got, far_got, side_got, terms, other_terms, probe
     )

time: 136 us -> 118 us (0.87)
  the two profiles are of different devices: /device:TPU:0 before, /device:TPU:18 now
where the time goes in v3:
time: 118 us
  waiting for transfers between devices  56.1 us (48%)
  Pallas kernels  26 us (22%)
  starting transfers between devices  17.7 us (15%)
  local copies, waits for them, and re-layouts  10.9 us (9%)
  other arithmetic  5.65 us (5%)
  between operations  1.89 us (2%)
    ppermute x6, waiting for transfers between devices, swap(): return lax.ppermute(x, axis, pairs)  33.7 us
    ppermute x8, waiting for transfers between devices, partner(): return lax.ppermute(x, axis, [(i, i ^ bit) for i in range(size)])  22.4 us
    pallas_call x1, Pallas kernels, positions_call(): pl.pallas_call(functools.partial(positions_kernel, sides), out_shape=(sha...  19.8 us
    ppermute x6, starting transfers between devices, swap(): return lax.ppermute(x, axis, pairs)  7.12 us
    ppermute x8, starting transfers between devices, partner(): return lax.ppermute(x, axis, [(i, i ^ bit) for i in range(size)])  6.93 us
    unnamed x30, local copies, waits for them, and re-layouts  6.82 us
    ppermute x2, starting transfers between devices, to_corners(): got.append(lax.ppermute(band, ('wide', 'narrow'), pairs))  3.61 us
    dynamic_slice x3, local copies, waits for them, and re-layouts, cut_out(): piece = lax.dynamic_slice(tile, (0, row, col), (2, height, width))  3.26 us
  transfers between devices with their start and end apart: 16, of which 11 were waited for; matrix products, arithmetic and copies ran while one was open for 3% of the time, Pallas kernels for 3%

profile of v3, /device:TPU:18, one launch (start us, length us, event | category | flops | bytes accessed | tf_op | source)
XLA Modules:
  0.0 118.2 jit_solution(17188080477951774170)
XLA Ops:
  0.7 1.0 constant_dynamic-slice_fusion.5
  1.7 1.0 constant_dynamic-slice_fusion.3
  2.7 1.3 %constant_dynamic-slice_fusion.6 = (f32[2,128,512]{2,1,0:T(8,128)S(1)}, f32[2,128,512]{2,1,0:T(8,128)S(1)}) fusion(f32[2,256,512]{2,1,0:T(8,128)} %refs_1_.3, s32[]{:T(128)S(6)} %select_n.102, s32[]{:T(128)S(6)} %select_n.101), kind=kLoop, calls=%fused_computation.41 | loop fusion | bytes 2097160 | tf_op jit(solution)/shard_map/dynamic_slice | solution.py:498
  4.0 0.0 copy-start
  4.8 0.1 add_convert_fusion
  4.9 0.7 pad_maximum_fusion.4
  5.6 1.1 fusion.1
  6.7 1.0 collective-permute-start.3
  7.7 2.7 %collective-permute-start.4 = (f32[2,136,128]{2,1,0:T(8,128)}, f32[2,136,128]{2,1,0:T(8,128)S(1)}, u32[]{:S(2)}, u32[]{:S(2)}) collective-permute-start(f32[2,136,128]{2,1,0:T(8,128)} %get-tuple-element.21), channel_id=1, source_target_pairs={{2,5},{4,3},{3,4},{5,2},{6,9},{8,7},{7,8},{9,6},{10,13},{12,11},{1... | collective-permute-start | bytes 417800 | tf_op jit(solution)/shard_map/ppermute | solution.py:472
  10.3 1.6 %collective-permute-start.2 = (f32[2,264,128]{2,1,0:T(8,128)S(1)}, f32[2,264,128]{2,1,0:T(8,128)S(1)}, u32[]{:S(2)}, u32[]{:S(2)}) collective-permute-start(f32[2,264,128]{2,1,0:T(8,128)S(1)} %pad_maximum_fusion.2), channel_id=1, source_target_pairs={{0,1},{1,0},{2,3},{3,2},{4,5},{5,4},{6,7},{7,6},{8,9},{9,8},{10,11... | collective-permute-start | bytes 811016 | tf_op jit(solution)/shard_map/ppermute | solution.py:408
  11.9 0.6 collective-permute-start
  12.5 2.8 %collective-permute-start.1 = (f32[2,136,512]{2,1,0:T(8,128)}, f32[2,136,512]{2,1,0:T(8,128)S(1)}, u32[]{:S(2)}, u32[]{:S(2)}) collective-permute-start(f32[2,136,512]{2,1,0:T(8,128)} %get-tuple-element.18), channel_id=1, source_target_pairs={{2,4},{4,2},{6,8},{8,6},{10,12},{12,10},{14,16},{16,14},{18,20},{2... | collective-permute-start | bytes 1671176 | tf_op jit(solution)/shard_map/ppermute | solution.py:408
  15.3 0.1 pad_add_fusion.refs_0_.place
  15.4 7.0 %collective-permute-done.2.refs_7_ = f32[2,264,128]{2,1,0:T(8,128)S(1)} collective-permute-done((f32[2,264,128]{2,1,0:T(8,128)S(1)}, f32[2,264,128]{2,1,0:T(8,128)S(1)}, u32[]{:S(2)}, u32[]{:S(2)}) %collective-permute-start.2) | collective-permute-done | bytes 270368 | tf_op jit(solution)/shard_map/ppermute | solution.py:408
  22.4 7.1 %collective-permute-done.1.refs_6_ = f32[2,136,512]{2,1,0:T(8,128)S(1)} collective-permute-done((f32[2,136,512]{2,1,0:T(8,128)}, f32[2,136,512]{2,1,0:T(8,128)S(1)}, u32[]{:S(2)}, u32[]{:S(2)}) %collective-permute-start.1) | collective-permute-done | bytes 557088 | tf_op jit(solution)/shard_map/ppermute | solution.py:408
  29.5 0.8 copy-done.6
  30.3 1.1 copy-done.7
  31.4 1.6 %copy-done.8 = f32[1,1,8,256,256]{4,3,2,1,0:T(8,128)S(1)} copy-done((f32[1,1,8,256,256]{4,3,2,1,0:T(8,128)S(1)}, f32[1,1,8,256,256]{4,3,2,1,0:T(8,128)}, u32[]{:S(2)}) %copy-start.8) | copy-done | bytes 2097176
  32.9 1.4 %copy-done.11 = bf16[1536,512]{1,0:T(8,128)(2,1)S(1)} copy-done((bf16[1536,512]{1,0:T(8,128)(2,1)S(1)}, bf16[1536,512]{1,0:T(8,128)(2,1)}, u32[]{:S(2)}) %copy-start.11) | copy-done | bytes 1572888
  34.4 1.1 copy-done.12
  35.5 19.8 %positions.1 = (f32[2,256,512]{2,1,0:T(8,128)S(1)}, f32[2,128,640]{2,1,0:T(8,128)S(1)}, f32[2,128,640]{2,1,0:T(8,128)S(1)}, f32[2,256,128]{2,1,0:T(8,128)S(1)}, f32[2,3,256,128]{3,2,1,0:T(8,128)S(1)}) custom-call(s32[2]{0:T(128)S(1)} %pad_add_fusion.refs_0_.place, s32[1,1,8]{2,1,0:T(1,128)S(1)} %copy-done.4, s32[1,1,8]{2,1,0:T(1,128)S(1)} %copy-done.5, ...), custom_call_target="tpu_custom_call" | custom-call | flops 12884901888 | bytes 16000000 | tf_op jit(solution)/shard_map/positions/pallas_call | solution.py:310
  55.4 0.1 collective-permute-start.5
  55.5 1.7 %collective-permute-done.5 = f32[768,128]{1,0:T(8,128)S(1)} collective-permute-done((f32[768,128]{1,0:T(8,128)S(1)}, f32[768,128]{1,0:T(8,128)S(1)}, u32[]{:S(2)}, u32[]{:S(2)}) %collective-permute-start.5) | collective-permute-done | bytes 393248 | tf_op jit(solution)/shard_map/ppermute | solution.py:429
  57.3 1.1 collective-permute-start.6
  58.3 0.7 slice_bitcast_fusion.3
  59.0 5.3 %collective-permute-done.6 = f32[384,128]{1,0:T(8,128)S(1)} collective-permute-done((f32[384,128]{1,0:T(8,128)S(1)}, f32[384,128]{1,0:T(8,128)S(1)}, u32[]{:S(2)}, u32[]{:S(2)}) %collective-permute-start.6) | collective-permute-done | bytes 196640 | tf_op jit(solution)/shard_map/ppermute | solution.py:429
  64.3 0.1 collective-permute-start.7
  64.5 3.2 %cover.1 = (f32[256,512]{1,0:T(8,128)S(1)}, f32[8,128]{1,0:T(8,128)S(1)}) custom-call(s32[2]{0:T(128)S(1)} %pad_add_fusion.refs_0_.place, s32[6,32]{1,0:T(8,128)S(1)} %convert_element_type.10.info, f32[2,256,256]{2,1,0:T(8,128)S(1)} %copy-done.1), custom_call_target="tpu_custom_call" | custom-call | flops 4000000 | bytes 8000000 | tf_op jit(solution)/shard_map/cover/pallas_call | solution.py:115
  67.7 0.8 copy-done.2
  68.5 0.5 collective-permute-done.7
  69.0 0.7 collective-permute-start.8
  69.8 4.0 %collective-permute-done.8 = f32[200,128]{1,0:T(8,128)S(1)} collective-permute-done((f32[200,128]{1,0:T(8,128)S(1)}, f32[200,128]{1,0:T(8,128)S(1)}, u32[]{:S(2)}, u32[]{:S(2)}) %collective-permute-start.8) | collective-permute-done | bytes 102432 | tf_op jit(solution)/shard_map/ppermute | solution.py:429
  73.8 0.2 collective-permute-start.9
  74.0 5.6 %collective-permute-done.9 = f32[200,128]{1,0:T(8,128)S(1)} collective-permute-done((f32[200,128]{1,0:T(8,128)S(1)}, f32[200,128]{1,0:T(8,128)S(1)}, u32[]{:S(2)}, u32[]{:S(2)}) %collective-permute-start.9) | collective-permute-done | bytes 102432 | tf_op jit(solution)/shard_map/ppermute | solution.py:429
  79.6 1.3 %collective-permute-start.10 = (f32[200,128]{1,0:T(8,128)S(1)}, f32[200,128]{1,0:T(8,128)S(1)}, u32[]{:S(2)}, u32[]{:S(2)}) collective-permute-start(f32[200,128]{1,0:T(8,128)S(1)} %pad_maximum_fusion.9), channel_id=1, source_target_pairs={{0,1},{1,0},{2,3},{3,2},{4,5},{5,4},{6,7},{7,6},{8,9},{9,8},{10,11... | collective-permute-start | bytes 307208 | tf_op jit(solution)/shard_map/ppermute | solution.py:429
  80.9 3.4 %collective-permute-done.10 = f32[200,128]{1,0:T(8,128)S(1)} collective-permute-done((f32[200,128]{1,0:T(8,128)S(1)}, f32[200,128]{1,0:T(8,128)S(1)}, u32[]{:S(2)}, u32[]{:S(2)}) %collective-permute-start.10) | collective-permute-done | bytes 102432 | tf_op jit(solution)/shard_map/ppermute | solution.py:429
  84.3 0.7 pad_maximum_fusion.3
  85.1 3.5 %collective-permute-start.11 = (f32[392,128]{1,0:T(8,128)}, f32[392,128]{1,0:T(8,128)}, u32[]{:S(2)}, u32[]{:S(2)}) collective-permute-start(f32[392,128]{1,0:T(8,128)} %pad_maximum_fusion.3), channel_id=1, source_target_pairs={{0,4},{2,6},{4,0},{6,2},{8,12},{10,14},{12,8},{14,10},{16,20},{18,... | collective-permute-start | bytes 602120 | tf_op jit(solution)/shard_map/ppermute | solution.py:429
  88.6 2.1 %collective-permute-start.13 = (f32[2,128,640]{2,1,0:T(8,128)}, f32[2,128,640]{2,1,0:T(8,128)}, u32[]{:S(2)}, u32[]{:S(2)}) collective-permute-start(f32[2,128,640]{2,1,0:T(8,128)} %copy-done.9), channel_id=1, source_target_pairs={{2,4},{4,2},{6,8},{8,6},{10,12},{12,10},{14,16},{16,14},{18,20},{2... | collective-permute-start | bytes 1966088 | tf_op jit(solution)/shard_map/ppermute | solution.py:408
  90.7 1.9 %collective-permute-done.11 = f32[392,128]{1,0:T(8,128)} collective-permute-done((f32[392,128]{1,0:T(8,128)}, f32[392,128]{1,0:T(8,128)}, u32[]{:S(2)}, u32[]{:S(2)}) %collective-permute-start.11) | collective-permute-done | bytes 200736 | tf_op jit(solution)/shard_map/ppermute | solution.py:429
  92.6 0.7 slice_maximum_fusion.refs_4_
  93.3 1.1 slice_select_fusion.1
  94.4 0.1 collective-permute-start.15
  94.4 13.4 %collective-permute-done.13.refs_6_ = f32[2,128,640]{2,1,0:T(8,128)} collective-permute-done((f32[2,128,640]{2,1,0:T(8,128)}, f32[2,128,640]{2,1,0:T(8,128)}, u32[]{:S(2)}, u32[]{:S(2)}) %collective-permute-start.13) | collective-permute-done | bytes 655392 | tf_op jit(solution)/shard_map/ppermute | solution.py:408
  107.8 0.9 slice_select_fusion.3
  108.8 0.1 collective-permute-start.14
  108.9 6.3 %collective-permute-done.14.refs_7_ = f32[2,256,128]{2,1,0:T(8,128)S(1)} collective-permute-done((f32[2,256,128]{2,1,0:T(8,128)S(1)}, f32[2,256,128]{2,1,0:T(8,128)S(1)}, u32[]{:S(2)}, u32[]{:S(2)}) %collective-permute-start.14) | collective-permute-done | bytes 262176 | tf_op jit(solution)/shard_map/ppermute | solution.py:408
  115.2 3.0 %update.1 = (f32[2,256,512]{2,1,0:T(8,128)}, f32[2,256,256]{2,1,0:T(8,128)}) custom-call(s32[2]{0:T(128)S(1)} %pad_add_fusion.refs_0_.place, f32[2,256,512]{2,1,0:T(8,128)S(1)} %copy-done, f32[2,256,512]{2,1,0:T(8,128)S(1)} %get-tuple-element.22.refs_2_, f32[256,512]{1,0:T(8,128)S(1)} %copy-done.3, f32[8,128]{1,0:T(8,128)S(1)} %slice_maximum_fusion.refs_4_, ...), custom_call_target="tpu_custom_call" | custom-call | tf_op jit(solution)/shard_map/update/pallas_call | solution.py:392
  (62 shorter events, 0.5 us)
Async XLA Ops:
  0.6 4.1 %copy-start.4 = (s32[1,1,8]{2,1,0:T(1,128)S(1)}, s32[1,1,8]{2,1,0:T(1,128)}, u32[]{:S(2)}) copy-start(s32[1,1,8]{2,1,0:T(1,128)} %refs_1_.2) | copy-start | bytes 100
  0.6 4.1 %copy-start.5 = (s32[1,1,8]{2,1,0:T(1,128)S(1)}, s32[1,1,8]{2,1,0:T(1,128)}, u32[]{:S(2)}) copy-start(s32[1,1,8]{2,1,0:T(1,128)} %refs_2_.1) | copy-start | bytes 100
  4.0 26.3 %copy-start = (f32[2,256,512]{2,1,0:T(8,128)S(1)}, f32[2,256,512]{2,1,0:T(8,128)}, u32[]{:S(2)}) copy-start(f32[2,256,512]{2,1,0:T(8,128)} %refs_1_.3) | copy-start | bytes 3145732
  4.0 26.3 %copy-start.1 = (f32[2,256,256]{2,1,0:T(8,128)S(1)}, f32[2,256,256]{2,1,0:T(8,128)}, u32[]{:S(2)}) copy-start(f32[2,256,256]{2,1,0:T(8,128)} %refs_10_.3) | copy-start | bytes 1572868
  6.7 8.7 %collective-permute-start.3 = (f32[2,136,128]{2,1,0:T(8,128)}, f32[2,136,128]{2,1,0:T(8,128)S(1)}, u32[]{:S(2)}, u32[]{:S(2)}) collective-permute-start(f32[2,136,128]{2,1,0:T(8,128)} %get-tuple-element.20), channel_id=1, source_target_pairs={{0,3},{2,1},{1,2},{3,0},{4,7},{6,5},{5,6},{7,4},{8,11},{10,9},{9,1... | collective-permute-start | bytes 417800 | tf_op jit(solution)/shard_map/ppermute | solution.py:472
  7.7 7.8 %collective-permute-start.4 = (f32[2,136,128]{2,1,0:T(8,128)}, f32[2,136,128]{2,1,0:T(8,128)S(1)}, u32[]{:S(2)}, u32[]{:S(2)}) collective-permute-start(f32[2,136,128]{2,1,0:T(8,128)} %get-tuple-element.21), channel_id=1, source_target_pairs={{2,5},{4,3},{3,4},{5,2},{6,9},{8,7},{7,8},{9,6},{10,13},{12,11},{1... | collective-permute-start | bytes 417800 | tf_op jit(solution)/shard_map/ppermute | solution.py:472
  10.3 12.1 %collective-permute-start.2 = (f32[2,264,128]{2,1,0:T(8,128)S(1)}, f32[2,264,128]{2,1,0:T(8,128)S(1)}, u32[]{:S(2)}, u32[]{:S(2)}) collective-permute-start(f32[2,264,128]{2,1,0:T(8,128)S(1)} %pad_maximum_fusion.2), channel_id=1, source_target_pairs={{0,1},{1,0},{2,3},{3,2},{4,5},{5,4},{6,7},{7,6},{8,9},{9,8},{10,11... | collective-permute-start | bytes 811016 | tf_op jit(solution)/shard_map/ppermute | solution.py:408
  11.9 10.5 %collective-permute-start = (f32[2,136,512]{2,1,0:T(8,128)}, f32[2,136,512]{2,1,0:T(8,128)}, u32[]{:S(2)}, u32[]{:S(2)}) collective-permute-start(f32[2,136,512]{2,1,0:T(8,128)} %get-tuple-element.17), channel_id=1, source_target_pairs={{0,2},{2,0},{4,6},{6,4},{8,10},{10,8},{12,14},{14,12},{16,18},{18,... | collective-permute-start | bytes 1671176 | tf_op jit(solution)/shard_map/ppermute | solution.py:408
  12.5 17.0 %collective-permute-start.1 = (f32[2,136,512]{2,1,0:T(8,128)}, f32[2,136,512]{2,1,0:T(8,128)S(1)}, u32[]{:S(2)}, u32[]{:S(2)}) collective-permute-start(f32[2,136,512]{2,1,0:T(8,128)} %get-tuple-element.18), channel_id=1, source_target_pairs={{2,4},{4,2},{6,8},{8,6},{10,12},{12,10},{14,16},{16,14},{18,20},{2... | collective-permute-start | bytes 1671176 | tf_op jit(solution)/shard_map/ppermute | solution.py:408
  29.5 0.8 copy-start.6
  30.3 1.1 copy-start.7
  31.3 1.6 %copy-start.8 = (f32[1,1,8,256,256]{4,3,2,1,0:T(8,128)S(1)}, f32[1,1,8,256,256]{4,3,2,1,0:T(8,128)}, u32[]{:S(2)}) copy-start(f32[1,1,8,256,256]{4,3,2,1,0:T(8,128)} %refs_11_.1) | copy-start | bytes 6291460
  32.9 1.4 %copy-start.11 = (bf16[1536,512]{1,0:T(8,128)(2,1)S(1)}, bf16[1536,512]{1,0:T(8,128)(2,1)}, u32[]{:S(2)}) copy-start(bf16[1536,512]{1,0:T(8,128)(2,1)} %constant.92.clone.refs_13_) | copy-start | bytes 4718596
  34.3 1.1 copy-start.12
  55.3 9.1 %copy-start.9 = (f32[2,128,640]{2,1,0:T(8,128)}, f32[2,128,640]{2,1,0:T(8,128)S(1)}, u32[]{:S(2)}) copy-start(f32[2,128,640]{2,1,0:T(8,128)S(1)} %get-tuple-element.30) | copy-start | bytes 1966084
  55.3 9.1 %copy-start.10 = (f32[2,128,640]{2,1,0:T(8,128)}, f32[2,128,640]{2,1,0:T(8,128)S(1)}, u32[]{:S(2)}) copy-start(f32[2,128,640]{2,1,0:T(8,128)S(1)} %get-tuple-element.28) | copy-start | bytes 1966084
  55.4 1.8 %collective-permute-start.5 = (f32[768,128]{1,0:T(8,128)S(1)}, f32[768,128]{1,0:T(8,128)S(1)}, u32[]{:S(2)}, u32[]{:S(2)}) collective-permute-start(f32[768,128]{1,0:T(8,128)S(1)} %constant_dynamic-slice_fusion.2), channel_id=1, source_target_pairs={{0,2},{2,0},{4,6},{6,4},{8,10},{10,8},{12,14},{14,12},{16,18},{18,... | collective-permute-start | bytes 1179656 | tf_op jit(solution)/shard_map/ppermute | solution.py:429
  57.3 7.0 %collective-permute-start.6 = (f32[384,128]{1,0:T(8,128)S(1)}, f32[384,128]{1,0:T(8,128)S(1)}, u32[]{:S(2)}, u32[]{:S(2)}) collective-permute-start(f32[384,128]{1,0:T(8,128)S(1)} %constant_dynamic-slice_fusion.1), channel_id=1, source_target_pairs={{0,4},{2,6},{4,0},{6,2},{8,12},{10,14},{12,8},{14,10},{16,20},{18,... | collective-permute-start | bytes 589832 | tf_op jit(solution)/shard_map/ppermute | solution.py:429
  64.3 4.7 %collective-permute-start.7 = (f32[192,128]{1,0:T(8,128)S(1)}, f32[192,128]{1,0:T(8,128)S(1)}, u32[]{:S(2)}, u32[]{:S(2)}) collective-permute-start(f32[192,128]{1,0:T(8,128)S(1)} %constant_dynamic-slice_fusion), channel_id=1, source_target_pairs={{0,1},{1,0},{2,3},{3,2},{4,5},{5,4},{6,7},{7,6},{8,9},{9,8},{10,11... | collective-permute-start | bytes 294920 | tf_op jit(solution)/shard_map/ppermute | solution.py:429
  67.7 0.8 copy-start.2
  69.0 4.7 %collective-permute-start.8 = (f32[200,128]{1,0:T(8,128)S(1)}, f32[200,128]{1,0:T(8,128)S(1)}, u32[]{:S(2)}, u32[]{:S(2)}) collective-permute-start(f32[200,128]{1,0:T(8,128)S(1)} %pad_maximum_fusion.7), channel_id=1, source_target_pairs={{0,8},{2,10},{4,12},{6,14},{8,0},{10,2},{12,4},{14,6},{16,24},{18,... | collective-permute-start | bytes 307208 | tf_op jit(solution)/shard_map/ppermute | solution.py:429
  73.8 5.7 %collective-permute-start.9 = (f32[200,128]{1,0:T(8,128)S(1)}, f32[200,128]{1,0:T(8,128)S(1)}, u32[]{:S(2)}, u32[]{:S(2)}) collective-permute-start(f32[200,128]{1,0:T(8,128)S(1)} %pad_maximum_fusion.8), channel_id=1, source_target_pairs={{0,16},{2,18},{4,20},{6,22},{8,24},{10,26},{12,28},{14,30},{16,0},... | collective-permute-start | bytes 307208 | tf_op jit(solution)/shard_map/ppermute | solution.py:429
  79.6 4.7 %collective-permute-start.10 = (f32[200,128]{1,0:T(8,128)S(1)}, f32[200,128]{1,0:T(8,128)S(1)}, u32[]{:S(2)}, u32[]{:S(2)}) collective-permute-start(f32[200,128]{1,0:T(8,128)S(1)} %pad_maximum_fusion.9), channel_id=1, source_target_pairs={{0,1},{1,0},{2,3},{3,2},{4,5},{5,4},{6,7},{7,6},{8,9},{9,8},{10,11... | collective-permute-start | bytes 307208 | tf_op jit(solution)/shard_map/ppermute | solution.py:429
  84.3 4.2 %copy-start.13 = (f32[192,128]{1,0:T(8,128)}, f32[192,128]{1,0:T(8,128)S(1)}, u32[]{:S(2)}) copy-start(f32[192,128]{1,0:T(8,128)S(1)} %get-tuple-element.40) | copy-start | bytes 294916
  84.3 4.2 %copy-start.14 = (f32[192,128]{1,0:T(8,128)}, f32[192,128]{1,0:T(8,128)S(1)}, u32[]{:S(2)}) copy-start(f32[192,128]{1,0:T(8,128)S(1)} %get-tuple-element.41) | copy-start | bytes 294916
  85.1 7.5 %collective-permute-start.11 = (f32[392,128]{1,0:T(8,128)}, f32[392,128]{1,0:T(8,128)}, u32[]{:S(2)}, u32[]{:S(2)}) collective-permute-start(f32[392,128]{1,0:T(8,128)} %pad_maximum_fusion.3), channel_id=1, source_target_pairs={{0,4},{2,6},{4,0},{6,2},{8,12},{10,14},{12,8},{14,10},{16,20},{18,... | collective-permute-start | bytes 602120 | tf_op jit(solution)/shard_map/ppermute | solution.py:429
  88.6 5.9 %collective-permute-start.12 = (f32[2,128,640]{2,1,0:T(8,128)}, f32[2,128,640]{2,1,0:T(8,128)S(1)}, u32[]{:S(2)}, u32[]{:S(2)}) collective-permute-start(f32[2,128,640]{2,1,0:T(8,128)} %copy-done.10), channel_id=1, source_target_pairs={{0,2},{2,0},{4,6},{6,4},{8,10},{10,8},{12,14},{14,12},{16,18},{18,... | collective-permute-start | bytes 1966088 | tf_op jit(solution)/shard_map/ppermute | solution.py:408
  88.6 19.2 %collective-permute-start.13 = (f32[2,128,640]{2,1,0:T(8,128)}, f32[2,128,640]{2,1,0:T(8,128)}, u32[]{:S(2)}, u32[]{:S(2)}) collective-permute-start(f32[2,128,640]{2,1,0:T(8,128)} %copy-done.9), channel_id=1, source_target_pairs={{2,4},{4,2},{6,8},{8,6},{10,12},{12,10},{14,16},{16,14},{18,20},{2... | collective-permute-start | bytes 1966088 | tf_op jit(solution)/shard_map/ppermute | solution.py:408
  90.7 24.6 %copy-start.3 = (f32[256,512]{1,0:T(8,128)S(1)}, f32[256,512]{1,0:T(8,128)}, u32[]{:S(2)}) copy-start(f32[256,512]{1,0:T(8,128)} %copy-done.2) | copy-start | bytes 1572868
  94.4 20.9 %collective-permute-start.15 = (f32[776,128]{1,0:T(8,128)S(1)}, f32[776,128]{1,0:T(8,128)S(1)}, u32[]{:S(2)}, u32[]{:S(2)}) collective-permute-start(f32[776,128]{1,0:T(8,128)S(1)} %pad_maximum_fusion), channel_id=1, source_target_pairs={{0,2},{2,0},{4,6},{6,4},{8,10},{10,8},{12,14},{14,12},{16,18},{18,... | collective-permute-start | bytes 1191944 | tf_op jit(solution)/shard_map/ppermute | solution.py:429
  108.8 6.4 %collective-permute-start.14 = (f32[2,256,128]{2,1,0:T(8,128)S(1)}, f32[2,256,128]{2,1,0:T(8,128)S(1)}, u32[]{:S(2)}, u32[]{:S(2)}) collective-permute-start(f32[2,256,128]{2,1,0:T(8,128)S(1)} %maximum_add_fusion), channel_id=1, source_target_pairs={{0,1},{1,0},{2,3},{3,2},{4,5},{5,4},{6,7},{7,6},{8,9},{9,8},{10,11... | collective-permute-start | bytes 786440 | tf_op jit(solution)/shard_map/ppermute | solution.py:408

commit v4 on v3

--- a/solution.py
+++ b/solution.py
@@ -21,6 +21,7 @@
 MIX_PROBE = 0.5
 VMEM = pl.BlockSpec(memory_space=pltpu.VMEM)
 SMEM = pl.BlockSpec(memory_space=pltpu.SMEM)
+ANY = pl.BlockSpec(memory_space=pl.ANY)
 
 
 def rounded_pair(table):
@@ -130,45 +131,163 @@
     )(place, info, probe)
 
 
-def positions_kernel(sides, *refs):
+def pack_kernel(sides, place, rows, cols, count, tile, *refs):
+    far_band, near_band = refs[:2]
+    edges, far_ends, near_ends = [refs[2 + i * sides : 2 + (i + 1) * sides] for i in range(3)]
+    sems = refs[2 + 3 * sides]
+    tile_rows, tile_cols = tile.shape[1:]
+    even = place[0] % 2 == 0
+    near_start = pl.multiple_of(jnp.where(even, tile_rows - H, 0), 8)
+    far_start = pl.multiple_of(jnp.where(even, 0, tile_rows - H), 8)
+    if sides == 1:
+        starts = [pl.multiple_of(jnp.where(place[1] == 0, tile_cols - H, 0), LANES)]
+    else:
+        starts = [0, tile_cols - H]
+    bands = [(far_band, far_start, H, 0), (near_band, near_start, H, 0)]
+    for s, start in enumerate(starts):
+        bands += [(edges[s], 0, tile_rows, start), (far_ends[s], far_start, H, start)]
+        bands += [(near_ends[s], near_start, H, start)]
+    copies = []
+    for i, (band, row, height, col) in enumerate(bands):
+        copies.append(
+            pltpu.make_async_copy(
+                tile.at[:, pl.ds(row, height), pl.ds(col, band.shape[2])], band.at[:, pl.ds(0, height), :], sems.at[i]
+            )
+        )
+        copies[-1].start()
+    lanes = lax.broadcasted_iota(jnp.int32, (INFO, LANES), 1)
+    notes = jnp.where(lanes == 16, count[0, 0], 0)
+    for k in range(rows.shape[2]):
+        notes = jnp.where(lanes == k, rows[0, 0, k], jnp.where(lanes == 8 + k, cols[0, 0, k], notes))
+    notes = notes.astype(F32)
+    for band, row, height, col in bands:
+        for ch in range(2):
+            band[ch, height : height + INFO, 0:LANES] = notes
+            if band.shape[2] > LANES:
+                band[ch, height : height + INFO, LANES:] = jnp.zeros((INFO, band.shape[2] - LANES), F32)
+    for copy in copies:
+        copy.wait()
+
+
+def pack_call(place, rows, cols, count, tile, sides):
+    tile_rows, tile_cols = tile.shape[1:]
+    shape = lambda height, width: jax.ShapeDtypeStruct((2, height + INFO, width), F32)
+    shapes = [shape(H, tile_cols)] * 2 + [shape(tile_rows, LANES)] * sides + [shape(H, LANES)] * (2 * sides)
+    out = pl.pallas_call(
+        functools.partial(pack_kernel, sides),
+        out_shape=shapes,
+        in_specs=[SMEM] * 4 + [ANY],
+        out_specs=[VMEM] * len(shapes),
+        scratch_shapes=[pltpu.SemaphoreType.DMA((len(shapes),))],
+        compiler_params=pltpu.CompilerParams(vmem_limit_bytes=8 << 20),
+        name="pack",
+    )(place, rows, cols, count, tile)
+    return out[0], out[1], *[list(out[2 + i * sides : 2 + (i + 1) * sides]) for i in range(3)]
+
+
+def positions_kernel(sides, last, *refs):
     place, rows, cols, count = refs[:4]
-    tile, near, far_side = refs[4:7]
-    side_in, near_corners, far_corners = [refs[7 + i * sides : 7 + (i + 1) * sides] for i in range(3)]
-    probe, measured, left, right = refs[7 + 3 * sides : 11 + 3 * sides]
-    outs = refs[11 + 3 * sides :]
-    middle, near_rim, far_rim = outs[:3]
-    side_out = outs[3 : 3 + sides]
-    probe_sums = outs[3 + sides]
-    ext, grad = outs[4 + sides : 6 + sides]
-    scratch = outs[6 + sides :]
+    if last:
+        ext, grad_in, sums_in, probe, measured, left_in, right_in = refs[4:11]
+        outs = refs[11:]
+        middle, near_rim = outs[:2]
+        side_out = outs[2 : 2 + sides]
+        probe_sums = outs[2 + sides]
+        grad = outs[3 + sides]
+        scratch = outs[4 + sides :]
+    else:
+        tile, near, far_side = refs[4:7]
+        side_in, near_corners, far_corners = [refs[7 + i * sides : 7 + (i + 1) * sides] for i in range(3)]
+        probe, measured, left_in, right_in = refs[7 + 3 * sides : 11 + 3 * sides]
+        far_rim, info, ext, grad, probe_sums = refs[11 + 3 * sides : 16 + 3 * sides]
+        scratch = refs[16 + 3 * sides :]
+    left, right, levels, order = scratch[:4]
+    table_sems, level_sems, ext_sems = scratch[4:7]
+    scratch = scratch[7:]
     patches, exits, stacks, wides, fields = [scratch[i * WAYS : (i + 1) * WAYS] for i in range(5)]
 
     pr = probe.shape[1]
     pieces = pr // LANES
-    tile_rows, tile_cols = tile.shape[1:]
-    ext_rows = tile_rows + 2 * H
-    blocks = (tile_cols + 2 * H) // LANES
-    own_blocks = tile_cols // LANES
+    ext_rows = ext.shape[1]
+    blocks = ext.shape[0] // 2
+    own_blocks = blocks - 2
+    tile_rows, tile_cols = ext_rows - 2 * H, own_blocks * LANES
     even = place[0] % 2 == 0
     near_row = pl.multiple_of(jnp.where(even, tile_rows + H, 0), 8)
     far_row = pl.multiple_of(jnp.where(even, 0, tile_rows + H), 8)
     side_blocks = [side_block(place, s, sides, blocks) for s in range(sides)]
     own, near_rows, far_rows = pl.ds(H, tile_rows), pl.ds(near_row, H), pl.ds(far_row, H)
-    for ch in range(2):
+
+    copies = []
+
+    def fetch(source, target):
+        copies.append(pltpu.make_async_copy(source, target, ext_sems.at[len(copies)]))
+        copies[-1].start()
+
+    if not last:
+        for ch in range(2):
+            for b in range(own_blocks):
+                at, cut = ch * blocks + 1 + b, pl.ds(b * LANES, LANES)
+                fetch(tile.at[ch, :, cut], ext.at[at, own, :])
+                fetch(near.at[ch, pl.ds(0, H), cut], ext.at[at, near_rows, :])
+                fetch(far_side.at[ch, pl.ds(0, H), cut], ext.at[at, far_rows, :])
+            for s in range(sides):
+                at = ch * blocks + side_blocks[s]
+                fetch(side_in[s].at[ch, pl.ds(0, tile_rows), :], ext.at[at, own, :])
+                fetch(near_corners[s].at[ch, pl.ds(0, H), :], ext.at[at, near_rows, :])
+                fetch(far_corners[s].at[ch, pl.ds(0, H), :], ext.at[at, far_rows, :])
+        for s in range(sides):
+            fetch(side_in[s].at[0, pl.ds(tile_rows, INFO), :], info.at[s])
+            fetch(near_corners[s].at[0, pl.ds(H, INFO), :], info.at[sides + 1 + s])
+            fetch(far_corners[s].at[0, pl.ds(H, INFO), :], info.at[2 * sides + 2 + s])
+        fetch(near.at[0, pl.ds(H, INFO), pl.ds(0, LANES)], info.at[sides])
+        fetch(far_side.at[0, pl.ds(H, INFO), pl.ds(0, LANES)], info.at[2 * sides + 1])
+    tables = [
+        pltpu.make_async_copy(left_in, left, table_sems.at[0]),
+        pltpu.make_async_copy(right_in, right, table_sems.at[1]),
+    ]
+    for copy in tables:
+        copy.start()
+
+    live_slots = count[0, 0]
+
+    def touches(k):
+        return jnp.where(even, rows[0, 0, k] < H, rows[0, 0, k] > tile_rows - H)
+
+    def pick(wanted):
+        def step(k, n):
+            @pl.when(touches(k) == wanted)
+            def _():
+                order[n] = k
+
+            return n + jnp.where(touches(k) == wanted, 1, 0)
+
+        return step
+
+    far_slots = lax.fori_loop(0, live_slots, pick(True), 0)
+    lax.fori_loop(0, live_slots, pick(False), far_slots)
+    border = jnp.minimum((far_slots + WAYS - 1) // WAYS * WAYS, live_slots)
+    begin, end = (border, live_slots) if last else (0, border)
+
+    def level_copy(i):
+        return pltpu.make_async_copy(measured.at[0, 0, order[i]], levels.at[i], level_sems.at[i])
+
+    def start_level(i, carry):
+        level_copy(i).start()
+        return carry
+
+    lax.fori_loop(begin, end, start_level, 0)
+    if last:
+        grad[...] = grad_in[...]
+        probe_sums[...] = sums_in[...]
+    else:
         if sides == 1:
-            ext[ch * blocks + blocks - 1 - side_blocks[0]] = jnp.zeros((ext_rows, LANES), F32)
-        for b in range(own_blocks):
-            at, cut = ch * blocks + 1 + b, slice(b * LANES, (b + 1) * LANES)
-            ext[at, own, :] = tile[ch, :, cut]
-            ext[at, near_rows, :] = near[ch, 0:H, cut]
-            ext[at, far_rows, :] = far_side[ch, 0:H, cut]
-        for s in range(sides):
-            at = ch * blocks + side_blocks[s]
-            ext[at, own, :] = side_in[s][ch, 0:tile_rows, :]
-            ext[at, near_rows, :] = near_corners[s][ch, 0:H, :]
-            ext[at, far_rows, :] = far_corners[s][ch, 0:H, :]
-    grad[...] = jnp.zeros_like(grad)
-    probe_sums[...] = jnp.zeros_like(probe_sums)
+            for ch in range(2):
+                ext[ch * blocks + blocks - 1 - side_blocks[0]] = jnp.zeros((ext_rows, LANES), F32)
+        grad[...] = jnp.zeros_like(grad)
+        probe_sums[...] = jnp.zeros_like(probe_sums)
+    for copy in copies + tables:
+        copy.wait()
     lanes = lax.broadcasted_iota(jnp.int32, (CHUNK, LANES), 1)
 
     def put(stack, value, part, q, first):
@@ -197,7 +316,7 @@
         fields[w][...] = jnp.dot(stack, right[...], preferred_element_type=F32)
 
     def load(w, k):
-        row, col = rows[0, 0, k], cols[0, 0, k]
+        row, col = rows[0, 0, order[k]], cols[0, 0, order[k]]
         shift, block = col & (LANES - 1), col >> 7
         back = (LANES - shift) & (LANES - 1)
         keep = lanes < LANES - shift
@@ -226,12 +345,12 @@
         for q in range(pr // CHUNK):
             cut = slice(q * CHUNK, (q + 1) * CHUNK)
             real, imag = fields[w][cut, 0:pr], fields[w][cut, pr : 2 * pr]
-            factor = jnp.sqrt(measured[0, 0, k, cut, :]) * lax.rsqrt(real * real + imag * imag + 1.0)
+            factor = jnp.sqrt(levels[k, cut, :]) * lax.rsqrt(real * real + imag * imag + 1.0)
             put(stacks[w], real * factor, 0, q, 0)
             put(stacks[w], -(imag * factor), 1, q, 0)
 
     def finish(w, k, live):
-        row, col = rows[0, 0, k], cols[0, 0, k]
+        row, col = rows[0, 0, order[k]], cols[0, 0, order[k]]
         shift, block = col & (LANES - 1), col >> 7
         low = lanes < shift
         zero = jnp.zeros((CHUNK, LANES), F32)
@@ -262,11 +381,16 @@
                     grad[at + j, here, :] += jnp.where(low, turned[ch][j - 1], turned[ch][j])
                 grad[at + pieces, here, :] += jnp.where(low, turned[ch][-1], zero)
 
-    live_slots = count[0, 0]
-
     def visit(i, carry):
-        slots = [jnp.minimum(i * WAYS + w, live_slots - 1) for w in range(WAYS)]
-        lives = [None] + [jnp.where(i * WAYS + w < live_slots, 1.0, 0.0) for w in range(1, WAYS)]
+        first = begin + i * WAYS
+        slots = [jnp.minimum(first + w, end - 1) for w in range(WAYS)]
+        lives = [None] + [jnp.where(first + w < end, 1.0, 0.0) for w in range(1, WAYS)]
+        for w in range(WAYS):
+
+            @pl.when(first + w < end)
+            def _():
+                level_copy(slots[w]).wait()
+
         for w in range(WAYS):
             load(w, slots[w])
             times_left(w)
@@ -281,22 +405,26 @@
             finish(w, slots[w], lives[w])
         return carry
 
-    lax.fori_loop(0, (live_slots + WAYS - 1) // WAYS, visit, 0)
+    lax.fori_loop(0, (end - begin + WAYS - 1) // WAYS, visit, 0)
     for ch in range(2):
         for b in range(own_blocks):
             at, cut = ch * blocks + 1 + b, slice(b * LANES, (b + 1) * LANES)
-            middle[ch, :, cut] = grad[at, own, :]
-            near_rim[ch, :, cut] = grad[at, near_rows, :]
-            far_rim[ch, :, cut] = grad[at, far_rows, :]
+            if last:
+                middle[ch, :, cut] = grad[at, own, :]
+                near_rim[ch, :, cut] = grad[at, near_rows, :]
+            else:
+                far_rim[ch, :, cut] = grad[at, far_rows, :]
         for s in range(sides):
             at = ch * blocks + side_blocks[s]
             cut = slice(tile_cols + s * LANES, tile_cols + (s + 1) * LANES)
-            side_out[s][ch] = grad[at, own, :]
-            near_rim[ch, :, cut] = grad[at, near_rows, :]
-            far_rim[ch, :, cut] = grad[at, far_rows, :]
-
-
-def positions_call(
+            if last:
+                side_out[s][ch] = grad[at, own, :]
+                near_rim[ch, :, cut] = grad[at, near_rows, :]
+            else:
+                far_rim[ch, :, cut] = grad[at, far_rows, :]
+
+
+def positions_calls(
     place, rows, cols, count, tile, near, far_side, side_in, near_corners, far_corners, probe, measured
 ):
     pr = probe.shape[1]
@@ -304,35 +432,50 @@
     tile_rows, tile_cols = tile.shape[1:]
     ext_rows = tile_rows + 2 * H
     blocks = (tile_cols + 2 * H) // LANES
-    left, right = dft_tables(pr)
+    left, right = (jnp.asarray(table) for table in dft_tables(pr))
     shape = lambda *dims: jax.ShapeDtypeStruct(dims, F32)
     slots = measured.shape[2]
-    return pl.pallas_call(
-        functools.partial(positions_kernel, sides),
-        out_shape=(
-            shape(2, tile_rows, tile_cols),
-            shape(2, H, tile_cols + sides * LANES),
-            shape(2, H, tile_cols + sides * LANES),
-            *[shape(2, tile_rows, LANES)] * sides,
-            shape(pr // LANES, 3, pr, LANES),
+    sums = shape(pr // LANES, 3, pr, LANES)
+    field = shape(2 * blocks, ext_rows, LANES)
+    rim = shape(2, H, tile_cols + sides * LANES)
+    options = dict(
+        compiler_params=pltpu.CompilerParams(vmem_limit_bytes=34 << 20),
+        cost_estimate=pl.CostEstimate(
+            flops=slots * 48 * pr * pr * pr, bytes_accessed=16_000_000, transcendentals=slots * pr * pr
         ),
-        in_specs=[SMEM] * 4 + [VMEM] * (7 + 3 * sides),
-        out_specs=(VMEM,) * (4 + sides),
-        scratch_shapes=[
-            pltpu.VMEM((2 * blocks, ext_rows, LANES), F32),
-            pltpu.VMEM((2 * blocks, ext_rows, LANES), F32),
-            *[pltpu.VMEM((2, pr, pr), F32)] * (2 * WAYS),
-            *[pltpu.VMEM((4 * pr, 2 * pr), BF)] * WAYS,
-            *[pltpu.VMEM((pr, 4 * pr), BF)] * WAYS,
-            *[pltpu.VMEM((pr, 2 * pr), F32)] * WAYS,
-        ],
-        compiler_params=pltpu.CompilerParams(vmem_limit_bytes=28 << 20),
-        cost_estimate=pl.CostEstimate(
-            flops=slots * 96 * pr * pr * pr, bytes_accessed=16_000_000, transcendentals=slots * 2 * pr * pr
-        ),
-        name="positions",
-    )(place, rows, cols, count, tile, near, far_side, *side_in, *near_corners, *far_corners, probe, measured,
-      jnp.asarray(left), jnp.asarray(right))
+    )
+    scratch = [
+        pltpu.VMEM(left.shape, BF),
+        pltpu.VMEM(right.shape, BF),
+        pltpu.VMEM((slots, pr, pr), F32),
+        pltpu.SMEM((slots,), jnp.int32),
+        pltpu.SemaphoreType.DMA((2,)),
+        pltpu.SemaphoreType.DMA((slots,)),
+        pltpu.SemaphoreType.DMA((6 * blocks + 3 * sides + 2,)),
+        *[pltpu.VMEM((2, pr, pr), F32)] * (2 * WAYS),
+        *[pltpu.VMEM((4 * pr, 2 * pr), BF)] * WAYS,
+        *[pltpu.VMEM((pr, 4 * pr), BF)] * WAYS,
+        *[pltpu.VMEM((pr, 2 * pr), F32)] * WAYS,
+    ]
+    far_rim, info, ext, grad, probe_sums = pl.pallas_call(
+        functools.partial(positions_kernel, sides, False),
+        out_shape=(rim, shape(3 * sides + 2, INFO, LANES), field, field, sums),
+        in_specs=[SMEM] * 4 + [ANY] * (3 + 3 * sides) + [VMEM, ANY, ANY, ANY],
+        out_specs=(VMEM,) * 5,
+        scratch_shapes=scratch,
+        name="positions_far",
+        **options,
+    )(place, rows, cols, count, tile, near, far_side, *side_in, *near_corners, *far_corners, probe, measured, left, right)
+    out = pl.pallas_call(
+        functools.partial(positions_kernel, sides, True),
+        out_shape=(shape(2, tile_rows, tile_cols), rim, *[shape(2, tile_rows, LANES)] * sides, sums),
+        in_specs=[SMEM] * 4 + [VMEM] * 4 + [ANY] * 3,
+        out_specs=(VMEM,) * (3 + sides),
+        scratch_shapes=[pltpu.VMEM(field.shape, F32)] + scratch,
+        name="positions_near",
+        **options,
+    )(place, rows, cols, count, ext, grad, probe_sums, probe, measured, left, right)
+    return out[0], out[1], far_rim, list(out[2 : 2 + sides]), out[2 + sides], info
 
 
 def update_kernel(sides, *refs):
@@ -484,50 +627,26 @@
     even = wide % 2 == 0
     place = jnp.stack([wide, narrow]).astype(jnp.int32)
 
-    own_info = jnp.concatenate(
-        [rows.reshape(-1), cols.reshape(-1), counts.reshape(-1), jnp.zeros((LANES - 17,), jnp.int32)]
-    ).astype(F32)
-    info_rows = jnp.broadcast_to(own_info, (2, INFO, LANES))
-
-    near_start = jnp.where(even, tile_rows - H, 0)
-    far_start = jnp.where(even, 0, tile_rows - H)
-    side_start = jnp.where(narrow == 0, tile_cols - H, 0)
-    side_starts = [side_start] if sides == 1 else [0, tile_cols - H]
-
-    def cut_out(row, height, col, width):
-        piece = lax.dynamic_slice(tile, (0, row, col), (2, height, width))
-        notes = jnp.pad(info_rows, ((0, 0), (0, 0), (0, width - LANES)))
-        return jnp.concatenate([piece, notes], axis=1)
-
-    far_band = cut_out(far_start, H, 0, tile_cols)
-    near_band = cut_out(near_start, H, 0, tile_cols)
-    edges = [cut_out(0, tile_rows, start, H) for start in side_starts]
-    far_ends = [cut_out(far_start, H, start, H) for start in side_starts]
-    near_ends = [cut_out(near_start, H, start, H) for start in side_starts]
-    far_band, near_band, edges, far_ends, near_ends = lax.optimization_barrier(
-        (far_band, near_band, edges, far_ends, near_ends)
-    )
+    far_band, near_band, edges, far_ends, near_ends = pack_call(place, rows, cols, counts, tile, sides)
     far_side = swap(far_band, "wide", 1)
     far_corners = to_corners(far_ends, 1)
     side_in = to_sides(edges)
     near_corners = to_corners(near_ends, 0)
     near = swap(near_band, "wide", 0)
 
-    out = positions_call(place, rows, cols, counts, tile, near, far_side, side_in, near_corners, far_corners, probe, measured)
-    middle, near_rim, far_rim = out[:3]
-    side_rims, probe_sums = list(out[3 : 3 + sides]), out[3 + sides]
+    middle, near_rim, far_rim, side_rims, probe_sums, got_info = positions_calls(
+        place, rows, cols, counts, tile, near, far_side, side_in, near_corners, far_corners, probe, measured
+    )
+    far_got = swap(far_rim, "wide", 1)
+    own_info = edges[0][:1, tile_rows:]
 
     terms = probe_sums.reshape(-1, LANES)
     wide_bits, narrow_bits = bits_of("wide"), bits_of("narrow")
     terms = halve(terms, "wide", wide_bits[0])
     near_got = swap(after(near_rim, terms), "wide", 0)
-    notes = [side_in[s][0, tile_rows:] for s in range(sides)]
-    notes += [near[0, H:, :LANES]] + [c[0, H:] for c in near_corners]
-    notes += [far_side[0, H:, :LANES]] + [c[0, H:] for c in far_corners]
-    info = jnp.stack([own_info[:32]] + [x[0, :32] for x in notes]).astype(jnp.int32)
+    info = jnp.concatenate([own_info, got_info], axis=0)[:, 0, :32].astype(jnp.int32)
     cover, peak = cover_call(place, after(info, terms), probe, tile_rows, tile_cols, sides)
     terms = halve(terms, "wide", wide_bits[1])
-    far_got = swap(after(far_rim, terms), "wide", 1)
     for bit in narrow_bits:
         terms = halve(terms, "narrow", bit)
     for bit in wide_bits[2:]:

time: 118 us -> 123 us (1.042)
  the two profiles are of different devices: /device:TPU:18 before, /device:TPU:0 now
where the time goes in v4:
time: 123 us; the launch traced here: 122 us
  starting transfers between devices  44.5 us (36%)
  waiting for transfers between devices  41.4 us (34%)
  Pallas kernels  14.7 us (12%)
  local copies, waits for them, and re-layouts  13.7 us (11%)
  other arithmetic  6.26 us (5%)
  between operations  1.56 us (1%)
    ppermute x8, starting transfers between devices, partner(): return lax.ppermute(x, axis, [(i, i ^ bit) for i in range(size)])  32.7 us
    ppermute x8, waiting for transfers between devices, partner(): return lax.ppermute(x, axis, [(i, i ^ bit) for i in range(size)])  25.8 us
    unnamed x40, local copies, waits for them, and re-layouts  11.9 us
    ppermute x2, waiting for transfers between devices, to_corners(): got.append(lax.ppermute(band, ('wide', 'narrow'), pairs))  8.48 us
    ppermute x6, starting transfers between devices, swap(): return lax.ppermute(x, axis, pairs)  8.47 us
    pallas_call x1, Pallas kernels, positions_calls(): pl.pallas_call(functools.partial(positions_kernel, sides, False), out_sha...  7.13 us
    ppermute x6, waiting for transfers between devices, swap(): return lax.ppermute(x, axis, pairs)  7.07 us
    ppermute x2, starting transfers between devices, to_corners(): got.append(lax.ppermute(band, ('wide', 'narrow'), pairs))  3.31 us
  transfers between devices with their start and end apart: 16, of which 9 were waited for; matrix products, arithmetic and copies ran while one was open for 2% of the time, Pallas kernels for 2%

profile of v4, /device:TPU:0, one launch (start us, length us, event | category | flops | bytes accessed | tf_op | source)
XLA Modules:
  0.0 122.0 jit_solution(9358881429161761704)
XLA Ops:
  1.4 1.2 %copy-done = f32[2,256,512]{2,1,0:T(8,128)S(1)} copy-done((f32[2,256,512]{2,1,0:T(8,128)S(1)}, f32[2,256,512]{2,1,0:T(8,128)}, u32[]{:S(2)}) %copy-start) | copy-done | bytes 1048600
  2.6 0.7 copy-done.7
  3.2 0.7 copy-done.9
  3.9 0.8 pack.1
  4.7 0.5 collective-permute-start
  5.2 0.7 collective-permute-start.1
  5.9 2.6 %collective-permute-start.2 = (f32[2,264,128]{2,1,0:T(8,128)S(1)}, f32[2,264,128]{2,1,0:T(8,128)S(1)}, u32[]{:S(2)}, u32[]{:S(2)}) collective-permute-start(f32[2,264,128]{2,1,0:T(8,128)S(1)} %get-tuple-element.22), channel_id=1, source_target_pairs={{0,1},{1,0},{2,3},{3,2},{4,5},{5,4},{6,7},{7,6},{8,9},{9,8},{10,11... | collective-permute-start | bytes 811016 | tf_op jit(solution)/shard_map/ppermute | solution.py:551
  8.5 2.6 %collective-permute-start.3 = (f32[2,136,128]{2,1,0:T(8,128)S(1)}, f32[2,136,128]{2,1,0:T(8,128)S(1)}, u32[]{:S(2)}, u32[]{:S(2)}) collective-permute-start(f32[2,136,128]{2,1,0:T(8,128)S(1)} %get-tuple-element.23), channel_id=1, source_target_pairs={{0,3},{2,1},{1,2},{3,0},{4,7},{6,5},{5,6},{7,4},{8,11},{10,9},{9,1... | collective-permute-start | bytes 417800 | tf_op jit(solution)/shard_map/ppermute | solution.py:615
  11.1 0.7 collective-permute-start.4
  11.8 8.5 %collective-permute-done.3.refs_8_ = f32[2,136,128]{2,1,0:T(8,128)S(1)} collective-permute-done((f32[2,136,128]{2,1,0:T(8,128)S(1)}, f32[2,136,128]{2,1,0:T(8,128)S(1)}, u32[]{:S(2)}, u32[]{:S(2)}) %collective-permute-start.3) | collective-permute-done | bytes 139296 | tf_op jit(solution)/shard_map/ppermute | solution.py:615
  20.3 1.2 copy-done.1
  21.6 1.0 copy-done.3
  22.6 0.7 copy-done.8
  23.3 0.7 copy-done.10
  23.9 1.6 %copy-done.11 = f32[1,1,8,256,256]{4,3,2,1,0:T(8,128)S(1)} copy-done((f32[1,1,8,256,256]{4,3,2,1,0:T(8,128)S(1)}, f32[1,1,8,256,256]{4,3,2,1,0:T(8,128)}, u32[]{:S(2)}) %copy-start.11) | copy-done | bytes 2097176
  25.5 1.4 %copy-done.15 = bf16[1536,512]{1,0:T(8,128)(2,1)S(1)} copy-done((bf16[1536,512]{1,0:T(8,128)(2,1)S(1)}, bf16[1536,512]{1,0:T(8,128)(2,1)}, u32[]{:S(2)}) %copy-start.15) | copy-done | bytes 1572888
  26.9 1.1 copy-done.17
  28.1 7.1 %positions_far.1 = (f32[2,128,640]{2,1,0:T(8,128)S(1)}, f32[5,8,128]{2,1,0:T(8,128)S(1)}, f32[12,512,128]{2,1,0:T(8,128)S(1)}, f32[12,512,128]{2,1,0:T(8,128)S(1)}, f32[2,3,256,128]{3,2,1,0:T(8,128)S(1)}) custom-call(s32[2]{0:T(128)S(1)} %pad_add_fusion.place.refs_0_, s32[1,1,8]{2,1,0:T(1,128)S(1)} %copy-done.8, s32[1,1,8]{2,1,0:T(1,128)S(1)} %copy-done.10, ...), custom_call_target="tpu_custom_call" | custom-call | flops 6442450944 | bytes 16000000 | tf_op jit(solution)/shard_map/positions_far/pallas_call | solution.py:460
  35.2 0.8 copy-done.13
  36.1 1.7 %positions_near.1 = (f32[2,256,512]{2,1,0:T(8,128)S(1)}, f32[2,128,640]{2,1,0:T(8,128)S(1)}, f32[2,256,128]{2,1,0:T(8,128)S(1)}, f32[2,3,256,128]{3,2,1,0:T(8,128)S(1)}) custom-call(s32[2]{0:T(128)S(1)} %pad_add_fusion.place.refs_0_, s32[1,1,8]{2,1,0:T(1,128)S(1)} %copy-done.8, s32[1,1,8]{2,1,0:T(1,128)S(1)} %copy-done.10, s32[1,1]{1,0:T(1,128)S(6)} %copy.12.count.refs_3_, ...), custom_call_target="tpu_custom_call" | custom-call | flops 6442450944 | bytes 16000000 | tf_op jit(solution)/shard_map/positions_near/pallas_call | solution.py:469
  37.8 0.8 copy-done.14
  38.6 0.8 constant_dynamic-slice_fusion.2
  39.4 4.8 %collective-permute-start.5 = (f32[768,128]{1,0:T(8,128)}, f32[768,128]{1,0:T(8,128)}, u32[]{:S(2)}, u32[]{:S(2)}) collective-permute-start(f32[768,128]{1,0:T(8,128)} %constant_dynamic-slice_fusion.2), channel_id=1, source_target_pairs={{0,2},{2,0},{4,6},{6,4},{8,10},{10,8},{12,14},{14,12},{16,18},{18,... | collective-permute-start | bytes 1179656 | tf_op jit(solution)/shard_map/ppermute | solution.py:572
  44.2 1.7 %collective-permute-done.5 = f32[768,128]{1,0:T(8,128)} collective-permute-done((f32[768,128]{1,0:T(8,128)}, f32[768,128]{1,0:T(8,128)}, u32[]{:S(2)}, u32[]{:S(2)}) %collective-permute-start.5) | collective-permute-done | bytes 393248 | tf_op jit(solution)/shard_map/ppermute | solution.py:572
  45.9 1.8 %dynamic-slice_add_fusion = f32[768,128]{1,0:T(8,128)} fusion(f32[768,128]{1,0:T(8,128)} %collective-permute-done.5, f32[1536,128]{1,0:T(8,128)S(1)} %bitcast.7, s32[]{:T(128)S(6)} %select_n.84), kind=kLoop, calls=%fused_computation.2 | loop fusion | flops 98304 | bytes 1179652 | tf_op jit(solution)/shard_map/add | solution.py:586
  47.7 0.9 constant_dynamic-slice_fusion.1
  48.6 17.3 %collective-permute-start.6 = (f32[384,128]{1,0:T(8,128)S(1)}, f32[384,128]{1,0:T(8,128)S(1)}, u32[]{:S(2)}, u32[]{:S(2)}) collective-permute-start(f32[384,128]{1,0:T(8,128)S(1)} %constant_dynamic-slice_fusion.1), channel_id=1, source_target_pairs={{0,4},{2,6},{4,0},{6,2},{8,12},{10,14},{12,8},{14,10},{16,20},{18,... | collective-permute-start | bytes 589832 | tf_op jit(solution)/shard_map/ppermute | solution.py:572
  66.0 5.2 %collective-permute-done.6 = f32[384,128]{1,0:T(8,128)S(1)} collective-permute-done((f32[384,128]{1,0:T(8,128)S(1)}, f32[384,128]{1,0:T(8,128)S(1)}, u32[]{:S(2)}, u32[]{:S(2)}) %collective-permute-start.6) | collective-permute-done | bytes 196640 | tf_op jit(solution)/shard_map/ppermute | solution.py:572
  71.1 0.9 dynamic-slice_add_fusion.1
  72.2 2.1 %cover.1 = (f32[256,512]{1,0:T(8,128)S(1)}, f32[8,128]{1,0:T(8,128)S(1)}) custom-call(s32[2]{0:T(128)S(1)} %pad_add_fusion.place.refs_0_, s32[6,32]{1,0:T(8,128)S(1)} %fusion.1.info, f32[2,256,256]{2,1,0:T(8,128)S(1)} %copy-done.4), custom_call_target="tpu_custom_call" | custom-call | flops 4000000 | bytes 8000000 | tf_op jit(solution)/shard_map/cover/pallas_call | solution.py:116
  74.4 2.4 %collective-permute-done.7 = f32[192,128]{1,0:T(8,128)S(1)} collective-permute-done((f32[192,128]{1,0:T(8,128)S(1)}, f32[192,128]{1,0:T(8,128)S(1)}, u32[]{:S(2)}, u32[]{:S(2)}) %collective-permute-start.7) | collective-permute-done | bytes 98336 | tf_op jit(solution)/shard_map/ppermute | solution.py:572
  76.9 4.6 %collective-permute-done.8 = f32[200,128]{1,0:T(8,128)S(1)} collective-permute-done((f32[200,128]{1,0:T(8,128)S(1)}, f32[200,128]{1,0:T(8,128)S(1)}, u32[]{:S(2)}, u32[]{:S(2)}) %collective-permute-start.8) | collective-permute-done | bytes 102432 | tf_op jit(solution)/shard_map/ppermute | solution.py:572
  81.6 4.1 %collective-permute-start.9 = (f32[200,128]{1,0:T(8,128)S(1)}, f32[200,128]{1,0:T(8,128)S(1)}, u32[]{:S(2)}, u32[]{:S(2)}) collective-permute-start(f32[200,128]{1,0:T(8,128)S(1)} %pad_maximum_fusion.5), channel_id=1, source_target_pairs={{0,16},{2,18},{4,20},{6,22},{8,24},{10,26},{12,28},{14,30},{16,0},... | collective-permute-start | bytes 307208 | tf_op jit(solution)/shard_map/ppermute | solution.py:572
  85.7 2.7 %collective-permute-done.9 = f32[200,128]{1,0:T(8,128)S(1)} collective-permute-done((f32[200,128]{1,0:T(8,128)S(1)}, f32[200,128]{1,0:T(8,128)S(1)}, u32[]{:S(2)}, u32[]{:S(2)}) %collective-permute-start.9) | collective-permute-done | bytes 102432 | tf_op jit(solution)/shard_map/ppermute | solution.py:572
  88.5 0.7 pad_maximum_fusion.6
  89.1 0.9 collective-permute-start.10
  90.0 0.7 collective-permute-start.13
  90.7 2.8 %collective-permute-start.12 = (f32[2,128,640]{2,1,0:T(8,128)}, f32[2,128,640]{2,1,0:T(8,128)}, u32[]{:S(2)}, u32[]{:S(2)}) collective-permute-start(f32[2,128,640]{2,1,0:T(8,128)} %copy-done.14), channel_id=1, source_target_pairs={{0,2},{2,0},{4,6},{6,4},{8,10},{10,8},{12,14},{14,12},{16,18},{18,... | collective-permute-start | bytes 1966088 | tf_op jit(solution)/shard_map/ppermute | solution.py:551
  93.5 0.6 collective-permute-done.10
  94.1 0.7 slice_maximum_fusion.1
  94.8 1.0 slice_select_fusion.5
  95.8 1.2 collective-permute-start.11
  96.9 0.9 slice_select_fusion.3
  97.9 8.5 %collective-permute-done.11 = f32[392,128]{1,0:T(8,128)S(1)} collective-permute-done((f32[392,128]{1,0:T(8,128)S(1)}, f32[392,128]{1,0:T(8,128)S(1)}, u32[]{:S(2)}, u32[]{:S(2)}) %collective-permute-start.11) | collective-permute-done | bytes 200736 | tf_op jit(solution)/shard_map/ppermute | solution.py:572
  106.4 4.3 %collective-permute-start.15 = (f32[776,128]{1,0:T(8,128)S(1)}, f32[776,128]{1,0:T(8,128)S(1)}, u32[]{:S(2)}, u32[]{:S(2)}) collective-permute-start(f32[776,128]{1,0:T(8,128)S(1)} %pad_maximum_fusion), channel_id=1, source_target_pairs={{0,2},{2,0},{4,6},{6,4},{8,10},{10,8},{12,14},{14,12},{16,18},{18,... | collective-permute-start | bytes 1191944 | tf_op jit(solution)/shard_map/ppermute | solution.py:572
  110.8 1.2 collective-permute-start.14
  112.0 7.1 %collective-permute-done.14.refs_7_ = f32[2,256,128]{2,1,0:T(8,128)S(1)} collective-permute-done((f32[2,256,128]{2,1,0:T(8,128)S(1)}, f32[2,256,128]{2,1,0:T(8,128)S(1)}, u32[]{:S(2)}, u32[]{:S(2)}) %collective-permute-start.14) | collective-permute-done | bytes 262176 | tf_op jit(solution)/shard_map/ppermute | solution.py:551
  119.1 3.0 %update.1 = (f32[2,256,512]{2,1,0:T(8,128)}, f32[2,256,256]{2,1,0:T(8,128)}) custom-call(s32[2]{0:T(128)S(1)} %pad_add_fusion.place.refs_0_, f32[2,256,512]{2,1,0:T(8,128)S(1)} %copy-done.2, f32[2,256,512]{2,1,0:T(8,128)S(1)} %get-tuple-element.28.refs_2_, f32[256,512]{1,0:T(8,128)S(1)} %copy-done.6, f32[8,128]{1,0:T(8,128)S(1)} %slice_maximum_fusion.refs_4_, ...), custom_call_target="tpu_custom_call" | custom-call | tf_op jit(solution)/shard_map/update/pallas_call | solution.py:535
  (55 shorter events, 0.6 us)
Async XLA Ops:
  1.4 1.2 %copy-start = (f32[2,256,512]{2,1,0:T(8,128)S(1)}, f32[2,256,512]{2,1,0:T(8,128)}, u32[]{:S(2)}) copy-start(f32[2,256,512]{2,1,0:T(8,128)} %refs_1_.5) | copy-start | bytes 3145732
  2.6 0.7 copy-start.7
  3.2 0.7 copy-start.9
  4.7 15.6 %collective-permute-start = (f32[2,136,512]{2,1,0:T(8,128)S(1)}, f32[2,136,512]{2,1,0:T(8,128)S(1)}, u32[]{:S(2)}, u32[]{:S(2)}) collective-permute-start(f32[2,136,512]{2,1,0:T(8,128)S(1)} %get-tuple-element.20), channel_id=1, source_target_pairs={{0,2},{2,0},{4,6},{6,4},{8,10},{10,8},{12,14},{14,12},{16,18},{18,... | collective-permute-start | bytes 1671176 | tf_op jit(solution)/shard_map/ppermute | solution.py:551
  5.2 15.1 %collective-permute-start.1 = (f32[2,136,512]{2,1,0:T(8,128)S(1)}, f32[2,136,512]{2,1,0:T(8,128)S(1)}, u32[]{:S(2)}, u32[]{:S(2)}) collective-permute-start(f32[2,136,512]{2,1,0:T(8,128)S(1)} %get-tuple-element.21), channel_id=1, source_target_pairs={{2,4},{4,2},{6,8},{8,6},{10,12},{12,10},{14,16},{16,14},{18,20},{2... | collective-permute-start | bytes 1671176 | tf_op jit(solution)/shard_map/ppermute | solution.py:551
  5.9 14.4 %collective-permute-start.2 = (f32[2,264,128]{2,1,0:T(8,128)S(1)}, f32[2,264,128]{2,1,0:T(8,128)S(1)}, u32[]{:S(2)}, u32[]{:S(2)}) collective-permute-start(f32[2,264,128]{2,1,0:T(8,128)S(1)} %get-tuple-element.22), channel_id=1, source_target_pairs={{0,1},{1,0},{2,3},{3,2},{4,5},{5,4},{6,7},{7,6},{8,9},{9,8},{10,11... | collective-permute-start | bytes 811016 | tf_op jit(solution)/shard_map/ppermute | solution.py:551
  8.5 11.8 %collective-permute-start.3 = (f32[2,136,128]{2,1,0:T(8,128)S(1)}, f32[2,136,128]{2,1,0:T(8,128)S(1)}, u32[]{:S(2)}, u32[]{:S(2)}) collective-permute-start(f32[2,136,128]{2,1,0:T(8,128)S(1)} %get-tuple-element.23), channel_id=1, source_target_pairs={{0,3},{2,1},{1,2},{3,0},{4,7},{6,5},{5,6},{7,4},{8,11},{10,9},{9,1... | collective-permute-start | bytes 417800 | tf_op jit(solution)/shard_map/ppermute | solution.py:615
  11.1 9.2 %collective-permute-start.4 = (f32[2,136,128]{2,1,0:T(8,128)S(1)}, f32[2,136,128]{2,1,0:T(8,128)S(1)}, u32[]{:S(2)}, u32[]{:S(2)}) collective-permute-start(f32[2,136,128]{2,1,0:T(8,128)S(1)} %get-tuple-element.24), channel_id=1, source_target_pairs={{2,5},{4,3},{3,4},{5,2},{6,9},{8,7},{7,8},{9,6},{10,13},{12,11},{1... | collective-permute-start | bytes 417800 | tf_op jit(solution)/shard_map/ppermute | solution.py:615
  20.3 1.2 %copy-start.1 = (f32[2,256,512]{2,1,0:T(8,128)S(1)}, f32[2,256,512]{2,1,0:T(8,128)}, u32[]{:S(2)}) copy-start(f32[2,256,512]{2,1,0:T(8,128)} %refs_1_.5) | copy-start | bytes 3145732
  21.6 1.0 copy-start.3
  22.6 0.7 copy-start.8
  23.3 0.7 copy-start.10
  23.9 1.6 %copy-start.11 = (f32[1,1,8,256,256]{4,3,2,1,0:T(8,128)S(1)}, f32[1,1,8,256,256]{4,3,2,1,0:T(8,128)}, u32[]{:S(2)}) copy-start(f32[1,1,8,256,256]{4,3,2,1,0:T(8,128)} %refs_8_.1) | copy-start | bytes 6291460
  25.5 1.4 %copy-start.15 = (bf16[1536,512]{1,0:T(8,128)(2,1)S(1)}, bf16[1536,512]{1,0:T(8,128)(2,1)}, u32[]{:S(2)}) copy-start(bf16[1536,512]{1,0:T(8,128)(2,1)} %constant.82.clone.refs_13_.refs_10_) | copy-start | bytes 4718596
  26.9 1.1 copy-start.17
  28.0 8.0 %copy-start.4 = (f32[2,256,256]{2,1,0:T(8,128)S(1)}, f32[2,256,256]{2,1,0:T(8,128)}, u32[]{:S(2)}) copy-start(f32[2,256,256]{2,1,0:T(8,128)} %refs_10_.4) | copy-start | bytes 1572868
  28.1 8.0 %copy-start.12 = (f32[1,1,8,256,256]{4,3,2,1,0:T(8,128)S(1)}, f32[1,1,8,256,256]{4,3,2,1,0:T(8,128)}, u32[]{:S(2)}) copy-start(f32[1,1,8,256,256]{4,3,2,1,0:T(8,128)} %refs_8_.1) | copy-start | bytes 6291460
  28.1 8.0 %copy-start.16 = (bf16[1536,512]{1,0:T(8,128)(2,1)S(1)}, bf16[1536,512]{1,0:T(8,128)(2,1)}, u32[]{:S(2)}) copy-start(bf16[1536,512]{1,0:T(8,128)(2,1)} %constant.82.clone.refs_13_.refs_10_) | copy-start | bytes 4718596
  28.1 8.0 %copy-start.18 = (bf16[256,1536]{1,0:T(8,128)(2,1)S(1)}, bf16[256,1536]{1,0:T(8,128)(2,1)}, u32[]{:S(2)}) copy-start(bf16[256,1536]{1,0:T(8,128)(2,1)} %constant.81.clone.refs_12_.refs_9_) | copy-start | bytes 2359300
  35.2 0.8 copy-start.13
  37.8 0.8 copy-start.14
  39.4 6.5 %collective-permute-start.5 = (f32[768,128]{1,0:T(8,128)}, f32[768,128]{1,0:T(8,128)}, u32[]{:S(2)}, u32[]{:S(2)}) collective-permute-start(f32[768,128]{1,0:T(8,128)} %constant_dynamic-slice_fusion.2), channel_id=1, source_target_pairs={{0,2},{2,0},{4,6},{6,4},{8,10},{10,8},{12,14},{14,12},{16,18},{18,... | collective-permute-start | bytes 1179656 | tf_op jit(solution)/shard_map/ppermute | solution.py:572
  48.6 22.5 %collective-permute-start.6 = (f32[384,128]{1,0:T(8,128)S(1)}, f32[384,128]{1,0:T(8,128)S(1)}, u32[]{:S(2)}, u32[]{:S(2)}) collective-permute-start(f32[384,128]{1,0:T(8,128)S(1)} %constant_dynamic-slice_fusion.1), channel_id=1, source_target_pairs={{0,4},{2,6},{4,0},{6,2},{8,12},{10,14},{12,8},{14,10},{16,20},{18,... | collective-permute-start | bytes 589832 | tf_op jit(solution)/shard_map/ppermute | solution.py:572
  72.1 4.7 %collective-permute-start.7 = (f32[192,128]{1,0:T(8,128)S(1)}, f32[192,128]{1,0:T(8,128)S(1)}, u32[]{:S(2)}, u32[]{:S(2)}) collective-permute-start(f32[192,128]{1,0:T(8,128)S(1)} %constant_dynamic-slice_fusion), channel_id=1, source_target_pairs={{0,1},{1,0},{2,3},{3,2},{4,5},{5,4},{6,7},{7,6},{8,9},{9,8},{10,11... | collective-permute-start | bytes 294920 | tf_op jit(solution)/shard_map/ppermute | solution.py:572
  74.4 15.7 %copy-start.5 = (f32[256,512]{1,0:T(8,128)}, f32[256,512]{1,0:T(8,128)S(1)}, u32[]{:S(2)}) copy-start(f32[256,512]{1,0:T(8,128)S(1)} %get-tuple-element.32.refs_3_) | copy-start | bytes 1572868
  74.4 44.7 %copy-start.2 = (f32[2,256,512]{2,1,0:T(8,128)S(1)}, f32[2,256,512]{2,1,0:T(8,128)}, u32[]{:S(2)}) copy-start(f32[2,256,512]{2,1,0:T(8,128)} %refs_1_.5) | copy-start | bytes 3145732
  76.8 4.7 %collective-permute-start.8 = (f32[200,128]{1,0:T(8,128)S(1)}, f32[200,128]{1,0:T(8,128)S(1)}, u32[]{:S(2)}, u32[]{:S(2)}) collective-permute-start(f32[200,128]{1,0:T(8,128)S(1)} %pad_maximum_fusion.4), channel_id=1, source_target_pairs={{0,8},{2,10},{4,12},{6,14},{8,0},{10,2},{12,4},{14,6},{16,24},{18,... | collective-permute-start | bytes 307208 | tf_op jit(solution)/shard_map/ppermute | solution.py:572
  81.6 6.8 %collective-permute-start.9 = (f32[200,128]{1,0:T(8,128)S(1)}, f32[200,128]{1,0:T(8,128)S(1)}, u32[]{:S(2)}, u32[]{:S(2)}) collective-permute-start(f32[200,128]{1,0:T(8,128)S(1)} %pad_maximum_fusion.5), channel_id=1, source_target_pairs={{0,16},{2,18},{4,20},{6,22},{8,24},{10,26},{12,28},{14,30},{16,0},... | collective-permute-start | bytes 307208 | tf_op jit(solution)/shard_map/ppermute | solution.py:572
  88.4 1.6 %copy-start.19 = (f32[192,128]{1,0:T(8,128)}, f32[192,128]{1,0:T(8,128)S(1)}, u32[]{:S(2)}) copy-start(f32[192,128]{1,0:T(8,128)S(1)} %slice_add_fusion) | copy-start | bytes 294916
  89.1 5.0 %collective-permute-start.10 = (f32[200,128]{1,0:T(8,128)}, f32[200,128]{1,0:T(8,128)}, u32[]{:S(2)}, u32[]{:S(2)}) collective-permute-start(f32[200,128]{1,0:T(8,128)} %pad_maximum_fusion.6), channel_id=1, source_target_pairs={{0,1},{1,0},{2,3},{3,2},{4,5},{5,4},{6,7},{7,6},{8,9},{9,8},{10,11... | collective-permute-start | bytes 307208 | tf_op jit(solution)/shard_map/ppermute | solution.py:572
  90.0 6.9 %collective-permute-start.13 = (f32[2,128,640]{2,1,0:T(8,128)}, f32[2,128,640]{2,1,0:T(8,128)S(1)}, u32[]{:S(2)}, u32[]{:S(2)}) collective-permute-start(f32[2,128,640]{2,1,0:T(8,128)} %copy-done.13), channel_id=1, source_target_pairs={{2,4},{4,2},{6,8},{8,6},{10,12},{12,10},{14,16},{16,14},{18,20},{2... | collective-permute-start | bytes 1966088 | tf_op jit(solution)/shard_map/ppermute | solution.py:551
  90.7 6.2 %collective-permute-start.12 = (f32[2,128,640]{2,1,0:T(8,128)}, f32[2,128,640]{2,1,0:T(8,128)}, u32[]{:S(2)}, u32[]{:S(2)}) collective-permute-start(f32[2,128,640]{2,1,0:T(8,128)} %copy-done.14), channel_id=1, source_target_pairs={{0,2},{2,0},{4,6},{6,4},{8,10},{10,8},{12,14},{14,12},{16,18},{18,... | collective-permute-start | bytes 1966088 | tf_op jit(solution)/shard_map/ppermute | solution.py:551
  93.5 25.6 %copy-start.6 = (f32[256,512]{1,0:T(8,128)S(1)}, f32[256,512]{1,0:T(8,128)}, u32[]{:S(2)}) copy-start(f32[256,512]{1,0:T(8,128)} %copy-done.5) | copy-start | bytes 1572868
  95.8 10.6 %collective-permute-start.11 = (f32[392,128]{1,0:T(8,128)S(1)}, f32[392,128]{1,0:T(8,128)S(1)}, u32[]{:S(2)}, u32[]{:S(2)}) collective-permute-start(f32[392,128]{1,0:T(8,128)S(1)} %pad_maximum_fusion.2), channel_id=1, source_target_pairs={{0,4},{2,6},{4,0},{6,2},{8,12},{10,14},{12,8},{14,10},{16,20},{18,... | collective-permute-start | bytes 602120 | tf_op jit(solution)/shard_map/ppermute | solution.py:572
  106.4 12.6 %collective-permute-start.15 = (f32[776,128]{1,0:T(8,128)S(1)}, f32[776,128]{1,0:T(8,128)S(1)}, u32[]{:S(2)}, u32[]{:S(2)}) collective-permute-start(f32[776,128]{1,0:T(8,128)S(1)} %pad_maximum_fusion), channel_id=1, source_target_pairs={{0,2},{2,0},{4,6},{6,4},{8,10},{10,8},{12,14},{14,12},{16,18},{18,... | collective-permute-start | bytes 1191944 | tf_op jit(solution)/shard_map/ppermute | solution.py:572
  110.8 8.3 %collective-permute-start.14 = (f32[2,256,128]{2,1,0:T(8,128)S(1)}, f32[2,256,128]{2,1,0:T(8,128)S(1)}, u32[]{:S(2)}, u32[]{:S(2)}) collective-permute-start(f32[2,256,128]{2,1,0:T(8,128)S(1)} %maximum_add_fusion), channel_id=1, source_target_pairs={{0,1},{1,0},{2,3},{3,2},{4,5},{5,4},{6,7},{7,6},{8,9},{9,8},{10,11... | collective-permute-start | bytes 786440 | tf_op jit(solution)/shard_map/ppermute | solution.py:551

commit v5 on v4

--- a/solution.py
+++ b/solution.py
@@ -22,6 +22,8 @@
 VMEM = pl.BlockSpec(memory_space=pltpu.VMEM)
 SMEM = pl.BlockSpec(memory_space=pltpu.SMEM)
 ANY = pl.BlockSpec(memory_space=pl.ANY)
+HBM = pl.BlockSpec(memory_space=pltpu.HBM)
+COUNT, ROWS, COLS = 2, 3, 11
 
 
 def rounded_pair(table):
@@ -131,7 +133,7 @@
     )(place, info, probe)
 
 
-def pack_kernel(sides, place, rows, cols, count, tile, *refs):
+def pack_kernel(sides, place, tile, *refs):
     far_band, near_band = refs[:2]
     edges, far_ends, near_ends = [refs[2 + i * sides : 2 + (i + 1) * sides] for i in range(3)]
     sems = refs[2 + 3 * sides]
@@ -156,9 +158,9 @@
         )
         copies[-1].start()
     lanes = lax.broadcasted_iota(jnp.int32, (INFO, LANES), 1)
-    notes = jnp.where(lanes == 16, count[0, 0], 0)
-    for k in range(rows.shape[2]):
-        notes = jnp.where(lanes == k, rows[0, 0, k], jnp.where(lanes == 8 + k, cols[0, 0, k], notes))
+    notes = jnp.where(lanes == 16, place[COUNT], 0)
+    for k in range(8):
+        notes = jnp.where(lanes == k, place[ROWS + k], jnp.where(lanes == 8 + k, place[COLS + k], notes))
     notes = notes.astype(F32)
     for band, row, height, col in bands:
         for ch in range(2):
@@ -169,44 +171,44 @@
         copy.wait()
 
 
-def pack_call(place, rows, cols, count, tile, sides):
+def pack_call(place, tile, sides):
     tile_rows, tile_cols = tile.shape[1:]
     shape = lambda height, width: jax.ShapeDtypeStruct((2, height + INFO, width), F32)
     shapes = [shape(H, tile_cols)] * 2 + [shape(tile_rows, LANES)] * sides + [shape(H, LANES)] * (2 * sides)
     out = pl.pallas_call(
         functools.partial(pack_kernel, sides),
         out_shape=shapes,
-        in_specs=[SMEM] * 4 + [ANY],
+        in_specs=[SMEM, HBM],
         out_specs=[VMEM] * len(shapes),
         scratch_shapes=[pltpu.SemaphoreType.DMA((len(shapes),))],
         compiler_params=pltpu.CompilerParams(vmem_limit_bytes=8 << 20),
         name="pack",
-    )(place, rows, cols, count, tile)
+    )(place, tile)
     return out[0], out[1], *[list(out[2 + i * sides : 2 + (i + 1) * sides]) for i in range(3)]
 
 
 def positions_kernel(sides, last, *refs):
-    place, rows, cols, count = refs[:4]
+    place = refs[0]
     if last:
-        ext, grad_in, sums_in, probe, measured, left_in, right_in = refs[4:11]
-        outs = refs[11:]
-        middle, near_rim = outs[:2]
-        side_out = outs[2 : 2 + sides]
-        probe_sums = outs[2 + sides]
-        grad = outs[3 + sides]
-        scratch = outs[4 + sides :]
+        ext_in, grad_in, sums_in, far_side = refs[1:5]
+        far_corners = refs[5 : 5 + sides]
+        probe_in, measured, left_in, right_in = refs[5 + sides : 9 + sides]
+        middle, near_rim, far_rim, info = refs[9 + sides : 13 + sides]
+        side_out = refs[13 + sides : 13 + 2 * sides]
+        probe_sums, ext, grad = refs[13 + 2 * sides : 16 + 2 * sides]
+        scratch = refs[16 + 2 * sides :]
     else:
-        tile, near, far_side = refs[4:7]
-        side_in, near_corners, far_corners = [refs[7 + i * sides : 7 + (i + 1) * sides] for i in range(3)]
-        probe, measured, left_in, right_in = refs[7 + 3 * sides : 11 + 3 * sides]
-        far_rim, info, ext, grad, probe_sums = refs[11 + 3 * sides : 16 + 3 * sides]
-        scratch = refs[16 + 3 * sides :]
-    left, right, levels, order = scratch[:4]
-    table_sems, level_sems, ext_sems = scratch[4:7]
-    scratch = scratch[7:]
+        tile, near = refs[1:3]
+        side_in, near_corners = refs[3 : 3 + sides], refs[3 + sides : 3 + 2 * sides]
+        probe_in, measured, left_in, right_in = refs[3 + 2 * sides : 7 + 2 * sides]
+        info, ext, grad, probe_sums = refs[7 + 2 * sides : 11 + 2 * sides]
+        scratch = refs[11 + 2 * sides :]
+    left, right, levels, order, probe = scratch[:5]
+    table_sems, level_sems, ext_sems = scratch[5:8]
+    scratch = scratch[8:]
     patches, exits, stacks, wides, fields = [scratch[i * WAYS : (i + 1) * WAYS] for i in range(5)]
 
-    pr = probe.shape[1]
+    pr = probe_in.shape[1]
     pieces = pr // LANES
     ext_rows = ext.shape[1]
     blocks = ext.shape[0] // 2
@@ -224,35 +226,44 @@
         copies.append(pltpu.make_async_copy(source, target, ext_sems.at[len(copies)]))
         copies[-1].start()
 
-    if not last:
-        for ch in range(2):
-            for b in range(own_blocks):
-                at, cut = ch * blocks + 1 + b, pl.ds(b * LANES, LANES)
+    for ch in range(2):
+        for b in range(own_blocks):
+            at, cut = ch * blocks + 1 + b, pl.ds(b * LANES, LANES)
+            if last:
+                fetch(far_side.at[ch, pl.ds(0, H), cut], ext.at[at, far_rows, :])
+            else:
                 fetch(tile.at[ch, :, cut], ext.at[at, own, :])
                 fetch(near.at[ch, pl.ds(0, H), cut], ext.at[at, near_rows, :])
-                fetch(far_side.at[ch, pl.ds(0, H), cut], ext.at[at, far_rows, :])
-            for s in range(sides):
-                at = ch * blocks + side_blocks[s]
+        for s in range(sides):
+            at = ch * blocks + side_blocks[s]
+            if last:
+                fetch(far_corners[s].at[ch, pl.ds(0, H), :], ext.at[at, far_rows, :])
+            else:
                 fetch(side_in[s].at[ch, pl.ds(0, tile_rows), :], ext.at[at, own, :])
                 fetch(near_corners[s].at[ch, pl.ds(0, H), :], ext.at[at, near_rows, :])
-                fetch(far_corners[s].at[ch, pl.ds(0, H), :], ext.at[at, far_rows, :])
-        for s in range(sides):
+    for s in range(sides):
+        if last:
+            fetch(far_corners[s].at[0, pl.ds(H, INFO), :], info.at[1 + s])
+        else:
             fetch(side_in[s].at[0, pl.ds(tile_rows, INFO), :], info.at[s])
             fetch(near_corners[s].at[0, pl.ds(H, INFO), :], info.at[sides + 1 + s])
-            fetch(far_corners[s].at[0, pl.ds(H, INFO), :], info.at[2 * sides + 2 + s])
+    if last:
+        fetch(far_side.at[0, pl.ds(H, INFO), pl.ds(0, LANES)], info.at[0])
+    else:
         fetch(near.at[0, pl.ds(H, INFO), pl.ds(0, LANES)], info.at[sides])
-        fetch(far_side.at[0, pl.ds(H, INFO), pl.ds(0, LANES)], info.at[2 * sides + 1])
     tables = [
         pltpu.make_async_copy(left_in, left, table_sems.at[0]),
         pltpu.make_async_copy(right_in, right, table_sems.at[1]),
+        pltpu.make_async_copy(probe_in, probe, table_sems.at[2]),
     ]
     for copy in tables:
         copy.start()
 
-    live_slots = count[0, 0]
+    live_slots = place[COUNT]
 
     def touches(k):
-        return jnp.where(even, rows[0, 0, k] < H, rows[0, 0, k] > tile_rows - H)
+        row = place[ROWS + k]
+        return jnp.where(even, row < H, row > tile_rows - H)
 
     def pick(wanted):
         def step(k, n):
@@ -264,9 +275,9 @@
 
         return step
 
-    far_slots = lax.fori_loop(0, live_slots, pick(True), 0)
-    lax.fori_loop(0, live_slots, pick(False), far_slots)
-    border = jnp.minimum((far_slots + WAYS - 1) // WAYS * WAYS, live_slots)
+    near_slots = lax.fori_loop(0, live_slots, pick(False), 0)
+    lax.fori_loop(0, live_slots, pick(True), near_slots)
+    border = near_slots // WAYS * WAYS
     begin, end = (border, live_slots) if last else (0, border)
 
     def level_copy(i):
@@ -278,6 +289,12 @@
 
     lax.fori_loop(begin, end, start_level, 0)
     if last:
+        for at in range(2 * blocks):
+            ext[at, own, :] = ext_in[at, own, :]
+            ext[at, near_rows, :] = ext_in[at, near_rows, :]
+        if sides == 1:
+            for ch in range(2):
+                ext[ch * blocks + blocks - 1 - side_blocks[0], far_rows, :] = jnp.zeros((H, LANES), F32)
         grad[...] = grad_in[...]
         probe_sums[...] = sums_in[...]
     else:
@@ -316,7 +333,7 @@
         fields[w][...] = jnp.dot(stack, right[...], preferred_element_type=F32)
 
     def load(w, k):
-        row, col = rows[0, 0, order[k]], cols[0, 0, order[k]]
+        row, col = place[ROWS + order[k]], place[COLS + order[k]]
         shift, block = col & (LANES - 1), col >> 7
         back = (LANES - shift) & (LANES - 1)
         keep = lanes < LANES - shift
@@ -350,7 +367,7 @@
             put(stacks[w], -(imag * factor), 1, q, 0)
 
     def finish(w, k, live):
-        row, col = rows[0, 0, order[k]], cols[0, 0, order[k]]
+        row, col = place[ROWS + order[k]], place[COLS + order[k]]
         shift, block = col & (LANES - 1), col >> 7
         low = lanes < shift
         zero = jnp.zeros((CHUNK, LANES), F32)
@@ -406,27 +423,23 @@
         return carry
 
     lax.fori_loop(0, (end - begin + WAYS - 1) // WAYS, visit, 0)
+    if not last:
+        return
     for ch in range(2):
         for b in range(own_blocks):
             at, cut = ch * blocks + 1 + b, slice(b * LANES, (b + 1) * LANES)
-            if last:
-                middle[ch, :, cut] = grad[at, own, :]
-                near_rim[ch, :, cut] = grad[at, near_rows, :]
-            else:
-                far_rim[ch, :, cut] = grad[at, far_rows, :]
+            middle[ch, :, cut] = grad[at, own, :]
+            near_rim[ch, :, cut] = grad[at, near_rows, :]
+            far_rim[ch, :, cut] = grad[at, far_rows, :]
         for s in range(sides):
             at = ch * blocks + side_blocks[s]
             cut = slice(tile_cols + s * LANES, tile_cols + (s + 1) * LANES)
-            if last:
-                side_out[s][ch] = grad[at, own, :]
-                near_rim[ch, :, cut] = grad[at, near_rows, :]
-            else:
-                far_rim[ch, :, cut] = grad[at, far_rows, :]
-
-
-def positions_calls(
-    place, rows, cols, count, tile, near, far_side, side_in, near_corners, far_corners, probe, measured
-):
+            side_out[s][ch] = grad[at, own, :]
+            near_rim[ch, :, cut] = grad[at, near_rows, :]
+            far_rim[ch, :, cut] = grad[at, far_rows, :]
+
+
+def positions_calls(place, tile, near, far_side, side_in, near_corners, far_corners, probe, measured):
     pr = probe.shape[1]
     sides = len(side_in)
     tile_rows, tile_cols = tile.shape[1:]
@@ -438,44 +451,52 @@
     sums = shape(pr // LANES, 3, pr, LANES)
     field = shape(2 * blocks, ext_rows, LANES)
     rim = shape(2, H, tile_cols + sides * LANES)
-    options = dict(
-        compiler_params=pltpu.CompilerParams(vmem_limit_bytes=34 << 20),
-        cost_estimate=pl.CostEstimate(
-            flops=slots * 48 * pr * pr * pr, bytes_accessed=16_000_000, transcendentals=slots * pr * pr
-        ),
-    )
+    params = pltpu.CompilerParams(vmem_limit_bytes=34 << 20)
     scratch = [
         pltpu.VMEM(left.shape, BF),
         pltpu.VMEM(right.shape, BF),
         pltpu.VMEM((slots, pr, pr), F32),
         pltpu.SMEM((slots,), jnp.int32),
-        pltpu.SemaphoreType.DMA((2,)),
+        pltpu.VMEM(probe.shape, F32),
+        pltpu.SemaphoreType.DMA((3,)),
         pltpu.SemaphoreType.DMA((slots,)),
-        pltpu.SemaphoreType.DMA((6 * blocks + 3 * sides + 2,)),
+        pltpu.SemaphoreType.DMA((4 * blocks + 2 * sides + 1,)),
         *[pltpu.VMEM((2, pr, pr), F32)] * (2 * WAYS),
         *[pltpu.VMEM((4 * pr, 2 * pr), BF)] * WAYS,
         *[pltpu.VMEM((pr, 4 * pr), BF)] * WAYS,
         *[pltpu.VMEM((pr, 2 * pr), F32)] * WAYS,
     ]
-    far_rim, info, ext, grad, probe_sums = pl.pallas_call(
+    near_info, ext, grad, sums_so_far = pl.pallas_call(
         functools.partial(positions_kernel, sides, False),
-        out_shape=(rim, shape(3 * sides + 2, INFO, LANES), field, field, sums),
-        in_specs=[SMEM] * 4 + [ANY] * (3 + 3 * sides) + [VMEM, ANY, ANY, ANY],
-        out_specs=(VMEM,) * 5,
+        out_shape=(shape(2 * sides + 1, INFO, LANES), field, field, sums),
+        in_specs=[SMEM, HBM] + [ANY] * (1 + 2 * sides) + [HBM] * 4,
+        out_specs=(VMEM,) * 4,
         scratch_shapes=scratch,
+        compiler_params=params,
+        cost_estimate=pl.CostEstimate(flops=1, bytes_accessed=1, transcendentals=0),
+        name="positions_near",
+    )(place, tile, near, *side_in, *near_corners, probe, measured, left, right)
+    middle, near_rim, far_rim, far_info, *rest = pl.pallas_call(
+        functools.partial(positions_kernel, sides, True),
+        out_shape=(
+            shape(2, tile_rows, tile_cols),
+            rim,
+            rim,
+            shape(sides + 1, INFO, LANES),
+            *[shape(2, tile_rows, LANES)] * sides,
+            sums,
+        ),
+        in_specs=[SMEM] + [VMEM] * 3 + [ANY] * (1 + sides) + [HBM] * 4,
+        out_specs=(VMEM,) * (5 + sides),
+        scratch_shapes=[pltpu.VMEM(field.shape, F32)] * 2 + scratch,
+        compiler_params=params,
+        cost_estimate=pl.CostEstimate(
+            flops=slots * 48 * pr * pr * pr, bytes_accessed=16_000_000, transcendentals=slots * pr * pr
+        ),
         name="positions_far",
-        **options,
-    )(place, rows, cols, count, tile, near, far_side, *side_in, *near_corners, *far_corners, probe, measured, left, right)
-    out = pl.pallas_call(
-        functools.partial(positions_kernel, sides, True),
-        out_shape=(shape(2, tile_rows, tile_cols), rim, *[shape(2, tile_rows, LANES)] * sides, sums),
-        in_specs=[SMEM] * 4 + [VMEM] * 4 + [ANY] * 3,
-        out_specs=(VMEM,) * (3 + sides),
-        scratch_shapes=[pltpu.VMEM(field.shape, F32)] + scratch,
-        name="positions_near",
-        **options,
-    )(place, rows, cols, count, ext, grad, probe_sums, probe, measured, left, right)
-    return out[0], out[1], far_rim, list(out[2 : 2 + sides]), out[2 + sides], info
+    )(place, ext, grad, sums_so_far, far_side, *far_corners, probe, measured, left, right)
+    info = jnp.concatenate([near_info, far_info], axis=0)
+    return middle, near_rim, far_rim, rest[:sides], rest[sides], info
 
 
 def update_kernel(sides, *refs):
@@ -625,9 +646,11 @@
     sides = 1 if lax.axis_size("narrow") == 2 else 2
     tile_rows, tile_cols = tile.shape[1:]
     even = wide % 2 == 0
-    place = jnp.stack([wide, narrow]).astype(jnp.int32)
-
-    far_band, near_band, edges, far_ends, near_ends = pack_call(place, rows, cols, counts, tile, sides)
+    place = jnp.concatenate(
+        [jnp.stack([wide, narrow, counts[0, 0]]).astype(jnp.int32), rows.reshape(-1), cols.reshape(-1)]
+    )
+
+    far_band, near_band, edges, far_ends, near_ends = pack_call(place, tile, sides)
     far_side = swap(far_band, "wide", 1)
     far_corners = to_corners(far_ends, 1)
     side_in = to_sides(edges)
@@ -635,9 +658,8 @@
     near = swap(near_band, "wide", 0)
 
     middle, near_rim, far_rim, side_rims, probe_sums, got_info = positions_calls(
-        place, rows, cols, counts, tile, near, far_side, side_in, near_corners, far_corners, probe, measured
+        place, tile, near, far_side, side_in, near_corners, far_corners, probe, measured
     )
-    far_got = swap(far_rim, "wide", 1)
     own_info = edges[0][:1, tile_rows:]
 
     terms = probe_sums.reshape(-1, LANES)
@@ -647,9 +669,12 @@
     info = jnp.concatenate([own_info, got_info], axis=0)[:, 0, :32].astype(jnp.int32)
     cover, peak = cover_call(place, after(info, terms), probe, tile_rows, tile_cols, sides)
     terms = halve(terms, "wide", wide_bits[1])
+    far_got = swap(after(far_rim, terms), "wide", 1)
     for bit in narrow_bits:
         terms = halve(terms, "narrow", bit)
     for bit in wide_bits[2:]:
+        if bit == wide_bits[-1]:
+            terms = after(terms, far_got)
         terms, peak = double(terms, peak, "wide", bit)
     for bit in narrow_bits[::-1]:
         terms, peak = gather(terms, peak, "narrow", bit)

time: 123 us -> 120 us (0.976)
  starting transfers between devices: 44.5 us -> 28 us
  Pallas kernels: 14.7 us -> 30.1 us
  waiting for transfers between devices: 41.4 us -> 43.5 us
  other arithmetic: 6.26 us -> 4.48 us
  local copies, waits for them, and re-layouts: 13.7 us -> 12.3 us
    ppermute x8, starting transfers between devices: 32.7 us -> 18 us  [partner(): return lax.ppermute(x, axis, [(i, i ^ bit) for i in range(size)])]
    pallas_call x1, Pallas kernels: 1.72 us -> 15.4 us  [positions_calls(): pl.pallas_call(functools.partial(positions_kernel, sides, True), out_shap...]
    ppermute x6, starting transfers between devices: 8.47 us -> 6.66 us  [swap(): return lax.ppermute(x, axis, pairs)]
    add x3, other arithmetic: 2.74 us -> 1.07 us  [halve(): return half_of(terms, mine) + partner(half_of(terms, 1 - mine), axis, bit)]
    dynamic_slice x3, local copies, waits for them, and re-layouts: 1.73 us -> 0.07 us  [half_of(): return lax.dynamic_slice_in_dim(x, which * rows, rows, axis=0)]
    ppermute x6, waiting for transfers between devices: 7.07 us -> 8.66 us  [swap(): return lax.ppermute(x, axis, pairs)]
    unnamed x40 -> x36, local copies, waits for them, and re-layouts: 11.9 us -> 11.5 us
  transfers between devices with their start and end apart: 16 -> 16, of which waited for: 9 -> 9; matrix products, arithmetic and copies ran while one was open for 2% -> 2% of each run, Pallas kernels for 2% -> 8%
where the time goes in v5:
time: 120 us
  waiting for transfers between devices  43.5 us (36%)
  Pallas kernels  30.1 us (25%)
  starting transfers between devices  28 us (23%)
  local copies, waits for them, and re-layouts  12.3 us (10%)
  other arithmetic  4.48 us (4%)
  between operations  1.64 us (1%)
    ppermute x8, waiting for transfers between devices, partner(): return lax.ppermute(x, axis, [(i, i ^ bit) for i in range(size)])  26.3 us
    ppermute x8, starting transfers between devices, partner(): return lax.ppermute(x, axis, [(i, i ^ bit) for i in range(size)])  18 us
    pallas_call x1, Pallas kernels, positions_calls(): pl.pallas_call(functools.partial(positions_kernel, sides, True), out_shap...  15.4 us
    unnamed x36, local copies, waits for them, and re-layouts  11.5 us
    ppermute x6, waiting for transfers between devices, swap(): return lax.ppermute(x, axis, pairs)  8.66 us
    ppermute x2, waiting for transfers between devices, to_corners(): got.append(lax.ppermute(band, ('wide', 'narrow'), pairs))  8.48 us
    pallas_call x1, Pallas kernels, positions_calls(): pl.pallas_call(functools.partial(positions_kernel, sides, False), out_sha...  6.86 us
    ppermute x6, starting transfers between devices, swap(): return lax.ppermute(x, axis, pairs)  6.66 us
  transfers between devices with their start and end apart: 16, of which 9 were waited for; matrix products, arithmetic and copies ran while one was open for 2% of the time, Pallas kernels for 8%

profile of v5, /device:TPU:0, one launch (start us, length us, event | category | flops | bytes accessed | tf_op | source)
XLA Modules:
  0.0 120.0 jit_solution(15362679869245558647)
XLA Ops:
  1.3 0.7 concatenate.32.place.refs_0_
  2.0 1.2 %copy-done = f32[2,256,512]{2,1,0:T(8,128)S(1)} copy-done((f32[2,256,512]{2,1,0:T(8,128)S(1)}, f32[2,256,512]{2,1,0:T(8,128)}, u32[]{:S(2)}) %copy-start) | copy-done | bytes 1048600
  3.3 1.6 %pack.1 = (f32[2,136,512]{2,1,0:T(8,128)S(1)}, f32[2,136,512]{2,1,0:T(8,128)}, f32[2,264,128]{2,1,0:T(8,128)S(1)}, f32[2,136,128]{2,1,0:T(8,128)S(1)}, f32[2,136,128]{2,1,0:T(8,128)S(1)}) custom-call(s32[19]{0:T(128)S(1)} %concatenate.32.place.refs_0_, f32[2,256,512]{2,1,0:T(8,128)S(1)} %copy-done), custom_call_target="tpu_custom_call" | custom-call | tf_op jit(solution)/shard_map/pack/pallas_call | solution.py:178
  4.8 0.5 collective-permute-start
  5.4 0.7 collective-permute-start.3
  6.0 2.6 %collective-permute-start.1 = (f32[2,264,128]{2,1,0:T(8,128)S(1)}, f32[2,264,128]{2,1,0:T(8,128)S(1)}, u32[]{:S(2)}, u32[]{:S(2)}) collective-permute-start(f32[2,264,128]{2,1,0:T(8,128)S(1)} %get-tuple-element.24), channel_id=1, source_target_pairs={{0,1},{1,0},{2,3},{3,2},{4,5},{5,4},{6,7},{7,6},{8,9},{9,8},{10,11... | collective-permute-start | bytes 811016 | tf_op jit(solution)/shard_map/ppermute | solution.py:572
  8.7 2.6 %collective-permute-start.2 = (f32[2,136,128]{2,1,0:T(8,128)S(1)}, f32[2,136,128]{2,1,0:T(8,128)S(1)}, u32[]{:S(2)}, u32[]{:S(2)}) collective-permute-start(f32[2,136,128]{2,1,0:T(8,128)S(1)} %get-tuple-element.25), channel_id=1, source_target_pairs={{0,3},{2,1},{1,2},{3,0},{4,7},{6,5},{5,6},{7,4},{8,11},{10,9},{9,1... | collective-permute-start | bytes 417800 | tf_op jit(solution)/shard_map/ppermute | solution.py:636
  11.3 0.7 collective-permute-start.4
  12.0 8.5 %collective-permute-done.2.refs_4_ = f32[2,136,128]{2,1,0:T(8,128)S(1)} collective-permute-done((f32[2,136,128]{2,1,0:T(8,128)S(1)}, f32[2,136,128]{2,1,0:T(8,128)S(1)}, u32[]{:S(2)}, u32[]{:S(2)}) %collective-permute-start.2) | collective-permute-done | bytes 139296 | tf_op jit(solution)/shard_map/ppermute | solution.py:636
  20.5 1.2 %copy-done.1 = f32[2,256,512]{2,1,0:T(8,128)S(1)} copy-done((f32[2,256,512]{2,1,0:T(8,128)S(1)}, f32[2,256,512]{2,1,0:T(8,128)}, u32[]{:S(2)}) %copy-start.1) | copy-done | bytes 1048600
  21.7 1.0 copy-done.3
  22.7 1.6 %copy-done.5 = f32[1,1,8,256,256]{4,3,2,1,0:T(8,128)S(1)} copy-done((f32[1,1,8,256,256]{4,3,2,1,0:T(8,128)S(1)}, f32[1,1,8,256,256]{4,3,2,1,0:T(8,128)}, u32[]{:S(2)}) %copy-start.5) | copy-done | bytes 2097176
  24.3 1.4 %copy-done.7 = bf16[1536,512]{1,0:T(8,128)(2,1)S(1)} copy-done((bf16[1536,512]{1,0:T(8,128)(2,1)S(1)}, bf16[1536,512]{1,0:T(8,128)(2,1)}, u32[]{:S(2)}) %copy-start.7) | copy-done | bytes 1572888
  25.7 1.1 copy-done.9
  26.9 6.9 %positions_near.1 = (f32[3,8,128]{2,1,0:T(8,128)S(1)}, f32[12,512,128]{2,1,0:T(8,128)S(1)}, f32[12,512,128]{2,1,0:T(8,128)S(1)}, f32[2,3,256,128]{3,2,1,0:T(8,128)S(1)}) custom-call(s32[19]{0:T(128)S(1)} %concatenate.32.place.refs_0_, f32[2,256,512]{2,1,0:T(8,128)S(1)} %copy-done.1, f32[2,136,512]{2,1,0:T(8,128)S(1)} %collective-permute-done.refs_2_, ...), custom_call_target="tpu_custom_call" | custom-call | flops 1 | bytes 1 | tf_op jit(solution)/shard_map/positions_near/pallas_call | solution.py:469
  33.8 0.0 copy-start.15
  33.8 0.6 copy-done.15
  34.5 0.9 copy-done.16
  35.4 15.4 %positions_far.1 = (f32[2,256,512]{2,1,0:T(8,128)S(1)}, f32[2,128,640]{2,1,0:T(8,128)S(1)}, f32[2,128,640]{2,1,0:T(8,128)S(1)}, f32[2,8,128]{2,1,0:T(8,128)S(1)}...) custom-call(s32[19]{0:T(128)S(1)} %concatenate.32.place.refs_0_, ...), custom_call_target="tpu_custom_call" | custom-call | flops 6442450944 | bytes 16000000 | tf_op jit(solution)/shard_map/positions_far/pallas_call | solution.py:479
  50.8 0.8 copy-done.13
  51.6 0.9 copy-done.14
  52.5 0.1 collective-permute-start.5
  52.6 1.8 %collective-permute-done.5 = f32[768,128]{1,0:T(8,128)} collective-permute-done((f32[768,128]{1,0:T(8,128)S(1)}, f32[768,128]{1,0:T(8,128)}, u32[]{:S(2)}, u32[]{:S(2)}) %collective-permute-start.5) | collective-permute-done | bytes 393248 | tf_op jit(solution)/shard_map/ppermute | solution.py:593
  54.4 1.0 dynamic-slice_add_fusion
  55.5 3.5 %collective-permute-start.6 = (f32[384,128]{1,0:T(8,128)S(1)}, f32[384,128]{1,0:T(8,128)S(1)}, u32[]{:S(2)}, u32[]{:S(2)}) collective-permute-start(f32[384,128]{1,0:T(8,128)S(1)} %constant_dynamic-slice_fusion.1), channel_id=1, source_target_pairs={{0,4},{2,6},{4,0},{6,2},{8,12},{10,14},{12,8},{14,10},{16,20},{18,... | collective-permute-start | bytes 589832 | tf_op jit(solution)/shard_map/ppermute | solution.py:593
  59.0 5.2 %collective-permute-done.6 = f32[384,128]{1,0:T(8,128)S(1)} collective-permute-done((f32[384,128]{1,0:T(8,128)S(1)}, f32[384,128]{1,0:T(8,128)S(1)}, u32[]{:S(2)}, u32[]{:S(2)}) %collective-permute-start.6) | collective-permute-done | bytes 196640 | tf_op jit(solution)/shard_map/ppermute | solution.py:593
  64.3 0.4 collective-permute-start.7
  64.6 3.2 %cover.1 = (f32[256,512]{1,0:T(8,128)S(1)}, f32[8,128]{1,0:T(8,128)S(1)}) custom-call(s32[19]{0:T(128)S(1)} %concatenate.32.place.refs_0_, s32[6,32]{1,0:T(8,128)S(1)} %fusion.1.info, f32[2,256,256]{2,1,0:T(8,128)S(1)} %copy-done.4), custom_call_target="tpu_custom_call" | custom-call | flops 4000000 | bytes 8000000 | tf_op jit(solution)/shard_map/cover/pallas_call | solution.py:118
  67.9 0.8 collective-permute-start.9
  68.7 0.2 collective-permute-done.7
  69.0 3.6 %collective-permute-start.8 = (f32[200,128]{1,0:T(8,128)S(1)}, f32[200,128]{1,0:T(8,128)S(1)}, u32[]{:S(2)}, u32[]{:S(2)}) collective-permute-start(f32[200,128]{1,0:T(8,128)S(1)} %pad_maximum_fusion.4), channel_id=1, source_target_pairs={{0,8},{2,10},{4,12},{6,14},{8,0},{10,2},{12,4},{14,6},{16,24},{18,... | collective-permute-start | bytes 307208 | tf_op jit(solution)/shard_map/ppermute | solution.py:593
  72.6 10.8 %collective-permute-done.8 = f32[200,128]{1,0:T(8,128)S(1)} collective-permute-done((f32[200,128]{1,0:T(8,128)S(1)}, f32[200,128]{1,0:T(8,128)S(1)}, u32[]{:S(2)}, u32[]{:S(2)}) %collective-permute-start.8) | collective-permute-done | bytes 102432 | tf_op jit(solution)/shard_map/ppermute | solution.py:593
  83.5 3.4 %collective-permute-start.10 = (f32[200,128]{1,0:T(8,128)S(1)}, f32[200,128]{1,0:T(8,128)S(1)}, u32[]{:S(2)}, u32[]{:S(2)}) collective-permute-start(f32[200,128]{1,0:T(8,128)S(1)} %pad_maximum_fusion.5), channel_id=1, source_target_pairs={{0,16},{2,18},{4,20},{6,22},{8,24},{10,26},{12,28},{14,30},{16,0},... | collective-permute-start | bytes 307208 | tf_op jit(solution)/shard_map/ppermute | solution.py:593
  86.9 3.7 %collective-permute-done.10 = f32[200,128]{1,0:T(8,128)S(1)} collective-permute-done((f32[200,128]{1,0:T(8,128)S(1)}, f32[200,128]{1,0:T(8,128)S(1)}, u32[]{:S(2)}, u32[]{:S(2)}) %collective-permute-start.10) | collective-permute-done | bytes 102432 | tf_op jit(solution)/shard_map/ppermute | solution.py:593
  90.7 0.6 copy-done.17
  91.3 0.6 pad_maximum_fusion.6
  92.0 1.2 %collective-permute-start.11 = (f32[200,128]{1,0:T(8,128)}, f32[200,128]{1,0:T(8,128)}, u32[]{:S(2)}, u32[]{:S(2)}) collective-permute-start(f32[200,128]{1,0:T(8,128)} %pad_maximum_fusion.6), channel_id=1, source_target_pairs={{0,1},{1,0},{2,3},{3,2},{4,5},{5,4},{6,7},{7,6},{8,9},{9,8},{10,11... | collective-permute-start | bytes 307208 | tf_op jit(solution)/shard_map/ppermute | solution.py:593
  93.2 1.9 %collective-permute-start.13 = (f32[2,128,640]{2,1,0:T(8,128)}, f32[2,128,640]{2,1,0:T(8,128)}, u32[]{:S(2)}, u32[]{:S(2)}) collective-permute-start(f32[2,128,640]{2,1,0:T(8,128)} %copy-done.13), channel_id=1, source_target_pairs={{0,2},{2,0},{4,6},{6,4},{8,10},{10,8},{12,14},{14,12},{16,18},{18,... | collective-permute-start | bytes 1966088 | tf_op jit(solution)/shard_map/ppermute | solution.py:572
  95.1 1.8 %collective-permute-done.11 = f32[200,128]{1,0:T(8,128)} collective-permute-done((f32[200,128]{1,0:T(8,128)}, f32[200,128]{1,0:T(8,128)}, u32[]{:S(2)}, u32[]{:S(2)}) %collective-permute-start.11) | collective-permute-done | bytes 102432 | tf_op jit(solution)/shard_map/ppermute | solution.py:593
  96.9 0.7 slice_maximum_fusion.1
  97.6 1.0 slice_select_fusion.5
  98.6 5.7 %collective-permute-start.12 = (f32[392,128]{1,0:T(8,128)S(1)}, f32[392,128]{1,0:T(8,128)S(1)}, u32[]{:S(2)}, u32[]{:S(2)}) collective-permute-start(f32[392,128]{1,0:T(8,128)S(1)} %pad_maximum_fusion.2), channel_id=1, source_target_pairs={{0,4},{2,6},{4,0},{6,2},{8,12},{10,14},{12,8},{14,10},{16,20},{18,... | collective-permute-start | bytes 602120 | tf_op jit(solution)/shard_map/ppermute | solution.py:593
  104.3 0.9 slice_select_fusion.3
  105.2 2.8 %collective-permute-done.12 = f32[392,128]{1,0:T(8,128)S(1)} collective-permute-done((f32[392,128]{1,0:T(8,128)S(1)}, f32[392,128]{1,0:T(8,128)S(1)}, u32[]{:S(2)}, u32[]{:S(2)}) %collective-permute-start.12) | collective-permute-done | bytes 200736 | tf_op jit(solution)/shard_map/ppermute | solution.py:593
  108.1 0.1 collective-permute-start.15
  108.2 0.1 collective-permute-start.14
  108.3 8.6 %collective-permute-done.14.refs_7_ = f32[2,256,128]{2,1,0:T(8,128)S(1)} collective-permute-done((f32[2,256,128]{2,1,0:T(8,128)S(1)}, f32[2,256,128]{2,1,0:T(8,128)S(1)}, u32[]{:S(2)}, u32[]{:S(2)}) %collective-permute-start.14) | collective-permute-done | bytes 262176 | tf_op jit(solution)/shard_map/ppermute | solution.py:572
  117.0 3.0 %update.1 = (f32[2,256,512]{2,1,0:T(8,128)}, f32[2,256,256]{2,1,0:T(8,128)}) custom-call(s32[19]{0:T(128)S(1)} %concatenate.32.place.refs_0_, f32[2,256,512]{2,1,0:T(8,128)S(1)} %copy-done.2, f32[2,256,512]{2,1,0:T(8,128)S(1)} %get-tuple-element.31.refs_2_, f32[256,512]{1,0:T(8,128)S(1)} %copy-done.12, f32[8,128]{1,0:T(8,128)S(1)} %slice_maximum_fusion.refs_4_, ...), custom_call_target="tpu_custom_call" | custom-call | tf_op jit(solution)/shard_map/update/pallas_call | solution.py:556
  (52 shorter events, 0.4 us)
Async XLA Ops:
  2.0 1.2 %copy-start = (f32[2,256,512]{2,1,0:T(8,128)S(1)}, f32[2,256,512]{2,1,0:T(8,128)}, u32[]{:S(2)}) copy-start(f32[2,256,512]{2,1,0:T(8,128)} %refs_1_.3) | copy-start | bytes 3145732
  4.8 15.6 %collective-permute-start = (f32[2,136,512]{2,1,0:T(8,128)}, f32[2,136,512]{2,1,0:T(8,128)S(1)}, u32[]{:S(2)}, u32[]{:S(2)}) collective-permute-start(f32[2,136,512]{2,1,0:T(8,128)} %get-tuple-element.23), channel_id=1, source_target_pairs={{0,2},{2,0},{4,6},{6,4},{8,10},{10,8},{12,14},{14,12},{16,18},{18,... | collective-permute-start | bytes 1671176 | tf_op jit(solution)/shard_map/ppermute | solution.py:572
  5.4 29.1 %collective-permute-start.3 = (f32[2,136,512]{2,1,0:T(8,128)S(1)}, f32[2,136,512]{2,1,0:T(8,128)S(1)}, u32[]{:S(2)}, u32[]{:S(2)}) collective-permute-start(f32[2,136,512]{2,1,0:T(8,128)S(1)} %get-tuple-element.29), channel_id=1, source_target_pairs={{2,4},{4,2},{6,8},{8,6},{10,12},{12,10},{14,16},{16,14},{18,20},{2... | collective-permute-start | bytes 1671176 | tf_op jit(solution)/shard_map/ppermute | solution.py:572
  6.0 14.4 %collective-permute-start.1 = (f32[2,264,128]{2,1,0:T(8,128)S(1)}, f32[2,264,128]{2,1,0:T(8,128)S(1)}, u32[]{:S(2)}, u32[]{:S(2)}) collective-permute-start(f32[2,264,128]{2,1,0:T(8,128)S(1)} %get-tuple-element.24), channel_id=1, source_target_pairs={{0,1},{1,0},{2,3},{3,2},{4,5},{5,4},{6,7},{7,6},{8,9},{9,8},{10,11... | collective-permute-start | bytes 811016 | tf_op jit(solution)/shard_map/ppermute | solution.py:572
  8.7 11.8 %collective-permute-start.2 = (f32[2,136,128]{2,1,0:T(8,128)S(1)}, f32[2,136,128]{2,1,0:T(8,128)S(1)}, u32[]{:S(2)}, u32[]{:S(2)}) collective-permute-start(f32[2,136,128]{2,1,0:T(8,128)S(1)} %get-tuple-element.25), channel_id=1, source_target_pairs={{0,3},{2,1},{1,2},{3,0},{4,7},{6,5},{5,6},{7,4},{8,11},{10,9},{9,1... | collective-permute-start | bytes 417800 | tf_op jit(solution)/shard_map/ppermute | solution.py:636
  11.3 22.5 %collective-permute-start.4 = (f32[2,136,128]{2,1,0:T(8,128)S(1)}, f32[2,136,128]{2,1,0:T(8,128)S(1)}, u32[]{:S(2)}, u32[]{:S(2)}) collective-permute-start(f32[2,136,128]{2,1,0:T(8,128)S(1)} %get-tuple-element.30), channel_id=1, source_target_pairs={{2,5},{4,3},{3,4},{5,2},{6,9},{8,7},{7,8},{9,6},{10,13},{12,11},{1... | collective-permute-start | bytes 417800 | tf_op jit(solution)/shard_map/ppermute | solution.py:636
  20.5 1.2 %copy-start.1 = (f32[2,256,512]{2,1,0:T(8,128)S(1)}, f32[2,256,512]{2,1,0:T(8,128)}, u32[]{:S(2)}) copy-start(f32[2,256,512]{2,1,0:T(8,128)} %refs_1_.3) | copy-start | bytes 3145732
  21.7 1.0 copy-start.3
  22.7 1.6 %copy-start.5 = (f32[1,1,8,256,256]{4,3,2,1,0:T(8,128)S(1)}, f32[1,1,8,256,256]{4,3,2,1,0:T(8,128)}, u32[]{:S(2)}) copy-start(f32[1,1,8,256,256]{4,3,2,1,0:T(8,128)} %refs_7_.2) | copy-start | bytes 6291460
  24.3 1.4 %copy-start.7 = (bf16[1536,512]{1,0:T(8,128)(2,1)S(1)}, bf16[1536,512]{1,0:T(8,128)(2,1)}, u32[]{:S(2)}) copy-start(bf16[1536,512]{1,0:T(8,128)(2,1)} %constant.82.clone.refs_8_.refs_9_) | copy-start | bytes 4718596
  25.7 1.1 copy-start.9
  26.9 7.6 %copy-start.4 = (f32[2,256,256]{2,1,0:T(8,128)S(1)}, f32[2,256,256]{2,1,0:T(8,128)}, u32[]{:S(2)}) copy-start(f32[2,256,256]{2,1,0:T(8,128)} %refs_10_.1) | copy-start | bytes 1572868
  26.9 7.6 %copy-start.6 = (f32[1,1,8,256,256]{4,3,2,1,0:T(8,128)S(1)}, f32[1,1,8,256,256]{4,3,2,1,0:T(8,128)}, u32[]{:S(2)}) copy-start(f32[1,1,8,256,256]{4,3,2,1,0:T(8,128)} %refs_7_.2) | copy-start | bytes 6291460
  26.9 7.6 %copy-start.8 = (bf16[1536,512]{1,0:T(8,128)(2,1)S(1)}, bf16[1536,512]{1,0:T(8,128)(2,1)}, u32[]{:S(2)}) copy-start(bf16[1536,512]{1,0:T(8,128)(2,1)} %constant.82.clone.refs_8_.refs_9_) | copy-start | bytes 4718596
  26.9 7.6 %copy-start.10 = (bf16[256,1536]{1,0:T(8,128)(2,1)S(1)}, bf16[256,1536]{1,0:T(8,128)(2,1)}, u32[]{:S(2)}) copy-start(bf16[256,1536]{1,0:T(8,128)(2,1)} %constant.81.clone.refs_7_.refs_8_) | copy-start | bytes 2359300
  33.8 0.7 copy-start.15
  34.5 0.9 copy-start.16
  50.8 0.8 copy-start.13
  51.6 0.9 copy-start.14
  52.5 1.9 %collective-permute-start.5 = (f32[768,128]{1,0:T(8,128)S(1)}, f32[768,128]{1,0:T(8,128)}, u32[]{:S(2)}, u32[]{:S(2)}) collective-permute-start(f32[768,128]{1,0:T(8,128)S(1)} %constant_dynamic-slice_fusion.2), channel_id=1, source_target_pairs={{0,2},{2,0},{4,6},{6,4},{8,10},{10,8},{12,14},{14,12},{16,18},{18,... | collective-permute-start | bytes 1179656 | tf_op jit(solution)/shard_map/ppermute | solution.py:593
  55.5 8.7 %collective-permute-start.6 = (f32[384,128]{1,0:T(8,128)S(1)}, f32[384,128]{1,0:T(8,128)S(1)}, u32[]{:S(2)}, u32[]{:S(2)}) collective-permute-start(f32[384,128]{1,0:T(8,128)S(1)} %constant_dynamic-slice_fusion.1), channel_id=1, source_target_pairs={{0,4},{2,6},{4,0},{6,2},{8,12},{10,14},{12,8},{14,10},{16,20},{18,... | collective-permute-start | bytes 589832 | tf_op jit(solution)/shard_map/ppermute | solution.py:593
  64.3 4.7 %collective-permute-start.7 = (f32[192,128]{1,0:T(8,128)S(1)}, f32[192,128]{1,0:T(8,128)S(1)}, u32[]{:S(2)}, u32[]{:S(2)}) collective-permute-start(f32[192,128]{1,0:T(8,128)S(1)} %constant_dynamic-slice_fusion), channel_id=1, source_target_pairs={{0,1},{1,0},{2,3},{3,2},{4,5},{5,4},{6,7},{7,6},{8,9},{9,8},{10,11... | collective-permute-start | bytes 294920 | tf_op jit(solution)/shard_map/ppermute | solution.py:593
  67.9 15.6 %copy-start.11 = (f32[256,512]{1,0:T(8,128)}, f32[256,512]{1,0:T(8,128)S(1)}, u32[]{:S(2)}) copy-start(f32[256,512]{1,0:T(8,128)S(1)} %get-tuple-element.36.refs_3_) | copy-start | bytes 1572868
  67.9 49.1 %copy-start.2 = (f32[2,256,512]{2,1,0:T(8,128)S(1)}, f32[2,256,512]{2,1,0:T(8,128)}, u32[]{:S(2)}) copy-start(f32[2,256,512]{2,1,0:T(8,128)} %refs_1_.3) | copy-start | bytes 3145732
  67.9 15.6 %collective-permute-start.9 = (f32[2,128,640]{2,1,0:T(8,128)}, f32[2,128,640]{2,1,0:T(8,128)S(1)}, u32[]{:S(2)}, u32[]{:S(2)}) collective-permute-start(f32[2,128,640]{2,1,0:T(8,128)} %copy-done.14), channel_id=1, source_target_pairs={{2,4},{4,2},{6,8},{8,6},{10,12},{12,10},{14,16},{16,14},{18,20},{2... | collective-permute-start | bytes 1966088 | tf_op jit(solution)/shard_map/ppermute | solution.py:572
  69.0 14.5 %collective-permute-start.8 = (f32[200,128]{1,0:T(8,128)S(1)}, f32[200,128]{1,0:T(8,128)S(1)}, u32[]{:S(2)}, u32[]{:S(2)}) collective-permute-start(f32[200,128]{1,0:T(8,128)S(1)} %pad_maximum_fusion.4), channel_id=1, source_target_pairs={{0,8},{2,10},{4,12},{6,14},{8,0},{10,2},{12,4},{14,6},{16,24},{18,... | collective-permute-start | bytes 307208 | tf_op jit(solution)/shard_map/ppermute | solution.py:593
  83.5 7.2 %collective-permute-start.10 = (f32[200,128]{1,0:T(8,128)S(1)}, f32[200,128]{1,0:T(8,128)S(1)}, u32[]{:S(2)}, u32[]{:S(2)}) collective-permute-start(f32[200,128]{1,0:T(8,128)S(1)} %pad_maximum_fusion.5), channel_id=1, source_target_pairs={{0,16},{2,18},{4,20},{6,22},{8,24},{10,26},{12,28},{14,30},{16,0},... | collective-permute-start | bytes 307208 | tf_op jit(solution)/shard_map/ppermute | solution.py:593
  90.7 0.6 copy-start.17
  92.0 5.0 %collective-permute-start.11 = (f32[200,128]{1,0:T(8,128)}, f32[200,128]{1,0:T(8,128)}, u32[]{:S(2)}, u32[]{:S(2)}) collective-permute-start(f32[200,128]{1,0:T(8,128)} %pad_maximum_fusion.6), channel_id=1, source_target_pairs={{0,1},{1,0},{2,3},{3,2},{4,5},{5,4},{6,7},{7,6},{8,9},{9,8},{10,11... | collective-permute-start | bytes 307208 | tf_op jit(solution)/shard_map/ppermute | solution.py:593
  93.2 11.1 %collective-permute-start.13 = (f32[2,128,640]{2,1,0:T(8,128)}, f32[2,128,640]{2,1,0:T(8,128)}, u32[]{:S(2)}, u32[]{:S(2)}) collective-permute-start(f32[2,128,640]{2,1,0:T(8,128)} %copy-done.13), channel_id=1, source_target_pairs={{0,2},{2,0},{4,6},{6,4},{8,10},{10,8},{12,14},{14,12},{16,18},{18,... | collective-permute-start | bytes 1966088 | tf_op jit(solution)/shard_map/ppermute | solution.py:572
  95.1 21.8 %copy-start.12 = (f32[256,512]{1,0:T(8,128)S(1)}, f32[256,512]{1,0:T(8,128)}, u32[]{:S(2)}) copy-start(f32[256,512]{1,0:T(8,128)} %copy-done.11) | copy-start | bytes 1572868
  98.6 9.4 %collective-permute-start.12 = (f32[392,128]{1,0:T(8,128)S(1)}, f32[392,128]{1,0:T(8,128)S(1)}, u32[]{:S(2)}, u32[]{:S(2)}) collective-permute-start(f32[392,128]{1,0:T(8,128)S(1)} %pad_maximum_fusion.2), channel_id=1, source_target_pairs={{0,4},{2,6},{4,0},{6,2},{8,12},{10,14},{12,8},{14,10},{16,20},{18,... | collective-permute-start | bytes 602120 | tf_op jit(solution)/shard_map/ppermute | solution.py:593
  108.1 8.9 %collective-permute-start.15 = (f32[776,128]{1,0:T(8,128)S(1)}, f32[776,128]{1,0:T(8,128)S(1)}, u32[]{:S(2)}, u32[]{:S(2)}) collective-permute-start(f32[776,128]{1,0:T(8,128)S(1)} %pad_maximum_fusion), channel_id=1, source_target_pairs={{0,2},{2,0},{4,6},{6,4},{8,10},{10,8},{12,14},{14,12},{16,18},{18,... | collective-permute-start | bytes 1191944 | tf_op jit(solution)/shard_map/ppermute | solution.py:593
  108.2 8.8 %collective-permute-start.14 = (f32[2,256,128]{2,1,0:T(8,128)S(1)}, f32[2,256,128]{2,1,0:T(8,128)S(1)}, u32[]{:S(2)}, u32[]{:S(2)}) collective-permute-start(f32[2,256,128]{2,1,0:T(8,128)S(1)} %maximum_add_fusion), channel_id=1, source_target_pairs={{0,1},{1,0},{2,3},{3,2},{4,5},{5,4},{6,7},{7,6},{8,9},{9,8},{10,11... | collective-permute-start | bytes 786440 | tf_op jit(solution)/shard_map/ppermute | solution.py:572

commit v6 on v5

--- a/solution.py
+++ b/solution.py
@@ -8,7 +8,7 @@
 from jax import lax
 from jax.experimental import pallas as pl
 from jax.experimental.pallas import tpu as pltpu
-from jax.sharding import PartitionSpec as P
+from jax.sharding import Mesh, PartitionSpec as P
 
 H = 128
 LANES = 128
@@ -187,25 +187,17 @@
     return out[0], out[1], *[list(out[2 + i * sides : 2 + (i + 1) * sides]) for i in range(3)]
 
 
-def positions_kernel(sides, last, *refs):
-    place = refs[0]
-    if last:
-        ext_in, grad_in, sums_in, far_side = refs[1:5]
-        far_corners = refs[5 : 5 + sides]
-        probe_in, measured, left_in, right_in = refs[5 + sides : 9 + sides]
-        middle, near_rim, far_rim, info = refs[9 + sides : 13 + sides]
-        side_out = refs[13 + sides : 13 + 2 * sides]
-        probe_sums, ext, grad = refs[13 + 2 * sides : 16 + 2 * sides]
-        scratch = refs[16 + 2 * sides :]
-    else:
-        tile, near = refs[1:3]
-        side_in, near_corners = refs[3 : 3 + sides], refs[3 + sides : 3 + 2 * sides]
-        probe_in, measured, left_in, right_in = refs[3 + 2 * sides : 7 + 2 * sides]
-        info, ext, grad, probe_sums = refs[7 + 2 * sides : 11 + 2 * sides]
-        scratch = refs[11 + 2 * sides :]
-    left, right, levels, order, probe = scratch[:5]
-    table_sems, level_sems, ext_sems = scratch[5:8]
-    scratch = scratch[8:]
+def positions_kernel(sides, *refs):
+    place, tile, near, far_side = refs[:4]
+    side_in, near_corners, far_corners = [refs[4 + i * sides : 4 + (i + 1) * sides] for i in range(3)]
+    probe_in, measured, left_in, right_in = refs[4 + 3 * sides : 8 + 3 * sides]
+    middle, near_rim, far_rim, info = refs[8 + 3 * sides : 12 + 3 * sides]
+    side_out = refs[12 + 3 * sides : 12 + 4 * sides]
+    probe_sums, ext, grad = refs[12 + 4 * sides : 15 + 4 * sides]
+    scratch = refs[15 + 4 * sides :]
+    left, right, levels, probe = scratch[:4]
+    table_sems, level_sems, ext_sems = scratch[4:7]
+    scratch = scratch[7:]
     patches, exits, stacks, wides, fields = [scratch[i * WAYS : (i + 1) * WAYS] for i in range(5)]
 
     pr = probe_in.shape[1]
@@ -229,28 +221,20 @@
     for ch in range(2):
         for b in range(own_blocks):
             at, cut = ch * blocks + 1 + b, pl.ds(b * LANES, LANES)
-            if last:
-                fetch(far_side.at[ch, pl.ds(0, H), cut], ext.at[at, far_rows, :])
-            else:
-                fetch(tile.at[ch, :, cut], ext.at[at, own, :])
-                fetch(near.at[ch, pl.ds(0, H), cut], ext.at[at, near_rows, :])
+            fetch(tile.at[ch, :, cut], ext.at[at, own, :])
+            fetch(near.at[ch, pl.ds(0, H), cut], ext.at[at, near_rows, :])
+            fetch(far_side.at[ch, pl.ds(0, H), cut], ext.at[at, far_rows, :])
         for s in range(sides):
             at = ch * blocks + side_blocks[s]
-            if last:
-                fetch(far_corners[s].at[ch, pl.ds(0, H), :], ext.at[at, far_rows, :])
-            else:
-                fetch(side_in[s].at[ch, pl.ds(0, tile_rows), :], ext.at[at, own, :])
-                fetch(near_corners[s].at[ch, pl.ds(0, H), :], ext.at[at, near_rows, :])
+            fetch(side_in[s].at[ch, pl.ds(0, tile_rows), :], ext.at[at, own, :])
+            fetch(near_corners[s].at[ch, pl.ds(0, H), :], ext.at[at, near_rows, :])
+            fetch(far_corners[s].at[ch, pl.ds(0, H), :], ext.at[at, far_rows, :])
     for s in range(sides):
-        if last:
-            fetch(far_corners[s].at[0, pl.ds(H, INFO), :], info.at[1 + s])
-        else:
-            fetch(side_in[s].at[0, pl.ds(tile_rows, INFO), :], info.at[s])
-            fetch(near_corners[s].at[0, pl.ds(H, INFO), :], info.at[sides + 1 + s])
-    if last:
-        fetch(far_side.at[0, pl.ds(H, INFO), pl.ds(0, LANES)], info.at[0])
-    else:
-        fetch(near.at[0, pl.ds(H, INFO), pl.ds(0, LANES)], info.at[sides])
+        fetch(side_in[s].at[0, pl.ds(tile_rows, INFO), :], info.at[s])
+        fetch(near_corners[s].at[0, pl.ds(H, INFO), :], info.at[sides + 1 + s])
+        fetch(far_corners[s].at[0, pl.ds(H, INFO), :], info.at[2 * sides + 2 + s])
+    fetch(near.at[0, pl.ds(H, INFO), pl.ds(0, LANES)], info.at[sides])
+    fetch(far_side.at[0, pl.ds(H, INFO), pl.ds(0, LANES)], info.at[2 * sides + 1])
     tables = [
         pltpu.make_async_copy(left_in, left, table_sems.at[0]),
         pltpu.make_async_copy(right_in, right, table_sems.at[1]),
@@ -261,48 +245,19 @@
 
     live_slots = place[COUNT]
 
-    def touches(k):
-        row = place[ROWS + k]
-        return jnp.where(even, row < H, row > tile_rows - H)
-
-    def pick(wanted):
-        def step(k, n):
-            @pl.when(touches(k) == wanted)
-            def _():
-                order[n] = k
-
-            return n + jnp.where(touches(k) == wanted, 1, 0)
-
-        return step
-
-    near_slots = lax.fori_loop(0, live_slots, pick(False), 0)
-    lax.fori_loop(0, live_slots, pick(True), near_slots)
-    border = near_slots // WAYS * WAYS
-    begin, end = (border, live_slots) if last else (0, border)
-
     def level_copy(i):
-        return pltpu.make_async_copy(measured.at[0, 0, order[i]], levels.at[i], level_sems.at[i])
+        return pltpu.make_async_copy(measured.at[0, 0, i], levels.at[i], level_sems.at[i])
 
     def start_level(i, carry):
         level_copy(i).start()
         return carry
 
-    lax.fori_loop(begin, end, start_level, 0)
-    if last:
-        for at in range(2 * blocks):
-            ext[at, own, :] = ext_in[at, own, :]
-            ext[at, near_rows, :] = ext_in[at, near_rows, :]
-        if sides == 1:
-            for ch in range(2):
-                ext[ch * blocks + blocks - 1 - side_blocks[0], far_rows, :] = jnp.zeros((H, LANES), F32)
-        grad[...] = grad_in[...]
-        probe_sums[...] = sums_in[...]
-    else:
-        if sides == 1:
-            for ch in range(2):
-                ext[ch * blocks + blocks - 1 - side_blocks[0]] = jnp.zeros((ext_rows, LANES), F32)
-        grad[...] = jnp.zeros_like(grad)
-        probe_sums[...] = jnp.zeros_like(probe_sums)
+    lax.fori_loop(0, live_slots, start_level, 0)
+    if sides == 1:
+        for ch in range(2):
+            ext[ch * blocks + blocks - 1 - side_blocks[0]] = jnp.zeros((ext_rows, LANES), F32)
+    grad[...] = jnp.zeros_like(grad)
+    probe_sums[...] = jnp.zeros_like(probe_sums)
     for copy in copies + tables:
         copy.wait()
     lanes = lax.broadcasted_iota(jnp.int32, (CHUNK, LANES), 1)
@@ -333,7 +288,7 @@
         fields[w][...] = jnp.dot(stack, right[...], preferred_element_type=F32)
 
     def load(w, k):
-        row, col = place[ROWS + order[k]], place[COLS + order[k]]
+        row, col = place[ROWS + k], place[COLS + k]
         shift, block = col & (LANES - 1), col >> 7
         back = (LANES - shift) & (LANES - 1)
         keep = lanes < LANES - shift
@@ -367,7 +322,7 @@
             put(stacks[w], -(imag * factor), 1, q, 0)
 
     def finish(w, k, live):
-        row, col = place[ROWS + order[k]], place[COLS + order[k]]
+        row, col = place[ROWS + k], place[COLS + k]
         shift, block = col & (LANES - 1), col >> 7
         low = lanes < shift
         zero = jnp.zeros((CHUNK, LANES), F32)
@@ -399,12 +354,12 @@
                 grad[at + pieces, here, :] += jnp.where(low, turned[ch][-1], zero)
 
     def visit(i, carry):
-        first = begin + i * WAYS
-        slots = [jnp.minimum(first + w, end - 1) for w in range(WAYS)]
-        lives = [None] + [jnp.where(first + w < end, 1.0, 0.0) for w in range(1, WAYS)]
+        first = i * WAYS
+        slots = [jnp.minimum(first + w, live_slots - 1) for w in range(WAYS)]
+        lives = [None] + [jnp.where(first + w < live_slots, 1.0, 0.0) for w in range(1, WAYS)]
         for w in range(WAYS):
 
-            @pl.when(first + w < end)
+            @pl.when(first + w < live_slots)
             def _():
                 level_copy(slots[w]).wait()
 
@@ -422,9 +377,7 @@
             finish(w, slots[w], lives[w])
         return carry
 
-    lax.fori_loop(0, (end - begin + WAYS - 1) // WAYS, visit, 0)
-    if not last:
-        return
+    lax.fori_loop(0, (live_slots + WAYS - 1) // WAYS, visit, 0)
     for ch in range(2):
         for b in range(own_blocks):
             at, cut = ch * blocks + 1 + b, slice(b * LANES, (b + 1) * LANES)
@@ -439,7 +392,7 @@
             far_rim[ch, :, cut] = grad[at, far_rows, :]
 
 
-def positions_calls(place, tile, near, far_side, side_in, near_corners, far_corners, probe, measured):
+def positions_call(place, tile, near, far_side, side_in, near_corners, far_corners, probe, measured):
     pr = probe.shape[1]
     sides = len(side_in)
     tile_rows, tile_cols = tile.shape[1:]
@@ -448,54 +401,39 @@
     left, right = (jnp.asarray(table) for table in dft_tables(pr))
     shape = lambda *dims: jax.ShapeDtypeStruct(dims, F32)
     slots = measured.shape[2]
-    sums = shape(pr // LANES, 3, pr, LANES)
-    field = shape(2 * blocks, ext_rows, LANES)
     rim = shape(2, H, tile_cols + sides * LANES)
-    params = pltpu.CompilerParams(vmem_limit_bytes=34 << 20)
-    scratch = [
-        pltpu.VMEM(left.shape, BF),
-        pltpu.VMEM(right.shape, BF),
-        pltpu.VMEM((slots, pr, pr), F32),
-        pltpu.SMEM((slots,), jnp.int32),
-        pltpu.VMEM(probe.shape, F32),
-        pltpu.SemaphoreType.DMA((3,)),
-        pltpu.SemaphoreType.DMA((slots,)),
-        pltpu.SemaphoreType.DMA((4 * blocks + 2 * sides + 1,)),
-        *[pltpu.VMEM((2, pr, pr), F32)] * (2 * WAYS),
-        *[pltpu.VMEM((4 * pr, 2 * pr), BF)] * WAYS,
-        *[pltpu.VMEM((pr, 4 * pr), BF)] * WAYS,
-        *[pltpu.VMEM((pr, 2 * pr), F32)] * WAYS,
-    ]
-    near_info, ext, grad, sums_so_far = pl.pallas_call(
-        functools.partial(positions_kernel, sides, False),
-        out_shape=(shape(2 * sides + 1, INFO, LANES), field, field, sums),
-        in_specs=[SMEM, HBM] + [ANY] * (1 + 2 * sides) + [HBM] * 4,
-        out_specs=(VMEM,) * 4,
-        scratch_shapes=scratch,
-        compiler_params=params,
-        cost_estimate=pl.CostEstimate(flops=1, bytes_accessed=1, transcendentals=0),
-        name="positions_near",
-    )(place, tile, near, *side_in, *near_corners, probe, measured, left, right)
-    middle, near_rim, far_rim, far_info, *rest = pl.pallas_call(
-        functools.partial(positions_kernel, sides, True),
+    middle, near_rim, far_rim, info, *rest = pl.pallas_call(
+        functools.partial(positions_kernel, sides),
         out_shape=(
             shape(2, tile_rows, tile_cols),
             rim,
             rim,
-            shape(sides + 1, INFO, LANES),
+            shape(3 * sides + 2, INFO, LANES),
             *[shape(2, tile_rows, LANES)] * sides,
-            sums,
+            shape(pr // LANES, 3, pr, LANES),
         ),
-        in_specs=[SMEM] + [VMEM] * 3 + [ANY] * (1 + sides) + [HBM] * 4,
+        in_specs=[SMEM, HBM] + [ANY] * (2 + 3 * sides) + [HBM] * 4,
         out_specs=(VMEM,) * (5 + sides),
-        scratch_shapes=[pltpu.VMEM(field.shape, F32)] * 2 + scratch,
-        compiler_params=params,
+        scratch_shapes=[
+            *[pltpu.VMEM((2 * blocks, ext_rows, LANES), F32)] * 2,
+            pltpu.VMEM(left.shape, BF),
+            pltpu.VMEM(right.shape, BF),
+            pltpu.VMEM((slots, pr, pr), F32),
+            pltpu.VMEM(probe.shape, F32),
+            pltpu.SemaphoreType.DMA((3,)),
+            pltpu.SemaphoreType.DMA((slots,)),
+            pltpu.SemaphoreType.DMA((6 * blocks + 3 * sides + 2,)),
+            *[pltpu.VMEM((2, pr, pr), F32)] * (2 * WAYS),
+            *[pltpu.VMEM((4 * pr, 2 * pr), BF)] * WAYS,
+            *[pltpu.VMEM((pr, 4 * pr), BF)] * WAYS,
+            *[pltpu.VMEM((pr, 2 * pr), F32)] * WAYS,
+        ],
+        compiler_params=pltpu.CompilerParams(vmem_limit_bytes=52 << 20),
         cost_estimate=pl.CostEstimate(
-            flops=slots * 48 * pr * pr * pr, bytes_accessed=16_000_000, transcendentals=slots * pr * pr
+            flops=slots * 96 * pr * pr * pr, bytes_accessed=16_000_000, transcendentals=slots * 2 * pr * pr
         ),
-        name="positions_far",
-    )(place, ext, grad, sums_so_far, far_side, *far_corners, probe, measured, left, right)
-    info = jnp.concatenate([near_info, far_info], axis=0)
+        name="positions",
+    )(place, tile, near, far_side, *side_in, *near_corners, *far_corners, probe, measured, left, right)
     return middle, near_rim, far_rim, rest[:sides], rest[sides], info
 
 
@@ -564,6 +502,10 @@
     )(place, tile, middle, cover, peak, near, far_side, *side_in, own_terms, other_terms, probe)
 
 
+WIDE = ("rest", "core")
+CHIPS = ("rest", "narrow")
+
+
 def swap(x, axis, first):
     size = lax.axis_size(axis)
     pairs = []
@@ -583,46 +525,8 @@
     return [shifted(pieces[1], "narrow", 1), shifted(pieces[0], "narrow", -1)]
 
 
-def bits_of(axis):
-    size = lax.axis_size(axis)
-    return [1 << b for b in range(size.bit_length() - 1)]
-
-
-def partner(x, axis, bit):
-    size = lax.axis_size(axis)
-    return lax.ppermute(x, axis, [(i, i ^ bit) for i in range(size)])
-
-
-def half_of(x, which):
-    rows = x.shape[0] // 2
-    return lax.dynamic_slice_in_dim(x, which * rows, rows, axis=0)
-
-
-def bit_state(axis, bit):
-    return (lax.axis_index(axis) // bit) % 2
-
-
-def halve(terms, axis, bit):
-    mine = bit_state(axis, bit)
-    return half_of(terms, mine) + partner(half_of(terms, 1 - mine), axis, bit)
-
-
-def double(terms, peak, axis, bit):
-    got = partner(jnp.concatenate([terms, peak], axis=0), axis, bit)
-    rows = terms.shape[0]
-    return terms + got[:rows], jnp.maximum(peak, got[rows:])
-
-
-def gather(terms, peak, axis, bit):
-    first = bit_state(axis, bit) == 0
-    got = partner(jnp.concatenate([terms, peak], axis=0), axis, bit)
-    rows = terms.shape[0]
-    other, peak = got[:rows], jnp.maximum(peak, got[rows:])
-    return jnp.concatenate([jnp.where(first, terms, other), jnp.where(first, other, terms)], axis=0), peak
-
-
 def to_corners(bands, first):
-    wide, narrow = lax.axis_size("wide"), lax.axis_size("narrow")
+    wide, narrow = lax.axis_size(WIDE), lax.axis_size("narrow")
     steps = [0] if len(bands) == 1 else [-1, 1]
     got = []
     for s, step in enumerate(steps):
@@ -633,8 +537,17 @@
                 if 0 <= m < narrow:
                     pairs += [(i * narrow + n, (i + 1) * narrow + m), ((i + 1) * narrow + n, i * narrow + m)]
         band = bands[0] if step == 0 else bands[1 - s]
-        got.append(lax.ppermute(band, ("wide", "narrow"), pairs))
+        got.append(lax.ppermute(band, (*WIDE, "narrow"), pairs))
     return got
+
+
+def half_of(x, which):
+    rows = x.shape[0] // 2
+    return lax.dynamic_slice_in_dim(x, which * rows, rows, axis=0)
+
+
+def chip_exchange(chunks):
+    return lax.all_to_all(chunks.reshape(-1, LANES), CHIPS, 0, 0, tiled=True).reshape(chunks.shape)
 
 
 def after(x, *others):
@@ -642,7 +555,7 @@
 
 
 def body(tile, probe, measured, rows, cols, counts):
-    wide, narrow = lax.axis_index("wide"), lax.axis_index("narrow")
+    wide, narrow = lax.axis_index(WIDE), lax.axis_index("narrow")
     sides = 1 if lax.axis_size("narrow") == 2 else 2
     tile_rows, tile_cols = tile.shape[1:]
     even = wide % 2 == 0
@@ -651,33 +564,32 @@
     )
 
     far_band, near_band, edges, far_ends, near_ends = pack_call(place, tile, sides)
-    far_side = swap(far_band, "wide", 1)
+    far_side = swap(far_band, WIDE, 1)
     far_corners = to_corners(far_ends, 1)
     side_in = to_sides(edges)
     near_corners = to_corners(near_ends, 0)
-    near = swap(near_band, "wide", 0)
-
-    middle, near_rim, far_rim, side_rims, probe_sums, got_info = positions_calls(
+    near = swap(near_band, "core", 0)
+
+    middle, near_rim, far_rim, side_rims, probe_sums, got_info = positions_call(
         place, tile, near, far_side, side_in, near_corners, far_corners, probe, measured
     )
     own_info = edges[0][:1, tile_rows:]
 
+    core = lax.axis_index("core")
     terms = probe_sums.reshape(-1, LANES)
-    wide_bits, narrow_bits = bits_of("wide"), bits_of("narrow")
-    terms = halve(terms, "wide", wide_bits[0])
-    near_got = swap(after(near_rim, terms), "wide", 0)
+    terms = half_of(terms, core) + swap(half_of(terms, 1 - core), "core", 0)
+    near_got = swap(after(near_rim, terms), "core", 0)
+    far_got = swap(after(far_rim, terms), WIDE, 1)
     info = jnp.concatenate([own_info, got_info], axis=0)[:, 0, :32].astype(jnp.int32)
     cover, peak = cover_call(place, after(info, terms), probe, tile_rows, tile_cols, sides)
-    terms = halve(terms, "wide", wide_bits[1])
-    far_got = swap(after(far_rim, terms), "wide", 1)
-    for bit in narrow_bits:
-        terms = halve(terms, "narrow", bit)
-    for bit in wide_bits[2:]:
-        if bit == wide_bits[-1]:
-            terms = after(terms, far_got)
-        terms, peak = double(terms, peak, "wide", bit)
-    for bit in narrow_bits[::-1]:
-        terms, peak = gather(terms, peak, "narrow", bit)
+    chips = lax.axis_size(CHIPS)
+    got = chip_exchange(terms.reshape(chips, -1, LANES))
+    chunk = jnp.sum(got, axis=0)
+    rows_each = chunk.shape[0]
+    chunk = after(jnp.concatenate([chunk, peak], axis=0), far_got, near_got)
+    got = chip_exchange(jnp.broadcast_to(chunk, (chips, *chunk.shape)))
+    terms = got[:, :rows_each].reshape(-1, LANES)
+    peak = jnp.max(got[:, rows_each:], axis=0)
 
     def with_rims(piece, s):
         cut = slice(tile_cols + s * LANES, tile_cols + (s + 1) * LANES)
@@ -686,26 +598,27 @@
         return piece + jnp.concatenate([above, below], axis=1)
 
     side_got = to_sides([with_rims(piece, s) for s, piece in enumerate(side_rims)])
-    terms, peak = gather(terms, peak, "wide", wide_bits[1])
-    other_terms = partner(jnp.concatenate([terms, peak], axis=0), "wide", wide_bits[0])
+    other_terms = swap(after(jnp.concatenate([terms, peak], axis=0), *side_got), "core", 0)
     return update_call(
         place, tile, middle, cover, peak, near_got, far_got, side_got, terms, other_terms, probe
     )
 
 
 def solution(mesh):
+    wide, narrow = mesh.devices.shape
+    fine = Mesh(mesh.devices.reshape(wide // 2, 2, narrow), ("rest", "core", "narrow"))
     placed = (
-        P(None, "wide", "narrow"),
+        P(None, WIDE, "narrow"),
         P(),
-        P("wide", "narrow", None, None, None),
-        P("wide", "narrow", None),
-        P("wide", "narrow", None),
-        P("wide", "narrow"),
+        P(WIDE, "narrow", None, None, None),
+        P(WIDE, "narrow", None),
+        P(WIDE, "narrow", None),
+        P(WIDE, "narrow"),
     )
     return jax.shard_map(
         body,
-        mesh=mesh,
+        mesh=fine,
         in_specs=placed,
-        out_specs=(P(None, "wide", "narrow"), P()),
+        out_specs=(P(None, WIDE, "narrow"), P()),
         check_vma=False,
     )

time: 120 us -> 110 us (0.917); the launches traced: 120 us -> 108 us
  waiting for transfers between devices: 43.5 us -> 27.6 us
  starting transfers between devices: 28 us -> 36.8 us
  local copies, waits for them, and re-layouts: 12.3 us -> 8.58 us
    ppermute x10 -> x2, waiting for transfers between devices: 34.8 us -> 8.49 us  [to_corners(): got.append(lax.ppermute(band, (*WIDE, 'narrow'), pairs))]
    all_to_all x0 -> x2, starting transfers between devices: none -> 23.7 us  [chip_exchange(): lax.all_to_all(chunks.reshape(-1, LANES), CHIPS, 0, 0, tiled=True)]
    ppermute x10 -> x2, starting transfers between devices: 21.3 us -> 3.31 us  [to_corners(): got.append(lax.ppermute(band, (*WIDE, 'narrow'), pairs))]
    all_to_all x0 -> x2, waiting for transfers between devices: none -> 15.6 us  [chip_exchange(): lax.all_to_all(chunks.reshape(-1, LANES), CHIPS, 0, 0, tiled=True)]
    unnamed x36 -> x16, local copies, waits for them, and re-layouts: 11.5 us -> 4.91 us
    ppermute x6 -> x8, waiting for transfers between devices: 8.66 us -> 3.44 us  [swap(): return lax.ppermute(x, axis, pairs)]
    ppermute x6 -> x8, starting transfers between devices: 6.66 us -> 9.82 us  [swap(): return lax.ppermute(x, axis, pairs)]
    pallas_call x2 -> x1, Pallas kernels: 22.3 us -> 22.7 us  [positions_call(): pl.pallas_call(functools.partial(positions_kernel, sides), out_shape=(sha...]
  transfers between devices with their start and end apart: 16 -> 12, of which waited for: 9 -> 5; matrix products, arithmetic and copies ran while one was open for 2% -> 3% of each run, Pallas kernels for 8% -> 3%
where the time goes in v6:
time: 110 us; the launch traced here: 108 us
  starting transfers between devices  36.8 us (33%)
  Pallas kernels  29.3 us (27%)
  waiting for transfers between devices  27.6 us (25%)
  local copies, waits for them, and re-layouts  8.58 us (8%)
  other arithmetic  4.43 us (4%)
  between operations  1.51 us (1%)
    all_to_all x2, starting transfers between devices, chip_exchange(): lax.all_to_all(chunks.reshape(-1, LANES), CHIPS, 0, 0, tiled=True)  23.7 us
    pallas_call x1, Pallas kernels, positions_call(): pl.pallas_call(functools.partial(positions_kernel, sides), out_shape=(sha...  22.7 us
    all_to_all x2, waiting for transfers between devices, chip_exchange(): lax.all_to_all(chunks.reshape(-1, LANES), CHIPS, 0, 0, tiled=True)  15.6 us
    ppermute x8, starting transfers between devices, swap(): return lax.ppermute(x, axis, pairs)  9.82 us
    ppermute x2, waiting for transfers between devices, to_corners(): got.append(lax.ppermute(band, (*WIDE, 'narrow'), pairs))  8.49 us
    unnamed x16, local copies, waits for them, and re-layouts  4.91 us
    ppermute x8, waiting for transfers between devices, swap(): return lax.ppermute(x, axis, pairs)  3.44 us
    ppermute x2, starting transfers between devices, to_corners(): got.append(lax.ppermute(band, (*WIDE, 'narrow'), pairs))  3.31 us
  transfers between devices with their start and end apart: 12, of which 5 were waited for; matrix products, arithmetic and copies ran while one was open for 3% of the time, Pallas kernels for 3%

profile of v6, /device:TPU:0, one launch (start us, length us, event | category | flops | bytes accessed | tf_op | source)
XLA Modules:
  0.0 108.2 jit_solution(18200863629960222676)
XLA Ops:
  1.3 0.7 concatenate.15.place.refs_0_
  2.0 1.2 %copy-done = f32[2,256,512]{2,1,0:T(8,128)S(1)} copy-done((f32[2,256,512]{2,1,0:T(8,128)S(1)}, f32[2,256,512]{2,1,0:T(8,128)}, u32[]{:S(2)}) %copy-start) | copy-done | bytes 1048600
  3.3 0.8 pack.1
  4.0 0.5 collective-permute-start
  4.6 0.7 collective-permute-start.1
  5.2 2.6 %collective-permute-start.2 = (f32[2,264,128]{2,1,0:T(8,128)S(1)}, f32[2,264,128]{2,1,0:T(8,128)S(1)}, u32[]{:S(2)}, u32[]{:S(2)}) collective-permute-start(f32[2,264,128]{2,1,0:T(8,128)S(1)} %get-tuple-element.22), channel_id=1, source_target_pairs={{0,1},{1,0},{2,3},{3,2},{4,5},{5,4},{6,7},{7,6},{8,9},{9,8},{10,11... | collective-permute-start | bytes 811016 | tf_op jit(solution)/shard_map/ppermute | solution.py:514
  7.9 2.6 %collective-permute-start.3 = (f32[2,136,128]{2,1,0:T(8,128)S(1)}, f32[2,136,128]{2,1,0:T(8,128)S(1)}, u32[]{:S(2)}, u32[]{:S(2)}) collective-permute-start(f32[2,136,128]{2,1,0:T(8,128)S(1)} %get-tuple-element.23), channel_id=1, source_target_pairs={{0,3},{2,1},{1,2},{3,0},{4,7},{6,5},{5,6},{7,4},{8,11},{10,9},{9,1... | collective-permute-start | bytes 417800 | tf_op jit(solution)/shard_map/ppermute | solution.py:540
  10.5 0.7 collective-permute-start.4
  11.2 8.5 %collective-permute-done.3.refs_5_ = f32[2,136,128]{2,1,0:T(8,128)S(1)} collective-permute-done((f32[2,136,128]{2,1,0:T(8,128)S(1)}, f32[2,136,128]{2,1,0:T(8,128)S(1)}, u32[]{:S(2)}, u32[]{:S(2)}) %collective-permute-start.3) | collective-permute-done | bytes 139296 | tf_op jit(solution)/shard_map/ppermute | solution.py:540
  19.7 0.0 collective-permute-done.4.refs_6_
  19.7 0.0 collective-permute-done.2.refs_4_
  19.7 0.0 collective-permute-done.refs_2_
  19.7 0.0 collective-permute-done.1.refs_3_
  19.7 0.0 copy-start.7
  19.7 0.8 copy-done.7
  20.5 1.0 copy-done.2
  21.5 22.7 %positions.1 = (f32[2,256,512]{2,1,0:T(8,128)}, f32[2,128,640]{2,1,0:T(8,128)}, f32[2,128,640]{2,1,0:T(8,128)}, f32[5,8,128]{2,1,0:T(8,128)S(1)}, f32[2,256,128]...) custom-call(s32[19]{0:T(128)S(1)} %concatenate.15.place.refs_0_, f32[2,256,512]{2,1,0:T(8,128)} %refs_1_.3, ...), custom_call_target="tpu_custom_call" | custom-call | flops 12884901888 | bytes 16000000 | tf_op jit(solution)/shard_map/positions/pallas_call | solution.py:405
  44.3 0.0 copy-start.3
  44.3 1.1 %constant_dynamic-slice_fusion = f32[768,128]{1,0:T(8,128)S(1)} fusion(f32[1536,128]{1,0:T(8,128)} %bitcast.14, s32[]{:T(128)S(6)} %select_n.26), kind=kLoop, calls=%fused_computation.10 | loop fusion | bytes 786436 | tf_op jit(solution)/shard_map/dynamic_slice | solution.py:546
  45.4 0.1 collective-permute-start.5
  45.4 1.7 %collective-permute-done.5 = f32[768,128]{1,0:T(8,128)S(1)} collective-permute-done((f32[768,128]{1,0:T(8,128)S(1)}, f32[768,128]{1,0:T(8,128)S(1)}, u32[]{:S(2)}, u32[]{:S(2)}) %collective-permute-start.5) | collective-permute-done | bytes 393248 | tf_op jit(solution)/shard_map/ppermute | solution.py:514
  47.1 1.8 %dynamic-slice_add_fusion = f32[768,128]{1,0:T(8,128)} fusion(f32[768,128]{1,0:T(8,128)S(1)} %collective-permute-done.5, f32[1536,128]{1,0:T(8,128)} %bitcast.15, s32[]{:T(128)S(6)} %select_n.25), kind=kLoop, calls=%fused_computation.1 | loop fusion | flops 98304 | bytes 1179652 | tf_op jit(solution)/shard_map/add | solution.py:580
  49.0 9.8 %all-to-all-start = ((f32[16,48,128]{2,1,0:T(8,128)}), f32[16,48,128]{2,1,0:T(8,128)S(1)}, u32[]{:S(2)}, u32[]{:S(2)}) async-start(f32[16,48,128]{2,1,0:T(8,128)} %bitcast.8), calls=%async_computation | async-start | bytes 786432 | tf_op jit(solution)/shard_map/all_to_all | solution.py:550
  58.8 0.7 collective-permute-start.6
  59.5 3.3 %collective-permute-start.7 = (f32[2,128,640]{2,1,0:T(8,128)}, f32[2,128,640]{2,1,0:T(8,128)}, u32[]{:S(2)}, u32[]{:S(2)}) collective-permute-start(f32[2,128,640]{2,1,0:T(8,128)} %get-tuple-element.34), channel_id=1, source_target_pairs={{0,2},{2,0},{1,3},{3,1},{4,6},{6,4},{5,7},{7,5},{8,10},{10,8},{9,1... | collective-permute-start | bytes 1966088 | tf_op jit(solution)/shard_map/ppermute | solution.py:514
  62.8 0.0 copy-done.3
  62.9 2.8 %cover.1 = (f32[256,512]{1,0:T(8,128)S(1)}, f32[8,128]{1,0:T(8,128)S(1)}) custom-call(s32[19]{0:T(128)S(1)} %concatenate.15.place.refs_0_, s32[6,32]{1,0:T(8,128)S(1)} %fusion.1.info, f32[2,256,256]{2,1,0:T(8,128)S(1)} %copy-done.3), custom_call_target="tpu_custom_call" | custom-call | flops 4000000 | bytes 8000000 | tf_op jit(solution)/shard_map/cover/pallas_call | solution.py:118
  65.6 0.0 copy-start.5
  65.6 0.8 copy-done.5
  66.4 5.5 %all-to-all-done = f32[16,48,128]{2,1,0:T(8,128)S(1)} async-done(((f32[16,48,128]{2,1,0:T(8,128)}), f32[16,48,128]{2,1,0:T(8,128)S(1)}, u32[]{:S(2)}, u32[]{:S(2)}) %all-to-all-start) | async-done | bytes 393248 | tf_op jit(solution)/shard_map/all_to_all | solution.py:550
  72.0 0.0 copy-start.1
  72.0 0.0 copy-start.4
  72.0 0.0 collective-permute-done.6.refs_6_
  72.0 0.0 collective-permute-done.7.refs_5_
  72.0 0.8 broadcast_in_dim.3
  72.8 13.8 %all-to-all-start.1 = ((f32[16,56,128]{2,1,0:T(8,128)}), f32[16,56,128]{2,1,0:T(8,128)}, u32[]{:S(2)}, u32[]{:S(2)}) async-start(f32[16,56,128]{2,1,0:T(8,128)} %broadcast_in_dim.3), calls=%async_computation.1 | async-start | bytes 917504 | tf_op jit(solution)/shard_map/all_to_all | solution.py:550
  86.7 0.9 slice_select_fusion.1
  87.6 0.7 maximum_add_fusion
  88.4 1.9 %collective-permute-start.8 = (f32[2,256,128]{2,1,0:T(8,128)}, f32[2,256,128]{2,1,0:T(8,128)S(1)}, u32[]{:S(2)}, u32[]{:S(2)}) collective-permute-start(f32[2,256,128]{2,1,0:T(8,128)} %maximum_add_fusion), channel_id=1, source_target_pairs={{0,1},{1,0},{2,3},{3,2},{4,5},{5,4},{6,7},{7,6},{8,9},{9,8},{10,11... | collective-permute-start | bytes 786440 | tf_op jit(solution)/shard_map/ppermute | solution.py:514
  90.2 10.1 %all-to-all-done.1 = f32[16,56,128]{2,1,0:T(8,128)} async-done(((f32[16,56,128]{2,1,0:T(8,128)}), f32[16,56,128]{2,1,0:T(8,128)}, u32[]{:S(2)}, u32[]{:S(2)}) %all-to-all-start.1) | async-done | bytes 458784 | tf_op jit(solution)/shard_map/all_to_all | solution.py:550
  100.4 1.0 slice.29
  101.4 0.9 slice_reduce_fusion.refs_4_
  102.3 0.0 collective-permute-done.8.refs_7_
  102.3 0.1 collective-permute-start.9
  102.4 1.7 %collective-permute-done.9.refs_9_ = f32[776,128]{1,0:T(8,128)S(1)} collective-permute-done((f32[776,128]{1,0:T(8,128)S(1)}, f32[776,128]{1,0:T(8,128)S(1)}, u32[]{:S(2)}, u32[]{:S(2)}) %collective-permute-start.9) | collective-permute-done | bytes 397344 | tf_op jit(solution)/shard_map/ppermute | solution.py:514
  104.1 0.0 copy-done.1
  104.1 1.0 copy-done.6
  105.1 3.0 %update.1 = (f32[2,256,512]{2,1,0:T(8,128)}, f32[2,256,256]{2,1,0:T(8,128)}) custom-call(s32[19]{0:T(128)S(1)} %concatenate.15.place.refs_0_, f32[2,256,512]{2,1,0:T(8,128)S(1)} %copy-done.1, f32[2,256,512]{2,1,0:T(8,128)S(1)} %copy-done.4, f32[256,512]{1,0:T(8,128)S(1)} %copy-done.6, f32[8,128]{1,0:T(8,128)S(1)} %slice_reduce_fusion.refs_4_, ...), custom_call_target="tpu_custom_call" | custom-call | tf_op jit(solution)/shard_map/update/pallas_call | solution.py:494
  (10 shorter events, 0.1 us)
Async XLA Ops:
  2.0 1.2 %copy-start = (f32[2,256,512]{2,1,0:T(8,128)S(1)}, f32[2,256,512]{2,1,0:T(8,128)}, u32[]{:S(2)}) copy-start(f32[2,256,512]{2,1,0:T(8,128)} %refs_1_.3) | copy-start | bytes 3145732
  4.0 15.6 %collective-permute-start = (f32[2,136,512]{2,1,0:T(8,128)S(1)}, f32[2,136,512]{2,1,0:T(8,128)S(1)}, u32[]{:S(2)}, u32[]{:S(2)}) collective-permute-start(f32[2,136,512]{2,1,0:T(8,128)S(1)} %get-tuple-element.20), channel_id=1, source_target_pairs={{0,2},{2,0},{1,3},{3,1},{4,6},{6,4},{5,7},{7,5},{8,10},{10,8},{9,1... | collective-permute-start | bytes 1671176 | tf_op jit(solution)/shard_map/ppermute | solution.py:514
  4.6 15.1 %collective-permute-start.1 = (f32[2,136,512]{2,1,0:T(8,128)S(1)}, f32[2,136,512]{2,1,0:T(8,128)S(1)}, u32[]{:S(2)}, u32[]{:S(2)}) collective-permute-start(f32[2,136,512]{2,1,0:T(8,128)S(1)} %get-tuple-element.21), channel_id=1, source_target_pairs={{2,4},{4,2},{6,8},{8,6},{10,12},{12,10},{14,16},{16,14},{18,20},{2... | collective-permute-start | bytes 1671176 | tf_op jit(solution)/shard_map/ppermute | solution.py:514
  5.2 14.4 %collective-permute-start.2 = (f32[2,264,128]{2,1,0:T(8,128)S(1)}, f32[2,264,128]{2,1,0:T(8,128)S(1)}, u32[]{:S(2)}, u32[]{:S(2)}) collective-permute-start(f32[2,264,128]{2,1,0:T(8,128)S(1)} %get-tuple-element.22), channel_id=1, source_target_pairs={{0,1},{1,0},{2,3},{3,2},{4,5},{5,4},{6,7},{7,6},{8,9},{9,8},{10,11... | collective-permute-start | bytes 811016 | tf_op jit(solution)/shard_map/ppermute | solution.py:514
  7.9 11.8 %collective-permute-start.3 = (f32[2,136,128]{2,1,0:T(8,128)S(1)}, f32[2,136,128]{2,1,0:T(8,128)S(1)}, u32[]{:S(2)}, u32[]{:S(2)}) collective-permute-start(f32[2,136,128]{2,1,0:T(8,128)S(1)} %get-tuple-element.23), channel_id=1, source_target_pairs={{0,3},{2,1},{1,2},{3,0},{4,7},{6,5},{5,6},{7,4},{8,11},{10,9},{9,1... | collective-permute-start | bytes 417800 | tf_op jit(solution)/shard_map/ppermute | solution.py:540
  10.5 9.2 %collective-permute-start.4 = (f32[2,136,128]{2,1,0:T(8,128)S(1)}, f32[2,136,128]{2,1,0:T(8,128)S(1)}, u32[]{:S(2)}, u32[]{:S(2)}) collective-permute-start(f32[2,136,128]{2,1,0:T(8,128)S(1)} %get-tuple-element.24), channel_id=1, source_target_pairs={{2,5},{4,3},{3,4},{5,2},{6,9},{8,7},{7,8},{9,6},{10,13},{12,11},{1... | collective-permute-start | bytes 417800 | tf_op jit(solution)/shard_map/ppermute | solution.py:540
  19.7 0.8 copy-start.7
  20.5 1.0 copy-start.2
  44.3 18.6 %copy-start.3 = (f32[2,256,256]{2,1,0:T(8,128)S(1)}, f32[2,256,256]{2,1,0:T(8,128)}, u32[]{:S(2)}) copy-start(f32[2,256,256]{2,1,0:T(8,128)} %refs_10_.2) | copy-start | bytes 1572868
  45.4 1.8 %collective-permute-start.5 = (f32[768,128]{1,0:T(8,128)S(1)}, f32[768,128]{1,0:T(8,128)S(1)}, u32[]{:S(2)}, u32[]{:S(2)}) collective-permute-start(f32[768,128]{1,0:T(8,128)S(1)} %constant_dynamic-slice_fusion), channel_id=1, source_target_pairs={{0,2},{2,0},{1,3},{3,1},{4,6},{6,4},{5,7},{7,5},{8,10},{10,8},{9,1... | collective-permute-start | bytes 1179656 | tf_op jit(solution)/shard_map/ppermute | solution.py:514
  49.0 23.0 %all-to-all-start = ((f32[16,48,128]{2,1,0:T(8,128)}), f32[16,48,128]{2,1,0:T(8,128)S(1)}, u32[]{:S(2)}, u32[]{:S(2)}) async-start(f32[16,48,128]{2,1,0:T(8,128)} %bitcast.8), calls=%async_computation | async-start | bytes 786432 | tf_op jit(solution)/shard_map/all_to_all | solution.py:550
  58.8 13.2 %collective-permute-start.6 = (f32[2,128,640]{2,1,0:T(8,128)}, f32[2,128,640]{2,1,0:T(8,128)S(1)}, u32[]{:S(2)}, u32[]{:S(2)}) collective-permute-start(f32[2,128,640]{2,1,0:T(8,128)} %get-tuple-element.32), channel_id=1, source_target_pairs={{2,4},{4,2},{6,8},{8,6},{10,12},{12,10},{14,16},{16,14},{18,20},{2... | collective-permute-start | bytes 1966088 | tf_op jit(solution)/shard_map/ppermute | solution.py:514
  59.5 12.5 %collective-permute-start.7 = (f32[2,128,640]{2,1,0:T(8,128)}, f32[2,128,640]{2,1,0:T(8,128)}, u32[]{:S(2)}, u32[]{:S(2)}) collective-permute-start(f32[2,128,640]{2,1,0:T(8,128)} %get-tuple-element.34), channel_id=1, source_target_pairs={{0,2},{2,0},{1,3},{3,1},{4,6},{6,4},{5,7},{7,5},{8,10},{10,8},{9,1... | collective-permute-start | bytes 1966088 | tf_op jit(solution)/shard_map/ppermute | solution.py:514
  65.6 0.8 copy-start.5
  72.0 32.1 %copy-start.1 = (f32[2,256,512]{2,1,0:T(8,128)S(1)}, f32[2,256,512]{2,1,0:T(8,128)}, u32[]{:S(2)}) copy-start(f32[2,256,512]{2,1,0:T(8,128)} %refs_1_.3) | copy-start | bytes 3145732
  72.0 32.1 %copy-start.4 = (f32[2,256,512]{2,1,0:T(8,128)S(1)}, f32[2,256,512]{2,1,0:T(8,128)}, u32[]{:S(2)}) copy-start(f32[2,256,512]{2,1,0:T(8,128)} %get-tuple-element.25.refs_2_) | copy-start | bytes 3145732
  72.8 27.5 %all-to-all-start.1 = ((f32[16,56,128]{2,1,0:T(8,128)}), f32[16,56,128]{2,1,0:T(8,128)}, u32[]{:S(2)}, u32[]{:S(2)}) async-start(f32[16,56,128]{2,1,0:T(8,128)} %broadcast_in_dim.3), calls=%async_computation.1 | async-start | bytes 917504 | tf_op jit(solution)/shard_map/all_to_all | solution.py:550
  88.4 13.9 %collective-permute-start.8 = (f32[2,256,128]{2,1,0:T(8,128)}, f32[2,256,128]{2,1,0:T(8,128)S(1)}, u32[]{:S(2)}, u32[]{:S(2)}) collective-permute-start(f32[2,256,128]{2,1,0:T(8,128)} %maximum_add_fusion), channel_id=1, source_target_pairs={{0,1},{1,0},{2,3},{3,2},{4,5},{5,4},{6,7},{7,6},{8,9},{9,8},{10,11... | collective-permute-start | bytes 786440 | tf_op jit(solution)/shard_map/ppermute | solution.py:514
  102.3 1.8 %collective-permute-start.9 = (f32[776,128]{1,0:T(8,128)S(1)}, f32[776,128]{1,0:T(8,128)S(1)}, u32[]{:S(2)}, u32[]{:S(2)}) collective-permute-start(f32[776,128]{1,0:T(8,128)S(1)} %pad_maximum_fusion), channel_id=1, source_target_pairs={{0,2},{2,0},{1,3},{3,1},{4,6},{6,4},{5,7},{7,5},{8,10},{10,8},{9,1... | collective-permute-start | bytes 1191944 | tf_op jit(solution)/shard_map/ppermute | solution.py:514
  104.1 1.0 copy-start.6

commit v7 on v6

--- a/solution.py
+++ b/solution.py
@@ -193,8 +193,8 @@
     probe_in, measured, left_in, right_in = refs[4 + 3 * sides : 8 + 3 * sides]
     middle, near_rim, far_rim, info = refs[8 + 3 * sides : 12 + 3 * sides]
     side_out = refs[12 + 3 * sides : 12 + 4 * sides]
-    probe_sums, ext, grad = refs[12 + 4 * sides : 15 + 4 * sides]
-    scratch = refs[15 + 4 * sides :]
+    kept, sent, probe_sums, ext, grad = refs[12 + 4 * sides : 17 + 4 * sides]
+    scratch = refs[17 + 4 * sides :]
     left, right, levels, probe = scratch[:4]
     table_sems, level_sems, ext_sems = scratch[4:7]
     scratch = scratch[7:]
@@ -258,8 +258,9 @@
             ext[ch * blocks + blocks - 1 - side_blocks[0]] = jnp.zeros((ext_rows, LANES), F32)
     grad[...] = jnp.zeros_like(grad)
     probe_sums[...] = jnp.zeros_like(probe_sums)
-    for copy in copies + tables:
+    for copy in copies:
         copy.wait()
+    tables[2].wait()
     lanes = lax.broadcasted_iota(jnp.int32, (CHUNK, LANES), 1)
 
     def put(stack, value, part, q, first):
@@ -363,6 +364,11 @@
             def _():
                 level_copy(slots[w]).wait()
 
+        @pl.when(i == 0)
+        def _():
+            tables[0].wait()
+            tables[1].wait()
+
         for w in range(WAYS):
             load(w, slots[w])
             times_left(w)
@@ -378,6 +384,13 @@
         return carry
 
     lax.fori_loop(0, (live_slots + WAYS - 1) // WAYS, visit, 0)
+    core = place[0] % 2
+    span = pieces // 2
+    for j in range(span):
+        for ch in range(3):
+            at = pl.ds((j * 3 + ch) * pr, pr)
+            kept[at, :] = probe_sums[core * span + j, ch]
+            sent[at, :] = probe_sums[(1 - core) * span + j, ch]
     for ch in range(2):
         for b in range(own_blocks):
             at, cut = ch * blocks + 1 + b, slice(b * LANES, (b + 1) * LANES)
@@ -410,11 +423,13 @@
             rim,
             shape(3 * sides + 2, INFO, LANES),
             *[shape(2, tile_rows, LANES)] * sides,
-            shape(pr // LANES, 3, pr, LANES),
+            shape(3 * pr * pr // LANES // 2, LANES),
+            shape(3 * pr * pr // LANES // 2, LANES),
         ),
         in_specs=[SMEM, HBM] + [ANY] * (2 + 3 * sides) + [HBM] * 4,
-        out_specs=(VMEM,) * (5 + sides),
+        out_specs=(VMEM,) * (6 + sides),
         scratch_shapes=[
+            pltpu.VMEM((pr // LANES, 3, pr, LANES), F32),
             *[pltpu.VMEM((2 * blocks, ext_rows, LANES), F32)] * 2,
             pltpu.VMEM(left.shape, BF),
             pltpu.VMEM(right.shape, BF),
@@ -434,13 +449,13 @@
         ),
         name="positions",
     )(place, tile, near, far_side, *side_in, *near_corners, *far_corners, probe, measured, left, right)
-    return middle, near_rim, far_rim, rest[:sides], rest[sides], info
+    return middle, near_rim, far_rim, rest[:sides], rest[sides], rest[sides + 1], info
 
 
 def update_kernel(sides, *refs):
-    place, tile, middle, cover, peak, near, far_side = refs[:7]
-    side_in = refs[7 : 7 + sides]
-    own_terms, other_terms, probe, out, new_probe, sums = refs[7 + sides :]
+    place, tile, middle, cover, near, far_side = refs[:6]
+    side_in = refs[6 : 6 + sides]
+    own_got, other_got, probe, out, new_probe, sums = refs[6 + sides :]
     tile_rows, tile_cols = tile.shape[1:]
     own_blocks = tile_cols // LANES
     even = place[0] % 2 == 0
@@ -459,15 +474,16 @@
         else:
             where = 0 if s == 0 else own_blocks - 1
             sums[:, :, where * LANES : (where + 1) * LANES] += side_in[s][...]
-    rows = own_terms.shape[0]
-    top = MIX_OBJECT * jnp.maximum(peak[0:1, 0:1], other_terms[rows : rows + 1, 0:1])
+    rows = own_got.shape[1] - 8
+    peak = jnp.maximum(jnp.max(own_got[:, rows:, :], axis=0), jnp.max(other_got[:, rows:, :], axis=0))
+    top = MIX_OBJECT * jnp.max(peak, keepdims=True)
     inverse = 1.0 / ((1.0 - MIX_OBJECT) * cover[...] + top)
     for ch in range(2):
         out[ch] = tile[ch] + sums[ch] * inverse
 
     pr = probe.shape[1]
     pieces = pr // LANES
-    both = (own_terms, other_terms)
+    both = [ref[:, 0:rows, :].reshape(-1, LANES) for ref in (own_got, other_got)]
 
     def update(parts):
         flat = [parts[j * len(parts) // pieces] for j in range(pieces)]
@@ -486,20 +502,20 @@
 
         @pl.when(place[0] % 2 == first)
         def _():
-            update([both[first][0:rows, :], both[1 - first][0:rows, :]])
-
-
-def update_call(place, tile, middle, cover, peak, near, far_side, side_in, own_terms, other_terms, probe):
+            update([both[first], both[1 - first]])
+
+
+def update_call(place, tile, middle, cover, near, far_side, side_in, own, other, probe):
     sides = len(side_in)
     return pl.pallas_call(
         functools.partial(update_kernel, sides),
         out_shape=(jax.ShapeDtypeStruct(tile.shape, F32), jax.ShapeDtypeStruct(probe.shape, F32)),
-        in_specs=[SMEM] + [VMEM] * (9 + sides),
+        in_specs=[SMEM] + [VMEM] * (8 + sides),
         out_specs=(VMEM, VMEM),
         scratch_shapes=[pltpu.VMEM(tile.shape, F32)],
         compiler_params=pltpu.CompilerParams(vmem_limit_bytes=32 << 20),
         name="update",
-    )(place, tile, middle, cover, peak, near, far_side, *side_in, own_terms, other_terms, probe)
+    )(place, tile, middle, cover, near, far_side, *side_in, own, other, probe)
 
 
 WIDE = ("rest", "core")
@@ -541,11 +557,6 @@
     return got
 
 
-def half_of(x, which):
-    rows = x.shape[0] // 2
-    return lax.dynamic_slice_in_dim(x, which * rows, rows, axis=0)
-
-
 def chip_exchange(chunks):
     return lax.all_to_all(chunks.reshape(-1, LANES), CHIPS, 0, 0, tiled=True).reshape(chunks.shape)
 
@@ -570,14 +581,12 @@
     near_corners = to_corners(near_ends, 0)
     near = swap(near_band, "core", 0)
 
-    middle, near_rim, far_rim, side_rims, probe_sums, got_info = positions_call(
+    middle, near_rim, far_rim, side_rims, kept, sent, got_info = positions_call(
         place, tile, near, far_side, side_in, near_corners, far_corners, probe, measured
     )
     own_info = edges[0][:1, tile_rows:]
 
-    core = lax.axis_index("core")
-    terms = probe_sums.reshape(-1, LANES)
-    terms = half_of(terms, core) + swap(half_of(terms, 1 - core), "core", 0)
+    terms = kept + swap(sent, "core", 0)
     near_got = swap(after(near_rim, terms), "core", 0)
     far_got = swap(after(far_rim, terms), WIDE, 1)
     info = jnp.concatenate([own_info, got_info], axis=0)[:, 0, :32].astype(jnp.int32)
@@ -588,8 +597,9 @@
     rows_each = chunk.shape[0]
     chunk = after(jnp.concatenate([chunk, peak], axis=0), far_got, near_got)
     got = chip_exchange(jnp.broadcast_to(chunk, (chips, *chunk.shape)))
-    terms = got[:, :rows_each].reshape(-1, LANES)
-    peak = jnp.max(got[:, rows_each:], axis=0)
+    if rows_each % 8:
+        peak = jnp.max(got[:, rows_each:], axis=0)
+        got = jnp.concatenate([got[:, :rows_each].reshape(-1, LANES), peak], axis=0)[None]
 
     def with_rims(piece, s):
         cut = slice(tile_cols + s * LANES, tile_cols + (s + 1) * LANES)
@@ -598,10 +608,8 @@
         return piece + jnp.concatenate([above, below], axis=1)
 
     side_got = to_sides([with_rims(piece, s) for s, piece in enumerate(side_rims)])
-    other_terms = swap(after(jnp.concatenate([terms, peak], axis=0), *side_got), "core", 0)
-    return update_call(
-        place, tile, middle, cover, peak, near_got, far_got, side_got, terms, other_terms, probe
-    )
+    other = swap(after(got, *side_got), "core", 0)
+    return update_call(place, tile, middle, cover, near_got, far_got, side_got, got, other, probe)
 
 
 def solution(mesh):

time: 110 us -> 107 us (0.973)
  Pallas kernels: 29.3 us -> 25 us
  starting transfers between devices: 36.8 us -> 40.2 us
  waiting for transfers between devices: 27.6 us -> 30.3 us
  local copies, waits for them, and re-layouts: 8.58 us -> 6.22 us
  other arithmetic: 4.43 us -> 2.86 us
    ppermute x8, waiting for transfers between devices: 3.44 us -> 13.4 us  [swap(): return lax.ppermute(x, axis, pairs)]
    all_to_all x2, waiting for transfers between devices: 15.6 us -> 8.47 us  [chip_exchange(): lax.all_to_all(chunks.reshape(-1, LANES), CHIPS, 0, 0, tiled=True)]
    all_to_all x2, starting transfers between devices: 23.7 us -> 28.8 us  [chip_exchange(): lax.all_to_all(chunks.reshape(-1, LANES), CHIPS, 0, 0, tiled=True)]
    pallas_call x1, Pallas kernels: 22.7 us -> 18.3 us  [positions_call(): pl.pallas_call(functools.partial(positions_kernel, sides), out_shape=(sha...]
    ppermute x8, starting transfers between devices: 9.82 us -> 8.04 us  [swap(): return lax.ppermute(x, axis, pairs)]
  transfers between devices with their start and end apart: 12 -> 12, of which waited for: 5 -> 6; matrix products, arithmetic and copies ran while one was open for 3% -> 2% of each run, Pallas kernels for 3% -> 2%
where the time goes in v7:
time: 107 us; the launch traced here: 106 us
  starting transfers between devices  40.2 us (38%)
  waiting for transfers between devices  30.3 us (28%)
  Pallas kernels  25 us (23%)
  local copies, waits for them, and re-layouts  6.22 us (6%)
  other arithmetic  2.86 us (3%)
  between operations  1.47 us (1%)
    all_to_all x2, starting transfers between devices, chip_exchange(): lax.all_to_all(chunks.reshape(-1, LANES), CHIPS, 0, 0, tiled=True)  28.8 us
    pallas_call x1, Pallas kernels, positions_call(): pl.pallas_call(functools.partial(positions_kernel, sides), out_shape=(sha...  18.3 us
    ppermute x8, waiting for transfers between devices, swap(): return lax.ppermute(x, axis, pairs)  13.4 us
    ppermute x2, waiting for transfers between devices, to_corners(): got.append(lax.ppermute(band, (*WIDE, 'narrow'), pairs))  8.5 us
    all_to_all x2, waiting for transfers between devices, chip_exchange(): lax.all_to_all(chunks.reshape(-1, LANES), CHIPS, 0, 0, tiled=True)  8.47 us
    ppermute x8, starting transfers between devices, swap(): return lax.ppermute(x, axis, pairs)  8.04 us
    unnamed x16, local copies, waits for them, and re-layouts  4.66 us
    ppermute x2, starting transfers between devices, to_corners(): got.append(lax.ppermute(band, (*WIDE, 'narrow'), pairs))  3.31 us
  transfers between devices with their start and end apart: 12, of which 6 were waited for; matrix products, arithmetic and copies ran while one was open for 2% of the time, Pallas kernels for 2%

profile of v7, /device:TPU:0, one launch (start us, length us, event | category | flops | bytes accessed | tf_op | source)
XLA Modules:
  0.0 106.1 jit_solution(17997370096833992684)
XLA Ops:
  1.3 0.7 concatenate.12.place.refs_0_
  2.0 0.0 copy-start
  2.0 1.2 %copy-done = f32[2,256,512]{2,1,0:T(8,128)S(1)} copy-done((f32[2,256,512]{2,1,0:T(8,128)S(1)}, f32[2,256,512]{2,1,0:T(8,128)}, u32[]{:S(2)}) %copy-start) | copy-done | bytes 1048600
  3.3 0.8 pack.1
  4.0 0.5 collective-permute-start
  4.6 0.7 collective-permute-start.1
  5.2 2.6 %collective-permute-start.2 = (f32[2,264,128]{2,1,0:T(8,128)S(1)}, f32[2,264,128]{2,1,0:T(8,128)S(1)}, u32[]{:S(2)}, u32[]{:S(2)}) collective-permute-start(f32[2,264,128]{2,1,0:T(8,128)S(1)} %get-tuple-element.23), channel_id=1, source_target_pairs={{0,1},{1,0},{2,3},{3,2},{4,5},{5,4},{6,7},{7,6},{8,9},{9,8},{10,11... | collective-permute-start | bytes 811016 | tf_op jit(solution)/shard_map/ppermute | solution.py:530
  7.8 2.6 %collective-permute-start.3 = (f32[2,136,128]{2,1,0:T(8,128)S(1)}, f32[2,136,128]{2,1,0:T(8,128)S(1)}, u32[]{:S(2)}, u32[]{:S(2)}) collective-permute-start(f32[2,136,128]{2,1,0:T(8,128)S(1)} %get-tuple-element.24), channel_id=1, source_target_pairs={{0,3},{2,1},{1,2},{3,0},{4,7},{6,5},{5,6},{7,4},{8,11},{10,9},{9,1... | collective-permute-start | bytes 417800 | tf_op jit(solution)/shard_map/ppermute | solution.py:556
  10.5 0.7 collective-permute-start.4
  11.2 8.5 %collective-permute-done.3.refs_5_ = f32[2,136,128]{2,1,0:T(8,128)S(1)} collective-permute-done((f32[2,136,128]{2,1,0:T(8,128)S(1)}, f32[2,136,128]{2,1,0:T(8,128)S(1)}, u32[]{:S(2)}, u32[]{:S(2)}) %collective-permute-start.3) | collective-permute-done | bytes 139296 | tf_op jit(solution)/shard_map/ppermute | solution.py:556
  19.7 0.0 collective-permute-done.4.refs_6_
  19.7 0.0 collective-permute-done.2.refs_4_
  19.7 0.0 collective-permute-done.refs_2_
  19.7 0.0 copy-start.6
  19.7 0.0 collective-permute-done.1.refs_3_
  19.7 0.8 copy-done.6
  20.5 0.0 copy-start.7
  20.5 0.8 copy-done.7
  21.3 18.3 %positions.1 = (f32[2,256,512]{2,1,0:T(8,128)}, f32[2,128,640]{2,1,0:T(8,128)}, f32[2,128,640]{2,1,0:T(8,128)}, f32[5,8,128]{2,1,0:T(8,128)S(1)}, f32[2,256,128]...) custom-call(s32[19]{0:T(128)S(1)} %concatenate.12.place.refs_0_, f32[2,256,512]{2,1,0:T(8,128)} %refs_1_.3, ...), custom_call_target="tpu_custom_call" | custom-call | flops 12884901888 | bytes 16000000 | tf_op jit(solution)/shard_map/positions/pallas_call | solution.py:418
  39.6 0.0 copy-start.2
  39.6 0.6 collective-permute-start.5
  40.2 1.3 %collective-permute-done.5 = f32[768,128]{1,0:T(8,128)S(1)} collective-permute-done((f32[768,128]{1,0:T(8,128)S(1)}, f32[768,128]{1,0:T(8,128)S(1)}, u32[]{:S(2)}, u32[]{:S(2)}) %collective-permute-start.5) | collective-permute-done | bytes 393248 | tf_op jit(solution)/shard_map/ppermute | solution.py:530
  41.5 0.8 add.14
  42.3 15.8 %all-to-all-start = ((f32[16,48,128]{2,1,0:T(8,128)}), f32[16,48,128]{2,1,0:T(8,128)}, u32[]{:S(2)}, u32[]{:S(2)}) async-start(f32[16,48,128]{2,1,0:T(8,128)} %bitcast.7), calls=%async_computation | async-start | bytes 786432 | tf_op jit(solution)/shard_map/all_to_all | solution.py:561
  58.1 0.0 copy-start.1
  58.1 0.0 copy-start.3
  58.2 0.1 collective-permute-start.6
  58.2 1.6 %collective-permute-start.7 = (f32[2,128,640]{2,1,0:T(8,128)}, f32[2,128,640]{2,1,0:T(8,128)}, u32[]{:S(2)}, u32[]{:S(2)}) collective-permute-start(f32[2,128,640]{2,1,0:T(8,128)} %get-tuple-element.35), channel_id=1, source_target_pairs={{2,4},{4,2},{6,8},{8,6},{10,12},{12,10},{14,16},{16,14},{18,20},{2... | collective-permute-start | bytes 1966088 | tf_op jit(solution)/shard_map/ppermute | solution.py:530
  59.9 0.0 copy-done.2
  59.9 2.6 %cover.1 = (f32[256,512]{1,0:T(8,128)S(1)}, f32[8,128]{1,0:T(8,128)S(1)}) custom-call(s32[19]{0:T(128)S(1)} %concatenate.12.place.refs_0_, s32[6,32]{1,0:T(8,128)S(1)} %fusion.1.info, f32[2,256,256]{2,1,0:T(8,128)S(1)} %copy-done.2), custom_call_target="tpu_custom_call" | custom-call | flops 4000000 | bytes 8000000 | tf_op jit(solution)/shard_map/cover/pallas_call | solution.py:118
  62.5 0.0 copy-start.4
  62.5 0.8 copy-done.4
  63.3 7.8 %all-to-all-done = f32[16,48,128]{2,1,0:T(8,128)} async-done(((f32[16,48,128]{2,1,0:T(8,128)}), f32[16,48,128]{2,1,0:T(8,128)}, u32[]{:S(2)}, u32[]{:S(2)}) %all-to-all-start) | async-done | bytes 393248 | tf_op jit(solution)/shard_map/all_to_all | solution.py:561
  71.1 1.0 reduce_sum.9
  72.2 0.0 collective-permute-done.6.refs_4_
  72.2 0.0 collective-permute-done.7.refs_5_
  72.2 0.8 broadcast_in_dim.3
  73.0 13.0 %all-to-all-start.1 = ((f32[16,56,128]{2,1,0:T(8,128)}), f32[16,56,128]{2,1,0:T(8,128)S(1)}, u32[]{:S(2)}, u32[]{:S(2)}) async-start(f32[16,56,128]{2,1,0:T(8,128)} %broadcast_in_dim.3), calls=%async_computation.1 | async-start | bytes 917504 | tf_op jit(solution)/shard_map/all_to_all | solution.py:561
  86.0 1.0 slice_select_fusion.1
  87.1 2.0 %collective-permute-start.8 = (f32[2,256,128]{2,1,0:T(8,128)S(1)}, f32[2,256,128]{2,1,0:T(8,128)S(1)}, u32[]{:S(2)}, u32[]{:S(2)}) collective-permute-start(f32[2,256,128]{2,1,0:T(8,128)S(1)} %maximum_add_fusion), channel_id=1, source_target_pairs={{0,1},{1,0},{2,3},{3,2},{4,5},{5,4},{6,7},{7,6},{8,9},{9,8},{10,11... | collective-permute-start | bytes 786440 | tf_op jit(solution)/shard_map/ppermute | solution.py:530
  89.0 10.2 %collective-permute-done.8.refs_6_ = f32[2,256,128]{2,1,0:T(8,128)S(1)} collective-permute-done((f32[2,256,128]{2,1,0:T(8,128)S(1)}, f32[2,256,128]{2,1,0:T(8,128)S(1)}, u32[]{:S(2)}, u32[]{:S(2)}) %collective-permute-start.8) | collective-permute-done | bytes 262176 | tf_op jit(solution)/shard_map/ppermute | solution.py:530
  99.2 0.7 all-to-all-done.1.refs_7_
  99.9 0.0 collective-permute-start.9
  99.9 1.8 %collective-permute-done.9.refs_8_ = f32[16,56,128]{2,1,0:T(8,128)S(1)} collective-permute-done((f32[16,56,128]{2,1,0:T(8,128)S(1)}, f32[16,56,128]{2,1,0:T(8,128)S(1)}, u32[]{:S(2)}, u32[]{:S(2)}) %collective-permute-start.9) | collective-permute-done | bytes 458784 | tf_op jit(solution)/shard_map/ppermute | solution.py:530
  101.7 0.0 copy-done.1
  101.7 0.0 copy-done.3
  101.7 1.0 copy-done.5
  102.8 3.3 %update.1 = (f32[2,256,512]{2,1,0:T(8,128)}, f32[2,256,256]{2,1,0:T(8,128)}) custom-call(s32[19]{0:T(128)S(1)} %concatenate.12.place.refs_0_, f32[2,256,512]{2,1,0:T(8,128)S(1)} %copy-done.1, f32[2,256,512]{2,1,0:T(8,128)S(1)} %copy-done.3, f32[256,512]{1,0:T(8,128)S(1)} %copy-done.5, f32[2,128,640]{2,1,0:T(8,128)} %collective-permute-done.6.refs_4_, ...), custom_call_target="tpu_custom_call" | custom-call | tf_op jit(solution)/shard_map/update/pallas_call | solution.py:510
  (6 shorter events, 0.1 us)
Async XLA Ops:
  2.0 1.2 %copy-start = (f32[2,256,512]{2,1,0:T(8,128)S(1)}, f32[2,256,512]{2,1,0:T(8,128)}, u32[]{:S(2)}) copy-start(f32[2,256,512]{2,1,0:T(8,128)} %refs_1_.3) | copy-start | bytes 3145732
  4.0 15.6 %collective-permute-start = (f32[2,136,512]{2,1,0:T(8,128)S(1)}, f32[2,136,512]{2,1,0:T(8,128)S(1)}, u32[]{:S(2)}, u32[]{:S(2)}) collective-permute-start(f32[2,136,512]{2,1,0:T(8,128)S(1)} %get-tuple-element.21), channel_id=1, source_target_pairs={{0,2},{2,0},{1,3},{3,1},{4,6},{6,4},{5,7},{7,5},{8,10},{10,8},{9,1... | collective-permute-start | bytes 1671176 | tf_op jit(solution)/shard_map/ppermute | solution.py:530
  4.6 15.1 %collective-permute-start.1 = (f32[2,136,512]{2,1,0:T(8,128)S(1)}, f32[2,136,512]{2,1,0:T(8,128)S(1)}, u32[]{:S(2)}, u32[]{:S(2)}) collective-permute-start(f32[2,136,512]{2,1,0:T(8,128)S(1)} %get-tuple-element.22), channel_id=1, source_target_pairs={{2,4},{4,2},{6,8},{8,6},{10,12},{12,10},{14,16},{16,14},{18,20},{2... | collective-permute-start | bytes 1671176 | tf_op jit(solution)/shard_map/ppermute | solution.py:530
  5.2 14.4 %collective-permute-start.2 = (f32[2,264,128]{2,1,0:T(8,128)S(1)}, f32[2,264,128]{2,1,0:T(8,128)S(1)}, u32[]{:S(2)}, u32[]{:S(2)}) collective-permute-start(f32[2,264,128]{2,1,0:T(8,128)S(1)} %get-tuple-element.23), channel_id=1, source_target_pairs={{0,1},{1,0},{2,3},{3,2},{4,5},{5,4},{6,7},{7,6},{8,9},{9,8},{10,11... | collective-permute-start | bytes 811016 | tf_op jit(solution)/shard_map/ppermute | solution.py:530
  7.8 11.8 %collective-permute-start.3 = (f32[2,136,128]{2,1,0:T(8,128)S(1)}, f32[2,136,128]{2,1,0:T(8,128)S(1)}, u32[]{:S(2)}, u32[]{:S(2)}) collective-permute-start(f32[2,136,128]{2,1,0:T(8,128)S(1)} %get-tuple-element.24), channel_id=1, source_target_pairs={{0,3},{2,1},{1,2},{3,0},{4,7},{6,5},{5,6},{7,4},{8,11},{10,9},{9,1... | collective-permute-start | bytes 417800 | tf_op jit(solution)/shard_map/ppermute | solution.py:556
  10.5 9.2 %collective-permute-start.4 = (f32[2,136,128]{2,1,0:T(8,128)S(1)}, f32[2,136,128]{2,1,0:T(8,128)S(1)}, u32[]{:S(2)}, u32[]{:S(2)}) collective-permute-start(f32[2,136,128]{2,1,0:T(8,128)S(1)} %get-tuple-element.25), channel_id=1, source_target_pairs={{2,5},{4,3},{3,4},{5,2},{6,9},{8,7},{7,8},{9,6},{10,13},{12,11},{1... | collective-permute-start | bytes 417800 | tf_op jit(solution)/shard_map/ppermute | solution.py:556
  19.7 0.8 copy-start.6
  20.5 0.8 copy-start.7
  39.6 20.3 %copy-start.2 = (f32[2,256,256]{2,1,0:T(8,128)S(1)}, f32[2,256,256]{2,1,0:T(8,128)}, u32[]{:S(2)}) copy-start(f32[2,256,256]{2,1,0:T(8,128)} %refs_9_.2) | copy-start | bytes 1572868
  39.6 1.9 %collective-permute-start.5 = (f32[768,128]{1,0:T(8,128)S(1)}, f32[768,128]{1,0:T(8,128)S(1)}, u32[]{:S(2)}, u32[]{:S(2)}) collective-permute-start(f32[768,128]{1,0:T(8,128)S(1)} %get-tuple-element.29), channel_id=1, source_target_pairs={{0,2},{2,0},{1,3},{3,1},{4,6},{6,4},{5,7},{7,5},{8,10},{10,8},{9,1... | collective-permute-start | bytes 1179656 | tf_op jit(solution)/shard_map/ppermute | solution.py:530
  42.3 28.8 %all-to-all-start = ((f32[16,48,128]{2,1,0:T(8,128)}), f32[16,48,128]{2,1,0:T(8,128)}, u32[]{:S(2)}, u32[]{:S(2)}) async-start(f32[16,48,128]{2,1,0:T(8,128)} %bitcast.7), calls=%async_computation | async-start | bytes 786432 | tf_op jit(solution)/shard_map/all_to_all | solution.py:561
  58.1 43.6 %copy-start.1 = (f32[2,256,512]{2,1,0:T(8,128)S(1)}, f32[2,256,512]{2,1,0:T(8,128)}, u32[]{:S(2)}) copy-start(f32[2,256,512]{2,1,0:T(8,128)} %refs_1_.3) | copy-start | bytes 3145732
  58.1 43.6 %copy-start.3 = (f32[2,256,512]{2,1,0:T(8,128)S(1)}, f32[2,256,512]{2,1,0:T(8,128)}, u32[]{:S(2)}) copy-start(f32[2,256,512]{2,1,0:T(8,128)} %get-tuple-element.26.refs_2_) | copy-start | bytes 3145732
  58.2 14.0 %collective-permute-start.6 = (f32[2,128,640]{2,1,0:T(8,128)}, f32[2,128,640]{2,1,0:T(8,128)}, u32[]{:S(2)}, u32[]{:S(2)}) collective-permute-start(f32[2,128,640]{2,1,0:T(8,128)} %get-tuple-element.33), channel_id=1, source_target_pairs={{0,2},{2,0},{1,3},{3,1},{4,6},{6,4},{5,7},{7,5},{8,10},{10,8},{9,1... | collective-permute-start | bytes 1966088 | tf_op jit(solution)/shard_map/ppermute | solution.py:530
  58.2 13.9 %collective-permute-start.7 = (f32[2,128,640]{2,1,0:T(8,128)}, f32[2,128,640]{2,1,0:T(8,128)}, u32[]{:S(2)}, u32[]{:S(2)}) collective-permute-start(f32[2,128,640]{2,1,0:T(8,128)} %get-tuple-element.35), channel_id=1, source_target_pairs={{2,4},{4,2},{6,8},{8,6},{10,12},{12,10},{14,16},{16,14},{18,20},{2... | collective-permute-start | bytes 1966088 | tf_op jit(solution)/shard_map/ppermute | solution.py:530
  62.5 0.8 copy-start.4
  73.0 26.9 %all-to-all-start.1 = ((f32[16,56,128]{2,1,0:T(8,128)}), f32[16,56,128]{2,1,0:T(8,128)S(1)}, u32[]{:S(2)}, u32[]{:S(2)}) async-start(f32[16,56,128]{2,1,0:T(8,128)} %broadcast_in_dim.3), calls=%async_computation.1 | async-start | bytes 917504 | tf_op jit(solution)/shard_map/all_to_all | solution.py:561
  87.1 12.2 %collective-permute-start.8 = (f32[2,256,128]{2,1,0:T(8,128)S(1)}, f32[2,256,128]{2,1,0:T(8,128)S(1)}, u32[]{:S(2)}, u32[]{:S(2)}) collective-permute-start(f32[2,256,128]{2,1,0:T(8,128)S(1)} %maximum_add_fusion), channel_id=1, source_target_pairs={{0,1},{1,0},{2,3},{3,2},{4,5},{5,4},{6,7},{7,6},{8,9},{9,8},{10,11... | collective-permute-start | bytes 786440 | tf_op jit(solution)/shard_map/ppermute | solution.py:530
  99.9 1.8 %collective-permute-start.9 = (f32[16,56,128]{2,1,0:T(8,128)S(1)}, f32[16,56,128]{2,1,0:T(8,128)S(1)}, u32[]{:S(2)}, u32[]{:S(2)}) collective-permute-start(f32[16,56,128]{2,1,0:T(8,128)S(1)} %all-to-all-done.1.refs_7_), channel_id=1, source_target_pairs={{0,2},{2,0},{1,3},{3,1},{4,6},{6,4},{5,7},{7,5},{8,10},{10,8},{9,1... | collective-permute-start | bytes 1376264 | tf_op jit(solution)/shard_map/ppermute | solution.py:530
  101.7 1.0 copy-start.5

commit v8 on v7

--- a/solution.py
+++ b/solution.py
@@ -15,6 +15,7 @@
 CHUNK = 32
 WAYS = 2
 INFO = 8
+GRANT = 50176 << 10
 BF = jnp.bfloat16
 F32 = jnp.float32
 MIX_OBJECT = 0.5
@@ -127,7 +128,7 @@
             pltpu.VMEM((blocks, tile_rows + 2 * pr, LANES), F32),
             pltpu.VMEM((pr // LANES, pr, LANES), F32),
         ],
-        compiler_params=pltpu.CompilerParams(vmem_limit_bytes=24 << 20),
+        compiler_params=pltpu.CompilerParams(vmem_limit_bytes=16 << 20),
         cost_estimate=pl.CostEstimate(flops=4_000_000, bytes_accessed=8_000_000, transcendentals=0),
         name="cover",
     )(place, info, probe)
@@ -192,9 +193,9 @@
     side_in, near_corners, far_corners = [refs[4 + i * sides : 4 + (i + 1) * sides] for i in range(3)]
     probe_in, measured, left_in, right_in = refs[4 + 3 * sides : 8 + 3 * sides]
     middle, near_rim, far_rim, info = refs[8 + 3 * sides : 12 + 3 * sides]
-    side_out = refs[12 + 3 * sides : 12 + 4 * sides]
-    kept, sent, probe_sums, ext, grad = refs[12 + 4 * sides : 17 + 4 * sides]
-    scratch = refs[17 + 4 * sides :]
+    side_out, near_ends, far_ends = [refs[12 + i * sides : 12 + (i + 1) * sides] for i in range(3, 6)]
+    kept, sent, probe_sums, ext, grad = refs[12 + 6 * sides : 17 + 6 * sides]
+    scratch = refs[17 + 6 * sides :]
     left, right, levels, probe = scratch[:4]
     table_sems, level_sems, ext_sems = scratch[4:7]
     scratch = scratch[7:]
@@ -399,10 +400,9 @@
             far_rim[ch, :, cut] = grad[at, far_rows, :]
         for s in range(sides):
             at = ch * blocks + side_blocks[s]
-            cut = slice(tile_cols + s * LANES, tile_cols + (s + 1) * LANES)
             side_out[s][ch] = grad[at, own, :]
-            near_rim[ch, :, cut] = grad[at, near_rows, :]
-            far_rim[ch, :, cut] = grad[at, far_rows, :]
+            near_ends[s][ch] = grad[at, near_rows, :]
+            far_ends[s][ch] = grad[at, far_rows, :]
 
 
 def positions_call(place, tile, near, far_side, side_in, near_corners, far_corners, probe, measured):
@@ -414,7 +414,7 @@
     left, right = (jnp.asarray(table) for table in dft_tables(pr))
     shape = lambda *dims: jax.ShapeDtypeStruct(dims, F32)
     slots = measured.shape[2]
-    rim = shape(2, H, tile_cols + sides * LANES)
+    rim = shape(2, H, tile_cols)
     middle, near_rim, far_rim, info, *rest = pl.pallas_call(
         functools.partial(positions_kernel, sides),
         out_shape=(
@@ -423,11 +423,12 @@
             rim,
             shape(3 * sides + 2, INFO, LANES),
             *[shape(2, tile_rows, LANES)] * sides,
+            *[shape(2, H, LANES)] * (2 * sides),
             shape(3 * pr * pr // LANES // 2, LANES),
             shape(3 * pr * pr // LANES // 2, LANES),
         ),
         in_specs=[SMEM, HBM] + [ANY] * (2 + 3 * sides) + [HBM] * 4,
-        out_specs=(VMEM,) * (6 + sides),
+        out_specs=(VMEM,) * (6 + 3 * sides),
         scratch_shapes=[
             pltpu.VMEM((pr // LANES, 3, pr, LANES), F32),
             *[pltpu.VMEM((2 * blocks, ext_rows, LANES), F32)] * 2,
@@ -443,37 +444,37 @@
             *[pltpu.VMEM((pr, 4 * pr), BF)] * WAYS,
             *[pltpu.VMEM((pr, 2 * pr), F32)] * WAYS,
         ],
-        compiler_params=pltpu.CompilerParams(vmem_limit_bytes=52 << 20),
+        compiler_params=pltpu.CompilerParams(vmem_limit_bytes=GRANT),
         cost_estimate=pl.CostEstimate(
             flops=slots * 96 * pr * pr * pr, bytes_accessed=16_000_000, transcendentals=slots * 2 * pr * pr
         ),
         name="positions",
     )(place, tile, near, far_side, *side_in, *near_corners, *far_corners, probe, measured, left, right)
-    return middle, near_rim, far_rim, rest[:sides], rest[sides], rest[sides + 1], info
+    ends = [rest[i * sides : (i + 1) * sides] for i in range(3)]
+    return middle, near_rim, far_rim, *ends, *rest[3 * sides :], info
 
 
 def update_kernel(sides, *refs):
     place, tile, middle, cover, near, far_side = refs[:6]
-    side_in = refs[6 : 6 + sides]
-    own_got, other_got, probe, out, new_probe, sums = refs[6 + sides :]
+    side_in, near_ends, far_ends = [refs[6 + i * sides : 6 + (i + 1) * sides] for i in range(3)]
+    own_got, other_got, probe, out, new_probe, sums = refs[6 + 3 * sides :]
     tile_rows, tile_cols = tile.shape[1:]
     own_blocks = tile_cols // LANES
     even = place[0] % 2 == 0
     sums[...] = middle[...]
     near_row = pl.multiple_of(jnp.where(even, tile_rows - H, 0), 8)
     far_row = pl.multiple_of(jnp.where(even, 0, tile_rows - H), 8)
-    sums[:, pl.ds(near_row, H), :] += near[:, :, 0:tile_cols]
-    sums[:, pl.ds(far_row, H), :] += far_side[:, :, 0:tile_cols]
+    sums[:, pl.ds(near_row, H), :] += near[...]
+    sums[:, pl.ds(far_row, H), :] += far_side[...]
     for s in range(sides):
         if sides == 1:
-            for edge, where in ((0, own_blocks - 1), (1, 0)):
-
-                @pl.when((place[1] == 0) == (edge == 0))
-                def _():
-                    sums[:, :, where * LANES : (where + 1) * LANES] += side_in[s][...]
+            edge = jnp.where(place[1] == 0, tile_cols - LANES, 0)
         else:
-            where = 0 if s == 0 else own_blocks - 1
-            sums[:, :, where * LANES : (where + 1) * LANES] += side_in[s][...]
+            edge = 0 if s == 0 else tile_cols - LANES
+        at = pl.ds(pl.multiple_of(edge, LANES), LANES)
+        sums[:, :, at] += side_in[s][...]
+        sums[:, pl.ds(near_row, H), at] += near_ends[s][...]
+        sums[:, pl.ds(far_row, H), at] += far_ends[s][...]
     rows = own_got.shape[1] - 8
     peak = jnp.maximum(jnp.max(own_got[:, rows:, :], axis=0), jnp.max(other_got[:, rows:, :], axis=0))
     top = MIX_OBJECT * jnp.max(peak, keepdims=True)
@@ -505,17 +506,17 @@
             update([both[first], both[1 - first]])
 
 
-def update_call(place, tile, middle, cover, near, far_side, side_in, own, other, probe):
+def update_call(place, tile, middle, cover, near, far_side, side_in, ends, own, other, probe):
     sides = len(side_in)
     return pl.pallas_call(
         functools.partial(update_kernel, sides),
         out_shape=(jax.ShapeDtypeStruct(tile.shape, F32), jax.ShapeDtypeStruct(probe.shape, F32)),
-        in_specs=[SMEM] + [VMEM] * (8 + sides),
+        in_specs=[SMEM] + [VMEM] * (8 + 3 * sides),
         out_specs=(VMEM, VMEM),
         scratch_shapes=[pltpu.VMEM(tile.shape, F32)],
-        compiler_params=pltpu.CompilerParams(vmem_limit_bytes=32 << 20),
+        compiler_params=pltpu.CompilerParams(vmem_limit_bytes=16 << 20),
         name="update",
-    )(place, tile, middle, cover, near, far_side, *side_in, own, other, probe)
+    )(place, tile, middle, cover, near, far_side, *side_in, *ends, own, other, probe)
 
 
 WIDE = ("rest", "core")
@@ -581,35 +582,32 @@
     near_corners = to_corners(near_ends, 0)
     near = swap(near_band, "core", 0)
 
-    middle, near_rim, far_rim, side_rims, kept, sent, got_info = positions_call(
+    middle, near_rim, far_rim, side_rims, near_rim_ends, far_rim_ends, kept, sent, got_info = positions_call(
         place, tile, near, far_side, side_in, near_corners, far_corners, probe, measured
     )
     own_info = edges[0][:1, tile_rows:]
 
     terms = kept + swap(sent, "core", 0)
-    near_got = swap(after(near_rim, terms), "core", 0)
-    far_got = swap(after(far_rim, terms), WIDE, 1)
+    near_got = swap(near_rim, "core", 0)
+    far_got = swap(far_rim, WIDE, 1)
+    side_got = to_sides(side_rims)
     info = jnp.concatenate([own_info, got_info], axis=0)[:, 0, :32].astype(jnp.int32)
     cover, peak = cover_call(place, after(info, terms), probe, tile_rows, tile_cols, sides)
     chips = lax.axis_size(CHIPS)
     got = chip_exchange(terms.reshape(chips, -1, LANES))
     chunk = jnp.sum(got, axis=0)
     rows_each = chunk.shape[0]
-    chunk = after(jnp.concatenate([chunk, peak], axis=0), far_got, near_got)
+    chunk = after(jnp.concatenate([chunk, peak], axis=0), far_got, near_got, *side_got)
     got = chip_exchange(jnp.broadcast_to(chunk, (chips, *chunk.shape)))
     if rows_each % 8:
         peak = jnp.max(got[:, rows_each:], axis=0)
         got = jnp.concatenate([got[:, :rows_each].reshape(-1, LANES), peak], axis=0)[None]
 
-    def with_rims(piece, s):
-        cut = slice(tile_cols + s * LANES, tile_cols + (s + 1) * LANES)
-        below = jnp.where(even, near_got[:, :, cut], far_got[:, :, cut])
-        above = jnp.where(even, far_got[:, :, cut], near_got[:, :, cut])
-        return piece + jnp.concatenate([above, below], axis=1)
-
-    side_got = to_sides([with_rims(piece, s) for s, piece in enumerate(side_rims)])
-    other = swap(after(got, *side_got), "core", 0)
-    return update_call(place, tile, middle, cover, near_got, far_got, side_got, got, other, probe)
+    near_ends_got = to_corners(near_rim_ends, 0)
+    far_ends_got = to_corners(far_rim_ends, 1)
+    ends_got = near_ends_got + far_ends_got
+    other = swap(after(got, *ends_got), "core", 0)
+    return update_call(place, tile, middle, cover, near_got, far_got, side_got, ends_got, got, other, probe)
 
 
 def solution(mesh):

time: 107 us -> 105 us (0.981)
  starting transfers between devices: 40.2 us -> 37.8 us
  local copies, waits for them, and re-layouts: 6.22 us -> 7.88 us
    ppermute x8, waiting for transfers between devices: 13.4 us -> 3.54 us  [swap(): return lax.ppermute(x, axis, pairs)]
    ppermute x2 -> x4, waiting for transfers between devices: 8.5 us -> 17.3 us  [to_corners(): got.append(lax.ppermute(band, (*WIDE, 'narrow'), pairs))]
    all_to_all x2, starting transfers between devices: 28.8 us -> 25.6 us  [chip_exchange(): lax.all_to_all(chunks.reshape(-1, LANES), CHIPS, 0, 0, tiled=True)]
    unnamed x16 -> x28, local copies, waits for them, and re-layouts: 4.66 us -> 6.31 us
    ppermute x2 -> x4, starting transfers between devices: 3.31 us -> 4.88 us  [to_corners(): got.append(lax.ppermute(band, (*WIDE, 'narrow'), pairs))]
    all_to_all x2, waiting for transfers between devices: 8.47 us -> 9.69 us  [chip_exchange(): lax.all_to_all(chunks.reshape(-1, LANES), CHIPS, 0, 0, tiled=True)]
  transfers between devices with their start and end apart: 12 -> 14, of which waited for: 6 -> 6; matrix products, arithmetic and copies ran while one was open for 2% -> 1% of each run, Pallas kernels for 2% -> 2%
where the time goes in v8:
time: 105 us; the launch traced here: 104 us
  starting transfers between devices  37.8 us (36%)
  waiting for transfers between devices  30.5 us (29%)
  Pallas kernels  24.1 us (23%)
  local copies, waits for them, and re-layouts  7.88 us (8%)
  other arithmetic  1.85 us (2%)
  between operations  1.48 us (1%)
    all_to_all x2, starting transfers between devices, chip_exchange(): lax.all_to_all(chunks.reshape(-1, LANES), CHIPS, 0, 0, tiled=True)  25.6 us
    pallas_call x1, Pallas kernels, positions_call(): pl.pallas_call(functools.partial(positions_kernel, sides), out_shape=(sha...  18 us
    ppermute x4, waiting for transfers between devices, to_corners(): got.append(lax.ppermute(band, (*WIDE, 'narrow'), pairs))  17.3 us
    all_to_all x2, waiting for transfers between devices, chip_exchange(): lax.all_to_all(chunks.reshape(-1, LANES), CHIPS, 0, 0, tiled=True)  9.69 us
    ppermute x8, starting transfers between devices, swap(): return lax.ppermute(x, axis, pairs)  7.24 us
    unnamed x28, local copies, waits for them, and re-layouts  6.31 us
    ppermute x4, starting transfers between devices, to_corners(): got.append(lax.ppermute(band, (*WIDE, 'narrow'), pairs))  4.88 us
    ppermute x8, waiting for transfers between devices, swap(): return lax.ppermute(x, axis, pairs)  3.54 us
  transfers between devices with their start and end apart: 14, of which 6 were waited for; matrix products, arithmetic and copies ran while one was open for 1% of the time, Pallas kernels for 2%

profile of v8, /device:TPU:0, one launch (start us, length us, event | category | flops | bytes accessed | tf_op | source)
XLA Modules:
  0.0 103.6 jit_solution(5663772639169431257)
XLA Ops:
  1.3 0.7 concatenate.9.place.refs_0_
  2.0 1.2 %copy-done = f32[2,256,512]{2,1,0:T(8,128)S(1)} copy-done((f32[2,256,512]{2,1,0:T(8,128)S(1)}, f32[2,256,512]{2,1,0:T(8,128)}, u32[]{:S(2)}) %copy-start) | copy-done | bytes 1048600
  3.3 0.8 pack.1
  4.0 0.5 collective-permute-start
  4.6 0.7 collective-permute-start.1
  5.2 2.6 %collective-permute-start.2 = (f32[2,264,128]{2,1,0:T(8,128)S(1)}, f32[2,264,128]{2,1,0:T(8,128)S(1)}, u32[]{:S(2)}, u32[]{:S(2)}) collective-permute-start(f32[2,264,128]{2,1,0:T(8,128)S(1)} %get-tuple-element.23), channel_id=1, source_target_pairs={{0,1},{1,0},{2,3},{3,2},{4,5},{5,4},{6,7},{7,6},{8,9},{9,8},{10,11... | collective-permute-start | bytes 811016 | tf_op jit(solution)/shard_map/ppermute | solution.py:531
  7.8 2.6 %collective-permute-start.3 = (f32[2,136,128]{2,1,0:T(8,128)S(1)}, f32[2,136,128]{2,1,0:T(8,128)S(1)}, u32[]{:S(2)}, u32[]{:S(2)}) collective-permute-start(f32[2,136,128]{2,1,0:T(8,128)S(1)} %get-tuple-element.24), channel_id=1, source_target_pairs={{0,3},{2,1},{1,2},{3,0},{4,7},{6,5},{5,6},{7,4},{8,11},{10,9},{9,1... | collective-permute-start | bytes 417800 | tf_op jit(solution)/shard_map/ppermute | solution.py:557
  10.5 0.7 collective-permute-start.4
  11.2 8.5 %collective-permute-done.3.refs_5_ = f32[2,136,128]{2,1,0:T(8,128)S(1)} collective-permute-done((f32[2,136,128]{2,1,0:T(8,128)S(1)}, f32[2,136,128]{2,1,0:T(8,128)S(1)}, u32[]{:S(2)}, u32[]{:S(2)}) %collective-permute-start.3) | collective-permute-done | bytes 139296 | tf_op jit(solution)/shard_map/ppermute | solution.py:557
  19.7 0.0 collective-permute-done.4.refs_6_
  19.7 0.0 collective-permute-done.2.refs_4_
  19.7 0.0 collective-permute-done.refs_2_
  19.7 0.0 collective-permute-done.1.refs_3_
  19.7 0.0 copy-start.2
  19.7 1.0 copy-done.2
  20.7 18.0 %positions.1 = (f32[2,256,512]{2,1,0:T(8,128)}, f32[2,128,512]{2,1,0:T(8,128)S(1)}, f32[2,128,512]{2,1,0:T(8,128)S(1)}, f32[5,8,128]{2,1,0:T(8,128)S(1)}, f32[2,...) custom-call(s32[19]{0:T(128)S(1)} %concatenate.9.place.refs_0_, ...), custom_call_target="tpu_custom_call" | custom-call | flops 12884901888 | bytes 16000000 | tf_op jit(solution)/shard_map/positions/pallas_call | solution.py:418
  38.8 0.6 copy-done.13
  39.4 0.0 copy-start.3
  39.5 0.1 collective-permute-start.5
  39.5 1.7 %collective-permute-done.5 = f32[768,128]{1,0:T(8,128)S(1)} collective-permute-done((f32[768,128]{1,0:T(8,128)S(1)}, f32[768,128]{1,0:T(8,128)S(1)}, u32[]{:S(2)}, u32[]{:S(2)}) %collective-permute-start.5) | collective-permute-done | bytes 393248 | tf_op jit(solution)/shard_map/ppermute | solution.py:531
  41.2 0.8 add.7
  42.1 0.0 copy-done.11
  42.1 15.6 %all-to-all-start = ((f32[16,48,128]{2,1,0:T(8,128)}), f32[16,48,128]{2,1,0:T(8,128)}, u32[]{:S(2)}, u32[]{:S(2)}) async-start(f32[16,48,128]{2,1,0:T(8,128)} %bitcast.7), calls=%async_computation | async-start | bytes 786432 | tf_op jit(solution)/shard_map/all_to_all | solution.py:562
  57.7 0.1 collective-permute-start.6
  57.8 1.5 %collective-permute-start.7 = (f32[2,128,512]{2,1,0:T(8,128)}, f32[2,128,512]{2,1,0:T(8,128)}, u32[]{:S(2)}, u32[]{:S(2)}) collective-permute-start(f32[2,128,512]{2,1,0:T(8,128)} %copy-done.9), channel_id=1, source_target_pairs={{2,4},{4,2},{6,8},{8,6},{10,12},{12,10},{14,16},{16,14},{18,20},{2... | collective-permute-start | bytes 1572872 | tf_op jit(solution)/shard_map/ppermute | solution.py:531
  59.2 1.8 %collective-permute-start.8 = (f32[2,256,128]{2,1,0:T(8,128)}, f32[2,256,128]{2,1,0:T(8,128)S(1)}, u32[]{:S(2)}, u32[]{:S(2)}) collective-permute-start(f32[2,256,128]{2,1,0:T(8,128)} %copy-done.11), channel_id=1, source_target_pairs={{0,1},{1,0},{2,3},{3,2},{4,5},{5,4},{6,7},{7,6},{8,9},{9,8},{10,11... | collective-permute-start | bytes 786440 | tf_op jit(solution)/shard_map/ppermute | solution.py:531
  61.1 0.0 copy-done.3
  61.1 2.1 %cover.1 = (f32[256,512]{1,0:T(8,128)S(1)}, f32[8,128]{1,0:T(8,128)S(1)}) custom-call(s32[19]{0:T(128)S(1)} %concatenate.9.place.refs_0_, s32[6,32]{1,0:T(8,128)S(1)} %fusion.1.info, f32[2,256,256]{2,1,0:T(8,128)S(1)} %copy-done.3), custom_call_target="tpu_custom_call" | custom-call | flops 4000000 | bytes 8000000 | tf_op jit(solution)/shard_map/cover/pallas_call | solution.py:119
  63.2 0.0 copy-start.5
  63.2 0.8 copy-done.5
  64.0 6.7 %all-to-all-done = f32[16,48,128]{2,1,0:T(8,128)} async-done(((f32[16,48,128]{2,1,0:T(8,128)}), f32[16,48,128]{2,1,0:T(8,128)}, u32[]{:S(2)}, u32[]{:S(2)}) %all-to-all-start) | async-done | bytes 393248 | tf_op jit(solution)/shard_map/all_to_all | solution.py:562
  70.7 1.0 reduce_sum.9
  71.8 0.0 collective-permute-done.8.refs_6_
  71.8 0.0 collective-permute-done.6.refs_4_
  71.8 0.0 collective-permute-done.7.refs_5_
  71.8 0.8 broadcast_in_dim.3
  72.6 10.0 %all-to-all-start.1 = ((f32[16,56,128]{2,1,0:T(8,128)}), f32[16,56,128]{2,1,0:T(8,128)S(1)}, u32[]{:S(2)}, u32[]{:S(2)}) async-start(f32[16,56,128]{2,1,0:T(8,128)} %broadcast_in_dim.3), calls=%async_computation.1 | async-start | bytes 917504 | tf_op jit(solution)/shard_map/all_to_all | solution.py:562
  82.7 0.9 collective-permute-start.9
  83.6 0.7 collective-permute-start.10
  84.2 8.8 %collective-permute-done.9.refs_7_ = f32[2,128,128]{2,1,0:T(8,128)S(1)} collective-permute-done((f32[2,128,128]{2,1,0:T(8,128)}, f32[2,128,128]{2,1,0:T(8,128)S(1)}, u32[]{:S(2)}, u32[]{:S(2)}) %collective-permute-start.9) | collective-permute-done | bytes 131104 | tf_op jit(solution)/shard_map/ppermute | solution.py:557
  93.0 0.0 collective-permute-done.10.refs_8_
  93.0 0.6 copy-done.7
  93.7 3.0 %all-to-all-done.1.refs_9_ = f32[16,56,128]{2,1,0:T(8,128)S(1)} async-done(((f32[16,56,128]{2,1,0:T(8,128)}), f32[16,56,128]{2,1,0:T(8,128)S(1)}, u32[]{:S(2)}, u32[]{:S(2)}) %all-to-all-start.1) | async-done | bytes 458784 | tf_op jit(solution)/shard_map/all_to_all | solution.py:562
  96.6 0.0 collective-permute-start.11
  96.6 1.8 %collective-permute-done.11.refs_10_ = f32[16,56,128]{2,1,0:T(8,128)S(1)} collective-permute-done((f32[16,56,128]{2,1,0:T(8,128)S(1)}, f32[16,56,128]{2,1,0:T(8,128)S(1)}, u32[]{:S(2)}, u32[]{:S(2)}) %collective-permute-start.11) | collective-permute-done | bytes 458784 | tf_op jit(solution)/shard_map/ppermute | solution.py:531
  98.5 1.0 %copy-done.6 = f32[256,512]{1,0:T(8,128)S(1)} copy-done((f32[256,512]{1,0:T(8,128)S(1)}, f32[256,512]{1,0:T(8,128)}, u32[]{:S(2)}) %copy-start.6) | copy-done | bytes 524312
  99.5 0.9 copy-done.8
  100.4 3.2 %update.1 = (f32[2,256,512]{2,1,0:T(8,128)}, f32[2,256,256]{2,1,0:T(8,128)}) custom-call(s32[19]{0:T(128)S(1)} %concatenate.9.place.refs_0_, f32[2,256,512]{2,1,0:T(8,128)S(1)} %copy-done.1, f32[2,256,512]{2,1,0:T(8,128)S(1)} %copy-done.4, f32[256,512]{1,0:T(8,128)S(1)} %copy-done.6, f32[2,128,512]{2,1,0:T(8,128)} %collective-permute-done.6.refs_4_, ...), custom_call_target="tpu_custom_call" | custom-call | tf_op jit(solution)/shard_map/update/pallas_call | solution.py:511
  (20 shorter events, 0.1 us)
Async XLA Ops:
  2.0 1.2 %copy-start = (f32[2,256,512]{2,1,0:T(8,128)S(1)}, f32[2,256,512]{2,1,0:T(8,128)}, u32[]{:S(2)}) copy-start(f32[2,256,512]{2,1,0:T(8,128)} %refs_1_.3) | copy-start | bytes 3145732
  4.0 15.6 %collective-permute-start = (f32[2,136,512]{2,1,0:T(8,128)S(1)}, f32[2,136,512]{2,1,0:T(8,128)S(1)}, u32[]{:S(2)}, u32[]{:S(2)}) collective-permute-start(f32[2,136,512]{2,1,0:T(8,128)S(1)} %get-tuple-element.21), channel_id=1, source_target_pairs={{0,2},{2,0},{1,3},{3,1},{4,6},{6,4},{5,7},{7,5},{8,10},{10,8},{9,1... | collective-permute-start | bytes 1671176 | tf_op jit(solution)/shard_map/ppermute | solution.py:531
  4.6 15.1 %collective-permute-start.1 = (f32[2,136,512]{2,1,0:T(8,128)S(1)}, f32[2,136,512]{2,1,0:T(8,128)S(1)}, u32[]{:S(2)}, u32[]{:S(2)}) collective-permute-start(f32[2,136,512]{2,1,0:T(8,128)S(1)} %get-tuple-element.22), channel_id=1, source_target_pairs={{2,4},{4,2},{6,8},{8,6},{10,12},{12,10},{14,16},{16,14},{18,20},{2... | collective-permute-start | bytes 1671176 | tf_op jit(solution)/shard_map/ppermute | solution.py:531
  5.2 14.4 %collective-permute-start.2 = (f32[2,264,128]{2,1,0:T(8,128)S(1)}, f32[2,264,128]{2,1,0:T(8,128)S(1)}, u32[]{:S(2)}, u32[]{:S(2)}) collective-permute-start(f32[2,264,128]{2,1,0:T(8,128)S(1)} %get-tuple-element.23), channel_id=1, source_target_pairs={{0,1},{1,0},{2,3},{3,2},{4,5},{5,4},{6,7},{7,6},{8,9},{9,8},{10,11... | collective-permute-start | bytes 811016 | tf_op jit(solution)/shard_map/ppermute | solution.py:531
  7.8 11.8 %collective-permute-start.3 = (f32[2,136,128]{2,1,0:T(8,128)S(1)}, f32[2,136,128]{2,1,0:T(8,128)S(1)}, u32[]{:S(2)}, u32[]{:S(2)}) collective-permute-start(f32[2,136,128]{2,1,0:T(8,128)S(1)} %get-tuple-element.24), channel_id=1, source_target_pairs={{0,3},{2,1},{1,2},{3,0},{4,7},{6,5},{5,6},{7,4},{8,11},{10,9},{9,1... | collective-permute-start | bytes 417800 | tf_op jit(solution)/shard_map/ppermute | solution.py:557
  10.5 9.2 %collective-permute-start.4 = (f32[2,136,128]{2,1,0:T(8,128)S(1)}, f32[2,136,128]{2,1,0:T(8,128)S(1)}, u32[]{:S(2)}, u32[]{:S(2)}) collective-permute-start(f32[2,136,128]{2,1,0:T(8,128)S(1)} %get-tuple-element.25), channel_id=1, source_target_pairs={{2,5},{4,3},{3,4},{5,2},{6,9},{8,7},{7,8},{9,6},{10,13},{12,11},{1... | collective-permute-start | bytes 417800 | tf_op jit(solution)/shard_map/ppermute | solution.py:557
  19.7 1.0 %copy-start.2 = (f32[2,256,256]{2,1,0:T(8,128)S(1)}, f32[2,256,256]{2,1,0:T(8,128)}, u32[]{:S(2)}) copy-start(f32[2,256,256]{2,1,0:T(8,128)} %refs_11_.1) | copy-start | bytes 1572868
  38.8 0.6 copy-start.13
  39.4 2.6 %copy-start.9 = (f32[2,128,512]{2,1,0:T(8,128)}, f32[2,128,512]{2,1,0:T(8,128)S(1)}, u32[]{:S(2)}) copy-start(f32[2,128,512]{2,1,0:T(8,128)S(1)} %get-tuple-element.33) | copy-start | bytes 1572868
  39.4 2.6 %copy-start.10 = (f32[2,128,512]{2,1,0:T(8,128)}, f32[2,128,512]{2,1,0:T(8,128)S(1)}, u32[]{:S(2)}) copy-start(f32[2,128,512]{2,1,0:T(8,128)S(1)} %get-tuple-element.32) | copy-start | bytes 1572868
  39.4 2.6 %copy-start.11 = (f32[2,256,128]{2,1,0:T(8,128)}, f32[2,256,128]{2,1,0:T(8,128)S(1)}, u32[]{:S(2)}) copy-start(f32[2,256,128]{2,1,0:T(8,128)S(1)} %get-tuple-element.34) | copy-start | bytes 786436
  39.4 2.6 %copy-start.12 = (f32[2,128,128]{2,1,0:T(8,128)}, f32[2,128,128]{2,1,0:T(8,128)S(1)}, u32[]{:S(2)}) copy-start(f32[2,128,128]{2,1,0:T(8,128)S(1)} %get-tuple-element.36) | copy-start | bytes 393220
  39.4 21.6 %copy-start.3 = (f32[2,256,256]{2,1,0:T(8,128)S(1)}, f32[2,256,256]{2,1,0:T(8,128)}, u32[]{:S(2)}) copy-start(f32[2,256,256]{2,1,0:T(8,128)} %refs_11_.1) | copy-start | bytes 1572868
  39.5 1.8 %collective-permute-start.5 = (f32[768,128]{1,0:T(8,128)S(1)}, f32[768,128]{1,0:T(8,128)S(1)}, u32[]{:S(2)}, u32[]{:S(2)}) collective-permute-start(f32[768,128]{1,0:T(8,128)S(1)} %get-tuple-element.29), channel_id=1, source_target_pairs={{0,2},{2,0},{1,3},{3,1},{4,6},{6,4},{5,7},{7,5},{8,10},{10,8},{9,1... | collective-permute-start | bytes 1179656 | tf_op jit(solution)/shard_map/ppermute | solution.py:531
  41.2 57.2 %copy-start.1 = (f32[2,256,512]{2,1,0:T(8,128)S(1)}, f32[2,256,512]{2,1,0:T(8,128)}, u32[]{:S(2)}) copy-start(f32[2,256,512]{2,1,0:T(8,128)} %refs_1_.3) | copy-start | bytes 3145732
  41.2 57.2 %copy-start.4 = (f32[2,256,512]{2,1,0:T(8,128)S(1)}, f32[2,256,512]{2,1,0:T(8,128)}, u32[]{:S(2)}) copy-start(f32[2,256,512]{2,1,0:T(8,128)} %get-tuple-element.26.refs_2_) | copy-start | bytes 3145732
  42.1 28.7 %all-to-all-start = ((f32[16,48,128]{2,1,0:T(8,128)}), f32[16,48,128]{2,1,0:T(8,128)}, u32[]{:S(2)}, u32[]{:S(2)}) async-start(f32[16,48,128]{2,1,0:T(8,128)} %bitcast.7), calls=%async_computation | async-start | bytes 786432 | tf_op jit(solution)/shard_map/all_to_all | solution.py:562
  57.7 14.1 %collective-permute-start.6 = (f32[2,128,512]{2,1,0:T(8,128)}, f32[2,128,512]{2,1,0:T(8,128)}, u32[]{:S(2)}, u32[]{:S(2)}) collective-permute-start(f32[2,128,512]{2,1,0:T(8,128)} %copy-done.10), channel_id=1, source_target_pairs={{0,2},{2,0},{1,3},{3,1},{4,6},{6,4},{5,7},{7,5},{8,10},{10,8},{9,1... | collective-permute-start | bytes 1572872 | tf_op jit(solution)/shard_map/ppermute | solution.py:531
  57.8 14.0 %collective-permute-start.7 = (f32[2,128,512]{2,1,0:T(8,128)}, f32[2,128,512]{2,1,0:T(8,128)}, u32[]{:S(2)}, u32[]{:S(2)}) collective-permute-start(f32[2,128,512]{2,1,0:T(8,128)} %copy-done.9), channel_id=1, source_target_pairs={{2,4},{4,2},{6,8},{8,6},{10,12},{12,10},{14,16},{16,14},{18,20},{2... | collective-permute-start | bytes 1572872 | tf_op jit(solution)/shard_map/ppermute | solution.py:531
  59.2 12.5 %collective-permute-start.8 = (f32[2,256,128]{2,1,0:T(8,128)}, f32[2,256,128]{2,1,0:T(8,128)S(1)}, u32[]{:S(2)}, u32[]{:S(2)}) collective-permute-start(f32[2,256,128]{2,1,0:T(8,128)} %copy-done.11), channel_id=1, source_target_pairs={{0,1},{1,0},{2,3},{3,2},{4,5},{5,4},{6,7},{7,6},{8,9},{9,8},{10,11... | collective-permute-start | bytes 786440 | tf_op jit(solution)/shard_map/ppermute | solution.py:531
  63.2 0.8 copy-start.5
  72.6 24.0 %all-to-all-start.1 = ((f32[16,56,128]{2,1,0:T(8,128)}), f32[16,56,128]{2,1,0:T(8,128)S(1)}, u32[]{:S(2)}, u32[]{:S(2)}) async-start(f32[16,56,128]{2,1,0:T(8,128)} %broadcast_in_dim.3), calls=%async_computation.1 | async-start | bytes 917504 | tf_op jit(solution)/shard_map/all_to_all | solution.py:562
  82.7 10.4 %collective-permute-start.9 = (f32[2,128,128]{2,1,0:T(8,128)}, f32[2,128,128]{2,1,0:T(8,128)S(1)}, u32[]{:S(2)}, u32[]{:S(2)}) collective-permute-start(f32[2,128,128]{2,1,0:T(8,128)} %copy-done.13), channel_id=1, source_target_pairs={{0,3},{2,1},{1,2},{3,0},{4,7},{6,5},{5,6},{7,4},{8,11},{10,9},{9,1... | collective-permute-start | bytes 393224 | tf_op jit(solution)/shard_map/ppermute | solution.py:557
  83.6 9.5 %collective-permute-start.10 = (f32[2,128,128]{2,1,0:T(8,128)}, f32[2,128,128]{2,1,0:T(8,128)S(1)}, u32[]{:S(2)}, u32[]{:S(2)}) collective-permute-start(f32[2,128,128]{2,1,0:T(8,128)} %copy-done.12), channel_id=1, source_target_pairs={{2,5},{4,3},{3,4},{5,2},{6,9},{8,7},{7,8},{9,6},{10,13},{12,11},{1... | collective-permute-start | bytes 393224 | tf_op jit(solution)/shard_map/ppermute | solution.py:557
  93.0 0.6 copy-start.7
  96.6 1.8 %collective-permute-start.11 = (f32[16,56,128]{2,1,0:T(8,128)S(1)}, f32[16,56,128]{2,1,0:T(8,128)S(1)}, u32[]{:S(2)}, u32[]{:S(2)}) collective-permute-start(f32[16,56,128]{2,1,0:T(8,128)S(1)} %all-to-all-done.1.refs_9_), channel_id=1, source_target_pairs={{0,2},{2,0},{1,3},{3,1},{4,6},{6,4},{5,7},{7,5},{8,10},{10,8},{9,1... | collective-permute-start | bytes 1376264 | tf_op jit(solution)/shard_map/ppermute | solution.py:531
  98.5 1.0 %copy-start.6 = (f32[256,512]{1,0:T(8,128)S(1)}, f32[256,512]{1,0:T(8,128)}, u32[]{:S(2)}) copy-start(f32[256,512]{1,0:T(8,128)} %copy-done.5) | copy-start | bytes 1572868
  99.5 0.9 copy-start.8

commit v9 on v8

--- a/solution.py
+++ b/solution.py
@@ -249,11 +249,14 @@
     def level_copy(i):
         return pltpu.make_async_copy(measured.at[0, 0, i], levels.at[i], level_sems.at[i])
 
-    def start_level(i, carry):
-        level_copy(i).start()
-        return carry
-
-    lax.fori_loop(0, live_slots, start_level, 0)
+    def start_levels(first):
+        for w in range(WAYS):
+
+            @pl.when(first + w < live_slots)
+            def _():
+                level_copy(first + w).start()
+
+    start_levels(0)
     if sides == 1:
         for ch in range(2):
             ext[ch * blocks + blocks - 1 - side_blocks[0]] = jnp.zeros((ext_rows, LANES), F32)
@@ -364,6 +367,8 @@
             @pl.when(first + w < live_slots)
             def _():
                 level_copy(slots[w]).wait()
+
+        start_levels(first + WAYS)
 
         @pl.when(i == 0)
         def _():
@@ -514,7 +519,7 @@
         in_specs=[SMEM] + [VMEM] * (8 + 3 * sides),
         out_specs=(VMEM, VMEM),
         scratch_shapes=[pltpu.VMEM(tile.shape, F32)],
-        compiler_params=pltpu.CompilerParams(vmem_limit_bytes=16 << 20),
+        compiler_params=pltpu.CompilerParams(vmem_limit_bytes=51 << 20),
         name="update",
     )(place, tile, middle, cover, near, far_side, *side_in, *ends, own, other, probe)
 

time: 105 us -> 102 us (0.971); the launches traced: 104 us -> 102 us
  local copies, waits for them, and re-layouts: 7.88 us -> 3.83 us
  waiting for transfers between devices: 30.5 us -> 32.1 us
    all_to_all x2, starting transfers between devices: 25.6 us -> 21.2 us  [chip_exchange(): lax.all_to_all(chunks.reshape(-1, LANES), CHIPS, 0, 0, tiled=True)]
    ppermute x8, starting transfers between devices: 7.24 us -> 11.4 us  [swap(): return lax.ppermute(x, axis, pairs)]
    unnamed x28 -> x6, local copies, waits for them, and re-layouts: 6.31 us -> 2.27 us
    all_to_all x2, waiting for transfers between devices: 9.69 us -> 12.7 us  [chip_exchange(): lax.all_to_all(chunks.reshape(-1, LANES), CHIPS, 0, 0, tiled=True)]
    ppermute x4, waiting for transfers between devices: 17.3 us -> 16.2 us  [to_corners(): got.append(lax.ppermute(band, (*WIDE, 'narrow'), pairs))]
where the time goes in v9:
time: 102 us
  starting transfers between devices  37.7 us (37%)
  waiting for transfers between devices  32.1 us (31%)
  Pallas kernels  25 us (25%)
  local copies, waits for them, and re-layouts  3.83 us (4%)
  other arithmetic  1.83 us (2%)
  between operations  1.44 us (1%)
    all_to_all x2, starting transfers between devices, chip_exchange(): lax.all_to_all(chunks.reshape(-1, LANES), CHIPS, 0, 0, tiled=True)  21.2 us
    pallas_call x1, Pallas kernels, positions_call(): pl.pallas_call(functools.partial(positions_kernel, sides), out_shape=(sha...  18 us
    ppermute x4, waiting for transfers between devices, to_corners(): got.append(lax.ppermute(band, (*WIDE, 'narrow'), pairs))  16.2 us
    all_to_all x2, waiting for transfers between devices, chip_exchange(): lax.all_to_all(chunks.reshape(-1, LANES), CHIPS, 0, 0, tiled=True)  12.7 us
    ppermute x8, starting transfers between devices, swap(): return lax.ppermute(x, axis, pairs)  11.4 us
    ppermute x4, starting transfers between devices, to_corners(): got.append(lax.ppermute(band, (*WIDE, 'narrow'), pairs))  5.03 us
    pallas_call x1, Pallas kernels, update_call(): pl.pallas_call(functools.partial(update_kernel, sides), out_shape=(jax.Sh...  3.71 us
    ppermute x8, waiting for transfers between devices, swap(): return lax.ppermute(x, axis, pairs)  3.18 us
  transfers between devices with their start and end apart: 14, of which 6 were waited for; matrix products, arithmetic and copies ran while one was open for 1% of the time, Pallas kernels for 2%

profile of v9, /device:TPU:0, one launch (start us, length us, event | category | flops | bytes accessed | tf_op | source)
XLA Modules:
  0.0 101.8 jit_solution(11210269253305292199)
XLA Ops:
  1.3 0.7 concatenate.9.place.refs_0_
  2.0 0.0 copy-start
  2.0 1.2 %copy-done = f32[2,256,512]{2,1,0:T(8,128)S(1)} copy-done((f32[2,256,512]{2,1,0:T(8,128)S(1)}, f32[2,256,512]{2,1,0:T(8,128)}, u32[]{:S(2)}) %copy-start) | copy-done | bytes 1048600
  3.3 0.8 pack.1
  4.0 0.5 collective-permute-start
  4.6 0.7 collective-permute-start.1
  5.2 2.6 %collective-permute-start.2 = (f32[2,264,128]{2,1,0:T(8,128)S(1)}, f32[2,264,128]{2,1,0:T(8,128)S(1)}, u32[]{:S(2)}, u32[]{:S(2)}) collective-permute-start(f32[2,264,128]{2,1,0:T(8,128)S(1)} %get-tuple-element.23), channel_id=1, source_target_pairs={{0,1},{1,0},{2,3},{3,2},{4,5},{5,4},{6,7},{7,6},{8,9},{9,8},{10,11... | collective-permute-start | bytes 811016 | tf_op jit(solution)/shard_map/ppermute | solution.py:536
  7.8 2.6 %collective-permute-start.3 = (f32[2,136,128]{2,1,0:T(8,128)S(1)}, f32[2,136,128]{2,1,0:T(8,128)S(1)}, u32[]{:S(2)}, u32[]{:S(2)}) collective-permute-start(f32[2,136,128]{2,1,0:T(8,128)S(1)} %get-tuple-element.24), channel_id=1, source_target_pairs={{0,3},{2,1},{1,2},{3,0},{4,7},{6,5},{5,6},{7,4},{8,11},{10,9},{9,1... | collective-permute-start | bytes 417800 | tf_op jit(solution)/shard_map/ppermute | solution.py:562
  10.5 0.7 collective-permute-start.4
  11.2 8.5 %collective-permute-done.3.refs_5_ = f32[2,136,128]{2,1,0:T(8,128)S(1)} collective-permute-done((f32[2,136,128]{2,1,0:T(8,128)S(1)}, f32[2,136,128]{2,1,0:T(8,128)S(1)}, u32[]{:S(2)}, u32[]{:S(2)}) %collective-permute-start.3) | collective-permute-done | bytes 139296 | tf_op jit(solution)/shard_map/ppermute | solution.py:562
  19.7 0.0 collective-permute-done.4.refs_6_
  19.7 0.0 collective-permute-done.2.refs_4_
  19.7 0.0 collective-permute-done.refs_2_
  19.7 0.0 collective-permute-done.1.refs_3_
  19.7 0.0 copy-start.1
  19.7 1.0 %copy-done.1 = f32[2,256,256]{2,1,0:T(8,128)S(1)} copy-done((f32[2,256,256]{2,1,0:T(8,128)S(1)}, f32[2,256,256]{2,1,0:T(8,128)}, u32[]{:S(2)}) %copy-start.1) | copy-done | bytes 524312
  20.7 18.0 %positions.1 = (f32[2,256,512]{2,1,0:T(8,128)}, f32[2,128,512]{2,1,0:T(8,128)}, f32[2,128,512]{2,1,0:T(8,128)S(1)}, f32[5,8,128]{2,1,0:T(8,128)S(1)}, f32[2,256,...) custom-call(s32[19]{0:T(128)S(1)} %concatenate.9.place.refs_0_, ...), custom_call_target="tpu_custom_call" | custom-call | flops 12884901888 | bytes 16000000 | tf_op jit(solution)/shard_map/positions/pallas_call | solution.py:423
  38.7 0.0 copy-start.2
  38.7 5.0 %collective-permute-start.5 = (f32[768,128]{1,0:T(8,128)S(1)}, f32[768,128]{1,0:T(8,128)S(1)}, u32[]{:S(2)}, u32[]{:S(2)}) collective-permute-start(f32[768,128]{1,0:T(8,128)S(1)} %get-tuple-element.29), channel_id=1, source_target_pairs={{0,2},{2,0},{1,3},{3,1},{4,6},{6,4},{5,7},{7,5},{8,10},{10,8},{9,1... | collective-permute-start | bytes 1179656 | tf_op jit(solution)/shard_map/ppermute | solution.py:536
  43.7 1.3 %collective-permute-done.5 = f32[768,128]{1,0:T(8,128)S(1)} collective-permute-done((f32[768,128]{1,0:T(8,128)S(1)}, f32[768,128]{1,0:T(8,128)S(1)}, u32[]{:S(2)}, u32[]{:S(2)}) %collective-permute-start.5) | collective-permute-done | bytes 393248 | tf_op jit(solution)/shard_map/ppermute | solution.py:536
  45.1 0.8 add.7
  45.9 11.5 %all-to-all-start = ((f32[16,48,128]{2,1,0:T(8,128)}), f32[16,48,128]{2,1,0:T(8,128)}, u32[]{:S(2)}, u32[]{:S(2)}) async-start(f32[16,48,128]{2,1,0:T(8,128)} %bitcast.7), calls=%async_computation | async-start | bytes 786432 | tf_op jit(solution)/shard_map/all_to_all | solution.py:567
  57.4 0.1 collective-permute-start.6
  57.5 0.7 collective-permute-start.7
  58.2 1.8 %collective-permute-start.8 = (f32[2,256,128]{2,1,0:T(8,128)S(1)}, f32[2,256,128]{2,1,0:T(8,128)S(1)}, u32[]{:S(2)}, u32[]{:S(2)}) collective-permute-start(f32[2,256,128]{2,1,0:T(8,128)S(1)} %get-tuple-element.34), channel_id=1, source_target_pairs={{0,1},{1,0},{2,3},{3,2},{4,5},{5,4},{6,7},{7,6},{8,9},{9,8},{10,11... | collective-permute-start | bytes 786440 | tf_op jit(solution)/shard_map/ppermute | solution.py:536
  60.1 0.0 copy-done.2
  60.1 2.5 %cover.1 = (f32[256,512]{1,0:T(8,128)S(1)}, f32[8,128]{1,0:T(8,128)S(1)}) custom-call(s32[19]{0:T(128)S(1)} %concatenate.9.place.refs_0_, s32[6,32]{1,0:T(8,128)S(1)} %fusion.1.info, f32[2,256,256]{2,1,0:T(8,128)S(1)} %copy-done.2), custom_call_target="tpu_custom_call" | custom-call | flops 4000000 | bytes 8000000 | tf_op jit(solution)/shard_map/cover/pallas_call | solution.py:119
  62.6 8.0 %all-to-all-done = f32[16,48,128]{2,1,0:T(8,128)} async-done(((f32[16,48,128]{2,1,0:T(8,128)}), f32[16,48,128]{2,1,0:T(8,128)}, u32[]{:S(2)}, u32[]{:S(2)}) %all-to-all-start) | async-done | bytes 393248 | tf_op jit(solution)/shard_map/all_to_all | solution.py:567
  70.6 1.0 %reduce_sum.9 = f32[48,128]{1,0:T(8,128)S(1)} reduce(f32[16,48,128]{2,1,0:T(8,128)} %all-to-all-done, f32[]{:T(128)} %constant.19.clone.1), dimensions={0}, to_apply=%region_0.0 | reduce | flops 92160 | bytes 417796 | tf_op jit(solution)/shard_map/reduce_sum | solution.py:603
  71.6 0.0 collective-permute-done.8.refs_6_
  71.6 0.0 collective-permute-done.6.refs_4_
  71.6 0.0 collective-permute-done.7.refs_5_
  71.6 0.8 broadcast_in_dim.3
  72.4 9.7 %all-to-all-start.1 = ((f32[16,56,128]{2,1,0:T(8,128)}), f32[16,56,128]{2,1,0:T(8,128)S(1)}, u32[]{:S(2)}, u32[]{:S(2)}) async-start(f32[16,56,128]{2,1,0:T(8,128)} %broadcast_in_dim.3), calls=%async_computation.1 | async-start | bytes 917504 | tf_op jit(solution)/shard_map/all_to_all | solution.py:567
  82.2 1.1 %collective-permute-start.9 = (f32[2,128,128]{2,1,0:T(8,128)}, f32[2,128,128]{2,1,0:T(8,128)S(1)}, u32[]{:S(2)}, u32[]{:S(2)}) collective-permute-start(f32[2,128,128]{2,1,0:T(8,128)} %get-tuple-element.35), channel_id=1, source_target_pairs={{0,3},{2,1},{1,2},{3,0},{4,7},{6,5},{5,6},{7,4},{8,11},{10,9},{9,1... | collective-permute-start | bytes 393224 | tf_op jit(solution)/shard_map/ppermute | solution.py:562
  83.2 0.7 collective-permute-start.10
  83.9 7.7 %collective-permute-done.9.refs_7_ = f32[2,128,128]{2,1,0:T(8,128)S(1)} collective-permute-done((f32[2,128,128]{2,1,0:T(8,128)}, f32[2,128,128]{2,1,0:T(8,128)S(1)}, u32[]{:S(2)}, u32[]{:S(2)}) %collective-permute-start.9) | collective-permute-done | bytes 131104 | tf_op jit(solution)/shard_map/ppermute | solution.py:562
  91.6 0.0 collective-permute-done.10.refs_8_
  91.6 4.7 %all-to-all-done.1.refs_9_ = f32[16,56,128]{2,1,0:T(8,128)S(1)} async-done(((f32[16,56,128]{2,1,0:T(8,128)}), f32[16,56,128]{2,1,0:T(8,128)S(1)}, u32[]{:S(2)}, u32[]{:S(2)}) %all-to-all-start.1) | async-done | bytes 458784 | tf_op jit(solution)/shard_map/all_to_all | solution.py:567
  96.3 0.0 collective-permute-start.11
  96.3 1.8 %collective-permute-done.11.refs_10_ = f32[16,56,128]{2,1,0:T(8,128)S(1)} collective-permute-done((f32[16,56,128]{2,1,0:T(8,128)S(1)}, f32[16,56,128]{2,1,0:T(8,128)S(1)}, u32[]{:S(2)}, u32[]{:S(2)}) %collective-permute-start.11) | collective-permute-done | bytes 458784 | tf_op jit(solution)/shard_map/ppermute | solution.py:536
  98.1 3.7 %update.1 = (f32[2,256,512]{2,1,0:T(8,128)}, f32[2,256,256]{2,1,0:T(8,128)}) custom-call(s32[19]{0:T(128)S(1)} %concatenate.9.place.refs_0_, f32[2,256,512]{2,1,0:T(8,128)} %refs_1_.3, f32[2,256,512]{2,1,0:T(8,128)} %get-tuple-element.26.refs_2_, f32[256,512]{1,0:T(8,128)S(1)} %get-tuple-element.31.refs_3_, ...), custom_call_target="tpu_custom_call" | custom-call | tf_op jit(solution)/shard_map/update/pallas_call | solution.py:516
  (4 shorter events, 0.0 us)
Async XLA Ops:
  2.0 1.2 %copy-start = (f32[2,256,512]{2,1,0:T(8,128)S(1)}, f32[2,256,512]{2,1,0:T(8,128)}, u32[]{:S(2)}) copy-start(f32[2,256,512]{2,1,0:T(8,128)} %refs_1_.3) | copy-start | bytes 3145732
  4.0 15.6 %collective-permute-start = (f32[2,136,512]{2,1,0:T(8,128)S(1)}, f32[2,136,512]{2,1,0:T(8,128)S(1)}, u32[]{:S(2)}, u32[]{:S(2)}) collective-permute-start(f32[2,136,512]{2,1,0:T(8,128)S(1)} %get-tuple-element.21), channel_id=1, source_target_pairs={{0,2},{2,0},{1,3},{3,1},{4,6},{6,4},{5,7},{7,5},{8,10},{10,8},{9,1... | collective-permute-start | bytes 1671176 | tf_op jit(solution)/shard_map/ppermute | solution.py:536
  4.6 15.1 %collective-permute-start.1 = (f32[2,136,512]{2,1,0:T(8,128)S(1)}, f32[2,136,512]{2,1,0:T(8,128)S(1)}, u32[]{:S(2)}, u32[]{:S(2)}) collective-permute-start(f32[2,136,512]{2,1,0:T(8,128)S(1)} %get-tuple-element.22), channel_id=1, source_target_pairs={{2,4},{4,2},{6,8},{8,6},{10,12},{12,10},{14,16},{16,14},{18,20},{2... | collective-permute-start | bytes 1671176 | tf_op jit(solution)/shard_map/ppermute | solution.py:536
  5.2 14.4 %collective-permute-start.2 = (f32[2,264,128]{2,1,0:T(8,128)S(1)}, f32[2,264,128]{2,1,0:T(8,128)S(1)}, u32[]{:S(2)}, u32[]{:S(2)}) collective-permute-start(f32[2,264,128]{2,1,0:T(8,128)S(1)} %get-tuple-element.23), channel_id=1, source_target_pairs={{0,1},{1,0},{2,3},{3,2},{4,5},{5,4},{6,7},{7,6},{8,9},{9,8},{10,11... | collective-permute-start | bytes 811016 | tf_op jit(solution)/shard_map/ppermute | solution.py:536
  7.8 11.8 %collective-permute-start.3 = (f32[2,136,128]{2,1,0:T(8,128)S(1)}, f32[2,136,128]{2,1,0:T(8,128)S(1)}, u32[]{:S(2)}, u32[]{:S(2)}) collective-permute-start(f32[2,136,128]{2,1,0:T(8,128)S(1)} %get-tuple-element.24), channel_id=1, source_target_pairs={{0,3},{2,1},{1,2},{3,0},{4,7},{6,5},{5,6},{7,4},{8,11},{10,9},{9,1... | collective-permute-start | bytes 417800 | tf_op jit(solution)/shard_map/ppermute | solution.py:562
  10.5 9.2 %collective-permute-start.4 = (f32[2,136,128]{2,1,0:T(8,128)S(1)}, f32[2,136,128]{2,1,0:T(8,128)S(1)}, u32[]{:S(2)}, u32[]{:S(2)}) collective-permute-start(f32[2,136,128]{2,1,0:T(8,128)S(1)} %get-tuple-element.25), channel_id=1, source_target_pairs={{2,5},{4,3},{3,4},{5,2},{6,9},{8,7},{7,8},{9,6},{10,13},{12,11},{1... | collective-permute-start | bytes 417800 | tf_op jit(solution)/shard_map/ppermute | solution.py:562
  19.7 1.0 %copy-start.1 = (f32[2,256,256]{2,1,0:T(8,128)S(1)}, f32[2,256,256]{2,1,0:T(8,128)}, u32[]{:S(2)}) copy-start(f32[2,256,256]{2,1,0:T(8,128)} %refs_11_.1) | copy-start | bytes 1572868
  38.7 21.3 %copy-start.2 = (f32[2,256,256]{2,1,0:T(8,128)S(1)}, f32[2,256,256]{2,1,0:T(8,128)}, u32[]{:S(2)}) copy-start(f32[2,256,256]{2,1,0:T(8,128)} %refs_11_.1) | copy-start | bytes 1572868
  38.7 6.3 %collective-permute-start.5 = (f32[768,128]{1,0:T(8,128)S(1)}, f32[768,128]{1,0:T(8,128)S(1)}, u32[]{:S(2)}, u32[]{:S(2)}) collective-permute-start(f32[768,128]{1,0:T(8,128)S(1)} %get-tuple-element.29), channel_id=1, source_target_pairs={{0,2},{2,0},{1,3},{3,1},{4,6},{6,4},{5,7},{7,5},{8,10},{10,8},{9,1... | collective-permute-start | bytes 1179656 | tf_op jit(solution)/shard_map/ppermute | solution.py:536
  45.9 24.7 %all-to-all-start = ((f32[16,48,128]{2,1,0:T(8,128)}), f32[16,48,128]{2,1,0:T(8,128)}, u32[]{:S(2)}, u32[]{:S(2)}) async-start(f32[16,48,128]{2,1,0:T(8,128)} %bitcast.7), calls=%async_computation | async-start | bytes 786432 | tf_op jit(solution)/shard_map/all_to_all | solution.py:567
  57.4 14.2 %collective-permute-start.6 = (f32[2,128,512]{2,1,0:T(8,128)}, f32[2,128,512]{2,1,0:T(8,128)S(1)}, u32[]{:S(2)}, u32[]{:S(2)}) collective-permute-start(f32[2,128,512]{2,1,0:T(8,128)} %get-tuple-element.32), channel_id=1, source_target_pairs={{0,2},{2,0},{1,3},{3,1},{4,6},{6,4},{5,7},{7,5},{8,10},{10,8},{9,1... | collective-permute-start | bytes 1572872 | tf_op jit(solution)/shard_map/ppermute | solution.py:536
  57.5 14.1 %collective-permute-start.7 = (f32[2,128,512]{2,1,0:T(8,128)S(1)}, f32[2,128,512]{2,1,0:T(8,128)S(1)}, u32[]{:S(2)}, u32[]{:S(2)}) collective-permute-start(f32[2,128,512]{2,1,0:T(8,128)S(1)} %get-tuple-element.33), channel_id=1, source_target_pairs={{2,4},{4,2},{6,8},{8,6},{10,12},{12,10},{14,16},{16,14},{18,20},{2... | collective-permute-start | bytes 1572872 | tf_op jit(solution)/shard_map/ppermute | solution.py:536
  58.2 13.4 %collective-permute-start.8 = (f32[2,256,128]{2,1,0:T(8,128)S(1)}, f32[2,256,128]{2,1,0:T(8,128)S(1)}, u32[]{:S(2)}, u32[]{:S(2)}) collective-permute-start(f32[2,256,128]{2,1,0:T(8,128)S(1)} %get-tuple-element.34), channel_id=1, source_target_pairs={{0,1},{1,0},{2,3},{3,2},{4,5},{5,4},{6,7},{7,6},{8,9},{9,8},{10,11... | collective-permute-start | bytes 786440 | tf_op jit(solution)/shard_map/ppermute | solution.py:536
  72.4 23.9 %all-to-all-start.1 = ((f32[16,56,128]{2,1,0:T(8,128)}), f32[16,56,128]{2,1,0:T(8,128)S(1)}, u32[]{:S(2)}, u32[]{:S(2)}) async-start(f32[16,56,128]{2,1,0:T(8,128)} %broadcast_in_dim.3), calls=%async_computation.1 | async-start | bytes 917504 | tf_op jit(solution)/shard_map/all_to_all | solution.py:567
  82.2 9.4 %collective-permute-start.9 = (f32[2,128,128]{2,1,0:T(8,128)}, f32[2,128,128]{2,1,0:T(8,128)S(1)}, u32[]{:S(2)}, u32[]{:S(2)}) collective-permute-start(f32[2,128,128]{2,1,0:T(8,128)} %get-tuple-element.35), channel_id=1, source_target_pairs={{0,3},{2,1},{1,2},{3,0},{4,7},{6,5},{5,6},{7,4},{8,11},{10,9},{9,1... | collective-permute-start | bytes 393224 | tf_op jit(solution)/shard_map/ppermute | solution.py:562
  83.2 8.4 %collective-permute-start.10 = (f32[2,128,128]{2,1,0:T(8,128)S(1)}, f32[2,128,128]{2,1,0:T(8,128)S(1)}, u32[]{:S(2)}, u32[]{:S(2)}) collective-permute-start(f32[2,128,128]{2,1,0:T(8,128)S(1)} %get-tuple-element.36), channel_id=1, source_target_pairs={{2,5},{4,3},{3,4},{5,2},{6,9},{8,7},{7,8},{9,6},{10,13},{12,11},{1... | collective-permute-start | bytes 393224 | tf_op jit(solution)/shard_map/ppermute | solution.py:562
  96.3 1.8 %collective-permute-start.11 = (f32[16,56,128]{2,1,0:T(8,128)S(1)}, f32[16,56,128]{2,1,0:T(8,128)S(1)}, u32[]{:S(2)}, u32[]{:S(2)}) collective-permute-start(f32[16,56,128]{2,1,0:T(8,128)S(1)} %all-to-all-done.1.refs_9_), channel_id=1, source_target_pairs={{0,2},{2,0},{1,3},{3,1},{4,6},{6,4},{5,7},{7,5},{8,10},{10,8},{9,1... | collective-permute-start | bytes 1376264 | tf_op jit(solution)/shard_map/ppermute | solution.py:536

commit v10 on v9

--- a/solution.py
+++ b/solution.py
@@ -189,8 +189,10 @@
 
 
 def positions_kernel(sides, *refs):
-    place, tile, near, far_side = refs[:4]
-    side_in, near_corners, far_corners = [refs[4 + i * sides : 4 + (i + 1) * sides] for i in range(3)]
+    place, tile, far_side, near = refs[0], refs[1], refs[2 + sides], refs[3 + 3 * sides]
+    far_corners, side_in, near_corners = [
+        refs[at : at + sides] for at in (2, 3 + sides, 3 + 2 * sides)
+    ]
     probe_in, measured, left_in, right_in = refs[4 + 3 * sides : 8 + 3 * sides]
     middle, near_rim, far_rim, info = refs[8 + 3 * sides : 12 + 3 * sides]
     side_out, near_ends, far_ends = [refs[12 + i * sides : 12 + (i + 1) * sides] for i in range(3, 6)]
@@ -454,7 +456,7 @@
             flops=slots * 96 * pr * pr * pr, bytes_accessed=16_000_000, transcendentals=slots * 2 * pr * pr
         ),
         name="positions",
-    )(place, tile, near, far_side, *side_in, *near_corners, *far_corners, probe, measured, left, right)
+    )(place, tile, *far_corners, far_side, *side_in, *near_corners, near, probe, measured, left, right)
     ends = [rest[i * sides : (i + 1) * sides] for i in range(3)]
     return middle, near_rim, far_rim, *ends, *rest[3 * sides :], info
 

time: 102 us -> 102 us (level)
  Pallas kernels: 25 us -> 30 us
  waiting for transfers between devices: 32.1 us -> 29 us
  starting transfers between devices: 37.7 us -> 35.3 us
    pallas_call x1, Pallas kernels: 18 us -> 22.4 us  [positions_call(): pl.pallas_call(functools.partial(positions_kernel, sides), out_shape=(sha...]
    ppermute x8, starting transfers between devices: 11.4 us -> 9.26 us  [swap(): return lax.ppermute(x, axis, pairs)]
    all_to_all x2, waiting for transfers between devices: 12.7 us -> 10.8 us  [chip_exchange(): lax.all_to_all(chunks.reshape(-1, LANES), CHIPS, 0, 0, tiled=True)]
    ppermute x4, waiting for transfers between devices: 16.2 us -> 14.6 us  [to_corners(): got.append(lax.ppermute(band, (*WIDE, 'narrow'), pairs))]
    all_to_all x2, starting transfers between devices: 21.2 us -> 19.8 us  [chip_exchange(): lax.all_to_all(chunks.reshape(-1, LANES), CHIPS, 0, 0, tiled=True)]
    ppermute x4, starting transfers between devices: 5.03 us -> 6.27 us  [to_corners(): got.append(lax.ppermute(band, (*WIDE, 'narrow'), pairs))]
  transfers between devices with their start and end apart: 14 -> 14, of which waited for: 6 -> 6; matrix products, arithmetic and copies ran while one was open for 1% -> 1% of each run, Pallas kernels for 2% -> 3%
where the time goes in v10:
time: 102 us; the launch traced here: 101 us
  starting transfers between devices  35.3 us (35%)
  Pallas kernels  30 us (29%)
  waiting for transfers between devices  29 us (28%)
  local copies, waits for them, and re-layouts  3.83 us (4%)
  other arithmetic  1.83 us (2%)
  between operations  1.45 us (1%)
    pallas_call x1, Pallas kernels, positions_call(): pl.pallas_call(functools.partial(positions_kernel, sides), out_shape=(sha...  22.4 us
    all_to_all x2, starting transfers between devices, chip_exchange(): lax.all_to_all(chunks.reshape(-1, LANES), CHIPS, 0, 0, tiled=True)  19.8 us
    ppermute x4, waiting for transfers between devices, to_corners(): got.append(lax.ppermute(band, (*WIDE, 'narrow'), pairs))  14.6 us
    all_to_all x2, waiting for transfers between devices, chip_exchange(): lax.all_to_all(chunks.reshape(-1, LANES), CHIPS, 0, 0, tiled=True)  10.8 us
    ppermute x8, starting transfers between devices, swap(): return lax.ppermute(x, axis, pairs)  9.26 us
    ppermute x4, starting transfers between devices, to_corners(): got.append(lax.ppermute(band, (*WIDE, 'narrow'), pairs))  6.27 us
    pallas_call x1, Pallas kernels, update_call(): pl.pallas_call(functools.partial(update_kernel, sides), out_shape=(jax.Sh...  3.71 us
    ppermute x8, waiting for transfers between devices, swap(): return lax.ppermute(x, axis, pairs)  3.54 us
  transfers between devices with their start and end apart: 14, of which 6 were waited for; matrix products, arithmetic and copies ran while one was open for 1% of the time, Pallas kernels for 3%

profile of v10, /device:TPU:0, one launch (start us, length us, event | category | flops | bytes accessed | tf_op | source)
XLA Modules:
  0.0 101.4 jit_solution(12837822581101139670)
XLA Ops:
  1.3 0.7 concatenate.9.place.refs_0_
  2.0 0.0 copy-start
  2.0 1.2 %copy-done = f32[2,256,512]{2,1,0:T(8,128)S(1)} copy-done((f32[2,256,512]{2,1,0:T(8,128)S(1)}, f32[2,256,512]{2,1,0:T(8,128)}, u32[]{:S(2)}) %copy-start) | copy-done | bytes 1048600
  3.3 0.8 pack.1
  4.0 0.7 collective-permute-start.1
  4.7 4.3 %collective-permute-start.4 = (f32[2,136,512]{2,1,0:T(8,128)S(1)}, f32[2,136,512]{2,1,0:T(8,128)S(1)}, u32[]{:S(2)}, u32[]{:S(2)}) collective-permute-start(f32[2,136,512]{2,1,0:T(8,128)S(1)} %get-tuple-element.25), channel_id=1, source_target_pairs={{0,2},{2,0},{1,3},{3,1},{4,6},{6,4},{5,7},{7,5},{8,10},{10,8},{9,1... | collective-permute-start | bytes 1671176 | tf_op jit(solution)/shard_map/ppermute | solution.py:538
  9.1 1.5 %collective-permute-start.2 = (f32[2,264,128]{2,1,0:T(8,128)S(1)}, f32[2,264,128]{2,1,0:T(8,128)S(1)}, u32[]{:S(2)}, u32[]{:S(2)}) collective-permute-start(f32[2,264,128]{2,1,0:T(8,128)S(1)} %get-tuple-element.23), channel_id=1, source_target_pairs={{0,1},{1,0},{2,3},{3,2},{4,5},{5,4},{6,7},{7,6},{8,9},{9,8},{10,11... | collective-permute-start | bytes 811016 | tf_op jit(solution)/shard_map/ppermute | solution.py:538
  10.6 0.7 collective-permute-start
  11.3 4.0 %collective-permute-start.3 = (f32[2,136,128]{2,1,0:T(8,128)S(1)}, f32[2,136,128]{2,1,0:T(8,128)S(1)}, u32[]{:S(2)}, u32[]{:S(2)}) collective-permute-start(f32[2,136,128]{2,1,0:T(8,128)S(1)} %get-tuple-element.24), channel_id=1, source_target_pairs={{0,3},{2,1},{1,2},{3,0},{4,7},{6,5},{5,6},{7,4},{8,11},{10,9},{9,1... | collective-permute-start | bytes 417800 | tf_op jit(solution)/shard_map/ppermute | solution.py:564
  15.3 0.0 collective-permute-done.refs_2_
  15.3 5.8 %collective-permute-done.3.refs_5_ = f32[2,136,128]{2,1,0:T(8,128)S(1)} collective-permute-done((f32[2,136,128]{2,1,0:T(8,128)S(1)}, f32[2,136,128]{2,1,0:T(8,128)S(1)}, u32[]{:S(2)}, u32[]{:S(2)}) %collective-permute-start.3) | collective-permute-done | bytes 139296 | tf_op jit(solution)/shard_map/ppermute | solution.py:564
  21.1 0.0 collective-permute-done.2.refs_4_
  21.1 0.0 collective-permute-done.1.refs_3_
  21.1 0.0 collective-permute-done.4.refs_6_
  21.1 0.0 copy-start.1
  21.2 1.0 %copy-done.1 = f32[2,256,256]{2,1,0:T(8,128)S(1)} copy-done((f32[2,256,256]{2,1,0:T(8,128)S(1)}, f32[2,256,256]{2,1,0:T(8,128)}, u32[]{:S(2)}) %copy-start.1) | copy-done | bytes 524312
  22.2 22.4 %positions.1 = (f32[2,256,512]{2,1,0:T(8,128)}, f32[2,128,512]{2,1,0:T(8,128)}, f32[2,128,512]{2,1,0:T(8,128)S(1)}, f32[5,8,128]{2,1,0:T(8,128)S(1)}, f32[2,256,...) custom-call(s32[19]{0:T(128)S(1)} %concatenate.9.place.refs_0_, ...), custom_call_target="tpu_custom_call" | custom-call | flops 12884901888 | bytes 16000000 | tf_op jit(solution)/shard_map/positions/pallas_call | solution.py:425
  44.6 0.0 copy-start.2
  44.6 0.1 collective-permute-start.5
  44.7 1.7 %collective-permute-done.5 = f32[768,128]{1,0:T(8,128)S(1)} collective-permute-done((f32[768,128]{1,0:T(8,128)S(1)}, f32[768,128]{1,0:T(8,128)S(1)}, u32[]{:S(2)}, u32[]{:S(2)}) %collective-permute-start.5) | collective-permute-done | bytes 393248 | tf_op jit(solution)/shard_map/ppermute | solution.py:538
  46.4 0.8 add.7
  47.2 10.0 %all-to-all-start = ((f32[16,48,128]{2,1,0:T(8,128)}), f32[16,48,128]{2,1,0:T(8,128)}, u32[]{:S(2)}, u32[]{:S(2)}) async-start(f32[16,48,128]{2,1,0:T(8,128)} %bitcast.7), calls=%async_computation | async-start | bytes 786432 | tf_op jit(solution)/shard_map/all_to_all | solution.py:569
  57.2 0.1 collective-permute-start.6
  57.2 0.7 collective-permute-start.7
  57.9 1.9 %collective-permute-start.8 = (f32[2,256,128]{2,1,0:T(8,128)S(1)}, f32[2,256,128]{2,1,0:T(8,128)S(1)}, u32[]{:S(2)}, u32[]{:S(2)}) collective-permute-start(f32[2,256,128]{2,1,0:T(8,128)S(1)} %get-tuple-element.34), channel_id=1, source_target_pairs={{0,1},{1,0},{2,3},{3,2},{4,5},{5,4},{6,7},{7,6},{8,9},{9,8},{10,11... | collective-permute-start | bytes 786440 | tf_op jit(solution)/shard_map/ppermute | solution.py:538
  59.8 0.0 copy-done.2
  59.9 3.1 %cover.1 = (f32[256,512]{1,0:T(8,128)S(1)}, f32[8,128]{1,0:T(8,128)S(1)}) custom-call(s32[19]{0:T(128)S(1)} %concatenate.9.place.refs_0_, s32[6,32]{1,0:T(8,128)S(1)} %fusion.1.info, f32[2,256,256]{2,1,0:T(8,128)S(1)} %copy-done.2), custom_call_target="tpu_custom_call" | custom-call | flops 4000000 | bytes 8000000 | tf_op jit(solution)/shard_map/cover/pallas_call | solution.py:119
  63.0 7.2 %all-to-all-done = f32[16,48,128]{2,1,0:T(8,128)} async-done(((f32[16,48,128]{2,1,0:T(8,128)}), f32[16,48,128]{2,1,0:T(8,128)}, u32[]{:S(2)}, u32[]{:S(2)}) %all-to-all-start) | async-done | bytes 393248 | tf_op jit(solution)/shard_map/all_to_all | solution.py:569
  70.2 1.0 %reduce_sum.9 = f32[48,128]{1,0:T(8,128)S(1)} reduce(f32[16,48,128]{2,1,0:T(8,128)} %all-to-all-done, f32[]{:T(128)} %constant.19.clone.1), dimensions={0}, to_apply=%region_0.0 | reduce | flops 92160 | bytes 417796 | tf_op jit(solution)/shard_map/reduce_sum | solution.py:605
  71.2 0.0 collective-permute-done.8.refs_6_
  71.2 0.0 collective-permute-done.6.refs_4_
  71.3 0.0 collective-permute-done.7.refs_5_
  71.3 0.8 broadcast_in_dim.3
  72.1 9.8 %all-to-all-start.1 = ((f32[16,56,128]{2,1,0:T(8,128)}), f32[16,56,128]{2,1,0:T(8,128)S(1)}, u32[]{:S(2)}, u32[]{:S(2)}) async-start(f32[16,56,128]{2,1,0:T(8,128)} %broadcast_in_dim.3), calls=%async_computation.1 | async-start | bytes 917504 | tf_op jit(solution)/shard_map/all_to_all | solution.py:569
  81.9 0.9 collective-permute-start.9
  82.8 0.7 collective-permute-start.10
  83.5 8.8 %collective-permute-done.9.refs_7_ = f32[2,128,128]{2,1,0:T(8,128)S(1)} collective-permute-done((f32[2,128,128]{2,1,0:T(8,128)}, f32[2,128,128]{2,1,0:T(8,128)S(1)}, u32[]{:S(2)}, u32[]{:S(2)}) %collective-permute-start.9) | collective-permute-done | bytes 131104 | tf_op jit(solution)/shard_map/ppermute | solution.py:564
  92.3 0.0 collective-permute-done.10.refs_8_
  92.3 3.6 %all-to-all-done.1.refs_9_ = f32[16,56,128]{2,1,0:T(8,128)S(1)} async-done(((f32[16,56,128]{2,1,0:T(8,128)}), f32[16,56,128]{2,1,0:T(8,128)S(1)}, u32[]{:S(2)}, u32[]{:S(2)}) %all-to-all-start.1) | async-done | bytes 458784 | tf_op jit(solution)/shard_map/all_to_all | solution.py:569
  95.9 0.0 collective-permute-start.11
  95.9 1.8 %collective-permute-done.11.refs_10_ = f32[16,56,128]{2,1,0:T(8,128)S(1)} collective-permute-done((f32[16,56,128]{2,1,0:T(8,128)S(1)}, f32[16,56,128]{2,1,0:T(8,128)S(1)}, u32[]{:S(2)}, u32[]{:S(2)}) %collective-permute-start.11) | collective-permute-done | bytes 458784 | tf_op jit(solution)/shard_map/ppermute | solution.py:538
  97.7 3.7 %update.1 = (f32[2,256,512]{2,1,0:T(8,128)}, f32[2,256,256]{2,1,0:T(8,128)}) custom-call(s32[19]{0:T(128)S(1)} %concatenate.9.place.refs_0_, f32[2,256,512]{2,1,0:T(8,128)} %refs_1_.3, f32[2,256,512]{2,1,0:T(8,128)} %get-tuple-element.26.refs_2_, f32[256,512]{1,0:T(8,128)S(1)} %get-tuple-element.31.refs_3_, ...), custom_call_target="tpu_custom_call" | custom-call | tf_op jit(solution)/shard_map/update/pallas_call | solution.py:518
  (4 shorter events, 0.0 us)
Async XLA Ops:
  2.0 1.2 %copy-start = (f32[2,256,512]{2,1,0:T(8,128)S(1)}, f32[2,256,512]{2,1,0:T(8,128)}, u32[]{:S(2)}) copy-start(f32[2,256,512]{2,1,0:T(8,128)} %refs_1_.3) | copy-start | bytes 3145732
  4.0 17.1 %collective-permute-start.1 = (f32[2,136,512]{2,1,0:T(8,128)S(1)}, f32[2,136,512]{2,1,0:T(8,128)S(1)}, u32[]{:S(2)}, u32[]{:S(2)}) collective-permute-start(f32[2,136,512]{2,1,0:T(8,128)S(1)} %get-tuple-element.22), channel_id=1, source_target_pairs={{2,4},{4,2},{6,8},{8,6},{10,12},{12,10},{14,16},{16,14},{18,20},{2... | collective-permute-start | bytes 1671176 | tf_op jit(solution)/shard_map/ppermute | solution.py:538
  4.7 16.4 %collective-permute-start.4 = (f32[2,136,512]{2,1,0:T(8,128)S(1)}, f32[2,136,512]{2,1,0:T(8,128)S(1)}, u32[]{:S(2)}, u32[]{:S(2)}) collective-permute-start(f32[2,136,512]{2,1,0:T(8,128)S(1)} %get-tuple-element.25), channel_id=1, source_target_pairs={{0,2},{2,0},{1,3},{3,1},{4,6},{6,4},{5,7},{7,5},{8,10},{10,8},{9,1... | collective-permute-start | bytes 1671176 | tf_op jit(solution)/shard_map/ppermute | solution.py:538
  9.1 12.1 %collective-permute-start.2 = (f32[2,264,128]{2,1,0:T(8,128)S(1)}, f32[2,264,128]{2,1,0:T(8,128)S(1)}, u32[]{:S(2)}, u32[]{:S(2)}) collective-permute-start(f32[2,264,128]{2,1,0:T(8,128)S(1)} %get-tuple-element.23), channel_id=1, source_target_pairs={{0,1},{1,0},{2,3},{3,2},{4,5},{5,4},{6,7},{7,6},{8,9},{9,8},{10,11... | collective-permute-start | bytes 811016 | tf_op jit(solution)/shard_map/ppermute | solution.py:538
  10.6 4.7 %collective-permute-start = (f32[2,136,128]{2,1,0:T(8,128)S(1)}, f32[2,136,128]{2,1,0:T(8,128)S(1)}, u32[]{:S(2)}, u32[]{:S(2)}) collective-permute-start(f32[2,136,128]{2,1,0:T(8,128)S(1)} %get-tuple-element.21), channel_id=1, source_target_pairs={{2,5},{4,3},{3,4},{5,2},{6,9},{8,7},{7,8},{9,6},{10,13},{12,11},{1... | collective-permute-start | bytes 417800 | tf_op jit(solution)/shard_map/ppermute | solution.py:564
  11.3 9.9 %collective-permute-start.3 = (f32[2,136,128]{2,1,0:T(8,128)S(1)}, f32[2,136,128]{2,1,0:T(8,128)S(1)}, u32[]{:S(2)}, u32[]{:S(2)}) collective-permute-start(f32[2,136,128]{2,1,0:T(8,128)S(1)} %get-tuple-element.24), channel_id=1, source_target_pairs={{0,3},{2,1},{1,2},{3,0},{4,7},{6,5},{5,6},{7,4},{8,11},{10,9},{9,1... | collective-permute-start | bytes 417800 | tf_op jit(solution)/shard_map/ppermute | solution.py:564
  21.1 1.0 %copy-start.1 = (f32[2,256,256]{2,1,0:T(8,128)S(1)}, f32[2,256,256]{2,1,0:T(8,128)}, u32[]{:S(2)}) copy-start(f32[2,256,256]{2,1,0:T(8,128)} %refs_11_.1) | copy-start | bytes 1572868
  44.6 15.3 %copy-start.2 = (f32[2,256,256]{2,1,0:T(8,128)S(1)}, f32[2,256,256]{2,1,0:T(8,128)}, u32[]{:S(2)}) copy-start(f32[2,256,256]{2,1,0:T(8,128)} %refs_11_.1) | copy-start | bytes 1572868
  44.6 1.8 %collective-permute-start.5 = (f32[768,128]{1,0:T(8,128)S(1)}, f32[768,128]{1,0:T(8,128)S(1)}, u32[]{:S(2)}, u32[]{:S(2)}) collective-permute-start(f32[768,128]{1,0:T(8,128)S(1)} %get-tuple-element.29), channel_id=1, source_target_pairs={{0,2},{2,0},{1,3},{3,1},{4,6},{6,4},{5,7},{7,5},{8,10},{10,8},{9,1... | collective-permute-start | bytes 1179656 | tf_op jit(solution)/shard_map/ppermute | solution.py:538
  47.2 23.0 %all-to-all-start = ((f32[16,48,128]{2,1,0:T(8,128)}), f32[16,48,128]{2,1,0:T(8,128)}, u32[]{:S(2)}, u32[]{:S(2)}) async-start(f32[16,48,128]{2,1,0:T(8,128)} %bitcast.7), calls=%async_computation | async-start | bytes 786432 | tf_op jit(solution)/shard_map/all_to_all | solution.py:569
  57.2 14.1 %collective-permute-start.6 = (f32[2,128,512]{2,1,0:T(8,128)}, f32[2,128,512]{2,1,0:T(8,128)S(1)}, u32[]{:S(2)}, u32[]{:S(2)}) collective-permute-start(f32[2,128,512]{2,1,0:T(8,128)} %get-tuple-element.32), channel_id=1, source_target_pairs={{0,2},{2,0},{1,3},{3,1},{4,6},{6,4},{5,7},{7,5},{8,10},{10,8},{9,1... | collective-permute-start | bytes 1572872 | tf_op jit(solution)/shard_map/ppermute | solution.py:538
  57.2 14.0 %collective-permute-start.7 = (f32[2,128,512]{2,1,0:T(8,128)S(1)}, f32[2,128,512]{2,1,0:T(8,128)S(1)}, u32[]{:S(2)}, u32[]{:S(2)}) collective-permute-start(f32[2,128,512]{2,1,0:T(8,128)S(1)} %get-tuple-element.33), channel_id=1, source_target_pairs={{2,4},{4,2},{6,8},{8,6},{10,12},{12,10},{14,16},{16,14},{18,20},{2... | collective-permute-start | bytes 1572872 | tf_op jit(solution)/shard_map/ppermute | solution.py:538
  57.9 13.3 %collective-permute-start.8 = (f32[2,256,128]{2,1,0:T(8,128)S(1)}, f32[2,256,128]{2,1,0:T(8,128)S(1)}, u32[]{:S(2)}, u32[]{:S(2)}) collective-permute-start(f32[2,256,128]{2,1,0:T(8,128)S(1)} %get-tuple-element.34), channel_id=1, source_target_pairs={{0,1},{1,0},{2,3},{3,2},{4,5},{5,4},{6,7},{7,6},{8,9},{9,8},{10,11... | collective-permute-start | bytes 786440 | tf_op jit(solution)/shard_map/ppermute | solution.py:538
  72.1 23.8 %all-to-all-start.1 = ((f32[16,56,128]{2,1,0:T(8,128)}), f32[16,56,128]{2,1,0:T(8,128)S(1)}, u32[]{:S(2)}, u32[]{:S(2)}) async-start(f32[16,56,128]{2,1,0:T(8,128)} %broadcast_in_dim.3), calls=%async_computation.1 | async-start | bytes 917504 | tf_op jit(solution)/shard_map/all_to_all | solution.py:569
  81.9 10.4 %collective-permute-start.9 = (f32[2,128,128]{2,1,0:T(8,128)}, f32[2,128,128]{2,1,0:T(8,128)S(1)}, u32[]{:S(2)}, u32[]{:S(2)}) collective-permute-start(f32[2,128,128]{2,1,0:T(8,128)} %get-tuple-element.35), channel_id=1, source_target_pairs={{0,3},{2,1},{1,2},{3,0},{4,7},{6,5},{5,6},{7,4},{8,11},{10,9},{9,1... | collective-permute-start | bytes 393224 | tf_op jit(solution)/shard_map/ppermute | solution.py:564
  82.8 9.5 %collective-permute-start.10 = (f32[2,128,128]{2,1,0:T(8,128)S(1)}, f32[2,128,128]{2,1,0:T(8,128)S(1)}, u32[]{:S(2)}, u32[]{:S(2)}) collective-permute-start(f32[2,128,128]{2,1,0:T(8,128)S(1)} %get-tuple-element.36), channel_id=1, source_target_pairs={{2,5},{4,3},{3,4},{5,2},{6,9},{8,7},{7,8},{9,6},{10,13},{12,11},{1... | collective-permute-start | bytes 393224 | tf_op jit(solution)/shard_map/ppermute | solution.py:564
  95.9 1.8 %collective-permute-start.11 = (f32[16,56,128]{2,1,0:T(8,128)S(1)}, f32[16,56,128]{2,1,0:T(8,128)S(1)}, u32[]{:S(2)}, u32[]{:S(2)}) collective-permute-start(f32[16,56,128]{2,1,0:T(8,128)S(1)} %all-to-all-done.1.refs_9_), channel_id=1, source_target_pairs={{0,2},{2,0},{1,3},{3,1},{4,6},{6,4},{5,7},{7,5},{8,10},{10,8},{9,1... | collective-permute-start | bytes 1376264 | tf_op jit(solution)/shard_map/ppermute | solution.py:538

commit v11 on v10

--- a/solution.py
+++ b/solution.py
@@ -375,11 +375,15 @@
         @pl.when(i == 0)
         def _():
             tables[0].wait()
-            tables[1].wait()
 
         for w in range(WAYS):
             load(w, slots[w])
             times_left(w)
+
+        @pl.when(i == 0)
+        def _():
+            tables[1].wait()
+
         for w in range(WAYS):
             times_right(w)
         for w in range(WAYS):

time: 102 us -> 102 us (level)
  starting transfers between devices: 35.3 us -> 40.1 us
  Pallas kernels: 30 us -> 25.4 us
    pallas_call x1, Pallas kernels: 22.4 us -> 18.1 us  [positions_call(): pl.pallas_call(functools.partial(positions_kernel, sides), out_shape=(sha...]
    ppermute x8, starting transfers between devices: 9.26 us -> 12.5 us  [swap(): return lax.ppermute(x, axis, pairs)]
    all_to_all x2, starting transfers between devices: 19.8 us -> 21.3 us  [chip_exchange(): lax.all_to_all(chunks.reshape(-1, LANES), CHIPS, 0, 0, tiled=True)]
where the time goes in v11:
time: 102 us
  starting transfers between devices  40.1 us (39%)
  waiting for transfers between devices  29 us (28%)
  Pallas kernels  25.4 us (25%)
  local copies, waits for them, and re-layouts  3.83 us (4%)
  other arithmetic  1.83 us (2%)
  between operations  1.44 us (1%)
    all_to_all x2, starting transfers between devices, chip_exchange(): lax.all_to_all(chunks.reshape(-1, LANES), CHIPS, 0, 0, tiled=True)  21.3 us
    pallas_call x1, Pallas kernels, positions_call(): pl.pallas_call(functools.partial(positions_kernel, sides), out_shape=(sha...  18.1 us
    ppermute x4, waiting for transfers between devices, to_corners(): got.append(lax.ppermute(band, (*WIDE, 'narrow'), pairs))  14.6 us
    ppermute x8, starting transfers between devices, swap(): return lax.ppermute(x, axis, pairs)  12.5 us
    all_to_all x2, waiting for transfers between devices, chip_exchange(): lax.all_to_all(chunks.reshape(-1, LANES), CHIPS, 0, 0, tiled=True)  11.2 us
    ppermute x4, starting transfers between devices, to_corners(): got.append(lax.ppermute(band, (*WIDE, 'narrow'), pairs))  6.27 us
    pallas_call x1, Pallas kernels, update_call(): pl.pallas_call(functools.partial(update_kernel, sides), out_shape=(jax.Sh...  3.71 us
    ppermute x8, waiting for transfers between devices, swap(): return lax.ppermute(x, axis, pairs)  3.18 us
  transfers between devices with their start and end apart: 14, of which 6 were waited for; matrix products, arithmetic and copies ran while one was open for 1% of the time, Pallas kernels for 3%

profile of v11, /device:TPU:0, one launch (start us, length us, event | category | flops | bytes accessed | tf_op | source)
XLA Modules:
  0.0 101.5 jit_solution(3405183224788691633)
XLA Ops:
  1.3 0.7 concatenate.9.place.refs_0_
  2.0 0.0 copy-start
  2.0 1.2 %copy-done = f32[2,256,512]{2,1,0:T(8,128)S(1)} copy-done((f32[2,256,512]{2,1,0:T(8,128)S(1)}, f32[2,256,512]{2,1,0:T(8,128)}, u32[]{:S(2)}) %copy-start) | copy-done | bytes 1048600
  3.3 0.8 pack.1
  4.0 0.7 collective-permute-start.1
  4.7 4.3 %collective-permute-start.4 = (f32[2,136,512]{2,1,0:T(8,128)S(1)}, f32[2,136,512]{2,1,0:T(8,128)S(1)}, u32[]{:S(2)}, u32[]{:S(2)}) collective-permute-start(f32[2,136,512]{2,1,0:T(8,128)S(1)} %get-tuple-element.25), channel_id=1, source_target_pairs={{0,2},{2,0},{1,3},{3,1},{4,6},{6,4},{5,7},{7,5},{8,10},{10,8},{9,1... | collective-permute-start | bytes 1671176 | tf_op jit(solution)/shard_map/ppermute | solution.py:542
  9.1 1.5 %collective-permute-start.2 = (f32[2,264,128]{2,1,0:T(8,128)S(1)}, f32[2,264,128]{2,1,0:T(8,128)S(1)}, u32[]{:S(2)}, u32[]{:S(2)}) collective-permute-start(f32[2,264,128]{2,1,0:T(8,128)S(1)} %get-tuple-element.23), channel_id=1, source_target_pairs={{0,1},{1,0},{2,3},{3,2},{4,5},{5,4},{6,7},{7,6},{8,9},{9,8},{10,11... | collective-permute-start | bytes 811016 | tf_op jit(solution)/shard_map/ppermute | solution.py:542
  10.6 0.7 collective-permute-start
  11.3 4.0 %collective-permute-start.3 = (f32[2,136,128]{2,1,0:T(8,128)S(1)}, f32[2,136,128]{2,1,0:T(8,128)S(1)}, u32[]{:S(2)}, u32[]{:S(2)}) collective-permute-start(f32[2,136,128]{2,1,0:T(8,128)S(1)} %get-tuple-element.24), channel_id=1, source_target_pairs={{0,3},{2,1},{1,2},{3,0},{4,7},{6,5},{5,6},{7,4},{8,11},{10,9},{9,1... | collective-permute-start | bytes 417800 | tf_op jit(solution)/shard_map/ppermute | solution.py:568
  15.3 0.0 collective-permute-done.refs_2_
  15.3 5.8 %collective-permute-done.3.refs_5_ = f32[2,136,128]{2,1,0:T(8,128)S(1)} collective-permute-done((f32[2,136,128]{2,1,0:T(8,128)S(1)}, f32[2,136,128]{2,1,0:T(8,128)S(1)}, u32[]{:S(2)}, u32[]{:S(2)}) %collective-permute-start.3) | collective-permute-done | bytes 139296 | tf_op jit(solution)/shard_map/ppermute | solution.py:568
  21.1 0.0 collective-permute-done.2.refs_4_
  21.1 0.0 collective-permute-done.1.refs_3_
  21.1 0.0 collective-permute-done.4.refs_6_
  21.1 0.0 copy-start.1
  21.2 1.0 %copy-done.1 = f32[2,256,256]{2,1,0:T(8,128)S(1)} copy-done((f32[2,256,256]{2,1,0:T(8,128)S(1)}, f32[2,256,256]{2,1,0:T(8,128)}, u32[]{:S(2)}) %copy-start.1) | copy-done | bytes 524312
  22.2 18.1 %positions.1 = (f32[2,256,512]{2,1,0:T(8,128)}, f32[2,128,512]{2,1,0:T(8,128)}, f32[2,128,512]{2,1,0:T(8,128)S(1)}, f32[5,8,128]{2,1,0:T(8,128)S(1)}, f32[2,256,...) custom-call(s32[19]{0:T(128)S(1)} %concatenate.9.place.refs_0_, ...), custom_call_target="tpu_custom_call" | custom-call | flops 12884901888 | bytes 16000000 | tf_op jit(solution)/shard_map/positions/pallas_call | solution.py:429
  40.3 0.0 copy-start.2
  40.3 3.3 %collective-permute-start.5 = (f32[768,128]{1,0:T(8,128)S(1)}, f32[768,128]{1,0:T(8,128)S(1)}, u32[]{:S(2)}, u32[]{:S(2)}) collective-permute-start(f32[768,128]{1,0:T(8,128)S(1)} %get-tuple-element.29), channel_id=1, source_target_pairs={{0,2},{2,0},{1,3},{3,1},{4,6},{6,4},{5,7},{7,5},{8,10},{10,8},{9,1... | collective-permute-start | bytes 1179656 | tf_op jit(solution)/shard_map/ppermute | solution.py:542
  43.6 1.3 %collective-permute-done.5 = f32[768,128]{1,0:T(8,128)S(1)} collective-permute-done((f32[768,128]{1,0:T(8,128)S(1)}, f32[768,128]{1,0:T(8,128)S(1)}, u32[]{:S(2)}, u32[]{:S(2)}) %collective-permute-start.5) | collective-permute-done | bytes 393248 | tf_op jit(solution)/shard_map/ppermute | solution.py:542
  45.0 0.8 add.7
  45.8 11.5 %all-to-all-start = ((f32[16,48,128]{2,1,0:T(8,128)}), f32[16,48,128]{2,1,0:T(8,128)}, u32[]{:S(2)}, u32[]{:S(2)}) async-start(f32[16,48,128]{2,1,0:T(8,128)} %bitcast.7), calls=%async_computation | async-start | bytes 786432 | tf_op jit(solution)/shard_map/all_to_all | solution.py:573
  57.3 0.1 collective-permute-start.6
  57.4 0.7 collective-permute-start.7
  58.1 1.9 %collective-permute-start.8 = (f32[2,256,128]{2,1,0:T(8,128)S(1)}, f32[2,256,128]{2,1,0:T(8,128)S(1)}, u32[]{:S(2)}, u32[]{:S(2)}) collective-permute-start(f32[2,256,128]{2,1,0:T(8,128)S(1)} %get-tuple-element.34), channel_id=1, source_target_pairs={{0,1},{1,0},{2,3},{3,2},{4,5},{5,4},{6,7},{7,6},{8,9},{9,8},{10,11... | collective-permute-start | bytes 786440 | tf_op jit(solution)/shard_map/ppermute | solution.py:542
  60.0 0.0 copy-done.2
  60.0 2.8 %cover.1 = (f32[256,512]{1,0:T(8,128)S(1)}, f32[8,128]{1,0:T(8,128)S(1)}) custom-call(s32[19]{0:T(128)S(1)} %concatenate.9.place.refs_0_, s32[6,32]{1,0:T(8,128)S(1)} %fusion.1.info, f32[2,256,256]{2,1,0:T(8,128)S(1)} %copy-done.2), custom_call_target="tpu_custom_call" | custom-call | flops 4000000 | bytes 8000000 | tf_op jit(solution)/shard_map/cover/pallas_call | solution.py:119
  62.8 7.6 %all-to-all-done = f32[16,48,128]{2,1,0:T(8,128)} async-done(((f32[16,48,128]{2,1,0:T(8,128)}), f32[16,48,128]{2,1,0:T(8,128)}, u32[]{:S(2)}, u32[]{:S(2)}) %all-to-all-start) | async-done | bytes 393248 | tf_op jit(solution)/shard_map/all_to_all | solution.py:573
  70.3 1.0 %reduce_sum.9 = f32[48,128]{1,0:T(8,128)S(1)} reduce(f32[16,48,128]{2,1,0:T(8,128)} %all-to-all-done, f32[]{:T(128)} %constant.19.clone.1), dimensions={0}, to_apply=%region_0.0 | reduce | flops 92160 | bytes 417796 | tf_op jit(solution)/shard_map/reduce_sum | solution.py:609
  71.4 0.0 collective-permute-done.8.refs_6_
  71.4 0.0 collective-permute-done.6.refs_4_
  71.4 0.0 collective-permute-done.7.refs_5_
  71.4 0.8 broadcast_in_dim.3
  72.2 9.8 %all-to-all-start.1 = ((f32[16,56,128]{2,1,0:T(8,128)}), f32[16,56,128]{2,1,0:T(8,128)S(1)}, u32[]{:S(2)}, u32[]{:S(2)}) async-start(f32[16,56,128]{2,1,0:T(8,128)} %broadcast_in_dim.3), calls=%async_computation.1 | async-start | bytes 917504 | tf_op jit(solution)/shard_map/all_to_all | solution.py:573
  82.0 0.9 collective-permute-start.9
  83.0 0.7 collective-permute-start.10
  83.6 8.8 %collective-permute-done.9.refs_7_ = f32[2,128,128]{2,1,0:T(8,128)S(1)} collective-permute-done((f32[2,128,128]{2,1,0:T(8,128)}, f32[2,128,128]{2,1,0:T(8,128)S(1)}, u32[]{:S(2)}, u32[]{:S(2)}) %collective-permute-start.9) | collective-permute-done | bytes 131104 | tf_op jit(solution)/shard_map/ppermute | solution.py:568
  92.4 0.0 collective-permute-done.10.refs_8_
  92.4 3.6 %all-to-all-done.1.refs_9_ = f32[16,56,128]{2,1,0:T(8,128)S(1)} async-done(((f32[16,56,128]{2,1,0:T(8,128)}), f32[16,56,128]{2,1,0:T(8,128)S(1)}, u32[]{:S(2)}, u32[]{:S(2)}) %all-to-all-start.1) | async-done | bytes 458784 | tf_op jit(solution)/shard_map/all_to_all | solution.py:573
  96.0 0.0 collective-permute-start.11
  96.0 1.8 %collective-permute-done.11.refs_10_ = f32[16,56,128]{2,1,0:T(8,128)S(1)} collective-permute-done((f32[16,56,128]{2,1,0:T(8,128)S(1)}, f32[16,56,128]{2,1,0:T(8,128)S(1)}, u32[]{:S(2)}, u32[]{:S(2)}) %collective-permute-start.11) | collective-permute-done | bytes 458784 | tf_op jit(solution)/shard_map/ppermute | solution.py:542
  97.8 3.7 %update.1 = (f32[2,256,512]{2,1,0:T(8,128)}, f32[2,256,256]{2,1,0:T(8,128)}) custom-call(s32[19]{0:T(128)S(1)} %concatenate.9.place.refs_0_, f32[2,256,512]{2,1,0:T(8,128)} %refs_1_.3, f32[2,256,512]{2,1,0:T(8,128)} %get-tuple-element.26.refs_2_, f32[256,512]{1,0:T(8,128)S(1)} %get-tuple-element.31.refs_3_, ...), custom_call_target="tpu_custom_call" | custom-call | tf_op jit(solution)/shard_map/update/pallas_call | solution.py:522
  (4 shorter events, 0.0 us)
Async XLA Ops:
  2.0 1.2 %copy-start = (f32[2,256,512]{2,1,0:T(8,128)S(1)}, f32[2,256,512]{2,1,0:T(8,128)}, u32[]{:S(2)}) copy-start(f32[2,256,512]{2,1,0:T(8,128)} %refs_1_.3) | copy-start | bytes 3145732
  4.0 17.1 %collective-permute-start.1 = (f32[2,136,512]{2,1,0:T(8,128)S(1)}, f32[2,136,512]{2,1,0:T(8,128)S(1)}, u32[]{:S(2)}, u32[]{:S(2)}) collective-permute-start(f32[2,136,512]{2,1,0:T(8,128)S(1)} %get-tuple-element.22), channel_id=1, source_target_pairs={{2,4},{4,2},{6,8},{8,6},{10,12},{12,10},{14,16},{16,14},{18,20},{2... | collective-permute-start | bytes 1671176 | tf_op jit(solution)/shard_map/ppermute | solution.py:542
  4.7 16.4 %collective-permute-start.4 = (f32[2,136,512]{2,1,0:T(8,128)S(1)}, f32[2,136,512]{2,1,0:T(8,128)S(1)}, u32[]{:S(2)}, u32[]{:S(2)}) collective-permute-start(f32[2,136,512]{2,1,0:T(8,128)S(1)} %get-tuple-element.25), channel_id=1, source_target_pairs={{0,2},{2,0},{1,3},{3,1},{4,6},{6,4},{5,7},{7,5},{8,10},{10,8},{9,1... | collective-permute-start | bytes 1671176 | tf_op jit(solution)/shard_map/ppermute | solution.py:542
  9.1 12.1 %collective-permute-start.2 = (f32[2,264,128]{2,1,0:T(8,128)S(1)}, f32[2,264,128]{2,1,0:T(8,128)S(1)}, u32[]{:S(2)}, u32[]{:S(2)}) collective-permute-start(f32[2,264,128]{2,1,0:T(8,128)S(1)} %get-tuple-element.23), channel_id=1, source_target_pairs={{0,1},{1,0},{2,3},{3,2},{4,5},{5,4},{6,7},{7,6},{8,9},{9,8},{10,11... | collective-permute-start | bytes 811016 | tf_op jit(solution)/shard_map/ppermute | solution.py:542
  10.6 4.7 %collective-permute-start = (f32[2,136,128]{2,1,0:T(8,128)S(1)}, f32[2,136,128]{2,1,0:T(8,128)S(1)}, u32[]{:S(2)}, u32[]{:S(2)}) collective-permute-start(f32[2,136,128]{2,1,0:T(8,128)S(1)} %get-tuple-element.21), channel_id=1, source_target_pairs={{2,5},{4,3},{3,4},{5,2},{6,9},{8,7},{7,8},{9,6},{10,13},{12,11},{1... | collective-permute-start | bytes 417800 | tf_op jit(solution)/shard_map/ppermute | solution.py:568
  11.3 9.9 %collective-permute-start.3 = (f32[2,136,128]{2,1,0:T(8,128)S(1)}, f32[2,136,128]{2,1,0:T(8,128)S(1)}, u32[]{:S(2)}, u32[]{:S(2)}) collective-permute-start(f32[2,136,128]{2,1,0:T(8,128)S(1)} %get-tuple-element.24), channel_id=1, source_target_pairs={{0,3},{2,1},{1,2},{3,0},{4,7},{6,5},{5,6},{7,4},{8,11},{10,9},{9,1... | collective-permute-start | bytes 417800 | tf_op jit(solution)/shard_map/ppermute | solution.py:568
  21.1 1.0 %copy-start.1 = (f32[2,256,256]{2,1,0:T(8,128)S(1)}, f32[2,256,256]{2,1,0:T(8,128)}, u32[]{:S(2)}) copy-start(f32[2,256,256]{2,1,0:T(8,128)} %refs_11_.1) | copy-start | bytes 1572868
  40.3 19.6 %copy-start.2 = (f32[2,256,256]{2,1,0:T(8,128)S(1)}, f32[2,256,256]{2,1,0:T(8,128)}, u32[]{:S(2)}) copy-start(f32[2,256,256]{2,1,0:T(8,128)} %refs_11_.1) | copy-start | bytes 1572868
  40.3 4.7 %collective-permute-start.5 = (f32[768,128]{1,0:T(8,128)S(1)}, f32[768,128]{1,0:T(8,128)S(1)}, u32[]{:S(2)}, u32[]{:S(2)}) collective-permute-start(f32[768,128]{1,0:T(8,128)S(1)} %get-tuple-element.29), channel_id=1, source_target_pairs={{0,2},{2,0},{1,3},{3,1},{4,6},{6,4},{5,7},{7,5},{8,10},{10,8},{9,1... | collective-permute-start | bytes 1179656 | tf_op jit(solution)/shard_map/ppermute | solution.py:542
  45.8 24.5 %all-to-all-start = ((f32[16,48,128]{2,1,0:T(8,128)}), f32[16,48,128]{2,1,0:T(8,128)}, u32[]{:S(2)}, u32[]{:S(2)}) async-start(f32[16,48,128]{2,1,0:T(8,128)} %bitcast.7), calls=%async_computation | async-start | bytes 786432 | tf_op jit(solution)/shard_map/all_to_all | solution.py:573
  57.3 14.1 %collective-permute-start.6 = (f32[2,128,512]{2,1,0:T(8,128)}, f32[2,128,512]{2,1,0:T(8,128)S(1)}, u32[]{:S(2)}, u32[]{:S(2)}) collective-permute-start(f32[2,128,512]{2,1,0:T(8,128)} %get-tuple-element.32), channel_id=1, source_target_pairs={{0,2},{2,0},{1,3},{3,1},{4,6},{6,4},{5,7},{7,5},{8,10},{10,8},{9,1... | collective-permute-start | bytes 1572872 | tf_op jit(solution)/shard_map/ppermute | solution.py:542
  57.4 14.0 %collective-permute-start.7 = (f32[2,128,512]{2,1,0:T(8,128)S(1)}, f32[2,128,512]{2,1,0:T(8,128)S(1)}, u32[]{:S(2)}, u32[]{:S(2)}) collective-permute-start(f32[2,128,512]{2,1,0:T(8,128)S(1)} %get-tuple-element.33), channel_id=1, source_target_pairs={{2,4},{4,2},{6,8},{8,6},{10,12},{12,10},{14,16},{16,14},{18,20},{2... | collective-permute-start | bytes 1572872 | tf_op jit(solution)/shard_map/ppermute | solution.py:542
  58.1 13.3 %collective-permute-start.8 = (f32[2,256,128]{2,1,0:T(8,128)S(1)}, f32[2,256,128]{2,1,0:T(8,128)S(1)}, u32[]{:S(2)}, u32[]{:S(2)}) collective-permute-start(f32[2,256,128]{2,1,0:T(8,128)S(1)} %get-tuple-element.34), channel_id=1, source_target_pairs={{0,1},{1,0},{2,3},{3,2},{4,5},{5,4},{6,7},{7,6},{8,9},{9,8},{10,11... | collective-permute-start | bytes 786440 | tf_op jit(solution)/shard_map/ppermute | solution.py:542
  72.2 23.8 %all-to-all-start.1 = ((f32[16,56,128]{2,1,0:T(8,128)}), f32[16,56,128]{2,1,0:T(8,128)S(1)}, u32[]{:S(2)}, u32[]{:S(2)}) async-start(f32[16,56,128]{2,1,0:T(8,128)} %broadcast_in_dim.3), calls=%async_computation.1 | async-start | bytes 917504 | tf_op jit(solution)/shard_map/all_to_all | solution.py:573
  82.0 10.4 %collective-permute-start.9 = (f32[2,128,128]{2,1,0:T(8,128)}, f32[2,128,128]{2,1,0:T(8,128)S(1)}, u32[]{:S(2)}, u32[]{:S(2)}) collective-permute-start(f32[2,128,128]{2,1,0:T(8,128)} %get-tuple-element.35), channel_id=1, source_target_pairs={{0,3},{2,1},{1,2},{3,0},{4,7},{6,5},{5,6},{7,4},{8,11},{10,9},{9,1... | collective-permute-start | bytes 393224 | tf_op jit(solution)/shard_map/ppermute | solution.py:568
  83.0 9.5 %collective-permute-start.10 = (f32[2,128,128]{2,1,0:T(8,128)S(1)}, f32[2,128,128]{2,1,0:T(8,128)S(1)}, u32[]{:S(2)}, u32[]{:S(2)}) collective-permute-start(f32[2,128,128]{2,1,0:T(8,128)S(1)} %get-tuple-element.36), channel_id=1, source_target_pairs={{2,5},{4,3},{3,4},{5,2},{6,9},{8,7},{7,8},{9,6},{10,13},{12,11},{1... | collective-permute-start | bytes 393224 | tf_op jit(solution)/shard_map/ppermute | solution.py:568
  96.0 1.8 %collective-permute-start.11 = (f32[16,56,128]{2,1,0:T(8,128)S(1)}, f32[16,56,128]{2,1,0:T(8,128)S(1)}, u32[]{:S(2)}, u32[]{:S(2)}) collective-permute-start(f32[16,56,128]{2,1,0:T(8,128)S(1)} %all-to-all-done.1.refs_9_), channel_id=1, source_target_pairs={{0,2},{2,0},{1,3},{3,1},{4,6},{6,4},{5,7},{7,5},{8,10},{10,8},{9,1... | collective-permute-start | bytes 1376264 | tf_op jit(solution)/shard_map/ppermute | solution.py:542

commit v12 on v10

--- a/solution.py
+++ b/solution.py
@@ -12,7 +12,7 @@
 
 H = 128
 LANES = 128
-CHUNK = 32
+CHUNK = 16
 WAYS = 2
 INFO = 8
 GRANT = 50176 << 10

time: 102 us -> 101 us (level)
  starting transfers between devices: 35.3 us -> 34 us
    all_to_all x2, waiting for transfers between devices: 10.8 us -> 12.5 us  [chip_exchange(): lax.all_to_all(chunks.reshape(-1, LANES), CHIPS, 0, 0, tiled=True)]
    all_to_all x2, starting transfers between devices: 19.8 us -> 18.4 us  [chip_exchange(): lax.all_to_all(chunks.reshape(-1, LANES), CHIPS, 0, 0, tiled=True)]
    ppermute x4, waiting for transfers between devices: 14.6 us -> 13.6 us  [to_corners(): got.append(lax.ppermute(band, (*WIDE, 'narrow'), pairs))]
where the time goes in v12:
time: 101 us; the launch traced here: 100 us
  starting transfers between devices  34 us (34%)
  Pallas kernels  29.6 us (29%)
  waiting for transfers between devices  29.6 us (29%)
  local copies, waits for them, and re-layouts  3.83 us (4%)
  other arithmetic  1.83 us (2%)
  between operations  1.44 us (1%)
    pallas_call x1, Pallas kernels, positions_call(): pl.pallas_call(functools.partial(positions_kernel, sides), out_shape=(sha...  22.4 us
    all_to_all x2, starting transfers between devices, chip_exchange(): lax.all_to_all(chunks.reshape(-1, LANES), CHIPS, 0, 0, tiled=True)  18.4 us
    ppermute x4, waiting for transfers between devices, to_corners(): got.append(lax.ppermute(band, (*WIDE, 'narrow'), pairs))  13.6 us
    all_to_all x2, waiting for transfers between devices, chip_exchange(): lax.all_to_all(chunks.reshape(-1, LANES), CHIPS, 0, 0, tiled=True)  12.5 us
    ppermute x8, starting transfers between devices, swap(): return lax.ppermute(x, axis, pairs)  9.27 us
    ppermute x4, starting transfers between devices, to_corners(): got.append(lax.ppermute(band, (*WIDE, 'narrow'), pairs))  6.41 us
    pallas_call x1, Pallas kernels, update_call(): pl.pallas_call(functools.partial(update_kernel, sides), out_shape=(jax.Sh...  3.71 us
    ppermute x8, waiting for transfers between devices, swap(): return lax.ppermute(x, axis, pairs)  3.54 us
  transfers between devices with their start and end apart: 14, of which 6 were waited for; matrix products, arithmetic and copies ran while one was open for 1% of the time, Pallas kernels for 3%

profile of v12, /device:TPU:0, one launch (start us, length us, event | category | flops | bytes accessed | tf_op | source)
XLA Modules:
  0.0 100.3 jit_solution(4581965232339358099)
XLA Ops:
  1.3 0.7 concatenate.9.place.refs_0_
  2.0 0.0 copy-start
  2.0 1.2 %copy-done = f32[2,256,512]{2,1,0:T(8,128)S(1)} copy-done((f32[2,256,512]{2,1,0:T(8,128)S(1)}, f32[2,256,512]{2,1,0:T(8,128)}, u32[]{:S(2)}) %copy-start) | copy-done | bytes 1048600
  3.3 0.8 pack.1
  4.0 0.7 collective-permute-start.1
  4.7 4.3 %collective-permute-start.4 = (f32[2,136,512]{2,1,0:T(8,128)S(1)}, f32[2,136,512]{2,1,0:T(8,128)S(1)}, u32[]{:S(2)}, u32[]{:S(2)}) collective-permute-start(f32[2,136,512]{2,1,0:T(8,128)S(1)} %get-tuple-element.25), channel_id=1, source_target_pairs={{0,2},{2,0},{1,3},{3,1},{4,6},{6,4},{5,7},{7,5},{8,10},{10,8},{9,1... | collective-permute-start | bytes 1671176 | tf_op jit(solution)/shard_map/ppermute | solution.py:538
  9.1 1.5 %collective-permute-start.2 = (f32[2,264,128]{2,1,0:T(8,128)S(1)}, f32[2,264,128]{2,1,0:T(8,128)S(1)}, u32[]{:S(2)}, u32[]{:S(2)}) collective-permute-start(f32[2,264,128]{2,1,0:T(8,128)S(1)} %get-tuple-element.23), channel_id=1, source_target_pairs={{0,1},{1,0},{2,3},{3,2},{4,5},{5,4},{6,7},{7,6},{8,9},{9,8},{10,11... | collective-permute-start | bytes 811016 | tf_op jit(solution)/shard_map/ppermute | solution.py:538
  10.6 0.7 collective-permute-start
  11.3 4.0 %collective-permute-start.3 = (f32[2,136,128]{2,1,0:T(8,128)S(1)}, f32[2,136,128]{2,1,0:T(8,128)S(1)}, u32[]{:S(2)}, u32[]{:S(2)}) collective-permute-start(f32[2,136,128]{2,1,0:T(8,128)S(1)} %get-tuple-element.24), channel_id=1, source_target_pairs={{0,3},{2,1},{1,2},{3,0},{4,7},{6,5},{5,6},{7,4},{8,11},{10,9},{9,1... | collective-permute-start | bytes 417800 | tf_op jit(solution)/shard_map/ppermute | solution.py:564
  15.3 0.0 collective-permute-done.refs_2_
  15.3 5.8 %collective-permute-done.3.refs_5_ = f32[2,136,128]{2,1,0:T(8,128)S(1)} collective-permute-done((f32[2,136,128]{2,1,0:T(8,128)S(1)}, f32[2,136,128]{2,1,0:T(8,128)S(1)}, u32[]{:S(2)}, u32[]{:S(2)}) %collective-permute-start.3) | collective-permute-done | bytes 139296 | tf_op jit(solution)/shard_map/ppermute | solution.py:564
  21.1 0.0 collective-permute-done.2.refs_4_
  21.1 0.0 collective-permute-done.1.refs_3_
  21.1 0.0 collective-permute-done.4.refs_6_
  21.1 0.0 copy-start.1
  21.2 1.0 %copy-done.1 = f32[2,256,256]{2,1,0:T(8,128)S(1)} copy-done((f32[2,256,256]{2,1,0:T(8,128)S(1)}, f32[2,256,256]{2,1,0:T(8,128)}, u32[]{:S(2)}) %copy-start.1) | copy-done | bytes 524312
  22.2 22.4 %positions.1 = (f32[2,256,512]{2,1,0:T(8,128)}, f32[2,128,512]{2,1,0:T(8,128)}, f32[2,128,512]{2,1,0:T(8,128)S(1)}, f32[5,8,128]{2,1,0:T(8,128)S(1)}, f32[2,256,...) custom-call(s32[19]{0:T(128)S(1)} %concatenate.9.place.refs_0_, ...), custom_call_target="tpu_custom_call" | custom-call | flops 12884901888 | bytes 16000000 | tf_op jit(solution)/shard_map/positions/pallas_call | solution.py:425
  44.6 0.0 copy-start.2
  44.6 0.1 collective-permute-start.5
  44.7 1.7 %collective-permute-done.5 = f32[768,128]{1,0:T(8,128)S(1)} collective-permute-done((f32[768,128]{1,0:T(8,128)S(1)}, f32[768,128]{1,0:T(8,128)S(1)}, u32[]{:S(2)}, u32[]{:S(2)}) %collective-permute-start.5) | collective-permute-done | bytes 393248 | tf_op jit(solution)/shard_map/ppermute | solution.py:538
  46.4 0.8 add.7
  47.2 8.6 %all-to-all-start = ((f32[16,48,128]{2,1,0:T(8,128)}), f32[16,48,128]{2,1,0:T(8,128)}, u32[]{:S(2)}, u32[]{:S(2)}) async-start(f32[16,48,128]{2,1,0:T(8,128)} %bitcast.7), calls=%async_computation | async-start | bytes 786432 | tf_op jit(solution)/shard_map/all_to_all | solution.py:569
  55.8 0.1 collective-permute-start.6
  56.0 0.7 collective-permute-start.7
  56.7 1.8 %collective-permute-start.8 = (f32[2,256,128]{2,1,0:T(8,128)S(1)}, f32[2,256,128]{2,1,0:T(8,128)S(1)}, u32[]{:S(2)}, u32[]{:S(2)}) collective-permute-start(f32[2,256,128]{2,1,0:T(8,128)S(1)} %get-tuple-element.34), channel_id=1, source_target_pairs={{0,1},{1,0},{2,3},{3,2},{4,5},{5,4},{6,7},{7,6},{8,9},{9,8},{10,11... | collective-permute-start | bytes 786440 | tf_op jit(solution)/shard_map/ppermute | solution.py:538
  58.5 0.0 copy-done.2
  58.5 2.7 %cover.1 = (f32[256,512]{1,0:T(8,128)S(1)}, f32[8,128]{1,0:T(8,128)S(1)}) custom-call(s32[19]{0:T(128)S(1)} %concatenate.9.place.refs_0_, s32[6,32]{1,0:T(8,128)S(1)} %fusion.1.info, f32[2,256,256]{2,1,0:T(8,128)S(1)} %copy-done.2), custom_call_target="tpu_custom_call" | custom-call | flops 4000000 | bytes 8000000 | tf_op jit(solution)/shard_map/cover/pallas_call | solution.py:119
  61.2 7.8 %all-to-all-done = f32[16,48,128]{2,1,0:T(8,128)} async-done(((f32[16,48,128]{2,1,0:T(8,128)}), f32[16,48,128]{2,1,0:T(8,128)}, u32[]{:S(2)}, u32[]{:S(2)}) %all-to-all-start) | async-done | bytes 393248 | tf_op jit(solution)/shard_map/all_to_all | solution.py:569
  69.0 1.0 %reduce_sum.9 = f32[48,128]{1,0:T(8,128)S(1)} reduce(f32[16,48,128]{2,1,0:T(8,128)} %all-to-all-done, f32[]{:T(128)} %constant.19.clone.1), dimensions={0}, to_apply=%region_0.0 | reduce | flops 92160 | bytes 417796 | tf_op jit(solution)/shard_map/reduce_sum | solution.py:605
  70.0 0.0 collective-permute-done.8.refs_6_
  70.1 0.0 collective-permute-done.6.refs_4_
  70.1 0.0 collective-permute-done.7.refs_5_
  70.1 0.8 broadcast_in_dim.3
  70.9 9.7 %all-to-all-start.1 = ((f32[16,56,128]{2,1,0:T(8,128)}), f32[16,56,128]{2,1,0:T(8,128)S(1)}, u32[]{:S(2)}, u32[]{:S(2)}) async-start(f32[16,56,128]{2,1,0:T(8,128)} %broadcast_in_dim.3), calls=%async_computation.1 | async-start | bytes 917504 | tf_op jit(solution)/shard_map/all_to_all | solution.py:569
  80.6 1.1 %collective-permute-start.9 = (f32[2,128,128]{2,1,0:T(8,128)}, f32[2,128,128]{2,1,0:T(8,128)S(1)}, u32[]{:S(2)}, u32[]{:S(2)}) collective-permute-start(f32[2,128,128]{2,1,0:T(8,128)} %get-tuple-element.35), channel_id=1, source_target_pairs={{0,3},{2,1},{1,2},{3,0},{4,7},{6,5},{5,6},{7,4},{8,11},{10,9},{9,1... | collective-permute-start | bytes 393224 | tf_op jit(solution)/shard_map/ppermute | solution.py:564
  81.7 0.7 collective-permute-start.10
  82.3 7.7 %collective-permute-done.9.refs_7_ = f32[2,128,128]{2,1,0:T(8,128)S(1)} collective-permute-done((f32[2,128,128]{2,1,0:T(8,128)}, f32[2,128,128]{2,1,0:T(8,128)S(1)}, u32[]{:S(2)}, u32[]{:S(2)}) %collective-permute-start.9) | collective-permute-done | bytes 131104 | tf_op jit(solution)/shard_map/ppermute | solution.py:564
  90.0 0.0 collective-permute-done.10.refs_8_
  90.0 4.7 %all-to-all-done.1.refs_9_ = f32[16,56,128]{2,1,0:T(8,128)S(1)} async-done(((f32[16,56,128]{2,1,0:T(8,128)}), f32[16,56,128]{2,1,0:T(8,128)S(1)}, u32[]{:S(2)}, u32[]{:S(2)}) %all-to-all-start.1) | async-done | bytes 458784 | tf_op jit(solution)/shard_map/all_to_all | solution.py:569
  94.7 0.0 collective-permute-start.11
  94.7 1.8 %collective-permute-done.11.refs_10_ = f32[16,56,128]{2,1,0:T(8,128)S(1)} collective-permute-done((f32[16,56,128]{2,1,0:T(8,128)S(1)}, f32[16,56,128]{2,1,0:T(8,128)S(1)}, u32[]{:S(2)}, u32[]{:S(2)}) %collective-permute-start.11) | collective-permute-done | bytes 458784 | tf_op jit(solution)/shard_map/ppermute | solution.py:538
  96.5 3.7 %update.1 = (f32[2,256,512]{2,1,0:T(8,128)}, f32[2,256,256]{2,1,0:T(8,128)}) custom-call(s32[19]{0:T(128)S(1)} %concatenate.9.place.refs_0_, f32[2,256,512]{2,1,0:T(8,128)} %refs_1_.3, f32[2,256,512]{2,1,0:T(8,128)} %get-tuple-element.26.refs_2_, f32[256,512]{1,0:T(8,128)S(1)} %get-tuple-element.31.refs_3_, ...), custom_call_target="tpu_custom_call" | custom-call | tf_op jit(solution)/shard_map/update/pallas_call | solution.py:518
  (4 shorter events, 0.0 us)
Async XLA Ops:
  2.0 1.2 %copy-start = (f32[2,256,512]{2,1,0:T(8,128)S(1)}, f32[2,256,512]{2,1,0:T(8,128)}, u32[]{:S(2)}) copy-start(f32[2,256,512]{2,1,0:T(8,128)} %refs_1_.3) | copy-start | bytes 3145732
  4.0 17.1 %collective-permute-start.1 = (f32[2,136,512]{2,1,0:T(8,128)S(1)}, f32[2,136,512]{2,1,0:T(8,128)S(1)}, u32[]{:S(2)}, u32[]{:S(2)}) collective-permute-start(f32[2,136,512]{2,1,0:T(8,128)S(1)} %get-tuple-element.22), channel_id=1, source_target_pairs={{2,4},{4,2},{6,8},{8,6},{10,12},{12,10},{14,16},{16,14},{18,20},{2... | collective-permute-start | bytes 1671176 | tf_op jit(solution)/shard_map/ppermute | solution.py:538
  4.7 16.4 %collective-permute-start.4 = (f32[2,136,512]{2,1,0:T(8,128)S(1)}, f32[2,136,512]{2,1,0:T(8,128)S(1)}, u32[]{:S(2)}, u32[]{:S(2)}) collective-permute-start(f32[2,136,512]{2,1,0:T(8,128)S(1)} %get-tuple-element.25), channel_id=1, source_target_pairs={{0,2},{2,0},{1,3},{3,1},{4,6},{6,4},{5,7},{7,5},{8,10},{10,8},{9,1... | collective-permute-start | bytes 1671176 | tf_op jit(solution)/shard_map/ppermute | solution.py:538
  9.1 12.1 %collective-permute-start.2 = (f32[2,264,128]{2,1,0:T(8,128)S(1)}, f32[2,264,128]{2,1,0:T(8,128)S(1)}, u32[]{:S(2)}, u32[]{:S(2)}) collective-permute-start(f32[2,264,128]{2,1,0:T(8,128)S(1)} %get-tuple-element.23), channel_id=1, source_target_pairs={{0,1},{1,0},{2,3},{3,2},{4,5},{5,4},{6,7},{7,6},{8,9},{9,8},{10,11... | collective-permute-start | bytes 811016 | tf_op jit(solution)/shard_map/ppermute | solution.py:538
  10.6 4.7 %collective-permute-start = (f32[2,136,128]{2,1,0:T(8,128)S(1)}, f32[2,136,128]{2,1,0:T(8,128)S(1)}, u32[]{:S(2)}, u32[]{:S(2)}) collective-permute-start(f32[2,136,128]{2,1,0:T(8,128)S(1)} %get-tuple-element.21), channel_id=1, source_target_pairs={{2,5},{4,3},{3,4},{5,2},{6,9},{8,7},{7,8},{9,6},{10,13},{12,11},{1... | collective-permute-start | bytes 417800 | tf_op jit(solution)/shard_map/ppermute | solution.py:564
  11.3 9.9 %collective-permute-start.3 = (f32[2,136,128]{2,1,0:T(8,128)S(1)}, f32[2,136,128]{2,1,0:T(8,128)S(1)}, u32[]{:S(2)}, u32[]{:S(2)}) collective-permute-start(f32[2,136,128]{2,1,0:T(8,128)S(1)} %get-tuple-element.24), channel_id=1, source_target_pairs={{0,3},{2,1},{1,2},{3,0},{4,7},{6,5},{5,6},{7,4},{8,11},{10,9},{9,1... | collective-permute-start | bytes 417800 | tf_op jit(solution)/shard_map/ppermute | solution.py:564
  21.1 1.0 %copy-start.1 = (f32[2,256,256]{2,1,0:T(8,128)S(1)}, f32[2,256,256]{2,1,0:T(8,128)}, u32[]{:S(2)}) copy-start(f32[2,256,256]{2,1,0:T(8,128)} %refs_11_.1) | copy-start | bytes 1572868
  44.6 13.9 %copy-start.2 = (f32[2,256,256]{2,1,0:T(8,128)S(1)}, f32[2,256,256]{2,1,0:T(8,128)}, u32[]{:S(2)}) copy-start(f32[2,256,256]{2,1,0:T(8,128)} %refs_11_.1) | copy-start | bytes 1572868
  44.6 1.8 %collective-permute-start.5 = (f32[768,128]{1,0:T(8,128)S(1)}, f32[768,128]{1,0:T(8,128)S(1)}, u32[]{:S(2)}, u32[]{:S(2)}) collective-permute-start(f32[768,128]{1,0:T(8,128)S(1)} %get-tuple-element.29), channel_id=1, source_target_pairs={{0,2},{2,0},{1,3},{3,1},{4,6},{6,4},{5,7},{7,5},{8,10},{10,8},{9,1... | collective-permute-start | bytes 1179656 | tf_op jit(solution)/shard_map/ppermute | solution.py:538
  47.2 21.8 %all-to-all-start = ((f32[16,48,128]{2,1,0:T(8,128)}), f32[16,48,128]{2,1,0:T(8,128)}, u32[]{:S(2)}, u32[]{:S(2)}) async-start(f32[16,48,128]{2,1,0:T(8,128)} %bitcast.7), calls=%async_computation | async-start | bytes 786432 | tf_op jit(solution)/shard_map/all_to_all | solution.py:569
  55.8 14.2 %collective-permute-start.6 = (f32[2,128,512]{2,1,0:T(8,128)}, f32[2,128,512]{2,1,0:T(8,128)S(1)}, u32[]{:S(2)}, u32[]{:S(2)}) collective-permute-start(f32[2,128,512]{2,1,0:T(8,128)} %get-tuple-element.32), channel_id=1, source_target_pairs={{0,2},{2,0},{1,3},{3,1},{4,6},{6,4},{5,7},{7,5},{8,10},{10,8},{9,1... | collective-permute-start | bytes 1572872 | tf_op jit(solution)/shard_map/ppermute | solution.py:538
  56.0 14.1 %collective-permute-start.7 = (f32[2,128,512]{2,1,0:T(8,128)S(1)}, f32[2,128,512]{2,1,0:T(8,128)S(1)}, u32[]{:S(2)}, u32[]{:S(2)}) collective-permute-start(f32[2,128,512]{2,1,0:T(8,128)S(1)} %get-tuple-element.33), channel_id=1, source_target_pairs={{2,4},{4,2},{6,8},{8,6},{10,12},{12,10},{14,16},{16,14},{18,20},{2... | collective-permute-start | bytes 1572872 | tf_op jit(solution)/shard_map/ppermute | solution.py:538
  56.7 13.4 %collective-permute-start.8 = (f32[2,256,128]{2,1,0:T(8,128)S(1)}, f32[2,256,128]{2,1,0:T(8,128)S(1)}, u32[]{:S(2)}, u32[]{:S(2)}) collective-permute-start(f32[2,256,128]{2,1,0:T(8,128)S(1)} %get-tuple-element.34), channel_id=1, source_target_pairs={{0,1},{1,0},{2,3},{3,2},{4,5},{5,4},{6,7},{7,6},{8,9},{9,8},{10,11... | collective-permute-start | bytes 786440 | tf_op jit(solution)/shard_map/ppermute | solution.py:538
  70.9 23.9 %all-to-all-start.1 = ((f32[16,56,128]{2,1,0:T(8,128)}), f32[16,56,128]{2,1,0:T(8,128)S(1)}, u32[]{:S(2)}, u32[]{:S(2)}) async-start(f32[16,56,128]{2,1,0:T(8,128)} %broadcast_in_dim.3), calls=%async_computation.1 | async-start | bytes 917504 | tf_op jit(solution)/shard_map/all_to_all | solution.py:569
  80.6 9.4 %collective-permute-start.9 = (f32[2,128,128]{2,1,0:T(8,128)}, f32[2,128,128]{2,1,0:T(8,128)S(1)}, u32[]{:S(2)}, u32[]{:S(2)}) collective-permute-start(f32[2,128,128]{2,1,0:T(8,128)} %get-tuple-element.35), channel_id=1, source_target_pairs={{0,3},{2,1},{1,2},{3,0},{4,7},{6,5},{5,6},{7,4},{8,11},{10,9},{9,1... | collective-permute-start | bytes 393224 | tf_op jit(solution)/shard_map/ppermute | solution.py:564
  81.7 8.4 %collective-permute-start.10 = (f32[2,128,128]{2,1,0:T(8,128)S(1)}, f32[2,128,128]{2,1,0:T(8,128)S(1)}, u32[]{:S(2)}, u32[]{:S(2)}) collective-permute-start(f32[2,128,128]{2,1,0:T(8,128)S(1)} %get-tuple-element.36), channel_id=1, source_target_pairs={{2,5},{4,3},{3,4},{5,2},{6,9},{8,7},{7,8},{9,6},{10,13},{12,11},{1... | collective-permute-start | bytes 393224 | tf_op jit(solution)/shard_map/ppermute | solution.py:564
  94.7 1.8 %collective-permute-start.11 = (f32[16,56,128]{2,1,0:T(8,128)S(1)}, f32[16,56,128]{2,1,0:T(8,128)S(1)}, u32[]{:S(2)}, u32[]{:S(2)}) collective-permute-start(f32[16,56,128]{2,1,0:T(8,128)S(1)} %all-to-all-done.1.refs_9_), channel_id=1, source_target_pairs={{0,2},{2,0},{1,3},{3,1},{4,6},{6,4},{5,7},{7,5},{8,10},{10,8},{9,1... | collective-permute-start | bytes 1376264 | tf_op jit(solution)/shard_map/ppermute | solution.py:538
